TPU v7x, 32 devices: a whole 2x2x4 slice. The times are simulated.
32 devices in a mesh: dp: 8 (over z, y), tensor: 4 (over x, core).
Axes of the slice: x: 2, y: 2, z: 4, core: 2. Of those that a mesh axis runs over, the one named last changes fastest.
Arguments:
- tokens: bfloat16 [1024, 2, 768], P(('dp', 'tensor')), may hold values from -6 to 6
- gain_attn: bfloat16 [768], P(('dp', 'tensor')), may hold values from 0.5 to 1.5
- gain_ffn: bfloat16 [768], P(('dp', 'tensor')), may hold values from 0.5 to 1.5
- w_qkv: bfloat16 [768, 3, 768], P('dp', None, 'tensor'), may hold values from -0.21875 to 0.21875
- w_rate: bfloat16 [768, 12], P('dp', 'tensor'), may hold values from -0.21875 to 0.21875
- w_out: bfloat16 [768, 768], P('tensor', 'dp'), may hold values from -0.21875 to 0.21875
- w_gate_up: bfloat16 [768, 2, 2048], P('dp', None, 'tensor'), may hold values from -0.21875 to 0.21875
- w_down: bfloat16 [2048, 768], P('tensor', 'dp'), may hold values from -0.25 to 0.25
- w_one: bfloat16 [12, 64, 256], P('tensor', None, 'dp'), may hold values from -0.75 to 0.75
- b_one: bfloat16 [12, 256], P('tensor', 'dp'), may hold values from -3 to 3
- w_two: bfloat16 [12, 256, 64], P('tensor', 'dp'), may hold values from -0.375 to 0.375
- b_two: bfloat16 [12, 64], P('tensor', 'dp'), may hold values from -3 to 3
- norm_gain_inner: bfloat16 [12, 64], P('tensor', 'dp'), may hold values from 0.5 to 1.5
- norm_bias_inner: bfloat16 [12, 64], P('tensor', 'dp'), may hold values from -3 to 3
- cotangent: bfloat16 [1024, 2, 768], P(('dp', 'tensor')), may hold values from -6 to 6
Outputs:
- output: bfloat16 [1024, 2, 768], P(('dp', 'tensor'))
- input_grad: float32 [1024, 2, 768], P(('dp', 'tensor'))
- grad_gain_attn: float32 [768], P(('dp', 'tensor'))
- grad_gain_ffn: float32 [768], P(('dp', 'tensor'))
- grad_w_qkv: float32 [768, 3, 768], P('dp', None, 'tensor')
- grad_w_rate: float32 [768, 12], P('dp', 'tensor')
- grad_w_out: float32 [768, 768], P('tensor', 'dp')
- grad_w_gate_up: float32 [768, 2, 2048], P('dp', None, 'tensor')
- grad_w_down: float32 [2048, 768], P('tensor', 'dp')
- grad_w_one: float32 [12, 64, 256], P('tensor', None, 'dp')
- grad_b_one: float32 [12, 256], P('tensor', 'dp')
- grad_w_two: float32 [12, 256, 64], P('tensor', 'dp')
- grad_b_two: float32 [12, 64], P('tensor', 'dp')
- grad_norm_gain_inner: float32 [12, 64], P('tensor', 'dp')
- grad_norm_bias_inner: float32 [12, 64], P('tensor', 'dp')
All inputs are finite; a program needn't handle non-finite values.
Results may differ from a plain program's by a relative error of at most 0.025.
Values may be sent and summed in bfloat16 or wider, within the bound.
No kernel may reach another device: no remote copies, remote signals or barrier semaphores. Data moves between devices by JAX's collectives and lax.ppermute only.
A program may use at most 64 MiB of HBM per device.

v0:
```python
import jax
import jax.numpy as jnp
from jax import lax
from jax.sharding import PartitionSpec as P

HEAD_DIM = 64
INNER = 256
MINI = 16


epsilon = 1e-05
inner_epsilon = 1e-06
highest = lax.Precision.HIGHEST
inner_rate = 0.5
root_half = 0.7071067811865476
normal_peak = 0.3989422804014327


def from_behind(value, axis, steps):
    count = lax.axis_size(axis)
    initial, last = (max(0, -steps), min(count, count - steps))
    return lax.ppermute(value, axis, [(source, source + steps) for source in range(initial, last)])


def gelu_exact(values):
    return 0.5 * values * (1.0 + lax.erf(values * root_half))


def gelu_slope(values):
    return (
        0.5 * (1.0 + lax.erf(values * root_half))
        + values * jnp.exp(-0.5 * values * values) * normal_peak
    )


def layer_norm(values, scaling):
    average = jnp.mean(values, axis=-1, keepdims=True)
    centred = values - average
    spread = jnp.mean(centred * centred, axis=-1, keepdims=True)
    return centred * lax.rsqrt(spread + epsilon) * scaling


def inner_norm_parts(values, norm_gain, norm_bias):
    average = jnp.mean(values, axis=-1, keepdims=True)
    centred = values - average
    inverse = lax.rsqrt(jnp.mean(centred * centred, axis=-1, keepdims=True) + inner_epsilon)
    normal = centred * inverse
    return (normal, inverse, normal * norm_gain + norm_bias)


def inner_step(norm_pair, state, batch):
    first_w, first_b, second_w, second_b = state
    norm_gain, norm_bias = norm_pair
    queries, keys_in, targets, step_rates = batch
    key_pre = jnp.einsum("mhe,hei->mhi", keys_in, first_w, precision=highest) + first_b
    activity = gelu_exact(key_pre)
    key_res = jnp.einsum("mhi,hie->mhe", activity, second_w, precision=highest) + second_b
    normal, inverse, key_normed = inner_norm_parts(key_res, norm_gain, norm_bias)
    errors = keys_in + key_normed - targets
    scaled = errors * step_rates[:, :, None] * norm_gain
    back_res = inverse * (
        scaled
        - jnp.mean(scaled, axis=-1, keepdims=True)
        - normal * jnp.mean(scaled * normal, axis=-1, keepdims=True)
    )
    back_act = jnp.einsum("mhe,hie->mhi", back_res, second_w, precision=highest)
    back_pre = back_act * gelu_slope(key_pre)
    count = queries.shape[0]
    causal = (
        lax.broadcasted_iota(jnp.int32, (count, count), 0)
        >= lax.broadcasted_iota(jnp.int32, (count, count), 1)
    ).astype(jnp.float32)
    first_mix = (jnp.einsum("mhe,nhe->hmn", queries, keys_in, precision=highest) + 1.0) * causal
    query_pre = (
        jnp.einsum("mhe,hei->mhi", queries, first_w, precision=highest)
        + first_b
        - jnp.einsum("hmn,nhi->mhi", first_mix, back_pre, precision=highest)
    )
    hidden = gelu_exact(query_pre)
    second_mix = (jnp.einsum("mhi,nhi->hmn", hidden, activity, precision=highest) + 1.0) * causal
    query_res = (
        jnp.einsum("mhi,hie->mhe", hidden, second_w, precision=highest)
        + second_b
        - jnp.einsum("hmn,nhe->mhe", second_mix, back_res, precision=highest)
    )
    outputs = queries + inner_norm_parts(query_res, norm_gain, norm_bias)[2]
    grad_second = jnp.einsum("mhi,mhe->hie", activity, back_res, precision=highest)
    grad_first = jnp.einsum("mhe,mhi->hei", keys_in, back_pre, precision=highest)
    updated = (
        first_w - grad_first,
        first_b - jnp.sum(back_pre, axis=0),
        second_w - grad_second,
        second_b - jnp.sum(back_res, axis=0),
    )
    return (updated, outputs)


def run_group(state, norm_pair, queries, keys_in, targets, step_rates):
    block_count = queries.shape[0] // MINI
    shaped = tuple(
        (
            member.reshape((block_count, MINI) + member.shape[1:])
            for member in (queries, keys_in, targets, step_rates)
        )
    )

    def one_step(carry, batch):
        return inner_step(norm_pair, carry, batch)

    final, outputs = lax.scan(jax.checkpoint(one_step), state, shaped)
    return (final, outputs.reshape(queries.shape))


def pack_state(first_w, first_b, second_w, second_b):
    head_count = first_w.shape[0]
    return jnp.concatenate(
        [first_w.reshape(head_count, -1), first_b, second_w.reshape(head_count, -1), second_b],
        axis=1,
    )


def unpack_state(packed):
    head_count = packed.shape[0]
    first_end = HEAD_DIM * INNER
    second_end = first_end + INNER
    third_end = second_end + INNER * HEAD_DIM
    return (
        packed[:, :first_end].reshape(head_count, HEAD_DIM, INNER),
        packed[:, first_end:second_end],
        packed[:, second_end:third_end].reshape(head_count, INNER, HEAD_DIM),
        packed[:, third_end:],
    )


def packed_group(packed, norm_gain, norm_bias, queries, keys_in, targets, step_rates):
    final, outputs = run_group(
        unpack_state(packed), (norm_gain, norm_bias), queries, keys_in, targets, step_rates
    )
    return (pack_state(final[0], final[1], final[2], final[3]), outputs)


def gather_rows(values):
    return lax.all_gather(values, "tensor", axis=0, tiled=True)


def gather_grads(values):
    return lax.all_gather(values, "tensor", axis=0, tiled=True)


def branch_sum(activations, matrix):

    def block_term(first_row, row_count):
        return jnp.einsum("csk,kd->csd", activations, matrix, preferred_element_type=jnp.float32)

    return lax.psum_scatter(
        block_term(
            jnp.int32(0), activations.shape[0] // lax.axis_size("tensor") * lax.axis_size("tensor")
        ).astype(jnp.bfloat16),
        "tensor",
        scatter_dimension=0,
        tiled=True,
    ).astype(jnp.float32)


def back_sum(block_term, local_rows):
    return lax.psum_scatter(
        block_term(jnp.int32(0), local_rows * lax.axis_size("tensor")).astype(jnp.bfloat16),
        "tensor",
        scatter_dimension=0,
        tiled=True,
    ).astype(jnp.float32)


def local(
    tokens,
    gain_attn,
    gain_ffn,
    w_qkv,
    w_rate,
    w_out,
    w_gate_up,
    w_down,
    w_one,
    b_one,
    w_two,
    b_two,
    norm_gain_inner,
    norm_bias_inner,
    cotangent,
):
    gains_full = (
        lax.all_gather(gain_attn, ("dp", "tensor"), axis=0, tiled=True),
        lax.all_gather(gain_ffn, ("dp", "tensor"), axis=0, tiled=True),
    )
    scale_attn = gains_full[0].astype(jnp.float32)
    scale_ffn = gains_full[1].astype(jnp.float32)
    gathered = (
        lax.all_gather(w_qkv, "dp", axis=0, tiled=True),
        lax.all_gather(w_rate, "dp", axis=0, tiled=True),
        lax.all_gather(w_out, "dp", axis=1, tiled=True),
        lax.all_gather(w_gate_up, "dp", axis=0, tiled=True),
        lax.all_gather(w_down, "dp", axis=1, tiled=True),
        lax.all_gather(w_one, "dp", axis=2, tiled=True),
        lax.all_gather(b_one, "dp", axis=1, tiled=True),
        lax.all_gather(w_two, "dp", axis=1, tiled=True),
        lax.all_gather(b_two, "dp", axis=1, tiled=True),
        lax.all_gather(norm_gain_inner, "dp", axis=1, tiled=True),
        lax.all_gather(norm_bias_inner, "dp", axis=1, tiled=True),
    )
    qkv_full, rate_full, out_full, gate_up_full, down_full = (
        gathered[0],
        gathered[1],
        gathered[2],
        gathered[3],
        gathered[4],
    )
    init_state = pack_state(
        gathered[5].astype(jnp.float32),
        gathered[6].astype(jnp.float32),
        gathered[7].astype(jnp.float32),
        gathered[8].astype(jnp.float32),
    )
    inner_gain = gathered[9].astype(jnp.float32)
    inner_bias = gathered[10].astype(jnp.float32)
    local_rows, seq_count, width = tokens.shape
    inputs = tokens.astype(jnp.float32)
    normed_attn = layer_norm(inputs, scale_attn).astype(jnp.bfloat16)
    attn_rows = gather_rows(normed_attn)
    group_len = attn_rows.shape[0]
    local_width = qkv_full.shape[2]
    head_count = local_width // HEAD_DIM
    qkv_matrix = qkv_full.reshape(width, 3 * local_width)
    projected = jnp.einsum("csd,dk->csk", attn_rows, qkv_matrix, preferred_element_type=jnp.float32)
    rate_logit = jnp.einsum("csd,dh->csh", attn_rows, rate_full, preferred_element_type=jnp.float32)
    rate_scale = inner_rate / (MINI * HEAD_DIM)
    step_rates, rate_pull = jax.vjp(lambda logits: jax.nn.sigmoid(logits) * rate_scale, rate_logit)
    head_shape = (group_len, seq_count, head_count, HEAD_DIM)
    seq_query = projected[:, :, :local_width].reshape(head_shape).transpose(1, 0, 2, 3)
    seq_keys = (
        projected[:, :, local_width : 2 * local_width].reshape(head_shape).transpose(1, 0, 2, 3)
    )
    seq_values = projected[:, :, 2 * local_width :].reshape(head_shape).transpose(1, 0, 2, 3)
    seq_rates = step_rates.transpose(1, 0, 2)
    device_count = lax.axis_size("dp")
    device_rank = lax.axis_index("dp")
    turn_count = device_count + seq_count - 1

    def forward_turn(turn_index, carry):
        arriving, entries, outputs = carry
        seq_index = turn_index - device_rank
        active = (seq_index >= 0) & (seq_index < seq_count)
        chosen = jnp.clip(seq_index, 0, seq_count - 1)
        entry = jnp.where(device_rank == 0, init_state, arriving)
        leaving, produced = packed_group(
            entry,
            inner_gain,
            inner_bias,
            seq_query[chosen],
            seq_keys[chosen],
            seq_values[chosen],
            seq_rates[chosen],
        )
        entries = entries.at[chosen].set(jnp.where(active, entry, entries[chosen]))
        outputs = outputs.at[chosen].set(jnp.where(active, produced, outputs[chosen]))
        arriving = from_behind(leaving, "dp", 1)
        return (arriving, entries, outputs)

    start_carry = (
        jnp.zeros_like(init_state),
        jnp.zeros((seq_count,) + init_state.shape, jnp.float32),
        jnp.zeros(seq_query.shape, jnp.float32),
    )
    forward_done = lax.fori_loop(0, turn_count, forward_turn, start_carry)
    entries = forward_done[1]
    inner_out = forward_done[2].transpose(1, 0, 2, 3)
    head_normed_full, head_pull = jax.vjp(lambda values: layer_norm(values, 1.0), inner_out)
    head_normed = head_normed_full.astype(jnp.bfloat16).reshape(group_len, seq_count, local_width)
    mixed = inputs + branch_sum(head_normed, out_full)
    normed_ffn = layer_norm(mixed, scale_ffn).astype(jnp.bfloat16)
    ffn_rows = gather_rows(normed_ffn)
    gate_up = jnp.einsum(
        "csd,dgf->csgf", ffn_rows, gate_up_full, preferred_element_type=jnp.float32
    )
    swiglu_full, swiglu_pull = jax.vjp(
        lambda gates, ups: jax.nn.silu(gates) * ups, gate_up[:, :, 0], gate_up[:, :, 1]
    )
    swiglu = swiglu_full.astype(jnp.bfloat16)
    result = (mixed + branch_sum(swiglu, down_full)).astype(jnp.bfloat16)
    grad_rows_out = gather_grads(cotangent)
    grad_down = jnp.einsum("csf,csd->fd", swiglu, grad_rows_out, preferred_element_type=jnp.float32)
    back_swiglu = jnp.einsum(
        "csd,fd->csf", grad_rows_out, down_full, preferred_element_type=jnp.float32
    )
    back_gate, back_up = swiglu_pull(back_swiglu)
    back_gate_up = jnp.stack([back_gate, back_up], axis=2).astype(jnp.bfloat16)
    grad_gate_up = jnp.einsum(
        "csd,csgf->dgf", ffn_rows, back_gate_up, preferred_element_type=jnp.float32
    )

    def ffn_term(first_row, row_count):
        return jnp.einsum(
            "csgf,dgf->csd", back_gate_up, gate_up_full, preferred_element_type=jnp.float32
        )

    back_normed_ffn = back_sum(ffn_term, local_rows)
    ffn_norm_pull = jax.vjp(layer_norm, mixed, scale_ffn)[1]
    back_mixed_part, grad_gain_ffn = ffn_norm_pull(back_normed_ffn)
    back_mixed = cotangent.astype(jnp.float32) + back_mixed_part
    attn_grads = gather_grads(back_mixed.astype(jnp.bfloat16))
    grad_out_w = jnp.einsum(
        "csk,csd->kd", head_normed, attn_grads, preferred_element_type=jnp.float32
    )
    back_head = jnp.einsum(
        "csd,kd->csk", attn_grads, out_full, preferred_element_type=jnp.float32
    ).reshape(head_shape)
    back_seq = head_pull(back_head)[0].transpose(1, 0, 2, 3)

    def backward_turn(turn_index, carry):
        (
            arriving,
            back_query,
            back_keys,
            back_values,
            back_rates,
            back_init,
            gain_total,
            bias_total,
        ) = carry
        seq_index = turn_index - (device_count - 1 - device_rank)
        active = (seq_index >= 0) & (seq_index < seq_count)
        chosen = jnp.clip(seq_index, 0, seq_count - 1)
        group_pull = jax.vjp(
            packed_group,
            entries[chosen],
            inner_gain,
            inner_bias,
            seq_query[chosen],
            seq_keys[chosen],
            seq_values[chosen],
            seq_rates[chosen],
        )[1]
        pulled = group_pull((arriving, back_seq[chosen]))
        back_query = back_query.at[chosen].set(jnp.where(active, pulled[3], back_query[chosen]))
        back_keys = back_keys.at[chosen].set(jnp.where(active, pulled[4], back_keys[chosen]))
        back_values = back_values.at[chosen].set(jnp.where(active, pulled[5], back_values[chosen]))
        back_rates = back_rates.at[chosen].set(jnp.where(active, pulled[6], back_rates[chosen]))
        back_init = back_init + jnp.where(active & (device_rank == 0), pulled[0], 0.0)
        gain_total = gain_total + jnp.where(active, pulled[1], 0.0)
        bias_total = bias_total + jnp.where(active, pulled[2], 0.0)
        arriving = from_behind(pulled[0].astype(jnp.bfloat16), "dp", -1).astype(jnp.float32)
        return (
            arriving,
            back_query,
            back_keys,
            back_values,
            back_rates,
            back_init,
            gain_total,
            bias_total,
        )

    back_carry = (
        jnp.zeros_like(init_state),
        jnp.zeros(seq_query.shape, jnp.float32),
        jnp.zeros(seq_query.shape, jnp.float32),
        jnp.zeros(seq_query.shape, jnp.float32),
        jnp.zeros(seq_rates.shape, jnp.float32),
        jnp.zeros_like(init_state),
        jnp.zeros_like(inner_gain),
        jnp.zeros_like(inner_bias),
    )
    backward_done = lax.fori_loop(0, turn_count, backward_turn, back_carry)
    flat_shape = (group_len, seq_count, local_width)
    back_projected = jnp.concatenate(
        [
            backward_done[1].transpose(1, 0, 2, 3).reshape(flat_shape),
            backward_done[2].transpose(1, 0, 2, 3).reshape(flat_shape),
            backward_done[3].transpose(1, 0, 2, 3).reshape(flat_shape),
        ],
        axis=2,
    ).astype(jnp.bfloat16)
    back_rate_logit = rate_pull(backward_done[4].transpose(1, 0, 2))[0].astype(jnp.bfloat16)
    init_grads = unpack_state(backward_done[5])
    inner_gain_grad = backward_done[6]
    inner_bias_grad = backward_done[7]
    grad_qkv = jnp.einsum(
        "csd,csk->dk", attn_rows, back_projected, preferred_element_type=jnp.float32
    ).reshape(qkv_full.shape)
    grad_rate = jnp.einsum(
        "csd,csh->dh", attn_rows, back_rate_logit, preferred_element_type=jnp.float32
    )

    def attn_term(first_row, row_count):
        return jnp.einsum(
            "csk,dk->csd", back_projected, qkv_matrix, preferred_element_type=jnp.float32
        ) + jnp.einsum(
            "csh,dh->csd", back_rate_logit, rate_full, preferred_element_type=jnp.float32
        )

    back_normed_attn = back_sum(attn_term, local_rows)
    attn_norm_pull = jax.vjp(layer_norm, inputs, scale_attn)[1]
    back_input_part, grad_gain_attn = attn_norm_pull(back_normed_attn)
    input_grad = back_mixed + back_input_part
    gain_sums = (
        lax.psum_scatter(grad_gain_attn, ("dp", "tensor"), scatter_dimension=0, tiled=True),
        lax.psum_scatter(grad_gain_ffn, ("dp", "tensor"), scatter_dimension=0, tiled=True),
    )
    summed = (
        lax.psum_scatter(
            grad_qkv.astype(jnp.bfloat16), "dp", scatter_dimension=0, tiled=True
        ).astype(jnp.float32),
        lax.psum_scatter(
            grad_rate.astype(jnp.bfloat16), "dp", scatter_dimension=0, tiled=True
        ).astype(jnp.float32),
        lax.psum_scatter(
            grad_out_w.astype(jnp.bfloat16), "dp", scatter_dimension=1, tiled=True
        ).astype(jnp.float32),
        lax.psum_scatter(
            grad_gate_up.astype(jnp.bfloat16), "dp", scatter_dimension=0, tiled=True
        ).astype(jnp.float32),
        lax.psum_scatter(
            grad_down.astype(jnp.bfloat16), "dp", scatter_dimension=1, tiled=True
        ).astype(jnp.float32),
        lax.psum_scatter(
            init_grads[0].astype(jnp.bfloat16), "dp", scatter_dimension=2, tiled=True
        ).astype(jnp.float32),
        lax.psum_scatter(
            init_grads[1].astype(jnp.bfloat16), "dp", scatter_dimension=1, tiled=True
        ).astype(jnp.float32),
        lax.psum_scatter(
            init_grads[2].astype(jnp.bfloat16), "dp", scatter_dimension=1, tiled=True
        ).astype(jnp.float32),
        lax.psum_scatter(
            init_grads[3].astype(jnp.bfloat16), "dp", scatter_dimension=1, tiled=True
        ).astype(jnp.float32),
        lax.psum_scatter(
            inner_gain_grad.astype(jnp.bfloat16), "dp", scatter_dimension=1, tiled=True
        ).astype(jnp.float32),
        lax.psum_scatter(
            inner_bias_grad.astype(jnp.bfloat16), "dp", scatter_dimension=1, tiled=True
        ).astype(jnp.float32),
    )
    return (
        result,
        input_grad,
        gain_sums[0],
        gain_sums[1],
        summed[0],
        summed[1],
        summed[2],
        summed[3],
        summed[4],
        summed[5],
        summed[6],
        summed[7],
        summed[8],
        summed[9],
        summed[10],
    )


def solution(mesh):
    placed = (
        P(("dp", "tensor"), None, None),
        P(("dp", "tensor")),
        P(("dp", "tensor")),
        P("dp", None, "tensor"),
        P("dp", "tensor"),
        P("tensor", "dp"),
        P("dp", None, "tensor"),
        P("tensor", "dp"),
        P("tensor", None, "dp"),
        P("tensor", "dp"),
        P("tensor", "dp", None),
        P("tensor", "dp"),
        P("tensor", "dp"),
        P("tensor", "dp"),
        P(("dp", "tensor"), None, None),
    )
    return jax.shard_map(
        local,
        mesh=mesh,
        in_specs=placed,
        out_specs=(
            P(("dp", "tensor"), None, None),
            P(("dp", "tensor"), None, None),
            P(("dp", "tensor")),
            P(("dp", "tensor")),
            P("dp", None, "tensor"),
            P("dp", "tensor"),
            P("tensor", "dp"),
            P("dp", None, "tensor"),
            P("tensor", "dp"),
            P("tensor", None, "dp"),
            P("tensor", "dp"),
            P("tensor", "dp", None),
            P("tensor", "dp"),
            P("tensor", "dp"),
            P("tensor", "dp"),
        ),
        check_vma=False,
    )
```

profile of v0, /device:TPU:0, one launch (start us, length us, event | category | flops | bytes accessed | tf_op | source)
XLA Modules:
  0.0 2948.6 jit_solution(13844568915991748588)
XLA Ops:
  11.9 42.0 %all-reduce.12 = (bf16[768]{0:T(1024)(128)(2,1)S(1)}, bf16[768]{0:T(1024)(128)(2,1)S(1)}) all-reduce(bf16[768]{0:T(1024)(128)(2,1)S(1)} %dynamic-update-slice.68, bf16[768]{0:T(1024)(128)(2,1)S(1)} %dynamic-update-slice.69), channel_id=1, replica_groups=mesh['dp'=8,'tensor'=4] {'dp','tensor'}, use_global_device_ids=true, to_apply=%add.4 | all-reduce | flops 1536 | bytes 6144
  53.9 20.5 all-gather.2
  145.8 30.8 %all_gather.51 = bf16[3,64,256]{1,2,0:T(8,128)(2,1)S(1)} all-gather(bf16[3,64,32]{1,2,0:T(8,128)(2,1)} %param.45), channel_id=1, replica_groups=mesh['dp'=8,'tensor'=4] {'dp'}, dimensions={2}, use_global_device_ids=true | all-gather | bytes 110592 | tf_op jit(solution)/shard_map/all_gather | solution.py:203
  176.9 30.8 %all_gather.53 = bf16[3,256,64]{2,1,0:T(8,128)(2,1)S(1)} all-gather(bf16[3,32,64]{2,1,0:T(8,128)(2,1)} %param.47), channel_id=1, replica_groups=mesh['dp'=8,'tensor'=4] {'dp'}, dimensions={1}, use_global_device_ids=true | all-gather | bytes 110592 | tf_op jit(solution)/shard_map/all_gather | solution.py:205
  214.4 33.3 %all_gather.61 = bf16[192,768]{0,1:T(8,128)(2,1)} all-gather(bf16[192,96]{0,1:T(8,128)(2,1)S(1)} %copy.213), channel_id=1, replica_groups=mesh['dp'=8,'tensor'=4] {'dp'}, dimensions={1}, use_global_device_ids=true | all-gather | bytes 331776 | tf_op jit(solution)/shard_map/all_gather | solution.py:200
  247.7 34.0 %all_gather.57 = bf16[768,3,192]{2,0,1:T(8,128)(2,1)S(1)} all-gather(bf16[96,3,192]{2,0,1:T(8,128)(2,1)S(1)} %copy-done.31), channel_id=1, replica_groups=mesh['dp'=8,'tensor'=4] {'dp'}, dimensions={0}, use_global_device_ids=true | all-gather | bytes 995328 | tf_op jit(solution)/shard_map/all_gather | solution.py:198
  286.1 473.9 %while.316 = (s32[]{:T(128)}, f32[3,33088]{1,0:T(4,128)S(1)}, f32[2,3,33088]{2,1,0:T(4,128)S(1)}, f32[2,128,3,64]{1,3,2,0:T(8,128)S(1)}, pred[]{:T(512)}, /*inde...) while((s32[]{:T(128)}, f32[3,33088]{1,0:T(4,128)S(1)}, ...), condition=%wide.region_15.16_spmd, body=%wide.region_2.15_spmd.sunk | while | flops 73166096 | bytes 14084942 | solution.py:273
  290.5 35.3 %while.320 = (s32[]{:T(128)}, f32[3,64,256]{2,1,0:T(8,128)S(1)}, f32[3,256]{1,0:T(4,128)S(1)}, f32[3,256,64]{1,2,0:T(8,128)S(1)}, f32[3,64]{1,0:T(4,128)S(1)}, /...) while((s32[]{:T(128)}, f32[3,64,256]{2,1,0:T(8,128)S(1)}, ...), condition=%wide.region_12.12_spmd, body=%wide.region_3.11_spmd.sunk | while | flops 72521312 | bytes 2835293 | solution.py:110
  340.0 35.3 %while.320 = (s32[]{:T(128)}, f32[3,64,256]{2,1,0:T(8,128)S(1)}, f32[3,256]{1,0:T(4,128)S(1)}, f32[3,256,64]{1,2,0:T(8,128)S(1)}, f32[3,64]{1,0:T(4,128)S(1)}, /...) while((s32[]{:T(128)}, f32[3,64,256]{2,1,0:T(8,128)S(1)}, ...), condition=%wide.region_12.12_spmd, body=%wide.region_3.11_spmd.sunk | while | flops 72521312 | bytes 2835293 | solution.py:110
  392.4 35.3 %while.320 = (s32[]{:T(128)}, f32[3,64,256]{2,1,0:T(8,128)S(1)}, f32[3,256]{1,0:T(4,128)S(1)}, f32[3,256,64]{1,2,0:T(8,128)S(1)}, f32[3,64]{1,0:T(4,128)S(1)}, /...) while((s32[]{:T(128)}, f32[3,64,256]{2,1,0:T(8,128)S(1)}, ...), condition=%wide.region_12.12_spmd, body=%wide.region_3.11_spmd.sunk | while | flops 72521312 | bytes 2835293 | solution.py:110
  444.9 35.3 %while.320 = (s32[]{:T(128)}, f32[3,64,256]{2,1,0:T(8,128)S(1)}, f32[3,256]{1,0:T(4,128)S(1)}, f32[3,256,64]{1,2,0:T(8,128)S(1)}, f32[3,64]{1,0:T(4,128)S(1)}, /...) while((s32[]{:T(128)}, f32[3,64,256]{2,1,0:T(8,128)S(1)}, ...), condition=%wide.region_12.12_spmd, body=%wide.region_3.11_spmd.sunk | while | flops 72521312 | bytes 2835293 | solution.py:110
  497.6 35.3 %while.320 = (s32[]{:T(128)}, f32[3,64,256]{2,1,0:T(8,128)S(1)}, f32[3,256]{1,0:T(4,128)S(1)}, f32[3,256,64]{1,2,0:T(8,128)S(1)}, f32[3,64]{1,0:T(4,128)S(1)}, /...) while((s32[]{:T(128)}, f32[3,64,256]{2,1,0:T(8,128)S(1)}, ...), condition=%wide.region_12.12_spmd, body=%wide.region_3.11_spmd.sunk | while | flops 72521312 | bytes 2835293 | solution.py:110
  550.9 35.3 %while.320 = (s32[]{:T(128)}, f32[3,64,256]{2,1,0:T(8,128)S(1)}, f32[3,256]{1,0:T(4,128)S(1)}, f32[3,256,64]{1,2,0:T(8,128)S(1)}, f32[3,64]{1,0:T(4,128)S(1)}, /...) while((s32[]{:T(128)}, f32[3,64,256]{2,1,0:T(8,128)S(1)}, ...), condition=%wide.region_12.12_spmd, body=%wide.region_3.11_spmd.sunk | while | flops 72521312 | bytes 2835293 | solution.py:110
  604.3 35.3 %while.320 = (s32[]{:T(128)}, f32[3,64,256]{2,1,0:T(8,128)S(1)}, f32[3,256]{1,0:T(4,128)S(1)}, f32[3,256,64]{1,2,0:T(8,128)S(1)}, f32[3,64]{1,0:T(4,128)S(1)}, /...) while((s32[]{:T(128)}, f32[3,64,256]{2,1,0:T(8,128)S(1)}, ...), condition=%wide.region_12.12_spmd, body=%wide.region_3.11_spmd.sunk | while | flops 72521312 | bytes 2835293 | solution.py:110
  657.6 35.3 %while.320 = (s32[]{:T(128)}, f32[3,64,256]{2,1,0:T(8,128)S(1)}, f32[3,256]{1,0:T(4,128)S(1)}, f32[3,256,64]{1,2,0:T(8,128)S(1)}, f32[3,64]{1,0:T(4,128)S(1)}, /...) while((s32[]{:T(128)}, f32[3,64,256]{2,1,0:T(8,128)S(1)}, ...), condition=%wide.region_12.12_spmd, body=%wide.region_3.11_spmd.sunk | while | flops 72521312 | bytes 2835293 | solution.py:110
  710.9 35.3 %while.320 = (s32[]{:T(128)}, f32[3,64,256]{2,1,0:T(8,128)S(1)}, f32[3,256]{1,0:T(4,128)S(1)}, f32[3,256,64]{1,2,0:T(8,128)S(1)}, f32[3,64]{1,0:T(4,128)S(1)}, /...) while((s32[]{:T(128)}, f32[3,64,256]{2,1,0:T(8,128)S(1)}, ...), condition=%wide.region_12.12_spmd, body=%wide.region_3.11_spmd.sunk | while | flops 72521312 | bytes 2835293 | solution.py:110
  769.3 37.3 %all_gather.65 = bf16[512,768]{0,1:T(8,128)(2,1)S(1)} all-gather(bf16[512,96]{0,1:T(8,128)(2,1)S(1)} %copy-done.34), channel_id=1, replica_groups=mesh['dp'=8,'tensor'=4] {'dp'}, dimensions={1}, use_global_device_ids=true | all-gather | bytes 884736 | tf_op jit(solution)/shard_map/all_gather | solution.py:202
  821.9 19.7 reduce-scatter.26.cloned.1.call-done
  856.0 1509.6 %while.319 = (s32[]{:T(128)}, f32[3,33088]{1,0:T(4,128)}, bf16[2,128,3,64]{3,2,1,0:T(4,128)(2,1)}, bf16[2,128,3,64]{3,2,1,0:T(4,128)(2,1)}, bf16[2,128,3,64]{3,2...) while((s32[]{:T(128)}, f32[3,33088]{1,0:T(4,128)}, ...), condition=%wide.region_63.64_spmd.clone, body=%wide.region_27.63_spmd.clone.sunk | while | flops 248247696 | bytes 27616360 | solution.py:372
  862.9 33.4 %while.321 = (s32[]{:T(128)}, f32[3,64,256]{2,1,0:T(8,128)S(1)}, f32[3,256]{1,0:T(4,128)S(1)}, f32[3,256,64]{1,2,0:T(8,128)S(1)}, f32[3,64]{1,0:T(4,128)S(1)}, /...) while((s32[]{:T(128)}, f32[3,64,256]{2,1,0:T(8,128)S(1)}, ...), condition=%wide.region_35.35_spmd, body=%wide.region_28.34_spmd.sunk | while | flops 47588400 | bytes 2679349 | solution.py:110
  896.4 113.6 %while.322 = (s32[]{:T(128)}, f32[3,64]{1,0:T(4,128)S(1)}, f32[3,64]{1,0:T(4,128)S(1)}, f32[3,64,256]{2,1,0:T(8,128)S(1)}, f32[3,256]{1,0:T(4,128)S(1)}, /*index...) while((s32[]{:T(128)}, f32[3,64]{1,0:T(4,128)S(1)}, ...), condition=%wide.region_60.60_spmd.clone, body=%wide.region_36.59_spmd.clone.sunk | while | flops 199616480 | bytes 9423784 | solution.py:110
  1031.8 33.4 %while.321 = (s32[]{:T(128)}, f32[3,64,256]{2,1,0:T(8,128)S(1)}, f32[3,256]{1,0:T(4,128)S(1)}, f32[3,256,64]{1,2,0:T(8,128)S(1)}, f32[3,64]{1,0:T(4,128)S(1)}, /...) while((s32[]{:T(128)}, f32[3,64,256]{2,1,0:T(8,128)S(1)}, ...), condition=%wide.region_35.35_spmd, body=%wide.region_28.34_spmd.sunk | while | flops 47588400 | bytes 2679349 | solution.py:110
  1065.3 113.6 %while.322 = (s32[]{:T(128)}, f32[3,64]{1,0:T(4,128)S(1)}, f32[3,64]{1,0:T(4,128)S(1)}, f32[3,64,256]{2,1,0:T(8,128)S(1)}, f32[3,256]{1,0:T(4,128)S(1)}, /*index...) while((s32[]{:T(128)}, f32[3,64]{1,0:T(4,128)S(1)}, ...), condition=%wide.region_60.60_spmd.clone, body=%wide.region_36.59_spmd.clone.sunk | while | flops 199616480 | bytes 9423784 | solution.py:110
  1200.5 33.4 %while.321 = (s32[]{:T(128)}, f32[3,64,256]{2,1,0:T(8,128)S(1)}, f32[3,256]{1,0:T(4,128)S(1)}, f32[3,256,64]{1,2,0:T(8,128)S(1)}, f32[3,64]{1,0:T(4,128)S(1)}, /...) while((s32[]{:T(128)}, f32[3,64,256]{2,1,0:T(8,128)S(1)}, ...), condition=%wide.region_35.35_spmd, body=%wide.region_28.34_spmd.sunk | while | flops 47588400 | bytes 2679349 | solution.py:110
  1234.0 113.6 %while.322 = (s32[]{:T(128)}, f32[3,64]{1,0:T(4,128)S(1)}, f32[3,64]{1,0:T(4,128)S(1)}, f32[3,64,256]{2,1,0:T(8,128)S(1)}, f32[3,256]{1,0:T(4,128)S(1)}, /*index...) while((s32[]{:T(128)}, f32[3,64]{1,0:T(4,128)S(1)}, ...), condition=%wide.region_60.60_spmd.clone, body=%wide.region_36.59_spmd.clone.sunk | while | flops 199616480 | bytes 9423784 | solution.py:110
  1368.5 33.4 %while.321 = (s32[]{:T(128)}, f32[3,64,256]{2,1,0:T(8,128)S(1)}, f32[3,256]{1,0:T(4,128)S(1)}, f32[3,256,64]{1,2,0:T(8,128)S(1)}, f32[3,64]{1,0:T(4,128)S(1)}, /...) while((s32[]{:T(128)}, f32[3,64,256]{2,1,0:T(8,128)S(1)}, ...), condition=%wide.region_35.35_spmd, body=%wide.region_28.34_spmd.sunk | while | flops 47588400 | bytes 2679349 | solution.py:110
  1402.1 113.6 %while.322 = (s32[]{:T(128)}, f32[3,64]{1,0:T(4,128)S(1)}, f32[3,64]{1,0:T(4,128)S(1)}, f32[3,64,256]{2,1,0:T(8,128)S(1)}, f32[3,256]{1,0:T(4,128)S(1)}, /*index...) while((s32[]{:T(128)}, f32[3,64]{1,0:T(4,128)S(1)}, ...), condition=%wide.region_60.60_spmd.clone, body=%wide.region_36.59_spmd.clone.sunk | while | flops 199616480 | bytes 9423784 | solution.py:110
  1535.9 33.4 %while.321 = (s32[]{:T(128)}, f32[3,64,256]{2,1,0:T(8,128)S(1)}, f32[3,256]{1,0:T(4,128)S(1)}, f32[3,256,64]{1,2,0:T(8,128)S(1)}, f32[3,64]{1,0:T(4,128)S(1)}, /...) while((s32[]{:T(128)}, f32[3,64,256]{2,1,0:T(8,128)S(1)}, ...), condition=%wide.region_35.35_spmd, body=%wide.region_28.34_spmd.sunk | while | flops 47588400 | bytes 2679349 | solution.py:110
  1569.4 113.6 %while.322 = (s32[]{:T(128)}, f32[3,64]{1,0:T(4,128)S(1)}, f32[3,64]{1,0:T(4,128)S(1)}, f32[3,64,256]{2,1,0:T(8,128)S(1)}, f32[3,256]{1,0:T(4,128)S(1)}, /*index...) while((s32[]{:T(128)}, f32[3,64]{1,0:T(4,128)S(1)}, ...), condition=%wide.region_60.60_spmd.clone, body=%wide.region_36.59_spmd.clone.sunk | while | flops 199616480 | bytes 9423784 | solution.py:110
  1703.4 33.4 %while.321 = (s32[]{:T(128)}, f32[3,64,256]{2,1,0:T(8,128)S(1)}, f32[3,256]{1,0:T(4,128)S(1)}, f32[3,256,64]{1,2,0:T(8,128)S(1)}, f32[3,64]{1,0:T(4,128)S(1)}, /...) while((s32[]{:T(128)}, f32[3,64,256]{2,1,0:T(8,128)S(1)}, ...), condition=%wide.region_35.35_spmd, body=%wide.region_28.34_spmd.sunk | while | flops 47588400 | bytes 2679349 | solution.py:110
  1736.9 113.6 %while.322 = (s32[]{:T(128)}, f32[3,64]{1,0:T(4,128)S(1)}, f32[3,64]{1,0:T(4,128)S(1)}, f32[3,64,256]{2,1,0:T(8,128)S(1)}, f32[3,256]{1,0:T(4,128)S(1)}, /*index...) while((s32[]{:T(128)}, f32[3,64]{1,0:T(4,128)S(1)}, ...), condition=%wide.region_60.60_spmd.clone, body=%wide.region_36.59_spmd.clone.sunk | while | flops 199616480 | bytes 9423784 | solution.py:110
  1870.9 33.4 %while.321 = (s32[]{:T(128)}, f32[3,64,256]{2,1,0:T(8,128)S(1)}, f32[3,256]{1,0:T(4,128)S(1)}, f32[3,256,64]{1,2,0:T(8,128)S(1)}, f32[3,64]{1,0:T(4,128)S(1)}, /...) while((s32[]{:T(128)}, f32[3,64,256]{2,1,0:T(8,128)S(1)}, ...), condition=%wide.region_35.35_spmd, body=%wide.region_28.34_spmd.sunk | while | flops 47588400 | bytes 2679349 | solution.py:110
  1904.4 113.6 %while.322 = (s32[]{:T(128)}, f32[3,64]{1,0:T(4,128)S(1)}, f32[3,64]{1,0:T(4,128)S(1)}, f32[3,64,256]{2,1,0:T(8,128)S(1)}, f32[3,256]{1,0:T(4,128)S(1)}, /*index...) while((s32[]{:T(128)}, f32[3,64]{1,0:T(4,128)S(1)}, ...), condition=%wide.region_60.60_spmd.clone, body=%wide.region_36.59_spmd.clone.sunk | while | flops 199616480 | bytes 9423784 | solution.py:110
  2038.4 33.4 %while.321 = (s32[]{:T(128)}, f32[3,64,256]{2,1,0:T(8,128)S(1)}, f32[3,256]{1,0:T(4,128)S(1)}, f32[3,256,64]{1,2,0:T(8,128)S(1)}, f32[3,64]{1,0:T(4,128)S(1)}, /...) while((s32[]{:T(128)}, f32[3,64,256]{2,1,0:T(8,128)S(1)}, ...), condition=%wide.region_35.35_spmd, body=%wide.region_28.34_spmd.sunk | while | flops 47588400 | bytes 2679349 | solution.py:110
  2072.0 113.6 %while.322 = (s32[]{:T(128)}, f32[3,64]{1,0:T(4,128)S(1)}, f32[3,64]{1,0:T(4,128)S(1)}, f32[3,64,256]{2,1,0:T(8,128)S(1)}, f32[3,256]{1,0:T(4,128)S(1)}, /*index...) while((s32[]{:T(128)}, f32[3,64]{1,0:T(4,128)S(1)}, ...), condition=%wide.region_60.60_spmd.clone, body=%wide.region_36.59_spmd.clone.sunk | while | flops 199616480 | bytes 9423784 | solution.py:110
  2206.0 33.4 %while.321 = (s32[]{:T(128)}, f32[3,64,256]{2,1,0:T(8,128)S(1)}, f32[3,256]{1,0:T(4,128)S(1)}, f32[3,256,64]{1,2,0:T(8,128)S(1)}, f32[3,64]{1,0:T(4,128)S(1)}, /...) while((s32[]{:T(128)}, f32[3,64,256]{2,1,0:T(8,128)S(1)}, ...), condition=%wide.region_35.35_spmd, body=%wide.region_28.34_spmd.sunk | while | flops 47588400 | bytes 2679349 | solution.py:110
  2239.5 113.6 %while.322 = (s32[]{:T(128)}, f32[3,64]{1,0:T(4,128)S(1)}, f32[3,64]{1,0:T(4,128)S(1)}, f32[3,64,256]{2,1,0:T(8,128)S(1)}, f32[3,256]{1,0:T(4,128)S(1)}, /*index...) while((s32[]{:T(128)}, f32[3,64]{1,0:T(4,128)S(1)}, ...), condition=%wide.region_60.60_spmd.clone, body=%wide.region_36.59_spmd.clone.sunk | while | flops 199616480 | bytes 9423784 | solution.py:110
  2384.1 28.4 all-reduce.13
  2413.8 23.3 reduce-scatter.44.cloned.1.call-done
  2438.5 62.6 %reduce-scatter.40.cloned.1.call-done = bf16[96,3]{1,0:T(8,128)(2,1)} async-done(((bf16[768,3]{1,0:T(8,128)(2,1)}), bf16[96,3]{1,0:T(8,128)(2,1)}) %reduce-scatter.40.cloned.1.call-update) | async-done | bytes 592
  2502.5 62.3 %reduce-scatter.38.cloned.1.call-done = bf16[3,32,64]{2,1,0:T(8,128)(2,1)} async-done(((bf16[3,256,64]{2,1,0:T(8,128)(2,1)}), bf16[3,32,64]{2,1,0:T(8,128)(2,1)}) %reduce-scatter.38.cloned.1.call-update) | async-done | bytes 12304 | tf_op jit(solution)/shard_map/reduce_scatter | solution.py:430
  2566.1 62.9 %reduce-scatter.36.cloned.1.call-done = bf16[3,64,32]{1,2,0:T(8,128)(2,1)} async-done(((bf16[3,64,256]{1,2,0:T(8,128)(2,1)}), bf16[3,64,32]{1,2,0:T(8,128)(2,1)}) %reduce-scatter.36.cloned.1.call-update) | async-done | bytes 12304 | tf_op jit(solution)/shard_map/reduce_scatter | solution.py:424
  2630.3 62.5 %reduce-scatter.42.cloned.1.call-done = bf16[96,192]{1,0:T(8,128)(2,1)} async-done(((bf16[768,192]{1,0:T(8,128)(2,1)}), bf16[96,192]{1,0:T(8,128)(2,1)}) %reduce-scatter.42.cloned.1.call-update) | async-done | bytes 36880
  2694.4 21.1 reduce-scatter.28.cloned.1.call-done
  2717.7 39.5 %all-reduce.11 = (f32[768]{0:T(1024)S(1)}, f32[768]{0:T(1024)S(1)}) all-reduce(f32[768]{0:T(1024)S(1)} %get-tuple-element.2224, f32[768]{0:T(1024)S(1)} %copy-done.62), channel_id=6, replica_groups=mesh['dp'=8,'tensor'=4] {'dp','tensor'}, use_global_device_ids=true, to_apply=%region_68.69.clone | all-reduce | flops 1536 | bytes 12288
  2761.1 43.3 %reduce-scatter.34.cloned.1.call-done = bf16[512,96]{0,1:T(8,128)(2,1)} async-done(((bf16[512,768]{0,1:T(8,128)(2,1)}), bf16[512,96]{0,1:T(8,128)(2,1)}) %reduce-scatter.34.cloned.1.call-update) | async-done | bytes 98320 | tf_op jit(solution)/shard_map/reduce_scatter | solution.py:421
  2806.0 65.4 %reduce-scatter.30.cloned.1.call-done = bf16[96,3,192]{2,0,1:T(8,128)(2,1)} async-done(((bf16[768,3,192]{2,0,1:T(8,128)(2,1)}), bf16[96,3,192]{2,0,1:T(8,128)(2,1)}) %reduce-scatter.30.cloned.1.call-update) | async-done | bytes 110608 | tf_op jit(solution)/shard_map/reduce_scatter | solution.py:409
  2873.1 66.0 %reduce-scatter.32.cloned.1.call-done = bf16[96,2,512]{2,0,1:T(8,128)(2,1)} async-done(((bf16[768,2,512]{2,0,1:T(8,128)(2,1)}), bf16[96,2,512]{2,0,1:T(8,128)(2,1)}) %reduce-scatter.32.cloned.1.call-update) | async-done | bytes 196624 | tf_op jit(solution)/shard_map/reduce_scatter | solution.py:418
  (9595 shorter events, 2098.7 us)
Async XLA Ops:
  8.0 199.9 %copy-start.2 = (bf16[32,2,768]{2,1,0:T(2,128)(2,1)S(1)}, bf16[32,2,768]{2,1,0:T(2,128)(2,1)}, u32[]{:S(2)}) copy-start(bf16[32,2,768]{2,1,0:T(2,128)(2,1)} %param.37) | copy-start | bytes 294916
  8.0 798.5 %reduce-scatter.22.cloned.1.call-start = ((), (), s32[]{:S(2)}) async-start(), calls=%async_computation.12 | async-start | bytes 491520 | tf_op jit(solution)/shard_map/reduce_scatter | solution.py:155
  9.1 238.6 %copy-start.53 = (f32[32,2]{0,1:T(2,128)}, f32[32,2]{0,1:T(2,128)S(1)}, u32[]{:S(2)}) copy-start(f32[32,2]{0,1:T(2,128)S(1)} %broadcast_multiply_fusion.14) | copy-start | bytes 772
  10.2 237.5 %copy-start.60 = (f32[32,2]{0,1:T(2,128)}, f32[32,2]{0,1:T(2,128)S(1)}, u32[]{:S(2)}) copy-start(f32[32,2]{0,1:T(2,128)S(1)} %fusion.216) | copy-start | bytes 772
  53.9 193.8 %copy-start.31 = (bf16[96,3,192]{2,0,1:T(8,128)(2,1)S(1)}, bf16[96,3,192]{2,0,1:T(8,128)(2,1)}, u32[]{:S(2)}) copy-start(bf16[96,3,192]{2,0,1:T(8,128)(2,1)} %param.40) | copy-start | bytes 331780
  53.9 227.8 %copy-start.32 = (f32[768]{0:T(1024)}, f32[768]{0:T(1024)S(1)}, u32[]{:S(2)}) copy-start(f32[768]{0:T(1024)S(1)} %convert_element_type.190) | copy-start | bytes 9220
  74.5 207.1 %copy-start.43 = (bf16[768,3,1]{0,1,2:T(4,128)(2,1)}, bf16[768,3,1]{0,1,2:T(4,128)(2,1)S(1)}, u32[]{:S(2)}) copy-start(bf16[768,3,1]{0,1,2:T(4,128)(2,1)S(1)} %reshape.921) | copy-start | bytes 13828
  327.2 8.3 collective-permute-start.1
  376.7 11.3 collective-permute-start.1
  429.1 11.3 collective-permute-start.1
  481.6 11.6 collective-permute-start.1
  534.3 12.2 collective-permute-start.1
  587.6 12.2 collective-permute-start.1
  641.0 12.2 collective-permute-start.1
  694.3 12.2 collective-permute-start.1
  747.7 12.2 collective-permute-start.1
  762.2 54.3 %all-gather.7.cloned.1.call-start = ((), (), s32[]{:S(2)}) async-start(), calls=%async_computation.13 | async-start | bytes 1769472 | tf_op jit(solution)/shard_map/all_gather | solution.py:201
  763.0 78.7 %reduce-scatter.26.cloned.1.call-start = ((), (), s32[]{:S(2)}) async-start(), calls=%async_computation.15 | async-start | bytes 491520 | tf_op jit(solution)/shard_map/reduce_scatter | solution.py:166
  821.9 1615.2 %reduce-scatter.44.cloned.1.call-start = ((), (), s32[]{:S(2)}) async-start(), calls=%async_computation.24 | async-start | bytes 73728
  1011.4 10.6 collective-permute-start
  1180.3 10.5 collective-permute-start
  1349.0 9.8 collective-permute-start
  1517.0 9.1 collective-permute-start
  1684.4 9.2 collective-permute-start
  1851.8 9.3 collective-permute-start
  2019.4 9.3 collective-permute-start
  2186.9 9.3 collective-permute-start
  2354.5 9.3 collective-permute-start
  2368.3 132.8 %reduce-scatter.40.cloned.1.call-start = ((), (), s32[]{:S(2)}) async-start(), calls=%async_computation.22 | async-start | bytes 221184
  2370.4 194.3 %reduce-scatter.38.cloned.1.call-start = ((), (), s32[]{:S(2)}) async-start(), calls=%async_computation.21 | async-start | bytes 221184 | tf_op jit(solution)/shard_map/reduce_scatter | solution.py:430
  2371.4 257.5 %reduce-scatter.36.cloned.1.call-start = ((), (), s32[]{:S(2)}) async-start(), calls=%async_computation.20 | async-start | bytes 221184 | tf_op jit(solution)/shard_map/reduce_scatter | solution.py:424
  2372.4 320.5 %reduce-scatter.42.cloned.1.call-start = ((), (), s32[]{:S(2)}) async-start(), calls=%async_computation.23 | async-start | bytes 442368
  2373.9 341.6 %reduce-scatter.28.cloned.1.call-start = ((), (), s32[]{:S(2)}) async-start(), calls=%async_computation.16 | async-start | bytes 491520 | tf_op jit(solution)/shard_map/reduce_scatter | solution.py:166
  2376.2 382.2 %reduce-scatter.24.cloned.1.call-start = ((), (), s32[]{:S(2)}) async-start(), calls=%async_computation.14 | async-start | bytes 491520 | tf_op jit(solution)/shard_map/reduce_scatter | solution.py:155
  2377.4 427.0 %reduce-scatter.34.cloned.1.call-start = ((), (), s32[]{:S(2)}) async-start(), calls=%async_computation.19 | async-start | bytes 884736 | tf_op jit(solution)/shard_map/reduce_scatter | solution.py:421
  2378.8 492.6 %reduce-scatter.30.cloned.1.call-start = ((), (), s32[]{:S(2)}) async-start(), calls=%async_computation.17 | async-start | bytes 1327104 | tf_op jit(solution)/shard_map/reduce_scatter | solution.py:409
  2380.8 558.3 %reduce-scatter.32.cloned.1.call-start = ((), (), s32[]{:S(2)}) async-start(), calls=%async_computation.18 | async-start | bytes 1769472 | tf_op jit(solution)/shard_map/reduce_scatter | solution.py:418
  2382.7 332.9 %copy-start.33 = (f32[768]{0:T(1024)S(1)}, f32[768]{0:T(1024)}, u32[]{:S(2)}) copy-start(f32[768]{0:T(1024)} %copy-done.32) | copy-start | bytes 9220
  2382.7 332.9 %copy-start.54 = (f32[32,2]{0,1:T(2,128)S(1)}, f32[32,2]{0,1:T(2,128)}, u32[]{:S(2)}) copy-start(f32[32,2]{0,1:T(2,128)} %copy-done.53) | copy-start | bytes 772
  2382.7 333.9 %copy-start.66 = (f32[32,2]{0,1:T(2,128)S(1)}, f32[32,2]{0,1:T(2,128)}, u32[]{:S(2)}) copy-start(f32[32,2]{0,1:T(2,128)} %copy-done.65) | copy-start | bytes 772
  2382.7 334.0 %copy-start.61 = (f32[32,2]{0,1:T(2,128)S(1)}, f32[32,2]{0,1:T(2,128)}, u32[]{:S(2)}) copy-start(f32[32,2]{0,1:T(2,128)} %copy-done.60) | copy-start | bytes 772
  2382.7 335.1 %copy-start.62 = (f32[768]{0:T(1024)S(1)}, f32[768]{0:T(1024)}, u32[]{:S(2)}) copy-start(f32[768]{0:T(1024)} %get-tuple-element.2222) | copy-start | bytes 9220
  2382.7 375.7 %copy-start.20 = (bf16[32,2,768]{2,0,1:T(8,128)(2,1)S(1)}, bf16[32,2,768]{2,0,1:T(8,128)(2,1)}, u32[]{:S(2)}) copy-start(bf16[32,2,768]{2,0,1:T(8,128)(2,1)} %reduce-scatter.26.cloned.1.call-done) | copy-start | bytes 294916
  2382.7 375.7 %copy-start.27 = (bf16[32,2,768]{2,1,0:T(2,128)(2,1)S(1)}, bf16[32,2,768]{2,1,0:T(2,128)(2,1)}, u32[]{:S(2)}) copy-start(bf16[32,2,768]{2,1,0:T(2,128)(2,1)} %param.51) | copy-start | bytes 294916
  2382.7 375.7 %copy-start.52 = (f32[32,2]{0,1:T(2,128)S(1)}, f32[32,2]{0,1:T(2,128)}, u32[]{:S(2)}) copy-start(f32[32,2]{0,1:T(2,128)} %copy-done.51) | copy-start | bytes 772
  2382.7 375.7 %copy-start.57 = (f32[32,2]{0,1:T(2,128)S(1)}, f32[32,2]{0,1:T(2,128)}, u32[]{:S(2)}) copy-start(f32[32,2]{0,1:T(2,128)} %copy-done.56) | copy-start | bytes 772
  2382.7 375.7 %copy-start.59 = (f32[32,2]{0,1:T(2,128)S(1)}, f32[32,2]{0,1:T(2,128)}, u32[]{:S(2)}) copy-start(f32[32,2]{0,1:T(2,128)} %copy-done.58) | copy-start | bytes 772
  2382.7 375.7 %copy-start.64 = (f32[32,2]{0,1:T(2,128)S(1)}, f32[32,2]{0,1:T(2,128)}, u32[]{:S(2)}) copy-start(f32[32,2]{0,1:T(2,128)} %copy-done.63) | copy-start | bytes 772
  (175 other events, 1169.6 us)
Sparse Core Ops, SparseCore 0:
  762.3 23.7 reduce-scatter.21
  822.0 19.6 reduce-scatter.25
Sparse Core Ops, SparseCore 1:
  765.5 51.0 all-gather.6
  2368.4 68.7 reduce-scatter.43
  2440.8 60.2 reduce-scatter.39
  2504.3 60.3 reduce-scatter.37
  2568.6 60.3 reduce-scatter.35
  2632.3 60.5 reduce-scatter.41
  2695.8 19.7 reduce-scatter.27
  2717.9 20.7 reduce-scatter.23
  2741.8 62.6 reduce-scatter.33
  2808.2 63.2 reduce-scatter.29
  2875.1 63.9 reduce-scatter.31
where the time goes:
time: 2960 us; the launch traced here: 2950 us
  matrix products  953 us (32%)
  waiting for transfers between devices  546 us (18%)
  local copies, waits for them, and re-layouts  520 us (18%)
  other arithmetic  421 us (14%)
  blocking collectives  391 us (13%)
  starting transfers between devices  52.8 us (2%)
  loops' own time  46.7 us (2%)
    squeeze x504, local copies, waits for them, and re-layouts, run_group(): final, outputs = lax.scan(jax.checkpoint(one_step), state, shaped)  243 us
    unnamed x16, waiting for transfers between devices  149 us
    dynamic_update_slice x432, local copies, waits for them, and re-layouts, run_group(): final, outputs = lax.scan(jax.checkpoint(one_step), state, shaped)  147 us
    dot_general x360, matrix products, inner_step(): jnp.einsum('mhi,hie->mhe', activity, second_w, precision=highest) + second_b  130 us
    dot_general x360, matrix products, inner_step(): back_act = jnp.einsum('mhe,hie->mhi', back_res, second_w, precision=highest)  112 us
    unnamed x3, blocking collectives  110 us
    dot_general x288, matrix products, inner_step(): jnp.einsum('mhi,mhe->hie', activity, back_res, precision=highest)  96.5 us
    dot_general x360, matrix products, inner_step(): jnp.einsum('mhe,hei->mhi', keys_in, first_w, precision=highest) + first_b  93.2 us

commit v1 on v0

v1 whole, which is shorter than its diff:
```python
import jax
import jax.numpy as jnp
from jax import lax
from jax.experimental import pallas as pl
from jax.experimental.pallas import tpu as pltpu
from jax.sharding import PartitionSpec as P

HEAD_DIM = 64
INNER = 256
MINI = 16
LANES = 256

epsilon = 1e-05
inner_epsilon = 1e-06
inner_rate = 0.5
rate_scale = inner_rate / (MINI * HEAD_DIM)
root_half = 0.7071067811865476
normal_peak = 0.3989422804014327

f32 = jnp.float32
bf16 = jnp.bfloat16


def dot_nn(a, b):
    return lax.dot_general(
        a.astype(bf16), b.astype(bf16), (((1,), (0,)), ((), ())), preferred_element_type=f32
    )


def dot_nt(a, b):
    return lax.dot_general(
        a.astype(bf16), b.astype(bf16), (((1,), (1,)), ((), ())), preferred_element_type=f32
    )


def dot_tn(a, b):
    return lax.dot_general(
        a.astype(bf16), b.astype(bf16), (((0,), (0,)), ((), ())), preferred_element_type=f32
    )


def row_mean(values):
    return jnp.mean(values, axis=-1, keepdims=True)


def density_and_share(values):
    density = jnp.exp(-0.5 * values * values) * normal_peak
    share = 0.5 * (1.0 + lax.erf(values * root_half))
    return density, share


def token_grid(count):
    rows = lax.broadcasted_iota(jnp.int32, (count, count), 0)
    cols = lax.broadcasted_iota(jnp.int32, (count, count), 1)
    return rows, cols


def unpack_chunk(packed, bias):
    query = packed[:, :HEAD_DIM]
    key = packed[:, HEAD_DIM : 2 * HEAD_DIM]
    value = packed[:, 2 * HEAD_DIM : 3 * HEAD_DIM]
    tail = packed[:, 3 * HEAD_DIM :].astype(f32)
    rate = jax.nn.sigmoid(tail[:, 0:1] + tail[:, 1:2]) * rate_scale
    miss = key.astype(f32) - value.astype(f32) + bias
    return query, key, rate, miss


def forward_kernel(
    packed_ref,
    first_w_in,
    first_b_in,
    second_w_in,
    second_b_in,
    gain_ref,
    bias_ref,
    normed_ref,
    act_ref,
    grad_pre_ref,
    hidden_ref,
    slope_ref,
    curve_ref,
    out_slope_ref,
    norms_ref,
    stats_ref,
    first_save,
    second_save,
    first_w,
    first_b,
    second_w,
    second_b,
    back_res_ref,
):
    @pl.when(pl.program_id(0) == 0)
    def _():
        first_w[...] = first_w_in[...]
        first_b[...] = first_b_in[...]
        second_w[...] = second_w_in[...]
        second_b[...] = second_b_in[...]

    gain = gain_ref[...]
    bias = bias_ref[...]
    chunk = packed_ref.shape[0]
    steps = chunk // MINI
    query, key, rate, miss = unpack_chunk(packed_ref[...], bias)
    base = miss * gain
    rate_base = rate * base
    rate_gain = rate * (gain * gain)
    base_mean = row_mean(rate_base)
    rows, cols = token_grid(chunk)
    before = cols // MINI + 1 < rows // MINI
    key_mix = jnp.where(before, dot_nt(key, key) + 1.0, 0.0).astype(bf16)
    first_low = first_w[...].astype(bf16)
    first_save[0] = first_low
    pre_all = dot_nn(key, first_low) + first_b[...]
    state = second_w[...]
    state_b = second_b[...]
    start_low = state.astype(bf16)
    start_b = state_b
    last_grad = None
    grads, acts, backs = [], [], []
    for step in range(steps):
        at = slice(step * MINI, (step + 1) * MINI)
        pre = pre_all[at]
        if step >= 2:
            past = (step - 1) * MINI
            older = jnp.concatenate(grads[: step - 1], axis=0) if step > 2 else grads[0]
            pre = pre - dot_nn(key_mix[at, :past], older)
        if step >= 1:
            pre = pre - dot_nn(
                dot_nt(key[at], key[(step - 1) * MINI : step * MINI]) + 1.0, last_grad
            )
        density, share = density_and_share(pre)
        act = (pre * share).astype(bf16)
        slope = share + pre * density
        state_low = state.astype(bf16)
        second_save[0, step] = state_low
        res = dot_nt(act, state_low) + state_b
        weighted = rate_gain[at] * res
        square = jnp.sum(res * res, axis=-1, keepdims=True)
        sum_gain = jnp.sum(weighted, axis=-1, keepdims=True)
        sum_base = jnp.sum(rate_base[at] * res, axis=-1, keepdims=True)
        sum_square = jnp.sum(weighted * res, axis=-1, keepdims=True)
        inverse = lax.rsqrt(square * (1.0 / HEAD_DIM) + inner_epsilon)
        scaled_mean = base_mean[at] + inverse * sum_gain * (1.0 / HEAD_DIM)
        along = inverse * (sum_base + inverse * sum_square) * (1.0 / HEAD_DIM)
        normal = res * inverse
        back_res = inverse * (rate_base[at] + rate_gain[at] * normal - scaled_mean - normal * along)
        back_low = back_res.astype(bf16)
        back_act = dot_nn(back_low, state_low)
        last_grad = (back_act * slope).astype(bf16)
        state = state - dot_tn(back_low, act)
        state_b = state_b - jnp.sum(back_res, axis=0, keepdims=True)
        grads.append(last_grad)
        acts.append(act)
        backs.append(back_low)
        slope_ref[at, :] = slope
        curve_ref[at, :] = back_act * density * (2.0 - pre * pre)
        act_ref[at, :] = act
        grad_pre_ref[at, :] = last_grad
        back_res_ref[at, :] = back_low
        norms_ref[at, :HEAD_DIM] = normal
        stats_ref[at, HEAD_DIM : HEAD_DIM + 1] = inverse
    grad_all = grad_pre_ref[...]
    act_all = act_ref[...]
    back_all = back_res_ref[...]
    start_first_b = first_b[...]
    first_w[...] = first_w[...] - dot_tn(key, grad_all)
    first_b[...] = start_first_b - jnp.sum(grad_all.astype(f32), axis=0, keepdims=True)
    second_w[...] = state
    second_b[...] = state_b

    causal = cols <= rows
    first_mix = jnp.where(causal, dot_nt(query, key) + 1.0, 0.0)
    query_pre = dot_nn(query, first_low) + start_first_b - dot_nn(first_mix, grad_all)
    density, share = density_and_share(query_pre)
    hidden = (query_pre * share).astype(bf16)
    out_slope_ref[...] = share + query_pre * density
    hidden_ref[...] = hidden
    second_mix = jnp.where(causal, dot_nt(hidden, act_all) + 1.0, 0.0)
    query_res = dot_nt(hidden, start_low) + start_b - dot_nn(second_mix, back_all)
    out_inverse = lax.rsqrt(row_mean(query_res * query_res) + inner_epsilon)
    out_normal = query_res * out_inverse
    norms_ref[:, HEAD_DIM:] = out_normal
    outputs = query.astype(f32) + out_normal * gain + bias
    centred = outputs - row_mean(outputs)
    head_inverse = lax.rsqrt(row_mean(centred * centred) + epsilon)
    head_normal = centred * head_inverse
    stats_ref[:, :HEAD_DIM] = head_normal
    stats_ref[:, HEAD_DIM + 1 : HEAD_DIM + 2] = out_inverse
    stats_ref[:, HEAD_DIM + 2 : HEAD_DIM + 3] = head_inverse
    normed_ref[...] = head_normal.astype(bf16)


def backward_kernel(
    packed_ref,
    head_grad_ref,
    act_ref,
    grad_pre_ref,
    hidden_ref,
    slope_ref,
    curve_ref,
    out_slope_ref,
    norms_ref,
    stats_ref,
    first_save,
    second_save,
    gain_ref,
    bias_ref,
    back_ref,
    first_w_out,
    first_b_out,
    second_w_out,
    second_b_out,
    gain_out,
    bias_out,
    first_w,
    first_b,
    second_w,
    second_b,
    gain_sum,
    bias_sum,
    known_ref,
    own_ref,
):
    @pl.when(pl.program_id(0) == 0)
    def _():
        first_w[...] = jnp.zeros_like(first_w)
        first_b[...] = jnp.zeros_like(first_b)
        second_w[...] = jnp.zeros_like(second_w)
        second_b[...] = jnp.zeros_like(second_b)
        gain_sum[...] = jnp.zeros_like(gain_sum)
        bias_sum[...] = jnp.zeros_like(bias_sum)
        known_ref[...] = jnp.zeros_like(known_ref)

    gain = gain_ref[...]
    bias = bias_ref[...]
    chunk = packed_ref.shape[0]
    steps = chunk // MINI
    query, key, rate, miss = unpack_chunk(packed_ref[...], bias)
    base = miss * gain
    rate_base = rate * base
    square_gain = gain * gain
    rate_gain = rate * square_gain
    normal = norms_ref[:, :HEAD_DIM]
    out_normal = norms_ref[:, HEAD_DIM:]
    head_normal = stats_ref[:, :HEAD_DIM]
    inverse = stats_ref[:, HEAD_DIM : HEAD_DIM + 1]
    out_inverse = stats_ref[:, HEAD_DIM + 1 : HEAD_DIM + 2]
    head_inverse = stats_ref[:, HEAD_DIM + 2 : HEAD_DIM + 3]
    act = act_ref[...]
    grad_pre = grad_pre_ref[...]
    hidden = hidden_ref[...]
    first_low = first_save[0]
    start_low = second_save[0, 0]
    gain_normal = rate_gain * normal
    scaled = rate_base + gain_normal
    scaled_mean = row_mean(scaled)
    along = row_mean(scaled * normal)
    back_res = (inverse * (scaled - scaled_mean - normal * along)).astype(bf16)
    coef_grad = rate_gain - along
    coef_beta = gain_normal + scaled
    gain_along = row_mean(gain_normal)
    gain_square = row_mean(gain_normal * normal)
    gain_level = row_mean(rate_gain)
    mix_cross = -(gain_along + scaled_mean)
    mix_beta = -(3.0 * along + gain_square)
    mix_alpha = -(along + gain_level)
    inverse_square = inverse * inverse

    rows, cols = token_grid(chunk)
    causal = cols <= rows
    later = rows <= cols
    head_grad = head_grad_ref[...].astype(f32)
    out_grad = head_inverse * (
        head_grad - row_mean(head_grad) - head_normal * row_mean(head_grad * head_normal)
    )
    gain_total = jnp.sum(out_grad * out_normal, axis=0, keepdims=True)
    bias_total = jnp.sum(out_grad, axis=0, keepdims=True)
    normal_grad = out_grad * gain
    res_grad = out_inverse * (
        normal_grad - row_mean(normal_grad) - out_normal * row_mean(normal_grad * out_normal)
    )
    res_grad_low = res_grad.astype(bf16)
    second_mix_grad = jnp.where(causal, -dot_nt(res_grad_low, back_res), 0.0)
    second_mix_grad_t = jnp.where(later, -dot_nt(back_res, res_grad_low), 0.0)
    hidden_grad = dot_nn(res_grad_low, start_low) + dot_nn(second_mix_grad, act)
    query_pre_grad = hidden_grad * out_slope_ref[...]
    query_pre_low = query_pre_grad.astype(bf16)
    first_mix_grad = jnp.where(causal, -dot_nt(query_pre_low, grad_pre), 0.0)
    first_mix_grad_t = jnp.where(later, -dot_nt(grad_pre, query_pre_low), 0.0)
    query_grad = out_grad + dot_nt(query_pre_low, first_low) + dot_nn(first_mix_grad, key)
    key_grad = dot_nn(first_mix_grad_t, query)
    act_grad = dot_nn(second_mix_grad_t, hidden)
    second_mix_t = jnp.where(later, dot_nt(act, hidden) + 1.0, 0.0)
    back_res_grad = -dot_nn(second_mix_t, res_grad_low)
    first_mix_t = jnp.where(later, dot_nt(key, query) + 1.0, 0.0)
    first_next = first_w[...]
    first_next_low = first_next.astype(bf16)
    pre_base = (
        -dot_nn(first_mix_t, query_pre_low) - dot_nn(key, first_next_low) - first_b[...]
    )
    after = cols // MINI > rows // MINI + 1
    near_mix = jnp.where(cols // MINI == rows // MINI + 1, dot_nt(key, key) + 1.0, 0.0).astype(bf16)
    key_mix = jnp.where(after, dot_nt(key, key) + 1.0, 0.0).astype(bf16)

    state = second_w[...]
    state_b = second_b[...]
    own_ref[...] = back_res
    pre_lows = [None] * steps
    back_grads = [None] * steps
    for step in reversed(range(steps)):
        at = slice(step * MINI, (step + 1) * MINI)
        grad = pre_base[at]
        if step + 2 < steps:
            grad = grad - dot_nn(key_mix[at], known_ref[...])
        state_low = state.astype(bf16)
        own_act = act_ref[at, :]
        own_back = own_ref[at, :]
        back_base = back_res_grad[at] - dot_nt(own_act, state_low) - state_b
        act_base = act_grad[at] - dot_nn(own_back, state_low)
        if step + 1 < steps:
            grad = grad - dot_nn(near_mix[at], known_ref[...])
        own_low = second_save[0, step]
        slope = slope_ref[at, :]
        back_act_grad = (grad * slope).astype(bf16)
        upon = back_base + dot_nt(back_act_grad, own_low)
        alpha = row_mean(upon)
        beta = row_mean(upon * normal[at])
        gamma = row_mean(upon * rate_gain[at])
        kappa = row_mean(upon * coef_beta[at])
        level = alpha * mix_alpha[at] + beta * mix_cross[at] + gamma
        tilt = alpha * mix_cross[at] + beta * mix_beta[at] + kappa
        key_res_grad = inverse_square[at] * (
            upon * coef_grad[at]
            - alpha * rate_gain[at]
            - beta * coef_beta[at]
            - level
            - normal[at] * tilt
        )
        key_res_low = key_res_grad.astype(bf16)
        pre_grad = (act_base + dot_nn(key_res_low, own_low)) * slope + grad * curve_ref[at, :]
        pre_lows[step] = pre_grad.astype(bf16)
        known_ref[at, :] = pre_lows[step]
        state = state + dot_tn(jnp.concatenate([key_res_low, own_back], axis=0), jnp.concatenate([own_act, back_act_grad], axis=0))
        state_b = state_b + jnp.sum(key_res_grad, axis=0, keepdims=True)
        back_grads[step] = upon
    pre_grad_all = known_ref[...]
    upon = jnp.concatenate(back_grads, axis=0)
    scaled_grad = inverse * (upon - row_mean(upon) - normal * row_mean(upon * normal))
    error_grad = scaled_grad * (rate * gain)
    rate_grad = jnp.sum(scaled_grad * (base + square_gain * normal), axis=-1, keepdims=True)
    error = miss + normal * gain
    gain_total += jnp.sum(scaled_grad * rate * error + error_grad * normal, axis=0, keepdims=True)
    bias_total += jnp.sum(error_grad, axis=0, keepdims=True)
    far = rows // MINI < cols // MINI
    near = rows // MINI > cols // MINI
    cross = jnp.where(far, dot_nt(grad_pre, pre_grad_all), 0.0)
    cross += jnp.where(near, dot_nt(pre_grad_all, grad_pre), 0.0)
    key_grad = (
        key_grad
        - dot_nt(grad_pre, first_next_low)
        + dot_nt(pre_grad_all, first_low)
        - dot_nn(cross, key)
        + error_grad
    )
    first_w[...] = first_next + dot_tn(key, pre_grad_all) + dot_tn(query, query_pre_low)
    first_b[...] += jnp.sum(pre_grad_all.astype(f32) + query_pre_grad, axis=0, keepdims=True)
    second_w[...] = state + dot_tn(res_grad_low, hidden)
    second_b[...] = state_b + jnp.sum(res_grad, axis=0, keepdims=True)
    gain_sum[...] += gain_total
    bias_sum[...] += bias_total
    back_rate = rate_grad * rate * (1.0 - rate * (1.0 / rate_scale))
    back_ref[:, :HEAD_DIM] = query_grad.astype(bf16)
    back_ref[:, HEAD_DIM : 2 * HEAD_DIM] = key_grad.astype(bf16)
    back_ref[:, 2 * HEAD_DIM : 3 * HEAD_DIM] = (-error_grad).astype(bf16)
    lane = lax.broadcasted_iota(jnp.int32, (chunk, HEAD_DIM), 1)
    back_ref[:, 3 * HEAD_DIM :] = jnp.where(lane == 0, back_rate, 0.0).astype(bf16)

    @pl.when(pl.program_id(0) == pl.num_programs(0) - 1)
    def _():
        first_w_out[...] = first_w[...]
        first_b_out[...] = first_b[...]
        second_w_out[...] = second_w[...]
        second_b_out[...] = second_b[...]
        gain_out[...] = gain_sum[...]
        bias_out[...] = bias_sum[...]


def whole_block(shape):
    return pl.BlockSpec(shape, lambda index: (0,) * len(shape))


STATE_SHAPES = ((HEAD_DIM, INNER), (1, INNER), (HEAD_DIM, INNER), (1, HEAD_DIM))


def saved_layout(length, chunk):
    blocks = length // chunk
    steps = chunk // MINI
    return (
        ((length, INNER), (chunk, INNER), bf16),
        ((length, INNER), (chunk, INNER), bf16),
        ((length, INNER), (chunk, INNER), bf16),
        ((length, INNER), (chunk, INNER), f32),
        ((length, INNER), (chunk, INNER), f32),
        ((length, INNER), (chunk, INNER), f32),
        ((length, 2 * HEAD_DIM), (chunk, 2 * HEAD_DIM), f32),
        ((length, 2 * HEAD_DIM), (chunk, 2 * HEAD_DIM), f32),
        ((blocks, HEAD_DIM, INNER), (1, HEAD_DIM, INNER), bf16),
        ((blocks, steps, HEAD_DIM, INNER), (1, steps, HEAD_DIM, INNER), bf16),
    )


def chain_forward(packed, state, gain, bias, chunk):
    length = packed.shape[0]
    blocks = length // chunk

    def forth(shape):
        return pl.BlockSpec(shape, lambda index: (index,) + (0,) * (len(shape) - 1))

    saved = saved_layout(length, chunk)
    row = (1, HEAD_DIM)
    return pl.pallas_call(
        forward_kernel,
        grid=(blocks,),
        in_specs=[forth((chunk, LANES))]
        + [whole_block(shape) for shape in STATE_SHAPES]
        + [whole_block(row)] * 2,
        out_specs=[forth((chunk, HEAD_DIM))] + [forth(block) for _, block, _ in saved],
        out_shape=[jax.ShapeDtypeStruct((length, HEAD_DIM), bf16)]
        + [jax.ShapeDtypeStruct(shape, dtype) for shape, _, dtype in saved],
        scratch_shapes=[pltpu.VMEM(shape, f32) for shape in STATE_SHAPES]
        + [pltpu.VMEM((chunk, HEAD_DIM), bf16)],
        compiler_params=pltpu.CompilerParams(
            dimension_semantics=("arbitrary",), vmem_limit_bytes=32 * 1024 * 1024
        ),
        name="chain_forward",
    )(packed, *state, gain, bias)


def chain_backward(packed, head_grad, saved_values, gain, bias, chunk):
    length = packed.shape[0]
    blocks = length // chunk

    def back(shape):
        return pl.BlockSpec(
            shape, lambda index: (blocks - 1 - index,) + (0,) * (len(shape) - 1)
        )

    saved = saved_layout(length, chunk)
    row = (1, HEAD_DIM)
    sums = STATE_SHAPES + (row, row)
    return pl.pallas_call(
        backward_kernel,
        grid=(blocks,),
        in_specs=[back((chunk, LANES)), back((chunk, HEAD_DIM))]
        + [back(block) for _, block, _ in saved]
        + [whole_block(row)] * 2,
        out_specs=[back((chunk, LANES))] + [whole_block(shape) for shape in sums],
        out_shape=[jax.ShapeDtypeStruct((length, LANES), bf16)]
        + [jax.ShapeDtypeStruct(shape, f32) for shape in sums],
        scratch_shapes=[pltpu.VMEM(shape, f32) for shape in sums]
        + [pltpu.VMEM((chunk, INNER), bf16), pltpu.VMEM((chunk, HEAD_DIM), bf16)],
        compiler_params=pltpu.CompilerParams(
            dimension_semantics=("arbitrary",), vmem_limit_bytes=32 * 1024 * 1024
        ),
        name="chain_backward",
    )(packed, head_grad, *saved_values, gain, bias)


def layer_norm_parts(values):
    centred = values - row_mean(values)
    inverse = lax.rsqrt(row_mean(centred * centred) + epsilon)
    return centred * inverse, inverse


def layer_norm_back(normal, inverse, scaling, grad):
    scaled = grad * scaling
    return inverse * (scaled - row_mean(scaled) - normal * row_mean(scaled * normal))


def dots(subscripts, left, right):
    return jnp.einsum(subscripts, left, right, preferred_element_type=f32)


def exchange(values, axis):
    return lax.all_to_all(values, axis, 0, 0, tiled=False)


def gather(values, axis):
    return lax.all_gather(values, axis, axis=0, tiled=True)


RATE_LANE = 3 * HEAD_DIM
VECTOR_LANE = RATE_LANE + 2
MATRIX_LANE = LANES - 32


def inner_block(matrix_one, matrix_two, vectors, rows):
    width = matrix_one.shape[-1]
    matrices = jnp.concatenate([matrix_one, matrix_two], axis=-2)
    column = jnp.concatenate(vectors, axis=-1)[..., None]
    lead = [(0, 0)] * (column.ndim - 2)
    column = jnp.pad(
        column,
        lead + [(0, rows - column.shape[-2]), (VECTOR_LANE, LANES - VECTOR_LANE - 1)],
    )
    matrices = jnp.pad(
        matrices,
        lead + [(0, rows - matrices.shape[-2]), (MATRIX_LANE, LANES - MATRIX_LANE - width)],
    )
    return column + matrices


def local(
    tokens,
    gain_attn,
    gain_ffn,
    w_qkv,
    w_rate,
    w_out,
    w_gate_up,
    w_down,
    w_one,
    b_one,
    w_two,
    b_two,
    norm_gain_inner,
    norm_bias_inner,
    cotangent,
):
    device_count = lax.axis_size("dp")
    tensor_count = lax.axis_size("tensor")
    local_rows, seq_count, width = tokens.shape
    row_count = local_rows * seq_count
    chunk = local_rows * tensor_count
    group_rows = chunk * seq_count
    head_count = w_rate.shape[1]
    local_width = head_count * HEAD_DIM
    shard = w_qkv.shape[0]
    part = gain_attn.shape[0]
    ff_local = w_down.shape[0]
    chain_count = seq_count * head_count
    inner_part = w_one.shape[2]
    feature_part = b_two.shape[1]
    assert chain_count <= device_count
    assert chunk % MINI == 0 and chunk >= 2 * HEAD_DIM and inner_part <= 32

    gain_rows = jnp.pad(
        jnp.concatenate([gain_attn, gain_ffn])[None], ((0, 0), (0, width - 2 * part))
    )
    out_rows = w_out.reshape(-1, width)
    row_pack = jnp.concatenate(
        [
            tokens.reshape(row_count, width),
            cotangent.reshape(row_count, width),
            out_rows,
            gain_rows,
        ],
        axis=0,
    )
    row_full = lax.all_gather(row_pack, "tensor", axis=0, tiled=False)
    group_tokens = row_full[:, :row_count].reshape(group_rows, width)
    group_cot = row_full[:, row_count : 2 * row_count].reshape(group_rows, width)
    out_columns = row_full[:, 2 * row_count : 2 * row_count + out_rows.shape[0]].reshape(
        tensor_count * local_width, shard
    )
    own_gains = row_full[:, -1, : 2 * part].reshape(tensor_count, 2, part)
    own_gains = own_gains.transpose(0, 2, 1).reshape(shard, 2)

    qkv_pack = jnp.concatenate([w_qkv.reshape(shard, 3 * local_width), w_rate, own_gains], axis=1)
    qkv_full = gather(qkv_pack, "dp")
    ffn_pack = jnp.concatenate(
        [w_gate_up.reshape(shard, 2 * ff_local), w_down.T, out_columns.T], axis=1
    )
    ffn_full = gather(ffn_pack, "dp")
    gate_up_full = ffn_full[:, : 2 * ff_local]
    down_full = ffn_full[:, 2 * ff_local : 3 * ff_local]
    out_full = ffn_full[:, 3 * ff_local :]
    scale_attn = qkv_full[:, -2].astype(f32)
    scale_ffn = qkv_full[:, -1].astype(f32)

    inputs = group_tokens.astype(f32)
    input_normal, _ = layer_norm_parts(inputs)
    normed_attn = (input_normal * scale_attn).astype(bf16)
    rate_columns = qkv_full[:, 3 * local_width : 3 * local_width + head_count]
    head_matrix = jnp.concatenate(
        [
            qkv_full[:, : 3 * local_width]
            .reshape(width, 3, head_count, HEAD_DIM)
            .transpose(0, 2, 1, 3)
            .reshape(width, head_count, 3 * HEAD_DIM),
            rate_columns[:, :, None],
            rate_columns[:, :, None],
            jnp.zeros((width, head_count, LANES - RATE_LANE - 2), bf16),
        ],
        axis=2,
    )
    projected = dots("rd,dhk->rhk", normed_attn, head_matrix)
    lane = lax.broadcasted_iota(jnp.int32, projected.shape, 2)
    rest = projected - lax.reduce_precision(projected, 8, 7)
    packed = jnp.where(lane == RATE_LANE + 1, rest, projected).astype(bf16)
    packed = packed.reshape(chunk, seq_count, head_count, LANES).transpose(1, 2, 0, 3)
    inner = inner_block(
        w_one,
        w_two.transpose(0, 2, 1),
        [b_one, b_two, norm_gain_inner, norm_bias_inner],
        chunk,
    )
    packed = (packed + inner[None]).reshape(chain_count, chunk, LANES)
    spare = jnp.zeros((device_count - chain_count, chunk, LANES), bf16)
    chain_in = exchange(jnp.concatenate([packed, spare], axis=0), "dp")

    normed_full = gather(normed_attn[None], "dp").reshape(
        device_count * chunk, seq_count, width
    )

    first_w = chain_in[:, :HEAD_DIM, MATRIX_LANE : MATRIX_LANE + inner_part]
    first_w = first_w.transpose(1, 0, 2).reshape(HEAD_DIM, INNER).astype(f32)
    second_w = chain_in[:, HEAD_DIM : 2 * HEAD_DIM, MATRIX_LANE : MATRIX_LANE + inner_part]
    second_w = second_w.transpose(1, 0, 2).reshape(HEAD_DIM, INNER).astype(f32)
    vectors = chain_in[:, :, VECTOR_LANE].astype(f32)
    first_b = vectors[:, :inner_part].reshape(1, INNER)
    small = vectors[:, inner_part : inner_part + 3 * feature_part]
    small = small.reshape(device_count, 3, feature_part).transpose(1, 0, 2).reshape(3, HEAD_DIM)
    second_b, inner_gain, inner_bias = small[0:1], small[1:2], small[2:3]
    second_w = second_w - jnp.mean(second_w, axis=0, keepdims=True)
    second_b = second_b - row_mean(second_b)
    chain_rows = chain_in.reshape(device_count * chunk, LANES)
    forward_out = chain_forward(
        chain_rows, (first_w, first_b, second_w, second_b), inner_gain, inner_bias, chunk
    )
    saved = forward_out[1:]
    head_send = forward_out[0].reshape(device_count, chunk, HEAD_DIM)
    head_back = exchange(head_send, "dp")[:chain_count]
    head_local = (
        head_back.reshape(seq_count, head_count, chunk, HEAD_DIM)
        .transpose(2, 0, 1, 3)
        .reshape(group_rows, local_width)
    )
    head_rows = lax.all_gather(head_local, "tensor", axis=1, tiled=True)

    mixed = inputs + dots("rk,dk->rd", head_rows, out_full)
    ffn_normal, _ = layer_norm_parts(mixed)
    normed_ffn = (ffn_normal * scale_ffn).astype(bf16)
    gate_up = dots("rd,df->rf", normed_ffn, gate_up_full)
    gate, up = gate_up[:, :ff_local], gate_up[:, ff_local:]
    share = jax.nn.sigmoid(gate)
    silu = gate * share
    swiglu = (silu * up).astype(bf16)
    back_swiglu = dots("rd,df->rf", group_cot, down_full)
    back_gate_up = jnp.concatenate(
        [back_swiglu * up * (share * (1.0 + gate * (1.0 - share))), back_swiglu * silu], axis=1
    ).astype(bf16)
    down_term = dots("rf,df->rd", swiglu, down_full).astype(bf16)
    ffn_term = dots("rf,df->rd", back_gate_up, gate_up_full).astype(bf16)
    terms = jnp.stack(
        [
            down_term.reshape(tensor_count, row_count, width),
            ffn_term.reshape(tensor_count, row_count, width),
        ],
        axis=1,
    )
    sums = exchange(terms, "tensor").astype(f32).sum(axis=0)
    rank = lax.axis_index("tensor")
    own_mixed = lax.dynamic_slice_in_dim(mixed, rank * row_count, row_count, 0)
    result = (own_mixed + sums[0]).astype(bf16)
    own_normal, own_inverse = layer_norm_parts(own_mixed)
    back_mixed = cotangent.reshape(row_count, width).astype(f32) + layer_norm_back(
        own_normal, own_inverse, scale_ffn, sums[1]
    )
    attn_grads = gather(back_mixed.astype(bf16), "tensor")
    own_out = lax.dynamic_slice_in_dim(out_full, rank * local_width, local_width, 1)
    back_head = dots("rd,dk->rk", attn_grads, own_out).astype(bf16)
    back_head = (
        back_head.reshape(chunk, seq_count, head_count, HEAD_DIM)
        .transpose(1, 2, 0, 3)
        .reshape(chain_count, chunk, HEAD_DIM)
    )
    spare = jnp.zeros((device_count - chain_count, chunk, HEAD_DIM), bf16)
    head_grad = exchange(jnp.concatenate([back_head, spare], axis=0), "dp")
    head_grad = head_grad.reshape(device_count * chunk, HEAD_DIM)

    matrix_grads = jnp.concatenate(
        [
            dots("rd,rf->df", normed_ffn, back_gate_up),
            dots("rd,rf->df", group_cot, swiglu),
            dots("rd,rk->dk", attn_grads, head_local),
        ],
        axis=1,
    ).astype(bf16)
    matrix_sums = lax.psum_scatter(matrix_grads, "dp", scatter_dimension=0, tiled=True)
    matrix_sums = matrix_sums.astype(f32)

    backward_out = chain_backward(chain_rows, head_grad, saved, inner_gain, inner_bias, chunk)
    back_packed, state_grads = backward_out[0], backward_out[1:]
    sequence = jnp.minimum(lax.axis_index("dp") // head_count, seq_count - 1)
    chain_normed = lax.dynamic_index_in_dim(normed_full, sequence, 1, keepdims=False)
    grad_packed = dots("rd,rk->dk", chain_normed, back_packed).astype(bf16)
    by_part = lambda values: (
        values.reshape(HEAD_DIM, device_count, inner_part).transpose(1, 0, 2).astype(bf16)
    )
    split = lambda values, size: values.reshape(device_count, size).astype(bf16)
    inner_grads = inner_block(
        by_part(state_grads[0]),
        by_part(state_grads[2]),
        [
            split(state_grads[1], inner_part),
            split(state_grads[3], feature_part),
            split(state_grads[4], feature_part),
            split(state_grads[5], feature_part),
        ],
        chunk,
    )
    send = jnp.concatenate(
        [
            back_packed.reshape(device_count, chunk, LANES) + inner_grads,
            grad_packed.reshape(device_count, shard, LANES),
        ],
        axis=1,
    )
    received = exchange(send, "dp")[:chain_count]
    back_rows = received[:, :chunk].reshape(seq_count, head_count, chunk, LANES)
    attn_term = dots("shck,dhk->csd", back_rows, head_matrix_back(head_matrix))
    attn_term = attn_term.reshape(tensor_count, row_count, width).astype(bf16)

    by_head = received.astype(f32).reshape(seq_count, head_count, chunk + shard, LANES).sum(axis=0)
    grad_block = by_head[:, chunk:]
    grad_qkv = (
        grad_block[:, :, :RATE_LANE]
        .reshape(head_count, shard, 3, HEAD_DIM)
        .transpose(1, 2, 0, 3)
        .reshape(shard, 3, local_width)
    )
    grad_rate = grad_block[:, :, RATE_LANE].T
    grad_one = by_head[:, :HEAD_DIM, MATRIX_LANE : MATRIX_LANE + inner_part]
    grad_two = by_head[:, HEAD_DIM : 2 * HEAD_DIM, MATRIX_LANE : MATRIX_LANE + inner_part]
    grad_two = grad_two.transpose(0, 2, 1)
    columns = by_head[:, :, VECTOR_LANE]
    ends = [inner_part + index * feature_part for index in range(4)]
    grad_b_one = columns[:, : ends[0]]
    grad_b_two, grad_gain_inner, grad_bias_inner = (
        columns[:, ends[index] : ends[index + 1]] for index in range(3)
    )

    gain_one = (
        jnp.sum(grad_qkv * w_qkv.astype(f32), axis=(1, 2))
        + jnp.sum(grad_rate * w_rate.astype(f32), axis=1)
    ) / own_gains[:, 0].astype(f32)
    grad_gate_up = matrix_sums[:, : 2 * ff_local].reshape(shard, 2, ff_local)
    gain_two = jnp.sum(grad_gate_up * w_gate_up.astype(f32), axis=(1, 2)) / own_gains[:, 1].astype(
        f32
    )
    gain_terms = jnp.stack([gain_one, gain_two]).reshape(2, tensor_count, part).transpose(1, 0, 2)
    gain_terms = gain_terms.reshape(tensor_count, 1, 2 * part)
    gain_high = gain_terms.astype(bf16)
    gain_low = (gain_terms - lax.reduce_precision(gain_terms, 8, 7)).astype(bf16)
    gain_send = jnp.pad(
        jnp.concatenate([gain_high, gain_low], axis=1), ((0, 0), (0, 0), (0, width - 2 * part))
    )
    tail = exchange(jnp.concatenate([attn_term, gain_send], axis=1), "tensor")
    tail = tail.astype(f32).sum(axis=0)
    gain_sums = tail[row_count, : 2 * part] + tail[row_count + 1, : 2 * part]
    own_inputs = tokens.reshape(row_count, width).astype(f32)
    own_normal, own_inverse = layer_norm_parts(own_inputs)
    input_grad = back_mixed + layer_norm_back(own_normal, own_inverse, scale_attn, tail[:row_count])

    return (
        result.reshape(tokens.shape),
        input_grad.reshape(tokens.shape),
        gain_sums[:part],
        gain_sums[part:],
        grad_qkv,
        grad_rate,
        matrix_sums[:, 3 * ff_local :].T,
        grad_gate_up,
        matrix_sums[:, 2 * ff_local : 3 * ff_local].T,
        grad_one,
        grad_b_one,
        grad_two,
        grad_b_two,
        grad_gain_inner,
        grad_bias_inner,
    )


def head_matrix_back(head_matrix):
    lane = lax.broadcasted_iota(jnp.int32, head_matrix.shape, 2)
    return jnp.where(lane <= RATE_LANE, head_matrix, jnp.zeros_like(head_matrix))


def solution(mesh):
    rows = P(("dp", "tensor"), None, None)
    gains = P(("dp", "tensor"))
    placed = (
        rows,
        gains,
        gains,
        P("dp", None, "tensor"),
        P("dp", "tensor"),
        P("tensor", "dp"),
        P("dp", None, "tensor"),
        P("tensor", "dp"),
        P("tensor", None, "dp"),
        P("tensor", "dp"),
        P("tensor", "dp", None),
        P("tensor", "dp"),
        P("tensor", "dp"),
        P("tensor", "dp"),
    )
    return jax.shard_map(
        local,
        mesh=mesh,
        in_specs=placed + (rows,),
        out_specs=(rows,) + placed,
        check_vma=False,
    )
```

time: 2960 us -> 384 us (0.13)
  matrix products: 953 us -> 18.7 us
  waiting for transfers between devices: 546 us -> 66.8 us
  local copies, waits for them, and re-layouts: 520 us -> 70.8 us
  other arithmetic: 421 us -> 21.1 us
  blocking collectives: 391 us -> 60.5 us
  Pallas kernels: 0 us -> 104 us
  loops' own time: 46.7 us -> 0 us
    dot_general x3399 -> x12, matrix products: 953 us -> 18.7 us  [dots(): return jnp.einsum(subscripts, left, right, preferred_element_type=f32)]
    reduce_scatter x9 -> x1, waiting for transfers between devices: 341 us -> 0.01 us  [local(): lax.psum_scatter(matrix_grads, 'dp', scatter_dimension=0, tiled=True)]
    squeeze x531 -> x0, local copies, waits for them, and re-layouts: 245 us -> none  [the longest x504 243 us: run_group(): final, outputs = lax.scan(jax.checkpoint(one_step), state, shaped)]
    all_gather x14 -> x4, blocking collectives: 281 us -> 60.5 us  [the longest x2 41.6 us: gather(): return lax.all_gather(values, axis, axis=0, tiled=True)]
    reduce_sum x1308 -> x17, other arithmetic: 195 us -> 7.61 us  [the longest x10 5.14 us: row_mean(): return jnp.mean(values, axis=-1, keepdims=True)]
    unnamed x16 -> x3, waiting for transfers between devices: 149 us -> 0.05 us
    dynamic_update_slice x432 -> x0, local copies, waits for them, and re-layouts: 147 us -> none  [run_group(): final, outputs = lax.scan(jax.checkpoint(one_step), state, shaped)]
    unnamed x3 -> x0, blocking collectives: 110 us -> none
where the time goes in v1:
time: 384 us; the launch traced here: 382 us
  Pallas kernels  104 us (27%)
  local copies, waits for them, and re-layouts  70.8 us (18%)
  waiting for transfers between devices  66.8 us (17%)
  blocking collectives  60.5 us (16%)
  starting transfers between devices  23.9 us (6%)
  other arithmetic  21.1 us (5%)
  matrix products  18.7 us (5%)
  between operations  15.7 us (4%)
    all_to_all x6, waiting for transfers between devices, exchange(): return lax.all_to_all(values, axis, 0, 0, tiled=False)  66.7 us
    pallas_call x1, Pallas kernels, chain_forward(): pl.pallas_call(forward_kernel, grid=(blocks,), in_specs=[forth((chunk, LA...  54.5 us
    pallas_call x1, Pallas kernels, chain_backward(): pl.pallas_call(backward_kernel, grid=(blocks,), in_specs=[back((chunk, LA...  49.9 us
    all_gather x2, blocking collectives, gather(): return lax.all_gather(values, axis, axis=0, tiled=True)  41.6 us
    unnamed x140, local copies, waits for them, and re-layouts  23.8 us
    all_to_all x6, starting transfers between devices, exchange(): return lax.all_to_all(values, axis, 0, 0, tiled=False)  23.6 us
    dot_general x12, matrix products, dots(): return jnp.einsum(subscripts, left, right, preferred_element_type=f32)  18.7 us
    all_gather x1, blocking collectives, local(): row_full = lax.all_gather(row_pack, 'tensor', axis=0, tiled=False)  11.2 us
  transfers between devices with their start and end apart: 9, of which 6 were waited for; matrix products, arithmetic and copies ran while one was open for 21% of the time, Pallas kernels for 27%

profile of v1, /device:TPU:0, one launch (start us, length us, event | category | flops | bytes accessed | tf_op | source)
XLA Modules:
  0.0 381.6 jit_solution(12709665122990432386)
XLA Ops:
  11.0 11.2 %all-gather.1 = bf16[4,153,768]{2,1,0:T(8,128)(2,1)S(1)} all-gather(bf16[1,153,768]{2,1,0:T(8,128)(2,1)S(1)} %fusion.45), channel_id=2, replica_groups=mesh['dp'=8,'tensor'=4] {'tensor'}, dimensions={0}, use_global_device_ids=true | all-gather | bytes 1175040 | tf_op jit(solution)/shard_map/all_gather | solution.py:561
  25.0 35.5 %all_gather.23 = bf16[768,581]{1,0:T(8,128)(2,1)S(1)} all-gather(bf16[96,581]{1,0:T(8,128)(2,1)S(1)} %copy.223), channel_id=1, replica_groups=mesh['dp'=8,'tensor'=4] {'dp'}, dimensions={0}, use_global_device_ids=true | all-gather | bytes 1003968 | tf_op jit(solution)/shard_map/all_gather | solution.py:490
  62.2 2.3 copy.227
  65.8 2.2 fusion.15
  69.5 5.4 %all-to-all-start = ((bf16[8,128,256]{2,1,0:T(8,128)(2,1)}), bf16[8,128,256]{2,1,0:T(8,128)(2,1)S(1)}, u32[]{:S(2)}, u32[]{:S(2)}) async-start(bf16[8,128,256]{2,1,0:T(8,128)(2,1)} %concatenate.57), calls=%async_computation | async-start | bytes 1048576 | tf_op jit(solution)/shard_map/all_to_all | solution.py:486
  77.6 25.2 %all-to-all-done = bf16[8,128,256]{2,1,0:T(8,128)(2,1)S(1)} async-done(((bf16[8,128,256]{2,1,0:T(8,128)(2,1)}), bf16[8,128,256]{2,1,0:T(8,128)(2,1)S(1)}, u32[]{:S(2)}, u32[]{:S(2)}) %all-to-all-start) | async-done | bytes 524320 | tf_op jit(solution)/shard_map/all_to_all | solution.py:486
  105.6 54.5 %chain_forward.1 = (bf16[1024,64]{1,0:T(8,128)(2,1)S(1)}, bf16[1024,256]{1,0:T(8,128)(2,1)S(1)}, bf16[1024,256]{1,0:T(8,128)(2,1)S(1)}, bf16[1024,256]{1,0:T(8,1...) custom-call(bf16[1024,256]{1,0:T(8,128)(2,1)S(1)} %bitcast.149, ...), custom_call_target="tpu_custom_call" | custom-call | tf_op jit(solution)/shard_map/chain_forward/pallas_call | solution.py:422
  166.9 1.8 copy.238
  168.7 3.4 all-to-all-start.1
  172.1 7.3 %all-to-all-done.1 = bf16[8,128,64]{1,2,0:T(8,128)(2,1)S(1)} async-done(((bf16[8,128,64]{1,2,0:T(8,128)(2,1)}), bf16[8,128,64]{1,2,0:T(8,128)(2,1)S(1)}, u32[]{:S(2)}, u32[]{:S(2)}) %all-to-all-start.1) | async-done | bytes 131104 | tf_op jit(solution)/shard_map/all_to_all | solution.py:486
  180.1 1.8 copy.239
  181.8 1.1 reshape.513
  183.7 7.6 %all_gather.24 = bf16[256,768]{0,1:T(8,128)(2,1)} all-gather(bf16[256,192]{0,1:T(8,128)(2,1)} %copy.240), channel_id=1, replica_groups=mesh['dp'=8,'tensor'=4] {'tensor'}, dimensions={1}, use_global_device_ids=true | all-gather | bytes 491520 | tf_op jit(solution)/shard_map/all_gather | solution.py:640
  191.3 2.4 fusion.64
  197.9 4.2 %all-to-all-start.2 = ((bf16[4,2,64,768]{3,2,1,0:T(8,128)(2,1)}), bf16[4,2,64,768]{3,2,1,0:T(8,128)(2,1)}, u32[]{:S(2)}, u32[]{:S(2)}) async-start(bf16[4,2,64,768]{3,2,1,0:T(8,128)(2,1)} %pad_maximum_fusion.2), calls=%async_computation.2 | async-start | bytes 1572864 | tf_op jit(solution)/shard_map/all_to_all | solution.py:486
  202.4 1.0 dynamic-slice_reduce_fusion
  203.9 1.1 multiply_reduce_fusion.6
  205.6 2.3 convolution_convert_fusion.1
  207.9 3.2 convolution_convert_fusion
  211.1 2.8 all-to-all-done.2
  213.9 1.3 convert_reduce_fusion
  215.2 1.1 fusion.51
  216.3 1.7 fusion.61
  218.1 6.1 %all_gather.26 = bf16[256,768]{1,0:T(8,128)(2,1)S(1)} all-gather(bf16[64,768]{1,0:T(8,128)(2,1)S(1)} %get-tuple-element.152), channel_id=1, replica_groups=mesh['dp'=8,'tensor'=4] {'tensor'}, dimensions={0}, use_global_device_ids=true | all-gather | bytes 491520 | tf_op jit(solution)/shard_map/all_gather | solution.py:490
  224.2 1.9 convolution_convert_fusion.3
  226.1 1.9 copy.259
  228.0 3.5 pad_maximum_fusion
  231.6 7.3 %reshape.522 = bf16[1024,2,768]{2,1,0:T(2,128)(2,1)} reshape(bf16[8,256,768]{2,1,0:T(8,128)(2,1)} %all-gather.7.cloned.1.call-done) | data formatting | bytes 6291456 | tf_op jit(solution)/shard_map/reshape | solution.py:613
  238.9 1.3 slice-done
  240.1 1.2 convolution_convert_fusion.4
  243.3 3.4 all-to-all-start.3
  246.7 6.8 %constant_dynamic-slice_fusion = bf16[1024,1,768]{2,1,0:T(2,128)(2,1)} fusion(bf16[1024,2,768]{2,1,0:T(2,128)(2,1)} %reshape.522, s32[]{:T(128)S(6)} %select_n.28), kind=kLoop, calls=%fused_computation.133 | loop fusion | bytes 3145732 | tf_op jit(solution)/shard_map/jit(dynamic_index_in_dim)/dynamic_slice | solution.py:697
  253.5 3.4 all-to-all-done.3
  257.1 1.2 copy-done.1
  258.3 1.2 copy-done.3
  259.6 1.2 copy-done.5
  260.8 1.0 copy-done.7
  261.8 1.0 copy-done.9
  262.9 1.1 copy-done.11
  264.0 1.0 copy-done.13
  266.0 49.9 %chain_backward.1 = (bf16[1024,256]{1,0:T(8,128)(2,1)S(1)}, f32[64,256]{1,0:T(8,128)S(1)}, f32[1,256]{1,0:T(1,128)S(1)}, f32[64,256]{1,0:T(8,128)S(1)}, f32[1,64...) custom-call(bf16[1024,256]{1,0:T(8,128)(2,1)S(1)} %bitcast.150, bf16[1024,64]{1,0:T(8,128)(2,1)S(1)} %bitcast.151, ...), custom_call_target="tpu_custom_call" | custom-call | tf_op jit(solution)/shard_map/chain_backward/pallas_call | solution.py:452
  318.3 1.4 copy.251
  320.0 2.6 fusion.10
  323.4 1.7 copy.253
  325.1 3.8 all-to-all-start.4
  330.5 21.6 %all-to-all-done.4 = bf16[8,224,256]{2,1,0:T(8,128)(2,1)S(1)} async-done(((bf16[8,224,256]{2,1,0:T(8,128)(2,1)}), bf16[8,224,256]{2,1,0:T(8,128)(2,1)S(1)}, u32[]{:S(2)}, u32[]{:S(2)}) %all-to-all-start.4) | async-done | bytes 917536 | tf_op jit(solution)/shard_map/all_to_all | solution.py:486
  361.9 3.5 all-to-all-start.5
  366.9 6.4 %all-to-all-done.5 = bf16[4,66,768]{2,1,0:T(8,128)(2,1)S(1)} async-done(((bf16[4,66,768]{2,1,0:T(8,128)(2,1)}), bf16[4,66,768]{2,1,0:T(8,128)(2,1)S(1)}, u32[]{:S(2)}, u32[]{:S(2)}) %all-to-all-start.5) | async-done | bytes 405536 | tf_op jit(solution)/shard_map/all_to_all | solution.py:486
  (287 shorter events, 50.1 us)
Async XLA Ops:
  7.2 15.5 %copy-start.35 = (bf16[96,2,512]{2,1,0:T(2,128)(2,1)S(1)}, bf16[96,2,512]{2,1,0:T(2,128)(2,1)}, u32[]{:S(2)}) copy-start(bf16[96,2,512]{2,1,0:T(2,128)(2,1)} %param.21) | copy-start | bytes 589828
  7.2 15.5 %copy-start.47 = (bf16[512,96]{0,1:T(8,128)(2,1)S(1)}, bf16[512,96]{0,1:T(8,128)(2,1)}, u32[]{:S(2)}) copy-start(bf16[512,96]{0,1:T(8,128)(2,1)} %param.22) | copy-start | bytes 294916
  7.2 184.1 %all-gather.5.cloned.1.call-start = ((), (), s32[]{:S(2)}) async-start(), calls=%async_computation.7 | async-start | bytes 3981312 | tf_op jit(solution)/shard_map/all_gather | solution.py:490
  8.3 15.4 %copy-start.24 = (bf16[64,768]{1,0:T(8,128)(2,1)}, bf16[64,768]{1,0:T(8,128)(2,1)S(1)}, u32[]{:S(2)}) copy-start(bf16[64,768]{1,0:T(8,128)(2,1)S(1)} %reshape.499) | copy-start | bytes 294916
  9.2 14.4 %copy-start.33 = (bf16[64,768]{1,0:T(8,128)(2,1)}, bf16[64,768]{1,0:T(8,128)(2,1)S(1)}, u32[]{:S(2)}) copy-start(bf16[64,768]{1,0:T(8,128)(2,1)S(1)} %reshape.500) | copy-start | bytes 294916
  11.0 13.3 %copy-start.44 = (bf16[96,3,192]{2,0,1:T(8,128)(2,1)S(1)}, bf16[96,3,192]{2,0,1:T(8,128)(2,1)}, u32[]{:S(2)}) copy-start(bf16[96,3,192]{2,0,1:T(8,128)(2,1)} %param.18) | copy-start | bytes 331780
  11.0 13.8 %copy-start.56 = (bf16[96,3]{0,1:T(4,128)(2,1)S(1)}, bf16[96,3]{0,1:T(4,128)(2,1)}, u32[]{:S(2)}) copy-start(bf16[96,3]{0,1:T(4,128)(2,1)} %param.19) | copy-start | bytes 1732
  24.5 37.7 %copy-start.28 = (bf16[96,3,192]{0,2,1:T(8,128)(2,1)}, bf16[96,3,192]{0,2,1:T(8,128)(2,1)S(1)}, u32[]{:S(2)}) copy-start(bf16[96,3,192]{0,2,1:T(8,128)(2,1)S(1)} %copy.221) | copy-start | bytes 331780
  65.0 2.9 copy-start.38
  65.1 2.8 copy-start.63
  65.4 10.3 %copy-start.45 = (f32[768]{0:T(1024)}, f32[768]{0:T(1024)S(1)}, u32[]{:S(2)}) copy-start(f32[768]{0:T(1024)S(1)} %get-tuple-element.142) | copy-start | bytes 9220
  65.7 2.4 copy-start.48
  65.7 2.5 copy-start.49
  65.7 2.5 copy-start.59
  65.7 2.5 copy-start.60
  65.7 2.5 copy-start.61
  65.7 2.5 copy-start.62
  69.5 33.3 %all-to-all-start = ((bf16[8,128,256]{2,1,0:T(8,128)(2,1)}), bf16[8,128,256]{2,1,0:T(8,128)(2,1)S(1)}, u32[]{:S(2)}, u32[]{:S(2)}) async-start(bf16[8,128,256]{2,1,0:T(8,128)(2,1)} %concatenate.57), calls=%async_computation | async-start | bytes 1048576 | tf_op jit(solution)/shard_map/all_to_all | solution.py:486
  74.9 156.7 %all-gather.7.cloned.1.call-start = ((), (), s32[]{:S(2)}) async-start(), calls=%async_computation.8 | async-start | bytes 3538944 | tf_op jit(solution)/shard_map/all_gather | solution.py:490
  166.9 26.8 %copy-start.15 = (bf16[8,64,256]{2,1,0:T(8,128)(2,1)}, bf16[8,64,256]{2,1,0:T(8,128)(2,1)S(1)}, u32[]{:S(2)}) copy-start(bf16[8,64,256]{2,1,0:T(8,128)(2,1)S(1)} %get-tuple-element.42.first_save) | copy-start | bytes 786436
  168.7 10.7 %all-to-all-start.1 = ((bf16[8,128,64]{1,2,0:T(8,128)(2,1)}), bf16[8,128,64]{1,2,0:T(8,128)(2,1)S(1)}, u32[]{:S(2)}, u32[]{:S(2)}) async-start(bf16[8,128,64]{1,2,0:T(8,128)(2,1)} %copy.238), calls=%async_computation.1 | async-start | bytes 262144 | tf_op jit(solution)/shard_map/all_to_all | solution.py:486
  183.0 11.8 %copy-start.30 = (bf16[256,192]{1,0:T(8,128)(2,1)}, bf16[256,192]{1,0:T(8,128)(2,1)S(1)}, u32[]{:S(2)}) copy-start(bf16[256,192]{1,0:T(8,128)(2,1)S(1)} %reshape.513) | copy-start | bytes 294916
  191.3 2.7 copy-start.21
  193.7 1.9 copy-start.19
  193.7 1.4 copy-start.26
  194.0 1.6 copy-start.55
  197.0 8.6 %copy-start.27 = (bf16[4,64,768]{2,1,0:T(8,128)(2,1)S(1)}, bf16[4,64,768]{2,1,0:T(8,128)(2,1)}, u32[]{:S(2)}) copy-start(bf16[4,64,768]{2,1,0:T(8,128)(2,1)} %get-tuple-element.159) | copy-start | bytes 1179652
  197.9 15.9 %all-to-all-start.2 = ((bf16[4,2,64,768]{3,2,1,0:T(8,128)(2,1)}), bf16[4,2,64,768]{3,2,1,0:T(8,128)(2,1)}, u32[]{:S(2)}, u32[]{:S(2)}) async-start(bf16[4,2,64,768]{3,2,1,0:T(8,128)(2,1)} %pad_maximum_fusion.2), calls=%async_computation.2 | async-start | bytes 1572864 | tf_op jit(solution)/shard_map/all_to_all | solution.py:486
  202.1 156.5 %reduce-scatter.2.cloned.1.call-start = ((), (), s32[]{:S(2)}) async-start(), calls=%async_computation.9 | async-start | bytes 3096576 | tf_op jit(solution)/shard_map/reduce_scatter | solution.py:691
  207.9 7.3 %copy-start.54 = (f32[64]{0:T(128)S(1)}, f32[64]{0:T(128)}, u32[]{:S(2)}) copy-start(f32[64]{0:T(128)} %copy-done.53) | copy-start | bytes 772
  207.9 7.3 %copy-start.58 = (f32[64]{0:T(128)S(1)}, f32[64]{0:T(128)}, u32[]{:S(2)}) copy-start(f32[64]{0:T(128)} %add_rsqrt_fusion.3) | copy-start | bytes 772
  207.9 8.5 %copy-start.34 = (bf16[64,768]{1,0:T(8,128)(2,1)S(1)}, bf16[64,768]{1,0:T(8,128)(2,1)}, u32[]{:S(2)}) copy-start(bf16[64,768]{1,0:T(8,128)(2,1)} %copy-done.33) | copy-start | bytes 294916
  243.3 13.6 %all-to-all-start.3 = ((bf16[8,128,64]{1,2,0:T(8,128)(2,1)}), bf16[8,128,64]{1,2,0:T(8,128)(2,1)S(1)}, u32[]{:S(2)}, u32[]{:S(2)}) async-start(bf16[8,128,64]{1,2,0:T(8,128)(2,1)} %concatenate.60), calls=%async_computation.3 | async-start | bytes 262144 | tf_op jit(solution)/shard_map/all_to_all | solution.py:486
  323.3 5.6 %copy-start.52 = (bf16[96,2]{0,1:T(2,128)(2,1)S(1)}, bf16[96,2]{0,1:T(2,128)(2,1)}, u32[]{:S(2)}) copy-start(bf16[96,2]{0,1:T(2,128)(2,1)} %copy-done.51) | copy-start | bytes 1156
  323.3 5.8 %copy-start.32 = (bf16[32,2,768]{2,1,0:T(2,128)(2,1)S(1)}, bf16[32,2,768]{2,1,0:T(2,128)(2,1)}, u32[]{:S(2)}) copy-start(bf16[32,2,768]{2,1,0:T(2,128)(2,1)} %param.15) | copy-start | bytes 294916
  323.3 6.4 %copy-start.40 = (bf16[64,768]{1,0:T(8,128)(2,1)S(1)}, bf16[64,768]{1,0:T(8,128)(2,1)}, u32[]{:S(2)}) copy-start(bf16[64,768]{1,0:T(8,128)(2,1)} %get-tuple-element.156) | copy-start | bytes 294916
  323.3 28.8 %copy-start.31 = (bf16[768,3,192]{2,0,1:T(8,128)(2,1)S(1)}, bf16[768,3,192]{2,0,1:T(8,128)(2,1)}, u32[]{:S(2)}) copy-start(bf16[768,3,192]{2,0,1:T(8,128)(2,1)} %copy.227) | copy-start | bytes 2654212
  323.3 28.8 %copy-start.39 = (bf16[768,3,1]{2,0,1:T(8,128)(2,1)S(1)}, bf16[768,3,1]{2,0,1:T(8,128)(2,1)}, u32[]{:S(2)}) copy-start(bf16[768,3,1]{2,0,1:T(8,128)(2,1)} %copy-done.38) | copy-start | bytes 13828
  323.4 28.8 %copy-start.64 = (bf16[256]{0:T(256)(128)(2,1)S(1)}, bf16[256]{0:T(256)(128)(2,1)}, u32[]{:S(2)}) copy-start(bf16[256]{0:T(256)(128)(2,1)} %copy-done.63) | copy-start | bytes 1540
  325.1 27.0 %all-to-all-start.4 = ((bf16[8,224,256]{2,1,0:T(8,128)(2,1)}), bf16[8,224,256]{2,1,0:T(8,128)(2,1)S(1)}, u32[]{:S(2)}, u32[]{:S(2)}) async-start(bf16[8,224,256]{2,1,0:T(8,128)(2,1)} %copy.253), calls=%async_computation.4 | async-start | bytes 1835008 | tf_op jit(solution)/shard_map/all_to_all | solution.py:486
  353.7 6.3 %copy-start.36 = (bf16[96,2,512]{2,1,0:T(2,128)(2,1)S(1)}, bf16[96,2,512]{2,1,0:T(2,128)(2,1)}, u32[]{:S(2)}) copy-start(bf16[96,2,512]{2,1,0:T(2,128)(2,1)} %param.21) | copy-start | bytes 589828
  354.2 7.7 %copy-start.50 = (f32[3,96]{1,0:T(4,128)}, f32[3,96]{1,0:T(4,128)S(1)}, u32[]{:S(2)}) copy-start(f32[3,96]{1,0:T(4,128)S(1)} %slice_reduce_fusion.1) | copy-start | bytes 3460
  358.6 6.7 %copy-start.22 = (bf16[96,1728]{1,0:T(8,128)(2,1)S(1)}, bf16[96,1728]{1,0:T(8,128)(2,1)}, u32[]{:S(2)}) copy-start(bf16[96,1728]{1,0:T(8,128)(2,1)} %reduce-scatter.2.cloned.1.call-done) | copy-start | bytes 995332
  360.0 13.3 %copy-start.23 = (f32[96,2,512]{2,1,0:T(2,128)}, f32[96,2,512]{2,1,0:T(2,128)S(1)}, u32[]{:S(2)}) copy-start(f32[96,2,512]{2,1,0:T(2,128)S(1)} %reshape.529) | copy-start | bytes 1179652
  360.0 13.3 %copy-start.25 = (bf16[64,768]{1,0:T(8,128)(2,1)S(1)}, bf16[64,768]{1,0:T(8,128)(2,1)}, u32[]{:S(2)}) copy-start(bf16[64,768]{1,0:T(8,128)(2,1)} %copy-done.24) | copy-start | bytes 294916
  360.0 13.3 %copy-start.46 = (f32[768]{0:T(1024)S(1)}, f32[768]{0:T(1024)}, u32[]{:S(2)}) copy-start(f32[768]{0:T(1024)} %copy-done.45) | copy-start | bytes 9220
  360.8 12.8 %copy-start.37 = (f32[64,768]{1,0:T(8,128)S(1)}, f32[64,768]{1,0:T(8,128)}, u32[]{:S(2)}) copy-start(f32[64,768]{1,0:T(8,128)} %get-tuple-element.153) | copy-start | bytes 589828
  361.9 11.4 %all-to-all-start.5 = ((bf16[4,66,768]{2,1,0:T(8,128)(2,1)}), bf16[4,66,768]{2,1,0:T(8,128)(2,1)S(1)}, u32[]{:S(2)}, u32[]{:S(2)}) async-start(bf16[4,66,768]{2,1,0:T(8,128)(2,1)} %fusion.39), calls=%async_computation.6 | async-start | bytes 884736 | tf_op jit(solution)/shard_map/all_to_all | solution.py:486
  (27 other events, 25.1 us)
Sparse Core Ops, SparseCore 0:
  23.6 82.7 all-gather.4
  108.7 59.6 all-gather.6
  231.6 71.1 reduce-scatter.1

commit v2 on v1

--- a/solution.py
+++ b/solution.py
@@ -1,3 +1,6 @@
+import functools
+
+
 import jax
 import jax.numpy as jnp
 from jax import lax
@@ -9,6 +12,11 @@
 INNER = 256
 MINI = 16
 LANES = 256
+RATE_LANE = 3 * HEAD_DIM
+VECTOR_LANE = RATE_LANE + 2
+MATRIX_LANE = LANES - 32
+VMEM_BYTES = 56 * 1024 * 1024
+GLUE_BYTES = 32 * 1024 * 1024
 
 epsilon = 1e-05
 inner_epsilon = 1e-06
@@ -66,13 +74,9 @@
 
 
 def forward_kernel(
+    inner_part,
+    feature_part,
     packed_ref,
-    first_w_in,
-    first_b_in,
-    second_w_in,
-    second_b_in,
-    gain_ref,
-    bias_ref,
     normed_ref,
     act_ref,
     grad_pre_ref,
@@ -84,24 +88,39 @@
     stats_ref,
     first_save,
     second_save,
+    gain_ref,
+    bias_ref,
     first_w,
     first_b,
     second_w,
     second_b,
     back_res_ref,
 ):
+    devices, chunk, _ = packed_ref.shape
+
     @pl.when(pl.program_id(0) == 0)
     def _():
-        first_w[...] = first_w_in[...]
-        first_b[...] = first_b_in[...]
-        second_w[...] = second_w_in[...]
-        second_b[...] = second_b_in[...]
+        for index in range(devices):
+            block = packed_ref[index, :, LANES - 128 :].astype(f32)
+            first = slice(index * inner_part, (index + 1) * inner_part)
+            lanes = slice(MATRIX_LANE - LANES + 128, MATRIX_LANE - LANES + 128 + inner_part)
+            first_w[:, first] = block[:HEAD_DIM, lanes]
+            second_w[:, first] = block[HEAD_DIM : 2 * HEAD_DIM, lanes]
+            at = VECTOR_LANE - LANES + 128
+            vector = jnp.transpose(block)[at : at + 1]
+            first_b[:, first] = vector[:, :inner_part]
+            small = slice(index * feature_part, (index + 1) * feature_part)
+            for number, target in enumerate((second_b, gain_ref, bias_ref)):
+                start = inner_part + number * feature_part
+                target[:, small] = vector[:, start : start + feature_part]
+        centred = second_w[...]
+        second_w[...] = centred - jnp.mean(centred, axis=0, keepdims=True)
+        second_b[...] = second_b[...] - row_mean(second_b[...])
 
     gain = gain_ref[...]
     bias = bias_ref[...]
-    chunk = packed_ref.shape[0]
     steps = chunk // MINI
-    query, key, rate, miss = unpack_chunk(packed_ref[...], bias)
+    query, key, rate, miss = unpack_chunk(packed_ref[pl.program_id(0)], bias)
     base = miss * gain
     rate_base = rate * base
     rate_gain = rate * (gain * gain)
@@ -188,10 +207,12 @@
     stats_ref[:, :HEAD_DIM] = head_normal
     stats_ref[:, HEAD_DIM + 1 : HEAD_DIM + 2] = out_inverse
     stats_ref[:, HEAD_DIM + 2 : HEAD_DIM + 3] = head_inverse
-    normed_ref[...] = head_normal.astype(bf16)
+    normed_ref[0] = jnp.transpose(head_normal).astype(bf16)
 
 
 def backward_kernel(
+    inner_part,
+    feature_part,
     packed_ref,
     head_grad_ref,
     act_ref,
@@ -207,12 +228,6 @@
     gain_ref,
     bias_ref,
     back_ref,
-    first_w_out,
-    first_b_out,
-    second_w_out,
-    second_b_out,
-    gain_out,
-    bias_out,
     first_w,
     first_b,
     second_w,
@@ -221,6 +236,7 @@
     bias_sum,
     known_ref,
     own_ref,
+    vector_ref,
 ):
     @pl.when(pl.program_id(0) == 0)
     def _():
@@ -234,9 +250,10 @@
 
     gain = gain_ref[...]
     bias = bias_ref[...]
-    chunk = packed_ref.shape[0]
+    devices, chunk, _ = packed_ref.shape
     steps = chunk // MINI
-    query, key, rate, miss = unpack_chunk(packed_ref[...], bias)
+    place = devices - 1 - pl.program_id(0)
+    query, key, rate, miss = unpack_chunk(packed_ref[place], bias)
     base = miss * gain
     rate_base = rate * base
     square_gain = gain * gain
@@ -270,7 +287,7 @@
     rows, cols = token_grid(chunk)
     causal = cols <= rows
     later = rows <= cols
-    head_grad = head_grad_ref[...].astype(f32)
+    head_grad = jnp.transpose(head_grad_ref[0].astype(f32))
     out_grad = head_inverse * (
         head_grad - row_mean(head_grad) - head_normal * row_mean(head_grad * head_normal)
     )
@@ -370,20 +387,29 @@
     gain_sum[...] += gain_total
     bias_sum[...] += bias_total
     back_rate = rate_grad * rate * (1.0 - rate * (1.0 / rate_scale))
-    back_ref[:, :HEAD_DIM] = query_grad.astype(bf16)
-    back_ref[:, HEAD_DIM : 2 * HEAD_DIM] = key_grad.astype(bf16)
-    back_ref[:, 2 * HEAD_DIM : 3 * HEAD_DIM] = (-error_grad).astype(bf16)
+    back_ref[place, :, :HEAD_DIM] = query_grad.astype(bf16)
+    back_ref[place, :, HEAD_DIM : 2 * HEAD_DIM] = key_grad.astype(bf16)
+    back_ref[place, :, 2 * HEAD_DIM : 3 * HEAD_DIM] = (-error_grad).astype(bf16)
     lane = lax.broadcasted_iota(jnp.int32, (chunk, HEAD_DIM), 1)
-    back_ref[:, 3 * HEAD_DIM :] = jnp.where(lane == 0, back_rate, 0.0).astype(bf16)
-
-    @pl.when(pl.program_id(0) == pl.num_programs(0) - 1)
+    back_ref[place, :, 3 * HEAD_DIM :] = jnp.where(lane == 0, back_rate, 0.0).astype(bf16)
+
+    @pl.when(pl.program_id(0) == devices - 1)
     def _():
-        first_w_out[...] = first_w[...]
-        first_b_out[...] = first_b[...]
-        second_w_out[...] = second_w[...]
-        second_b_out[...] = second_b[...]
-        gain_out[...] = gain_sum[...]
-        bias_out[...] = bias_sum[...]
+        vector_ref[...] = jnp.zeros_like(vector_ref)
+        for index in range(devices):
+            first = slice(index * inner_part, (index + 1) * inner_part)
+            small = slice(index * feature_part, (index + 1) * feature_part)
+            vector_ref[index : index + 1, :inner_part] = first_b[:, first]
+            for number, source in enumerate((second_b, gain_sum, bias_sum)):
+                start = inner_part + number * feature_part
+                vector_ref[index : index + 1, start : start + feature_part] = source[:, small]
+        columns = jnp.transpose(vector_ref[...]).astype(bf16)
+        lanes = slice(MATRIX_LANE, MATRIX_LANE + inner_part)
+        for index in range(devices):
+            first = slice(index * inner_part, (index + 1) * inner_part)
+            back_ref[index, :HEAD_DIM, lanes] = first_w[:, first].astype(bf16)
+            back_ref[index, HEAD_DIM : 2 * HEAD_DIM, lanes] = second_w[:, first].astype(bf16)
+            back_ref[index, :, VECTOR_LANE : VECTOR_LANE + 1] = columns[:, index : index + 1]
 
 
 def whole_block(shape):
@@ -410,61 +436,62 @@
     )
 
 
-def chain_forward(packed, state, gain, bias, chunk):
-    length = packed.shape[0]
-    blocks = length // chunk
+def chain_forward(packed, inner_part, feature_part):
+    blocks, chunk, _ = packed.shape
 
     def forth(shape):
         return pl.BlockSpec(shape, lambda index: (index,) + (0,) * (len(shape) - 1))
 
-    saved = saved_layout(length, chunk)
+    saved = saved_layout(blocks * chunk, chunk)
     row = (1, HEAD_DIM)
     return pl.pallas_call(
-        forward_kernel,
+        functools.partial(forward_kernel, inner_part, feature_part),
         grid=(blocks,),
-        in_specs=[forth((chunk, LANES))]
-        + [whole_block(shape) for shape in STATE_SHAPES]
+        in_specs=[whole_block(packed.shape)],
+        out_specs=[forth((1, HEAD_DIM, chunk))]
+        + [forth(block) for _, block, _ in saved]
         + [whole_block(row)] * 2,
-        out_specs=[forth((chunk, HEAD_DIM))] + [forth(block) for _, block, _ in saved],
-        out_shape=[jax.ShapeDtypeStruct((length, HEAD_DIM), bf16)]
-        + [jax.ShapeDtypeStruct(shape, dtype) for shape, _, dtype in saved],
+        out_shape=[jax.ShapeDtypeStruct((blocks, HEAD_DIM, chunk), bf16)]
+        + [jax.ShapeDtypeStruct(shape, dtype) for shape, _, dtype in saved]
+        + [jax.ShapeDtypeStruct(row, f32)] * 2,
         scratch_shapes=[pltpu.VMEM(shape, f32) for shape in STATE_SHAPES]
         + [pltpu.VMEM((chunk, HEAD_DIM), bf16)],
         compiler_params=pltpu.CompilerParams(
-            dimension_semantics=("arbitrary",), vmem_limit_bytes=32 * 1024 * 1024
+            dimension_semantics=("arbitrary",), vmem_limit_bytes=VMEM_BYTES
         ),
         name="chain_forward",
-    )(packed, *state, gain, bias)
-
-
-def chain_backward(packed, head_grad, saved_values, gain, bias, chunk):
-    length = packed.shape[0]
-    blocks = length // chunk
+    )(packed)
+
+
+def chain_backward(packed, head_grad, saved_values, inner_part, feature_part):
+    blocks, chunk, _ = packed.shape
 
     def back(shape):
         return pl.BlockSpec(
             shape, lambda index: (blocks - 1 - index,) + (0,) * (len(shape) - 1)
         )
 
-    saved = saved_layout(length, chunk)
+    saved = saved_layout(blocks * chunk, chunk)
     row = (1, HEAD_DIM)
-    sums = STATE_SHAPES + (row, row)
     return pl.pallas_call(
-        backward_kernel,
+        functools.partial(backward_kernel, inner_part, feature_part),
         grid=(blocks,),
-        in_specs=[back((chunk, LANES)), back((chunk, HEAD_DIM))]
+        in_specs=[whole_block(packed.shape), back((1, HEAD_DIM, chunk))]
         + [back(block) for _, block, _ in saved]
         + [whole_block(row)] * 2,
-        out_specs=[back((chunk, LANES))] + [whole_block(shape) for shape in sums],
-        out_shape=[jax.ShapeDtypeStruct((length, LANES), bf16)]
-        + [jax.ShapeDtypeStruct(shape, f32) for shape in sums],
-        scratch_shapes=[pltpu.VMEM(shape, f32) for shape in sums]
-        + [pltpu.VMEM((chunk, INNER), bf16), pltpu.VMEM((chunk, HEAD_DIM), bf16)],
+        out_specs=whole_block(packed.shape),
+        out_shape=jax.ShapeDtypeStruct(packed.shape, bf16),
+        scratch_shapes=[pltpu.VMEM(shape, f32) for shape in STATE_SHAPES + (row, row)]
+        + [
+            pltpu.VMEM((chunk, INNER), bf16),
+            pltpu.VMEM((chunk, HEAD_DIM), bf16),
+            pltpu.VMEM((chunk, 128), f32),
+        ],
         compiler_params=pltpu.CompilerParams(
-            dimension_semantics=("arbitrary",), vmem_limit_bytes=32 * 1024 * 1024
+            dimension_semantics=("arbitrary",), vmem_limit_bytes=VMEM_BYTES
         ),
         name="chain_backward",
-    )(packed, head_grad, *saved_values, gain, bias)
+    )(packed, head_grad, *saved_values)
 
 
 def layer_norm_parts(values):
@@ -478,6 +505,162 @@
     return inverse * (scaled - row_mean(scaled) - normal * row_mean(scaled * normal))
 
 
+def start_kernel(
+    head_count,
+    rows_ref,
+    weights_ref,
+    gain_ref,
+    inner_ref,
+    packed_ref,
+    normed_ref,
+    matrix_ref,
+):
+    tensor_count = rows_ref.shape[0]
+    seq_count, chunk, _ = normed_ref.shape
+    rows = chunk // tensor_count
+    matrix_ref[...] = jnp.zeros_like(matrix_ref)
+    for head in range(head_count):
+        first = head * 3 * HEAD_DIM
+        rate = head_count * 3 * HEAD_DIM + head
+        column = weights_ref[:, rate : rate + 1]
+        matrix_ref[head, :, : 3 * HEAD_DIM] = weights_ref[:, first : first + 3 * HEAD_DIM]
+        matrix_ref[head, :, RATE_LANE : RATE_LANE + 1] = column
+        matrix_ref[head, :, RATE_LANE + 1 : RATE_LANE + 2] = column
+    lane = lax.broadcasted_iota(jnp.int32, (chunk, LANES), 1)
+    for sequence in range(seq_count):
+        part = slice(sequence * rows, (sequence + 1) * rows)
+        values = jnp.concatenate([rows_ref[index, part] for index in range(tensor_count)], axis=0)
+        normal, _ = layer_norm_parts(values.astype(f32))
+        normed = (normal * gain_ref[...]).astype(bf16)
+        normed_ref[sequence] = normed
+        for head in range(head_count):
+            projected = dot_nn(normed, matrix_ref[head])
+            rest = projected - projected.astype(bf16).astype(f32)
+            projected = jnp.where(lane == RATE_LANE + 1, rest, projected).astype(bf16)
+            packed_ref[head * seq_count + sequence] = jnp.where(
+                lane >= VECTOR_LANE, inner_ref[head], projected
+            )
+    for index in range(head_count * seq_count, packed_ref.shape[0]):
+        packed_ref[index] = jnp.zeros((chunk, LANES), bf16)
+
+
+def feed_forward_kernel(
+    heads_ref,
+    rows_ref,
+    weights_ref,
+    out_ref,
+    gain_ref,
+    terms_ref,
+    mixed_ref,
+    normed_ref,
+    back_ref,
+    swiglu_ref,
+    cot_ref,
+):
+    tensor_count, head_count, seq_count, _, chunk = heads_ref.shape
+    ff_local = swiglu_ref.shape[1]
+    rows = chunk // tensor_count
+    total = seq_count * chunk
+    for sequence in range(seq_count):
+        part = slice(sequence * rows, (sequence + 1) * rows)
+        other = slice((seq_count + sequence) * rows, (seq_count + sequence + 1) * rows)
+        values = jnp.concatenate([rows_ref[index, part] for index in range(tensor_count)], axis=0)
+        mixed = values.astype(f32)
+        for index in range(tensor_count):
+            heads = [heads_ref[index, head, sequence] for head in range(head_count)]
+            heads = jnp.transpose(jnp.concatenate(heads, axis=0).astype(f32))
+            mixed = mixed + dot_nt(heads, out_ref[index])
+        for index in range(tensor_count):
+            mixed_ref[index, sequence] = mixed[index * rows : (index + 1) * rows]
+        normal, _ = layer_norm_parts(mixed)
+        at = slice(sequence * chunk, (sequence + 1) * chunk)
+        normed_ref[at] = (normal * gain_ref[...]).astype(bf16)
+        for index in range(tensor_count):
+            first = sequence * chunk + index * rows
+            cot_ref[first : first + rows] = rows_ref[index, other]
+    normed = normed_ref[...]
+    cot = cot_ref[...]
+    for first in range(0, ff_local, 256):
+        at = slice(first, first + 256)
+        beyond = slice(ff_local + first, ff_local + first + 256)
+        gate = dot_nn(normed, weights_ref[:, at])
+        up = dot_nn(normed, weights_ref[:, beyond])
+        back = dot_nn(cot, weights_ref[:, 2 * ff_local + first : 2 * ff_local + first + 256])
+        share = jax.nn.sigmoid(gate)
+        silu = gate * share
+        swiglu_ref[:, at] = (silu * up).astype(bf16)
+        back_ref[:, at] = (back * up * (share * (1.0 + gate * (1.0 - share)))).astype(bf16)
+        back_ref[:, beyond] = (back * silu).astype(bf16)
+    ffn_term = dot_nt(back_ref[...], weights_ref[:, : 2 * ff_local]).astype(bf16)
+    down_term = dot_nt(swiglu_ref[...], weights_ref[:, 2 * ff_local : 3 * ff_local]).astype(bf16)
+    for sequence in range(seq_count):
+        for index in range(tensor_count):
+            first = sequence * chunk + index * rows
+            terms_ref[index, sequence] = ffn_term[first : first + rows]
+            terms_ref[index, seq_count + sequence] = down_term[first : first + rows]
+
+
+def feed_forward_grad_kernel(normed_ref, back_ref, swiglu_ref, cot_ref, grads_ref):
+    normed = jnp.transpose(normed_ref[...].astype(f32)).astype(bf16)
+    cot = jnp.transpose(cot_ref[...].astype(f32)).astype(bf16)
+    width = back_ref.shape[1]
+    for first in range(0, width, 256):
+        at = slice(first, first + 256)
+        grads_ref[:, at] = dot_nn(normed, back_ref[:, at]).astype(bf16)
+    for first in range(0, swiglu_ref.shape[1], 256):
+        at = slice(width + first, width + first + 256)
+        grads_ref[:, at] = dot_nn(cot, swiglu_ref[:, first : first + 256]).astype(bf16)
+
+
+def head_back_kernel(grads_ref, out_ref, heads_ref, back_ref, out_grad_ref):
+    head_count, seq_count, _, chunk = heads_ref.shape
+    devices, shard, _ = out_grad_ref.shape
+    total = None
+    for sequence in range(seq_count):
+        grads = grads_ref[sequence]
+        back = jnp.transpose(dot_nn(grads, out_ref[...])).astype(bf16)
+        for head in range(head_count):
+            back_ref[head * seq_count + sequence] = back[head * HEAD_DIM : (head + 1) * HEAD_DIM]
+        heads = [heads_ref[head, sequence] for head in range(head_count)]
+        term = dot_nt(jnp.transpose(grads.astype(f32)), jnp.concatenate(heads, axis=0))
+        total = term if total is None else total + term
+    for index in range(head_count * seq_count, devices):
+        back_ref[index] = jnp.zeros((HEAD_DIM, chunk), bf16)
+    for index in range(devices):
+        out_grad_ref[index] = total[index * shard : (index + 1) * shard].astype(bf16)
+
+
+def attention_term_kernel(rows_ref, matrix_ref, terms_ref):
+    head_count = matrix_ref.shape[0]
+    tensor_count, seq_count, rows, _ = terms_ref.shape
+    chunk = tensor_count * rows
+    lane = lax.broadcasted_iota(jnp.int32, (chunk, LANES), 1)
+    for sequence in range(seq_count):
+        total = None
+        for head in range(head_count):
+            values = rows_ref[head * seq_count + sequence]
+            values = jnp.where(lane <= RATE_LANE, values, jnp.zeros_like(values))
+            term = dot_nt(values, matrix_ref[head])
+            total = term if total is None else total + term
+        for index in range(tensor_count):
+            part = total[index * rows : (index + 1) * rows]
+            terms_ref[index, sequence] = part.astype(bf16)
+
+
+def whole_call(kernel, name, operands, results, vmem_bytes=GLUE_BYTES):
+    def spec(shape):
+        return pl.BlockSpec(shape, lambda: (0,) * len(shape))
+
+    return pl.pallas_call(
+        kernel,
+        in_specs=[spec(operand.shape) for operand in operands],
+        out_specs=[spec(result.shape) for result in results],
+        out_shape=results,
+        compiler_params=pltpu.CompilerParams(vmem_limit_bytes=vmem_bytes),
+        name=name,
+    )(*operands)
+
+
 def dots(subscripts, left, right):
     return jnp.einsum(subscripts, left, right, preferred_element_type=f32)
 
@@ -486,13 +669,13 @@
     return lax.all_to_all(values, axis, 0, 0, tiled=False)
 
 
-def gather(values, axis):
-    return lax.all_gather(values, axis, axis=0, tiled=True)
-
-
-RATE_LANE = 3 * HEAD_DIM
-VECTOR_LANE = RATE_LANE + 2
-MATRIX_LANE = LANES - 32
+def share_out(values, axis):
+    count = lax.axis_size(axis)
+    return exchange(jnp.broadcast_to(values[None], (count,) + values.shape), axis)
+
+
+def ordered(first, then):
+    return lax.optimization_barrier((first, then))
 
 
 def inner_block(matrix_one, matrix_two, vectors, rows):
@@ -533,7 +716,6 @@
     local_rows, seq_count, width = tokens.shape
     row_count = local_rows * seq_count
     chunk = local_rows * tensor_count
-    group_rows = chunk * seq_count
     head_count = w_rate.shape[1]
     local_width = head_count * HEAD_DIM
     shard = w_qkv.shape[0]
@@ -543,188 +725,132 @@
     inner_part = w_one.shape[2]
     feature_part = b_two.shape[1]
     assert chain_count <= device_count
-    assert chunk % MINI == 0 and chunk >= 2 * HEAD_DIM and inner_part <= 32
-
-    gain_rows = jnp.pad(
-        jnp.concatenate([gain_attn, gain_ffn])[None], ((0, 0), (0, width - 2 * part))
-    )
-    out_rows = w_out.reshape(-1, width)
-    row_pack = jnp.concatenate(
-        [
-            tokens.reshape(row_count, width),
-            cotangent.reshape(row_count, width),
-            out_rows,
-            gain_rows,
-        ],
-        axis=0,
-    )
-    row_full = lax.all_gather(row_pack, "tensor", axis=0, tiled=False)
-    group_tokens = row_full[:, :row_count].reshape(group_rows, width)
-    group_cot = row_full[:, row_count : 2 * row_count].reshape(group_rows, width)
-    out_columns = row_full[:, 2 * row_count : 2 * row_count + out_rows.shape[0]].reshape(
-        tensor_count * local_width, shard
-    )
-    own_gains = row_full[:, -1, : 2 * part].reshape(tensor_count, 2, part)
-    own_gains = own_gains.transpose(0, 2, 1).reshape(shard, 2)
-
-    qkv_pack = jnp.concatenate([w_qkv.reshape(shard, 3 * local_width), w_rate, own_gains], axis=1)
-    qkv_full = gather(qkv_pack, "dp")
+    assert chunk == 2 * HEAD_DIM and inner_part <= 32 and part <= shard
+    rank = lax.axis_index("tensor")
+    place = lax.axis_index("dp")
+
+    own_tokens = tokens.transpose(1, 0, 2).reshape(row_count, width)
+    own_cot = cotangent.transpose(1, 0, 2).reshape(row_count, width)
+    row_full = share_out(jnp.concatenate([own_tokens, own_cot], axis=0), "tensor")
+    head_columns = w_qkv.reshape(shard, 3, head_count, HEAD_DIM).transpose(0, 2, 1, 3)
+    gain_columns = jnp.pad(jnp.stack([gain_attn, gain_ffn], axis=1), ((0, shard - part), (0, 0)))
+    qkv_pack = jnp.concatenate(
+        [head_columns.reshape(shard, 3 * local_width), w_rate, gain_columns], axis=1
+    )
+    qkv_full = lax.all_gather(qkv_pack, "dp", axis=0, tiled=True)
+    qkv_full, row_full = ordered(qkv_full, row_full)
+    some_gains = qkv_full[:, 3 * local_width + head_count :]
+    some_gains = some_gains.reshape(device_count, shard, 2)[:, :part].transpose(2, 0, 1)
+    gains = lax.all_gather(some_gains.reshape(2, device_count * part), "tensor", axis=0)
+    gains = gains.reshape(tensor_count, 2, device_count, part).transpose(1, 2, 0, 3)
+    gains = gains.reshape(2, width).astype(f32)
+    scale_attn, scale_ffn = gains[0:1], gains[1:2]
+
     ffn_pack = jnp.concatenate(
-        [w_gate_up.reshape(shard, 2 * ff_local), w_down.T, out_columns.T], axis=1
-    )
-    ffn_full = gather(ffn_pack, "dp")
-    gate_up_full = ffn_full[:, : 2 * ff_local]
-    down_full = ffn_full[:, 2 * ff_local : 3 * ff_local]
-    out_full = ffn_full[:, 3 * ff_local :]
-    scale_attn = qkv_full[:, -2].astype(f32)
-    scale_ffn = qkv_full[:, -1].astype(f32)
-
-    inputs = group_tokens.astype(f32)
-    input_normal, _ = layer_norm_parts(inputs)
-    normed_attn = (input_normal * scale_attn).astype(bf16)
-    rate_columns = qkv_full[:, 3 * local_width : 3 * local_width + head_count]
-    head_matrix = jnp.concatenate(
-        [
-            qkv_full[:, : 3 * local_width]
-            .reshape(width, 3, head_count, HEAD_DIM)
-            .transpose(0, 2, 1, 3)
-            .reshape(width, head_count, 3 * HEAD_DIM),
-            rate_columns[:, :, None],
-            rate_columns[:, :, None],
-            jnp.zeros((width, head_count, LANES - RATE_LANE - 2), bf16),
-        ],
-        axis=2,
-    )
-    projected = dots("rd,dhk->rhk", normed_attn, head_matrix)
-    lane = lax.broadcasted_iota(jnp.int32, projected.shape, 2)
-    rest = projected - lax.reduce_precision(projected, 8, 7)
-    packed = jnp.where(lane == RATE_LANE + 1, rest, projected).astype(bf16)
-    packed = packed.reshape(chunk, seq_count, head_count, LANES).transpose(1, 2, 0, 3)
+        [w_gate_up.reshape(shard, 2 * ff_local), w_down.T, w_out.T], axis=1
+    )
+    ffn_full = lax.all_gather(ffn_pack, "dp", axis=0, tiled=True)
+    own_out = ffn_full[:, 3 * ff_local :]
+
     inner = inner_block(
         w_one,
         w_two.transpose(0, 2, 1),
         [b_one, b_two, norm_gain_inner, norm_bias_inner],
         chunk,
     )
-    packed = (packed + inner[None]).reshape(chain_count, chunk, LANES)
-    spare = jnp.zeros((device_count - chain_count, chunk, LANES), bf16)
-    chain_in = exchange(jnp.concatenate([packed, spare], axis=0), "dp")
-
-    normed_full = gather(normed_attn[None], "dp").reshape(
-        device_count * chunk, seq_count, width
-    )
-
-    first_w = chain_in[:, :HEAD_DIM, MATRIX_LANE : MATRIX_LANE + inner_part]
-    first_w = first_w.transpose(1, 0, 2).reshape(HEAD_DIM, INNER).astype(f32)
-    second_w = chain_in[:, HEAD_DIM : 2 * HEAD_DIM, MATRIX_LANE : MATRIX_LANE + inner_part]
-    second_w = second_w.transpose(1, 0, 2).reshape(HEAD_DIM, INNER).astype(f32)
-    vectors = chain_in[:, :, VECTOR_LANE].astype(f32)
-    first_b = vectors[:, :inner_part].reshape(1, INNER)
-    small = vectors[:, inner_part : inner_part + 3 * feature_part]
-    small = small.reshape(device_count, 3, feature_part).transpose(1, 0, 2).reshape(3, HEAD_DIM)
-    second_b, inner_gain, inner_bias = small[0:1], small[1:2], small[2:3]
-    second_w = second_w - jnp.mean(second_w, axis=0, keepdims=True)
-    second_b = second_b - row_mean(second_b)
-    chain_rows = chain_in.reshape(device_count * chunk, LANES)
-    forward_out = chain_forward(
-        chain_rows, (first_w, first_b, second_w, second_b), inner_gain, inner_bias, chunk
-    )
+    shape = jax.ShapeDtypeStruct
+    packed, normed_attn, head_matrix = whole_call(
+        functools.partial(start_kernel, head_count),
+        "projections",
+        (row_full, qkv_full, scale_attn, inner),
+        (
+            shape((device_count, chunk, LANES), bf16),
+            shape((seq_count, chunk, width), bf16),
+            shape((head_count, width, LANES), bf16),
+        ),
+    )
+    chain_in = exchange(packed, "dp")
+    chain_in, own_out = ordered(chain_in, own_out)
+    out_full = lax.all_gather(own_out, "tensor", axis=0)
+
+    normed_full = lax.all_gather(normed_attn, "dp", axis=1, tiled=False)
+
+    forward_out = chain_forward(chain_in, inner_part, feature_part)
     saved = forward_out[1:]
-    head_send = forward_out[0].reshape(device_count, chunk, HEAD_DIM)
-    head_back = exchange(head_send, "dp")[:chain_count]
-    head_local = (
-        head_back.reshape(seq_count, head_count, chunk, HEAD_DIM)
-        .transpose(2, 0, 1, 3)
-        .reshape(group_rows, local_width)
-    )
-    head_rows = lax.all_gather(head_local, "tensor", axis=1, tiled=True)
-
-    mixed = inputs + dots("rk,dk->rd", head_rows, out_full)
-    ffn_normal, _ = layer_norm_parts(mixed)
-    normed_ffn = (ffn_normal * scale_ffn).astype(bf16)
-    gate_up = dots("rd,df->rf", normed_ffn, gate_up_full)
-    gate, up = gate_up[:, :ff_local], gate_up[:, ff_local:]
-    share = jax.nn.sigmoid(gate)
-    silu = gate * share
-    swiglu = (silu * up).astype(bf16)
-    back_swiglu = dots("rd,df->rf", group_cot, down_full)
-    back_gate_up = jnp.concatenate(
-        [back_swiglu * up * (share * (1.0 + gate * (1.0 - share))), back_swiglu * silu], axis=1
-    ).astype(bf16)
-    down_term = dots("rf,df->rd", swiglu, down_full).astype(bf16)
-    ffn_term = dots("rf,df->rd", back_gate_up, gate_up_full).astype(bf16)
-    terms = jnp.stack(
-        [
-            down_term.reshape(tensor_count, row_count, width),
-            ffn_term.reshape(tensor_count, row_count, width),
-        ],
-        axis=1,
-    )
-    sums = exchange(terms, "tensor").astype(f32).sum(axis=0)
-    rank = lax.axis_index("tensor")
-    own_mixed = lax.dynamic_slice_in_dim(mixed, rank * row_count, row_count, 0)
-    result = (own_mixed + sums[0]).astype(bf16)
+    head_local = exchange(forward_out[0], "dp")[:chain_count]
+    head_local = head_local.reshape(head_count, seq_count, HEAD_DIM, chunk)
+    head_rows = lax.all_gather(head_local, "tensor", axis=0, tiled=False)
+
+    group_rows = seq_count * chunk
+    terms, mixed, normed_ffn, back_gate_up, swiglu, group_cot = whole_call(
+        feed_forward_kernel,
+        "feed_forward",
+        (head_rows, row_full, ffn_full, out_full, scale_ffn),
+        (
+            shape((tensor_count, 2 * seq_count, local_rows, width), bf16),
+            shape((tensor_count, seq_count, local_rows, width), f32),
+            shape((group_rows, width), bf16),
+            shape((group_rows, 2 * ff_local), bf16),
+            shape((group_rows, ff_local), bf16),
+            shape((group_rows, width), bf16),
+        ),
+        VMEM_BYTES,
+    )
+    ffn_sums = exchange(terms, "tensor")
+    (ffn_grads,) = whole_call(
+        feed_forward_grad_kernel,
+        "feed_forward_grads",
+        (normed_ffn, back_gate_up, swiglu, group_cot),
+        (shape((width, 3 * ff_local), bf16),),
+        VMEM_BYTES,
+    )
+    ffn_grad_sums = lax.psum_scatter(ffn_grads, "dp", scatter_dimension=0, tiled=True).astype(f32)
+    ffn_sums, normed_full = ordered(ffn_sums, normed_full)
+    ffn_sums = ffn_sums.astype(f32).sum(axis=0)
+    own_mixed = lax.dynamic_index_in_dim(mixed, rank, 0, keepdims=False)
     own_normal, own_inverse = layer_norm_parts(own_mixed)
-    back_mixed = cotangent.reshape(row_count, width).astype(f32) + layer_norm_back(
-        own_normal, own_inverse, scale_ffn, sums[1]
-    )
-    attn_grads = gather(back_mixed.astype(bf16), "tensor")
-    own_out = lax.dynamic_slice_in_dim(out_full, rank * local_width, local_width, 1)
-    back_head = dots("rd,dk->rk", attn_grads, own_out).astype(bf16)
-    back_head = (
-        back_head.reshape(chunk, seq_count, head_count, HEAD_DIM)
-        .transpose(1, 2, 0, 3)
-        .reshape(chain_count, chunk, HEAD_DIM)
-    )
-    spare = jnp.zeros((device_count - chain_count, chunk, HEAD_DIM), bf16)
-    head_grad = exchange(jnp.concatenate([back_head, spare], axis=0), "dp")
-    head_grad = head_grad.reshape(device_count * chunk, HEAD_DIM)
-
-    matrix_grads = jnp.concatenate(
-        [
-            dots("rd,rf->df", normed_ffn, back_gate_up),
-            dots("rd,rf->df", group_cot, swiglu),
-            dots("rd,rk->dk", attn_grads, head_local),
-        ],
-        axis=1,
-    ).astype(bf16)
-    matrix_sums = lax.psum_scatter(matrix_grads, "dp", scatter_dimension=0, tiled=True)
-    matrix_sums = matrix_sums.astype(f32)
-
-    backward_out = chain_backward(chain_rows, head_grad, saved, inner_gain, inner_bias, chunk)
-    back_packed, state_grads = backward_out[0], backward_out[1:]
-    sequence = jnp.minimum(lax.axis_index("dp") // head_count, seq_count - 1)
-    chain_normed = lax.dynamic_index_in_dim(normed_full, sequence, 1, keepdims=False)
-    grad_packed = dots("rd,rk->dk", chain_normed, back_packed).astype(bf16)
-    by_part = lambda values: (
-        values.reshape(HEAD_DIM, device_count, inner_part).transpose(1, 0, 2).astype(bf16)
-    )
-    split = lambda values, size: values.reshape(device_count, size).astype(bf16)
-    inner_grads = inner_block(
-        by_part(state_grads[0]),
-        by_part(state_grads[2]),
-        [
-            split(state_grads[1], inner_part),
-            split(state_grads[3], feature_part),
-            split(state_grads[4], feature_part),
-            split(state_grads[5], feature_part),
-        ],
-        chunk,
-    )
-    send = jnp.concatenate(
-        [
-            back_packed.reshape(device_count, chunk, LANES) + inner_grads,
-            grad_packed.reshape(device_count, shard, LANES),
-        ],
-        axis=1,
-    )
-    received = exchange(send, "dp")[:chain_count]
-    back_rows = received[:, :chunk].reshape(seq_count, head_count, chunk, LANES)
-    attn_term = dots("shck,dhk->csd", back_rows, head_matrix_back(head_matrix))
-    attn_term = attn_term.reshape(tensor_count, row_count, width).astype(bf16)
-
-    by_head = received.astype(f32).reshape(seq_count, head_count, chunk + shard, LANES).sum(axis=0)
-    grad_block = by_head[:, chunk:]
+    back_mixed = own_cot.astype(f32).reshape(own_mixed.shape) + layer_norm_back(
+        own_normal, own_inverse, scale_ffn, ffn_sums[:seq_count]
+    )
+    result = (own_mixed + ffn_sums[seq_count:]).astype(bf16)
+    attn_grads = lax.all_gather(back_mixed.astype(bf16), "tensor", axis=1, tiled=True)
+    back_head, out_terms = whole_call(
+        head_back_kernel,
+        "head_back",
+        (attn_grads, own_out, head_local),
+        (
+            shape((device_count, HEAD_DIM, chunk), bf16),
+            shape((device_count, shard, local_width), bf16),
+        ),
+    )
+    head_grad = exchange(back_head, "dp")
+    out_sums = exchange(out_terms, "dp")
+
+    back_packed = chain_backward(chain_in, head_grad, saved, inner_part, feature_part)
+    back_rows = exchange(back_packed, "dp")
+    sequence = place % seq_count
+    chain_normed = lax.dynamic_index_in_dim(normed_full, sequence, 0, keepdims=False)
+    grad_packed = dots("pnd,pnk->dk", chain_normed, back_packed)
+    grad_packed = grad_packed.astype(bf16).reshape(device_count, shard, LANES)
+    back_rows, grad_packed = ordered(back_rows, grad_packed)
+    grad_block = exchange(grad_packed, "dp")
+
+    (attn_term,) = whole_call(
+        attention_term_kernel,
+        "attention_term",
+        (back_rows, head_matrix),
+        (shape((tensor_count, seq_count, local_rows, width), bf16),),
+    )
+    attn_sums = exchange(attn_term, "tensor").astype(f32).sum(axis=0)
+    back_rows = back_rows[:chain_count].reshape(head_count, seq_count, chunk, LANES)
+    own_inputs = tokens.transpose(1, 0, 2).astype(f32)
+    own_normal, own_inverse = layer_norm_parts(own_inputs)
+    input_grad = back_mixed + layer_norm_back(
+        own_normal, own_inverse, scale_attn, attn_sums
+    )
+
+    grad_block = grad_block[:chain_count].astype(f32)
+    grad_block = grad_block.reshape(head_count, seq_count, shard, LANES).sum(axis=1)
     grad_qkv = (
         grad_block[:, :, :RATE_LANE]
         .reshape(head_count, shard, 3, HEAD_DIM)
@@ -732,48 +858,43 @@
         .reshape(shard, 3, local_width)
     )
     grad_rate = grad_block[:, :, RATE_LANE].T
-    grad_one = by_head[:, :HEAD_DIM, MATRIX_LANE : MATRIX_LANE + inner_part]
-    grad_two = by_head[:, HEAD_DIM : 2 * HEAD_DIM, MATRIX_LANE : MATRIX_LANE + inner_part]
-    grad_two = grad_two.transpose(0, 2, 1)
-    columns = by_head[:, :, VECTOR_LANE]
+    state_block = back_rows[..., VECTOR_LANE:].astype(f32).sum(axis=1)
+    matrices = state_block[..., MATRIX_LANE - VECTOR_LANE :][..., :inner_part]
+    grad_one = matrices[:, :HEAD_DIM]
+    grad_two = matrices[:, HEAD_DIM : 2 * HEAD_DIM].transpose(0, 2, 1)
+    columns = state_block[:, :, 0]
     ends = [inner_part + index * feature_part for index in range(4)]
     grad_b_one = columns[:, : ends[0]]
     grad_b_two, grad_gain_inner, grad_bias_inner = (
         columns[:, ends[index] : ends[index + 1]] for index in range(3)
     )
 
-    gain_one = (
-        jnp.sum(grad_qkv * w_qkv.astype(f32), axis=(1, 2))
-        + jnp.sum(grad_rate * w_rate.astype(f32), axis=1)
-    ) / own_gains[:, 0].astype(f32)
-    grad_gate_up = matrix_sums[:, : 2 * ff_local].reshape(shard, 2, ff_local)
-    gain_two = jnp.sum(grad_gate_up * w_gate_up.astype(f32), axis=(1, 2)) / own_gains[:, 1].astype(
-        f32
-    )
-    gain_terms = jnp.stack([gain_one, gain_two]).reshape(2, tensor_count, part).transpose(1, 0, 2)
-    gain_terms = gain_terms.reshape(tensor_count, 1, 2 * part)
-    gain_high = gain_terms.astype(bf16)
-    gain_low = (gain_terms - lax.reduce_precision(gain_terms, 8, 7)).astype(bf16)
-    gain_send = jnp.pad(
-        jnp.concatenate([gain_high, gain_low], axis=1), ((0, 0), (0, 0), (0, width - 2 * part))
-    )
-    tail = exchange(jnp.concatenate([attn_term, gain_send], axis=1), "tensor")
-    tail = tail.astype(f32).sum(axis=0)
-    gain_sums = tail[row_count, : 2 * part] + tail[row_count + 1, : 2 * part]
-    own_inputs = tokens.reshape(row_count, width).astype(f32)
-    own_normal, own_inverse = layer_norm_parts(own_inputs)
-    input_grad = back_mixed + layer_norm_back(own_normal, own_inverse, scale_attn, tail[:row_count])
+    own_gains = lax.dynamic_slice_in_dim(gains, place * shard, shard, 1)
+    gain_one = jnp.sum(grad_qkv * w_qkv.astype(f32), axis=(1, 2)) + jnp.sum(
+        grad_rate * w_rate.astype(f32), axis=1
+    )
+    grad_gate_up = ffn_grad_sums[:, : 2 * ff_local].reshape(shard, 2, ff_local)
+    gain_two = jnp.sum(grad_gate_up * w_gate_up.astype(f32), axis=(1, 2))
+    gain_terms = jnp.stack([gain_one, gain_two]) / own_gains
+    gain_terms = gain_terms.reshape(2, tensor_count, part).transpose(1, 0, 2)
+    gain_terms = jnp.pad(
+        gain_terms.reshape(tensor_count, 1, 2 * part), ((0, 0), (0, 0), (0, 128 - 2 * part))
+    )
+    gain_sums = exchange(gain_terms, "tensor").sum(axis=0)[0]
+
+    def by_token(values):
+        return values.reshape(seq_count, local_rows, width).transpose(1, 0, 2)
 
     return (
-        result.reshape(tokens.shape),
-        input_grad.reshape(tokens.shape),
+        by_token(result),
+        by_token(input_grad),
         gain_sums[:part],
-        gain_sums[part:],
+        gain_sums[part : 2 * part],
         grad_qkv,
         grad_rate,
-        matrix_sums[:, 3 * ff_local :].T,
+        out_sums.astype(f32).sum(axis=0).T,
         grad_gate_up,
-        matrix_sums[:, 2 * ff_local : 3 * ff_local].T,
+        ffn_grad_sums[:, 2 * ff_local : 3 * ff_local].T,
         grad_one,
         grad_b_one,
         grad_two,
@@ -781,11 +902,6 @@
         grad_gain_inner,
         grad_bias_inner,
     )
-
-
-def head_matrix_back(head_matrix):
-    lane = lax.broadcasted_iota(jnp.int32, head_matrix.shape, 2)
-    return jnp.where(lane <= RATE_LANE, head_matrix, jnp.zeros_like(head_matrix))
 
 
 def solution(mesh):

time: 384 us -> 336 us (0.88)
  local copies, waits for them, and re-layouts: 70.8 us -> 18.9 us
  Pallas kernels: 104 us -> 126 us
  matrix products: 18.7 us -> 2.91 us
  starting transfers between devices: 23.9 us -> 36.7 us
  other arithmetic: 21.1 us -> 9.46 us
  waiting for transfers between devices: 66.8 us -> 58.6 us
  blocking collectives: 60.5 us -> 67.6 us
    pallas_call x2 -> x7, Pallas kernels: 104 us -> 126 us  [the longest x1 57.2 us: chain_forward(): pl.pallas_call(functools.partial(forward_kernel, inner_part, feature_part...]
    all_to_all x6 -> x9, waiting for transfers between devices: 66.7 us -> 45.3 us  [exchange(): return lax.all_to_all(values, axis, 0, 0, tiled=False)]
    reshape x20 -> x5, local copies, waits for them, and re-layouts: 20.6 us -> 0.65 us  [the longest x1 0.33 us: local(): grad_gate_up = ffn_grad_sums[:, :2 * ff_local].reshape(shard, 2, ff_local)]
    dot_general x12 -> x1, matrix products: 18.7 us -> 2.91 us  [dots(): return jnp.einsum(subscripts, left, right, preferred_element_type=f32)]
    unnamed x140 -> x54, local copies, waits for them, and re-layouts: 23.8 us -> 9.52 us
    all_to_all x0 -> x1, blocking collectives: none -> 13.5 us  [exchange(): return lax.all_to_all(values, axis, 0, 0, tiled=False)]
    all_to_all x6 -> x9, starting transfers between devices: 23.6 us -> 36.5 us  [exchange(): return lax.all_to_all(values, axis, 0, 0, tiled=False)]
    all_gather x2 -> x3, waiting for transfers between devices: 0.02 us -> 12.6 us  [the longest x1 12.6 us: local(): ffn_full = lax.all_gather(ffn_pack, 'dp', axis=0, tiled=True)]
  transfers between devices with their start and end apart: 9 -> 13, of which waited for: 6 -> 8; matrix products, arithmetic and copies ran while one was open for 21% -> 7% of each run, Pallas kernels for 27% -> 38%
where the time goes in v2:
time: 336 us; the launch traced here: 335 us
  Pallas kernels  126 us (38%)
  blocking collectives  67.6 us (20%)
  waiting for transfers between devices  58.6 us (17%)
  starting transfers between devices  36.7 us (11%)
  local copies, waits for them, and re-layouts  18.9 us (6%)
  between operations  14.3 us (4%)
  other arithmetic  9.46 us (3%)
    pallas_call x1, Pallas kernels, chain_forward(): pl.pallas_call(functools.partial(forward_kernel, inner_part, feature_part...  57.2 us
    pallas_call x1, Pallas kernels, chain_backward(): pl.pallas_call(functools.partial(backward_kernel, inner_part, feature_par...  53.6 us
    all_to_all x9, waiting for transfers between devices, exchange(): return lax.all_to_all(values, axis, 0, 0, tiled=False)  45.3 us
    all_to_all x9, starting transfers between devices, exchange(): return lax.all_to_all(values, axis, 0, 0, tiled=False)  36.5 us
    all_gather x1, blocking collectives, local(): qkv_full = lax.all_gather(qkv_pack, 'dp', axis=0, tiled=True)  35.9 us
    pallas_call x5, Pallas kernels, whole_call(): pl.pallas_call(kernel, in_specs=[spec(operand.shape) for operand in opera...  15.4 us
    all_to_all x1, blocking collectives, exchange(): return lax.all_to_all(values, axis, 0, 0, tiled=False)  13.5 us
    all_gather x1, waiting for transfers between devices, local(): ffn_full = lax.all_gather(ffn_pack, 'dp', axis=0, tiled=True)  12.6 us
  transfers between devices with their start and end apart: 13, of which 8 were waited for; matrix products, arithmetic and copies ran while one was open for 7% of the time, Pallas kernels for 38%

profile of v2, /device:TPU:0, one launch (start us, length us, event | category | flops | bytes accessed | tf_op | source)
XLA Modules:
  0.0 334.7 jit_solution(2586415639461448052)
XLA Ops:
  7.2 1.0 copy.152
  8.2 0.9 copy.134
  9.1 1.7 pad_maximum_fusion
  10.9 0.9 copy.128
  11.8 0.9 copy.129
  12.8 0.9 broadcast_in_dim.4
  13.7 4.2 %all-to-all-start = ((bf16[4,128,768]{2,1,0:T(8,128)(2,1)}), bf16[4,128,768]{2,1,0:T(8,128)(2,1)S(1)}, u32[]{:S(2)}, u32[]{:S(2)}) async-start(bf16[4,128,768]{2,1,0:T(8,128)(2,1)} %broadcast_in_dim.4), calls=%async_computation | async-start | bytes 1572864 | tf_op jit(solution)/shard_map/all_to_all | solution.py:669
  19.2 35.9 %all_gather.27.weights_ref = bf16[768,581]{1,0:T(8,128)(2,1)S(1)} all-gather(bf16[96,581]{1,0:T(8,128)(2,1)S(1)} %fusion.23), channel_id=1, replica_groups=mesh['dp'=8,'tensor'=4] {'dp'}, dimensions={0}, use_global_device_ids=true | all-gather | bytes 1003968 | tf_op jit(solution)/shard_map/all_gather | solution.py:740
  55.4 5.1 %all_gather.28 = bf16[4,2,192]{2,1,0:T(2,128)(2,1)S(1)} all-gather(bf16[1,2,192]{2,1,0:T(2,128)(2,1)S(1)} %copy.151), channel_id=1, replica_groups=mesh['dp'=8,'tensor'=4] {'tensor'}, dimensions={0}, use_global_device_ids=true | all-gather | bytes 3840 | tf_op jit(solution)/shard_map/all_gather | solution.py:744
  60.6 2.2 projections.1
  62.8 0.8 copy-done.2
  63.6 5.6 %all-to-all-start.1 = ((bf16[8,128,256]{2,1,0:T(8,128)(2,1)}), bf16[8,128,256]{2,1,0:T(8,128)(2,1)S(1)}, u32[]{:S(2)}, u32[]{:S(2)}) async-start(bf16[8,128,256]{2,1,0:T(8,128)(2,1)} %copy-done.2), calls=%async_computation.1 | async-start | bytes 1048576 | tf_op jit(solution)/shard_map/all_to_all | solution.py:669
  69.3 12.6 %all-gather.6.cloned.1.call-done.weights_ref = bf16[768,1728]{1,0:T(8,128)(2,1)} async-done(((bf16[96,1728]{1,0:T(8,128)(2,1)}), bf16[768,1728]{1,0:T(8,128)(2,1)}) %all-gather.6.cloned.1.call-update) | async-done | bytes 2654224 | tf_op jit(solution)/shard_map/all_gather | solution.py:752
  81.8 1.8 slice.117.out_ref
  83.6 4.0 %all-to-all-done.1.packed_ref = bf16[8,128,256]{2,1,0:T(8,128)(2,1)S(1)} async-done(((bf16[8,128,256]{2,1,0:T(8,128)(2,1)}), bf16[8,128,256]{2,1,0:T(8,128)(2,1)S(1)}, u32[]{:S(2)}, u32[]{:S(2)}) %all-to-all-start.1) | async-done | bytes 524320 | tf_op jit(solution)/shard_map/all_to_all | solution.py:669
  88.5 57.2 %chain_forward.1 = (bf16[8,64,128]{2,1,0:T(8,128)(2,1)}, bf16[1024,256]{1,0:T(8,128)(2,1)}, bf16[1024,256]{1,0:T(8,128)(2,1)}, bf16[1024,256]{1,0:T(8,128)(2,1)}...) custom-call(bf16[8,128,256]{2,1,0:T(8,128)(2,1)} %copy-done.3), custom_call_target="tpu_custom_call" | custom-call | tf_op jit(solution)/shard_map/chain_forward/pallas_call | solution.py:447
  145.6 3.5 %all-to-all-start.2 = ((bf16[8,64,128]{2,1,0:T(8,128)(2,1)}), bf16[8,64,128]{2,1,0:T(8,128)(2,1)S(1)}, u32[]{:S(2)}, u32[]{:S(2)}) async-start(bf16[8,64,128]{2,1,0:T(8,128)(2,1)} %get-tuple-element.51), calls=%async_computation.2 | async-start | bytes 262144 | tf_op jit(solution)/shard_map/all_to_all | solution.py:669
  149.8 9.9 %all-to-all-done.2 = bf16[8,64,128]{2,1,0:T(8,128)(2,1)S(1)} async-done(((bf16[8,64,128]{2,1,0:T(8,128)(2,1)}), bf16[8,64,128]{2,1,0:T(8,128)(2,1)S(1)}, u32[]{:S(2)}, u32[]{:S(2)}) %all-to-all-start.2) | async-done | bytes 131104 | tf_op jit(solution)/shard_map/all_to_all | solution.py:669
  159.7 7.0 %all_gather.30.heads_ref = bf16[4,3,2,64,128]{4,3,2,1,0:T(8,128)(2,1)} all-gather(bf16[1,3,2,64,128]{4,3,2,1,0:T(8,128)(2,1)S(1)} %bitcast.101), channel_id=1, replica_groups=mesh['dp'=8,'tensor'=4] {'tensor'}, dimensions={0}, use_global_device_ids=true | all-gather | bytes 491520 | tf_op jit(solution)/shard_map/all_gather | solution.py:782
  166.7 6.7 %feed_forward.1 = (bf16[4,4,32,768]{3,2,1,0:T(8,128)(2,1)}, f32[4,2,32,768]{3,2,1,0:T(8,128)}, bf16[256,768]{1,0:T(8,128)(2,1)}, bf16[256,1024]{1,0:T(8,128)(2,1...) custom-call(bf16[4,3,2,64,128]{4,3,2,1,0:T(8,128)(2,1)} %all_gather.30.heads_ref, bf16[4,128,768]{2,1,0:T(8,128)(2,1)} %copy-done, ...), custom_call_target="tpu_custom_call" | custom-call | tf_op jit(solution)/shard_map/feed_forward/pallas_call | solution.py:654
  173.4 3.5 %all-to-all-start.3 = ((bf16[4,4,32,768]{3,2,1,0:T(8,128)(2,1)}), bf16[4,4,32,768]{3,2,1,0:T(8,128)(2,1)S(1)}, u32[]{:S(2)}, u32[]{:S(2)}) async-start(bf16[4,4,32,768]{3,2,1,0:T(8,128)(2,1)} %get-tuple-element.54), calls=%async_computation.3 | async-start | bytes 1572864 | tf_op jit(solution)/shard_map/all_to_all | solution.py:669
  177.0 3.6 %feed_forward_grads.1 = bf16[768,1536]{1,0:T(8,128)(2,1)} custom-call(bf16[256,768]{1,0:T(8,128)(2,1)} %get-tuple-element.74.normed_ref, bf16[256,1024]{1,0:T(8,128)(2,1)} %get-tuple-element.75.back_ref, bf16[256,512]{1,0:T(8,128)(2,1)} %get-tuple-element.76.swiglu_ref, bf16[256,768]{1,0:T(8,128)(2,1)} %get-tuple-element.77.cot_ref), custom_call_target="tpu_custom_call" | custom-call | tf_op jit(solution)/shard_map/feed_forward_grads/pallas_call | solution.py:654
  180.7 1.1 dynamic-slice_reduce_fusion
  181.8 1.1 multiply_reduce_fusion.3
  182.9 5.6 %all-to-all-done.3 = bf16[4,4,32,768]{3,2,1,0:T(8,128)(2,1)S(1)} async-done(((bf16[4,4,32,768]{3,2,1,0:T(8,128)(2,1)}), bf16[4,4,32,768]{3,2,1,0:T(8,128)(2,1)S(1)}, u32[]{:S(2)}, u32[]{:S(2)}) %all-to-all-start.3) | async-done | bytes 786464 | tf_op jit(solution)/shard_map/all_to_all | solution.py:669
  188.6 1.1 fusion.22
  189.8 1.1 fusion.26
  190.8 6.1 %all_gather.35.grads_ref = bf16[2,128,768]{2,1,0:T(8,128)(2,1)S(1)} all-gather(bf16[2,32,768]{2,1,0:T(8,128)(2,1)S(1)} %fusion.26), channel_id=1, replica_groups=mesh['dp'=8,'tensor'=4] {'tensor'}, dimensions={1}, use_global_device_ids=true | all-gather | bytes 491520 | tf_op jit(solution)/shard_map/all_gather | solution.py:816
  197.0 1.3 head_back.1
  198.3 13.5 %all_to_all.50.head_grad_ref = bf16[8,64,128]{2,1,0:T(8,128)(2,1)} all-to-all(bf16[8,64,128]{2,1,0:T(8,128)(2,1)S(1)} %get-tuple-element.57), channel_id=1, replica_groups=mesh['dp'=8,'tensor'=4] {'dp'}, dimensions={0} | all-to-all | bytes 262144 | tf_op jit(solution)/shard_map/all_to_all | solution.py:669
  211.8 3.6 %all-to-all-start.9 = ((bf16[8,96,192]{2,1,0:T(8,128)(2,1)}), bf16[8,96,192]{2,1,0:T(8,128)(2,1)S(1)}, u32[]{:S(2)}, u32[]{:S(2)}) async-start(bf16[8,96,192]{2,1,0:T(8,128)(2,1)} %get-tuple-element.78), calls=%async_computation.10 | async-start | bytes 786432 | tf_op jit(solution)/shard_map/all_to_all | solution.py:669
  215.5 53.6 %chain_backward.1 = bf16[8,128,256]{2,1,0:T(8,128)(2,1)} custom-call(bf16[8,128,256]{2,1,0:T(8,128)(2,1)} %copy-done.3, bf16[8,64,128]{2,1,0:T(8,128)(2,1)} %all_to_all.50.head_grad_ref, bf16[1024,256]{1,0:T(8,128)(2,1)} %get-tuple-element.58.act_ref, bf16[1024,256]{1,0:T(8,128)(2,1)} %get-tuple-element.59.grad_pre_ref, ...), custom_call_target="tpu_custom_call" | custom-call | tf_op jit(solution)/shard_map/chain_backward/pallas_call | solution.py:476
  269.1 5.7 %all-to-all-start.5 = ((bf16[8,128,256]{2,1,0:T(8,128)(2,1)}), bf16[8,128,256]{2,1,0:T(8,128)(2,1)S(1)}, u32[]{:S(2)}, u32[]{:S(2)}) async-start(bf16[8,128,256]{2,1,0:T(8,128)(2,1)} %chain_backward.1), calls=%async_computation.5 | async-start | bytes 1048576 | tf_op jit(solution)/shard_map/all_to_all | solution.py:669
  275.3 2.9 fusion.6
  279.0 9.3 %all-to-all-done.5.rows_ref = bf16[8,128,256]{2,1,0:T(8,128)(2,1)S(1)} async-done(((bf16[8,128,256]{2,1,0:T(8,128)(2,1)}), bf16[8,128,256]{2,1,0:T(8,128)(2,1)S(1)}, u32[]{:S(2)}, u32[]{:S(2)}) %all-to-all-start.5) | async-done | bytes 524320 | tf_op jit(solution)/shard_map/all_to_all | solution.py:669
  288.4 1.6 attention_term.1
  290.0 3.5 %all-to-all-start.6 = ((bf16[4,2,32,768]{3,2,1,0:T(8,128)(2,1)}), bf16[4,2,32,768]{3,2,1,0:T(8,128)(2,1)S(1)}, u32[]{:S(2)}, u32[]{:S(2)}) async-start(bf16[4,2,32,768]{3,2,1,0:T(8,128)(2,1)} %attention_term.1), calls=%async_computation.6 | async-start | bytes 786432 | tf_op jit(solution)/shard_map/all_to_all | solution.py:669
  295.9 4.9 %all-to-all-done.6 = bf16[4,2,32,768]{3,2,1,0:T(8,128)(2,1)S(1)} async-done(((bf16[4,2,32,768]{3,2,1,0:T(8,128)(2,1)}), bf16[4,2,32,768]{3,2,1,0:T(8,128)(2,1)S(1)}, u32[]{:S(2)}, u32[]{:S(2)}) %all-to-all-start.6) | async-done | bytes 393248 | tf_op jit(solution)/shard_map/all_to_all | solution.py:669
  300.9 3.7 %all-to-all-start.7 = ((bf16[8,96,256]{2,1,0:T(8,128)(2,1)}), bf16[8,96,256]{2,1,0:T(8,128)(2,1)S(1)}, u32[]{:S(2)}, u32[]{:S(2)}) async-start(bf16[8,96,256]{2,1,0:T(8,128)(2,1)} %bitcast.113), calls=%async_computation.7 | async-start | bytes 786432 | tf_op jit(solution)/shard_map/all_to_all | solution.py:669
  304.8 1.1 fusion.18
  305.9 0.8 copy.146
  306.7 0.7 copy.145
  307.5 8.6 %all-to-all-done.7 = bf16[8,96,256]{2,1,0:T(8,128)(2,1)S(1)} async-done(((bf16[8,96,256]{2,1,0:T(8,128)(2,1)}), bf16[8,96,256]{2,1,0:T(8,128)(2,1)S(1)}, u32[]{:S(2)}, u32[]{:S(2)}) %all-to-all-start.7) | async-done | bytes 393248 | tf_op jit(solution)/shard_map/all_to_all | solution.py:669
  316.3 0.9 copy.147
  317.6 1.0 slice.125
  319.0 0.8 multiply_reduce_fusion
  320.6 3.2 all-to-all-start.8
  324.6 3.0 all-to-all-done.8
  (120 shorter events, 10.7 us)
Async XLA Ops:
  7.2 74.6 %all-gather.6.cloned.1.call-start = ((), (), s32[]{:S(2)}) async-start(), calls=%async_computation.11 | async-start | bytes 3096576 | tf_op jit(solution)/shard_map/all_gather | solution.py:752
  9.1 8.9 %copy-start.9 = (bf16[96,3,192]{2,0,1:T(8,128)(2,1)S(1)}, bf16[96,3,192]{2,0,1:T(8,128)(2,1)}, u32[]{:S(2)}) copy-start(bf16[96,3,192]{2,0,1:T(8,128)(2,1)} %param.18) | copy-start | bytes 331780
  10.8 7.5 %copy-start.14 = (bf16[96,3]{0,1:T(4,128)(2,1)S(1)}, bf16[96,3]{0,1:T(4,128)(2,1)}, u32[]{:S(2)}) copy-start(bf16[96,3]{0,1:T(4,128)(2,1)} %param.19) | copy-start | bytes 1732
  10.8 7.6 %copy-start.19 = (bf16[24]{0:T(256)(128)(2,1)S(1)}, bf16[24]{0:T(256)(128)(2,1)}, u32[]{:S(2)}) copy-start(bf16[24]{0:T(256)(128)(2,1)} %param.17) | copy-start | bytes 148
  10.8 7.6 %copy-start.20 = (bf16[24]{0:T(256)(128)(2,1)S(1)}, bf16[24]{0:T(256)(128)(2,1)}, u32[]{:S(2)}) copy-start(bf16[24]{0:T(256)(128)(2,1)} %param.16) | copy-start | bytes 148
  10.8 7.7 %copy-start.11 = (bf16[3,32,64]{2,1,0:T(8,128)(2,1)S(1)}, bf16[3,32,64]{2,1,0:T(8,128)(2,1)}, u32[]{:S(2)}) copy-start(bf16[3,32,64]{2,1,0:T(8,128)(2,1)} %param.25) | copy-start | bytes 36868
  10.8 7.7 %copy-start.12 = (bf16[3,64,32]{1,2,0:T(8,128)(2,1)S(1)}, bf16[3,64,32]{1,2,0:T(8,128)(2,1)}, u32[]{:S(2)}) copy-start(bf16[3,64,32]{1,2,0:T(8,128)(2,1)} %param.23) | copy-start | bytes 36868
  11.8 7.0 %copy-start.15 = (bf16[3,8]{1,0:T(4,128)(2,1)S(1)}, bf16[3,8]{1,0:T(4,128)(2,1)}, u32[]{:S(2)}) copy-start(bf16[3,8]{1,0:T(4,128)(2,1)} %param.28) | copy-start | bytes 148
  11.8 7.0 %copy-start.16 = (bf16[3,8]{1,0:T(4,128)(2,1)S(1)}, bf16[3,8]{1,0:T(4,128)(2,1)}, u32[]{:S(2)}) copy-start(bf16[3,8]{1,0:T(4,128)(2,1)} %param.27) | copy-start | bytes 148
  11.8 7.0 %copy-start.17 = (bf16[3,8]{1,0:T(4,128)(2,1)S(1)}, bf16[3,8]{1,0:T(4,128)(2,1)}, u32[]{:S(2)}) copy-start(bf16[3,8]{1,0:T(4,128)(2,1)} %param.26) | copy-start | bytes 148
  11.8 7.0 %copy-start.18 = (bf16[3,32]{1,0:T(4,128)(2,1)S(1)}, bf16[3,32]{1,0:T(4,128)(2,1)}, u32[]{:S(2)}) copy-start(bf16[3,32]{1,0:T(4,128)(2,1)} %param.24) | copy-start | bytes 580
  13.7 41.4 %all-to-all-start = ((bf16[4,128,768]{2,1,0:T(8,128)(2,1)}), bf16[4,128,768]{2,1,0:T(8,128)(2,1)S(1)}, u32[]{:S(2)}, u32[]{:S(2)}) async-start(bf16[4,128,768]{2,1,0:T(8,128)(2,1)} %broadcast_in_dim.4), calls=%async_computation | async-start | bytes 1572864 | tf_op jit(solution)/shard_map/all_to_all | solution.py:669
  55.1 28.5 %copy-start = (bf16[4,128,768]{2,1,0:T(8,128)(2,1)}, bf16[4,128,768]{2,1,0:T(8,128)(2,1)S(1)}, u32[]{:S(2)}) copy-start(bf16[4,128,768]{2,1,0:T(8,128)(2,1)S(1)} %all-to-all-done.rows_ref) | copy-start | bytes 2359300
  62.8 0.8 copy-start.2
  63.6 24.1 %all-to-all-start.1 = ((bf16[8,128,256]{2,1,0:T(8,128)(2,1)}), bf16[8,128,256]{2,1,0:T(8,128)(2,1)S(1)}, u32[]{:S(2)}, u32[]{:S(2)}) async-start(bf16[8,128,256]{2,1,0:T(8,128)(2,1)} %copy-done.2), calls=%async_computation.1 | async-start | bytes 1048576 | tf_op jit(solution)/shard_map/all_to_all | solution.py:669
  69.2 97.4 %all-gather.8.cloned.1.call-start = ((), (), s32[]{:S(2)}) async-start(), calls=%async_computation.13 | async-start | bytes 1966080 | tf_op jit(solution)/shard_map/all_gather | solution.py:774
  87.7 0.8 copy-start.3
  87.7 95.2 %all-gather.10.cloned.1.call-start = ((), (), s32[]{:S(2)}) async-start(), calls=%async_computation.14 | async-start | bytes 3538944 | tf_op jit(solution)/shard_map/all_gather | solution.py:776
  145.6 14.0 %all-to-all-start.2 = ((bf16[8,64,128]{2,1,0:T(8,128)(2,1)}), bf16[8,64,128]{2,1,0:T(8,128)(2,1)S(1)}, u32[]{:S(2)}, u32[]{:S(2)}) async-start(bf16[8,64,128]{2,1,0:T(8,128)(2,1)} %get-tuple-element.51), calls=%async_computation.2 | async-start | bytes 262144 | tf_op jit(solution)/shard_map/all_to_all | solution.py:669
  173.4 15.1 %all-to-all-start.3 = ((bf16[4,4,32,768]{3,2,1,0:T(8,128)(2,1)}), bf16[4,4,32,768]{3,2,1,0:T(8,128)(2,1)S(1)}, u32[]{:S(2)}, u32[]{:S(2)}) async-start(bf16[4,4,32,768]{3,2,1,0:T(8,128)(2,1)} %get-tuple-element.54), calls=%async_computation.3 | async-start | bytes 1572864 | tf_op jit(solution)/shard_map/all_to_all | solution.py:669
  176.9 140.7 %reduce-scatter.2.cloned.1.call-start = ((), (), s32[]{:S(2)}) async-start(), calls=%async_computation.12 | async-start | bytes 2654208 | tf_op jit(solution)/shard_map/reduce_scatter | solution.py:807
  180.7 9.1 %copy-start.7 = (bf16[32,2,768]{2,1,0:T(2,128)(2,1)S(1)}, bf16[32,2,768]{2,1,0:T(2,128)(2,1)}, u32[]{:S(2)}) copy-start(bf16[32,2,768]{2,1,0:T(2,128)(2,1)} %param.29) | copy-start | bytes 294916
  180.7 16.3 %copy-start.1 = (bf16[768,192]{1,0:T(8,128)(2,1)S(1)}, bf16[768,192]{1,0:T(8,128)(2,1)}, u32[]{:S(2)}) copy-start(bf16[768,192]{1,0:T(8,128)(2,1)} %slice.117.out_ref) | copy-start | bytes 884740
  188.5 26.9 %copy-start.4 = (bf16[32,2,768]{2,1,0:T(2,128)(2,1)S(1)}, bf16[32,2,768]{2,1,0:T(2,128)(2,1)}, u32[]{:S(2)}) copy-start(bf16[32,2,768]{2,1,0:T(2,128)(2,1)} %param.15) | copy-start | bytes 294916
  211.8 57.4 %all-to-all-start.9 = ((bf16[8,96,192]{2,1,0:T(8,128)(2,1)}), bf16[8,96,192]{2,1,0:T(8,128)(2,1)S(1)}, u32[]{:S(2)}, u32[]{:S(2)}) async-start(bf16[8,96,192]{2,1,0:T(8,128)(2,1)} %get-tuple-element.78), calls=%async_computation.10 | async-start | bytes 786432 | tf_op jit(solution)/shard_map/all_to_all | solution.py:669
  269.1 19.2 %all-to-all-start.5 = ((bf16[8,128,256]{2,1,0:T(8,128)(2,1)}), bf16[8,128,256]{2,1,0:T(8,128)(2,1)S(1)}, u32[]{:S(2)}, u32[]{:S(2)}) async-start(bf16[8,128,256]{2,1,0:T(8,128)(2,1)} %chain_backward.1), calls=%async_computation.5 | async-start | bytes 1048576 | tf_op jit(solution)/shard_map/all_to_all | solution.py:669
  290.0 10.9 %all-to-all-start.6 = ((bf16[4,2,32,768]{3,2,1,0:T(8,128)(2,1)}), bf16[4,2,32,768]{3,2,1,0:T(8,128)(2,1)S(1)}, u32[]{:S(2)}, u32[]{:S(2)}) async-start(bf16[4,2,32,768]{3,2,1,0:T(8,128)(2,1)} %attention_term.1), calls=%async_computation.6 | async-start | bytes 786432 | tf_op jit(solution)/shard_map/all_to_all | solution.py:669
  295.3 20.9 %copy-start.10 = (f32[3,128]{1,0:T(4,128)}, f32[3,128]{1,0:T(4,128)S(1)}, u32[]{:S(2)}) copy-start(f32[3,128]{1,0:T(4,128)S(1)} %slice_reduce_fusion) | copy-start | bytes 4612
  300.9 15.2 %all-to-all-start.7 = ((bf16[8,96,256]{2,1,0:T(8,128)(2,1)}), bf16[8,96,256]{2,1,0:T(8,128)(2,1)S(1)}, u32[]{:S(2)}, u32[]{:S(2)}) async-start(bf16[8,96,256]{2,1,0:T(8,128)(2,1)} %bitcast.113), calls=%async_computation.7 | async-start | bytes 786432 | tf_op jit(solution)/shard_map/all_to_all | solution.py:669
  316.2 2.8 copy-start.8
  317.4 10.7 %copy-start.13 = (f32[3,96]{1,0:T(4,128)}, f32[3,96]{1,0:T(4,128)S(1)}, u32[]{:S(2)}) copy-start(f32[3,96]{1,0:T(4,128)S(1)} %slice_reduce_fusion.1) | copy-start | bytes 3460
  317.6 6.2 %copy-start.5 = (bf16[96,1536]{1,0:T(8,128)(2,1)S(1)}, bf16[96,1536]{1,0:T(8,128)(2,1)}, u32[]{:S(2)}) copy-start(bf16[96,1536]{1,0:T(8,128)(2,1)} %reduce-scatter.2.cloned.1.call-done) | copy-start | bytes 884740
  319.0 9.2 %copy-start.6 = (f32[96,2,512]{2,1,0:T(2,128)}, f32[96,2,512]{2,1,0:T(2,128)S(1)}, u32[]{:S(2)}) copy-start(f32[96,2,512]{2,1,0:T(2,128)S(1)} %reshape.158) | copy-start | bytes 1179652
  320.6 6.9 %all-to-all-start.8 = ((f32[4,1,128]{2,1,0:T(1,128)}), f32[4,1,128]{2,1,0:T(1,128)S(1)}, u32[]{:S(2)}, u32[]{:S(2)}) async-start(f32[4,1,128]{2,1,0:T(1,128)} %bitcast.35), calls=%async_computation.9 | async-start | bytes 4096 | tf_op jit(solution)/shard_map/all_to_all | solution.py:669
Sparse Core Ops, SparseCore 0:
  10.9 70.8 all-gather.5
  87.8 18.8 all-gather.7
  109.5 61.9 all-gather.9
  180.9 73.3 reduce-scatter.1

commit v3 on v2

v3 whole, which is shorter than its diff:
```python
import functools


import jax
import jax.numpy as jnp
from jax import lax
from jax.experimental import pallas as pl
from jax.experimental.pallas import tpu as pltpu
from jax.sharding import PartitionSpec as P

HEAD_DIM = 64
INNER = 256
MINI = 16
LANES = 256
RATE_LANE = 3 * HEAD_DIM
VECTOR_LANE = RATE_LANE + 2
MATRIX_LANE = LANES - 32
VMEM_BYTES = 56 * 1024 * 1024
GLUE_BYTES = 32 * 1024 * 1024

epsilon = 1e-05
inner_epsilon = 1e-06
inner_rate = 0.5
rate_scale = inner_rate / (MINI * HEAD_DIM)
root_half = 0.7071067811865476
normal_peak = 0.3989422804014327

f32 = jnp.float32
bf16 = jnp.bfloat16


def dot_nn(a, b):
    return lax.dot_general(
        a.astype(bf16), b.astype(bf16), (((1,), (0,)), ((), ())), preferred_element_type=f32
    )


def dot_nt(a, b):
    return lax.dot_general(
        a.astype(bf16), b.astype(bf16), (((1,), (1,)), ((), ())), preferred_element_type=f32
    )


def dot_tn(a, b):
    return lax.dot_general(
        a.astype(bf16), b.astype(bf16), (((0,), (0,)), ((), ())), preferred_element_type=f32
    )


def row_mean(values):
    return jnp.mean(values, axis=-1, keepdims=True)


def density_and_share(values):
    density = jnp.exp(-0.5 * values * values) * normal_peak
    share = 0.5 * (1.0 + lax.erf(values * root_half))
    return density, share


def token_grid(count):
    rows = lax.broadcasted_iota(jnp.int32, (count, count), 0)
    cols = lax.broadcasted_iota(jnp.int32, (count, count), 1)
    return rows, cols


def wide_mean(values):
    high = values.astype(bf16)
    low = (values - high.astype(f32)).astype(bf16)
    ones = jnp.full((values.shape[1], 128), 1.0 / values.shape[1], bf16)
    return dot_nn(high, ones) + dot_nn(low, ones)


def mean_of(values):
    return wide_mean(values)[:, :HEAD_DIM]


def two_parts(packed):
    return packed[:, :HEAD_DIM], packed[:, HEAD_DIM : 2 * HEAD_DIM]


def rate_logit(packed):
    source = lax.broadcasted_iota(jnp.int32, (2 * HEAD_DIM, 128), 0)
    spread = jnp.where((source >= HEAD_DIM) & (source < HEAD_DIM + 2), 1.0, 0.0)
    return dot_nn(packed[:, 2 * HEAD_DIM :], spread)


def alternate(*generators):
    left = list(generators)
    while left:
        for generator in list(left):
            if next(generator, generator) is generator:
                left.remove(generator)
            else:
                yield


def interleave(generator, count):
    for _ in range(count):
        if next(generator, generator) is generator:
            return


def forward_kernel(
    inner_part,
    feature_part,
    packed_ref,
    normed_ref,
    act_ref,
    grad_pre_ref,
    slope_ref,
    curve_ref,
    norms_ref,
    first_save,
    second_save,
    hidden_ref,
    out_slope_ref,
    out_norms_ref,
    gain_ref,
    bias_ref,
    first_w,
    first_b,
    second_w,
    second_b,
    known_ref,
    back_res_ref,
    pre_ref,
    to_rows,
    to_level,
    to_mix,
    row_ref,
    level_ref,
    mix_ref,
    done_act,
    done_grad,
    done_back,
    done_first,
    done_second,
    done_first_b,
    done_second_b,
):
    devices, chunk, _ = packed_ref.shape
    steps = chunk // MINI
    turn = pl.program_id(0)

    @pl.when(turn == 0)
    def _():
        for index in range(devices):
            block = packed_ref[index, :, LANES - 128 :].astype(f32)
            first = slice(index * inner_part, (index + 1) * inner_part)
            lanes = slice(MATRIX_LANE - LANES + 128, MATRIX_LANE - LANES + 128 + inner_part)
            first_w[:, first] = block[:HEAD_DIM, lanes]
            second_w[:, first] = block[HEAD_DIM : 2 * HEAD_DIM, lanes]
            at = VECTOR_LANE - LANES + 128
            vector = jnp.transpose(block)[at : at + 1]
            first_b[:, first] = vector[:, :inner_part]
            small = slice(index * feature_part, (index + 1) * feature_part)
            for number, target in enumerate((second_b, gain_ref, bias_ref)):
                start = inner_part + number * feature_part
                target[:, small] = vector[:, start : start + feature_part]
        known_ref[...] = jnp.zeros_like(known_ref)
        centred = second_w[...]
        second_w[...] = centred - jnp.mean(centred, axis=0, keepdims=True)
        second_b[...] = second_b[...] - row_mean(second_b[...])

    gain = gain_ref[...]
    bias = bias_ref[...]
    rows, cols = token_grid(chunk)

    def finish():
        query, key = two_parts(packed_ref[jnp.maximum(turn - 1, 0)])
        causal = cols <= rows
        mix = dot_nt(query, key)
        query_base = dot_nn(query, done_first[...])
        yield
        first_mix = jnp.where(causal, mix + 1.0, 0.0)
        taken = dot_nn(first_mix, done_grad[...])
        yield
        query_pre = query_base + done_first_b[...] - taken
        density, share = density_and_share(query_pre)
        hidden = (query_pre * share).astype(bf16)
        hidden_ref[...] = hidden
        out_slope_ref[...] = share + query_pre * density
        yield
        mix = dot_nt(hidden, done_act[...])
        res_base = dot_nt(hidden, done_second[...])
        yield
        second_mix = jnp.where(causal, mix + 1.0, 0.0)
        taken = dot_nn(second_mix, done_back[...])
        yield
        query_res = res_base + done_second_b[...] - taken
        square = mean_of(query_res * query_res)
        yield
        out_inverse = lax.rsqrt(square + inner_epsilon)
        out_normal = query_res * out_inverse
        outputs = query.astype(f32) + out_normal * gain + bias
        middle = mean_of(outputs)
        out_norms_ref[:, :HEAD_DIM] = out_normal
        out_norms_ref[:, 2 * HEAD_DIM : 3 * HEAD_DIM] = out_inverse
        yield
        centred = outputs - middle
        square = mean_of(centred * centred)
        yield
        head_inverse = lax.rsqrt(square + epsilon)
        head_normal = centred * head_inverse
        out_norms_ref[:, HEAD_DIM : 2 * HEAD_DIM] = head_normal
        out_norms_ref[:, 3 * HEAD_DIM :] = head_inverse
        normed_ref[0] = jnp.transpose(head_normal).astype(bf16)

    def ahead(place):
        packed = packed_ref[place]
        _, key = two_parts(packed)
        value = packed[:, 2 * HEAD_DIM : 3 * HEAD_DIM]
        logit = rate_logit(packed)
        mix = dot_nt(key, key)
        yield
        rate = jax.nn.sigmoid(logit) * rate_scale
        square_gain = gain * gain
        level_gain = rate * row_mean(square_gain)
        rate_base = rate[:, :HEAD_DIM] * (
            (key.astype(f32) - value.astype(f32) + bias) * gain
        )
        middle = mean_of(rate_base)
        to_rows[0] = rate_base
        to_rows[1] = rate[:, :HEAD_DIM] * square_gain - level_gain[:, :HEAD_DIM]
        to_level[...] = level_gain * inner_epsilon
        to_mix[...] = jnp.where(cols // MINI < rows // MINI, mix + 1.0, 0.0).astype(bf16)
        yield
        to_rows[2] = middle

    def chain(others):
        _, key = two_parts(packed_ref[jnp.minimum(turn, devices - 1)])
        row_ref[...] = to_rows[...]
        level_ref[...] = to_level[...]
        mix_ref[...] = to_mix[...]
        first_low = first_w[...].astype(bf16)
        first_save[0] = first_low
        start_first_b = first_b[...]
        start_b = second_b[...]
        pre_ref[...] = dot_nn(key, first_low) + start_first_b
        state = second_w[...]
        start_low = state.astype(bf16)
        state_b = start_b
        for step in range(steps):
            at = slice(step * MINI, (step + 1) * MINI)
            own_base = row_ref[0, at, :]
            own_gain = row_ref[1, at, :]
            pre = pre_ref[at, :]
            if step >= 1:
                taken = dot_nn(mix_ref[at, :], known_ref[...])
                interleave(others, 1)
                pre = pre - taken
            density, share = density_and_share(pre)
            act = (pre * share).astype(bf16)
            state_low = state.astype(bf16)
            res = dot_nt(act, state_low)
            slope = share + pre * density
            second_save[0, step] = state_low
            interleave(others, 1)
            res = res + state_b
            weighted = own_gain * res
            parts = dot_nn(jnp.concatenate([res, weighted], axis=0), state_low)
            base_act = dot_nn(own_base, state_low)
            interleave(others, 1)
            square = jnp.sum(res * res, axis=-1, keepdims=True)
            sum_gain = jnp.sum(weighted, axis=-1, keepdims=True)
            sum_base = jnp.sum(own_base * res, axis=-1, keepdims=True)
            sum_square = jnp.sum(weighted * res, axis=-1, keepdims=True)
            inverse = lax.rsqrt(square * (1.0 / HEAD_DIM) + inner_epsilon)
            scaled_mean = row_ref[2, at, :] + inverse * sum_gain * (1.0 / HEAD_DIM)
            along = inverse * (sum_base + inverse * sum_square) * (1.0 / HEAD_DIM)
            square_inverse = inverse * inverse
            along_half = along - square_inverse * level_ref[at, :]
            along_wide = jnp.concatenate([along_half, along_half], axis=1)
            normal = res * inverse
            back_res = inverse * (
                own_base + own_gain * normal - scaled_mean - normal * along_half[:, :HEAD_DIM]
            )
            back_low = back_res.astype(bf16)
            back_act = inverse * base_act + square_inverse * (
                parts[MINI:] - along_wide * parts[:MINI]
            )
            grad = (back_act * slope).astype(bf16)
            known_ref[at, :] = grad
            state = state - dot_tn(back_low, act)
            state_b = state_b - jnp.sum(back_res, axis=0, keepdims=True)
            slope_ref[at, :] = slope
            curve_ref[at, :] = back_act * density * (2.0 - pre * pre)
            act_ref[at, :] = act
            grad_pre_ref[at, :] = grad
            back_res_ref[at, :] = back_low
            norms_ref[at, :HEAD_DIM] = normal
            norms_ref[at, HEAD_DIM:] = jnp.broadcast_to(inverse, (MINI, HEAD_DIM))
        for _ in others:
            pass
        grad_all = known_ref[...]
        first_w[...] = first_w[...] - dot_tn(key, grad_all)
        first_b[...] = start_first_b - jnp.sum(grad_all.astype(f32), axis=0, keepdims=True)
        second_w[...] = state
        second_b[...] = state_b
        done_act[...] = act_ref[...]
        done_grad[...] = grad_all
        done_back[...] = back_res_ref[...]
        done_first[...] = first_low
        done_second[...] = start_low
        done_first_b[...] = start_first_b
        done_second_b[...] = start_b

    @pl.when(turn == 0)
    def _():
        for _ in ahead(0):
            pass
        chain(ahead(1))

    @pl.when((turn > 0) & (turn < devices))
    def _():
        chain(alternate(finish(), ahead(jnp.minimum(turn + 1, devices - 1))))

    @pl.when(turn == devices)
    def _():
        for _ in finish():
            pass


def backward_kernel(
    inner_part,
    feature_part,
    sequence_ref,
    packed_ref,
    rows_ref,
    head_grad_ref,
    next_act,
    next_grad,
    next_hidden,
    next_out_slope,
    next_norms,
    next_out_norms,
    next_first,
    next_second,
    now_act,
    now_slope,
    now_curve,
    now_second,
    last_grad,
    last_norms,
    last_first,
    gain_ref,
    bias_ref,
    back_ref,
    first_w,
    first_b,
    second_w,
    second_b,
    gain_sum,
    bias_sum,
    known_ref,
    vector_ref,
    grad_sum,
    to_wide,
    to_rows,
    to_spread,
    to_low,
    to_mix,
    to_state,
    to_sums,
    wide_ref,
    row_ref,
    spread_ref,
    low_ref,
    mix_ref,
    state_ref,
    sums_ref,
    end_known,
    end_rows,
    end_first,
):
    devices, chunk, _ = packed_ref.shape
    steps = chunk // MINI
    turn = pl.program_id(0)
    shard = back_ref.shape[1] - chunk
    gain = gain_ref[...]
    bias = bias_ref[...]
    square_gain = gain * gain
    rows, cols = token_grid(chunk)

    @pl.when(turn == 0)
    def _():
        for ref in (
            first_w,
            first_b,
            second_w,
            second_b,
            gain_sum,
            bias_sum,
            known_ref,
            grad_sum,
            end_known,
            end_rows,
            end_first,
        ):
            ref[...] = jnp.zeros_like(ref)

    def unpack(place):
        packed = packed_ref[place]
        query, key = two_parts(packed)
        miss = key.astype(f32) - packed[:, 2 * HEAD_DIM : 3 * HEAD_DIM].astype(f32) + bias
        return query, key, miss, rate_logit(packed)

    def rate_of(logit):
        return jax.nn.sigmoid(logit[:, :HEAD_DIM]) * rate_scale

    def prepare():
        query, key, miss, logit = unpack(jnp.maximum(devices - 1 - turn, 0))
        head_grad = jnp.transpose(head_grad_ref[0].astype(f32))
        head_normal = next_out_norms[:, HEAD_DIM : 2 * HEAD_DIM]
        head_mean = mean_of(head_grad)
        head_tilt = mean_of(head_grad * head_normal)
        yield
        rate = rate_of(logit)
        normal = next_norms[:, :HEAD_DIM]
        rate_gain = rate * square_gain
        gain_normal = rate_gain * normal
        scaled = rate * (miss * gain) + gain_normal
        scaled_mean = mean_of(scaled)
        along = mean_of(scaled * normal)
        yield
        out_grad = next_out_norms[:, 3 * HEAD_DIM :] * (
            head_grad - head_mean - head_normal * head_tilt
        )
        out_normal = next_out_norms[:, :HEAD_DIM]
        normal_grad = out_grad * gain
        out_mean = mean_of(normal_grad)
        out_tilt = mean_of(normal_grad * out_normal)
        yield
        inverse = next_norms[:, HEAD_DIM:]
        back_res = (inverse * (scaled - scaled_mean - normal * along)).astype(bf16)
        gain_along = mean_of(gain_normal)
        gain_square = mean_of(gain_normal * normal)
        to_low[0] = back_res
        to_low[1] = key
        to_sums[2:3, :HEAD_DIM] = jnp.sum(out_grad * out_normal, axis=0, keepdims=True)
        to_sums[3:4, :HEAD_DIM] = jnp.sum(out_grad, axis=0, keepdims=True)
        yield
        res_grad = next_out_norms[:, 2 * HEAD_DIM : 3 * HEAD_DIM] * (
            normal_grad - out_mean - out_normal * out_tilt
        )
        to_sums[1:2, :HEAD_DIM] = jnp.sum(res_grad, axis=0, keepdims=True)
        res_grad_low = res_grad.astype(bf16)
        hidden_base = dot_nn(res_grad_low, next_second[0, 0])
        mix = dot_nt(res_grad_low, back_res)
        yield
        mix_t = dot_nt(back_res, res_grad_low)
        causal = cols <= rows
        later = rows <= cols
        second_grad = jnp.where(causal, -mix, 0.0)
        hidden_more = dot_nn(second_grad, next_act[...])
        yield
        second_grad_t = jnp.where(later, -mix_t, 0.0)
        to_rows[1] = normal
        to_rows[2] = rate_gain
        to_rows[3] = rate_gain - along
        to_rows[4] = gain_normal + scaled
        to_rows[5] = -(along + rate * row_mean(square_gain))
        yield
        for index, value in enumerate(
            (-(gain_along + scaled_mean), -(3.0 * along + gain_square), inverse * inverse)
        ):
            to_spread[index] = jnp.concatenate([value, value], axis=1)
        mix = dot_nt(next_act[...], next_hidden[...])
        yield
        query_pre_grad = (hidden_base + hidden_more) * next_out_slope[...]
        query_pre_low = query_pre_grad.astype(bf16)
        to_sums[0:1] = jnp.sum(query_pre_grad, axis=0, keepdims=True)
        first = dot_nt(query_pre_low, next_grad[...])
        yield
        second_mix_t = jnp.where(later, mix + 1.0, 0.0)
        to_rows[0] = -dot_nn(second_mix_t, res_grad_low)
        first_t = dot_nt(next_grad[...], query_pre_low)
        yield
        first_grad = jnp.where(causal, -first, 0.0)
        mix = dot_nt(key, query)
        query_grad = dot_nt(query_pre_low, next_first[0])
        query_more = dot_nn(first_grad, key)
        yield
        first_grad_t = jnp.where(later, -first_t, 0.0)
        to_rows[6] = dot_nn(first_grad_t, query)
        first_mix_t = jnp.where(later, mix + 1.0, 0.0).astype(bf16)
        yield
        to_rows[7] = out_grad + query_grad + query_more
        to_wide[1] = dot_nn(second_grad_t, next_hidden[...])
        yield
        to_wide[0] = -dot_nn(first_mix_t, query_pre_low)
        mix = dot_nt(key, key)
        yield
        to_mix[...] = jnp.where(cols // MINI > rows // MINI, mix + 1.0, 0.0).astype(bf16)
        to_state[0] = dot_tn(query, query_pre_low)
        yield
        to_state[1] = dot_tn(res_grad_low, next_hidden[...])

    def conclude():
        place = jnp.minimum(devices + 1 - turn, devices - 1)
        _, key, miss, logit = unpack(place)
        normal = last_norms[:, :HEAD_DIM]
        upon = end_rows[0]
        upon_mean = mean_of(upon)
        upon_tilt = mean_of(upon * normal)
        yield
        pre_grad = end_known[...]
        mix = dot_nt(last_grad[...], pre_grad)
        mix_t = dot_nt(pre_grad, last_grad[...])
        yield
        rate = rate_of(logit)
        scaled_grad = last_norms[:, HEAD_DIM:] * (upon - upon_mean - normal * upon_tilt)
        error_grad = scaled_grad * (rate * gain)
        rate_grad = mean_of(scaled_grad * (miss * gain + square_gain * normal))
        yield
        error = miss + normal * gain
        gain_sum[...] += jnp.sum(
            scaled_grad * rate * error + error_grad * normal, axis=0, keepdims=True
        )
        bias_sum[...] += jnp.sum(error_grad, axis=0, keepdims=True)
        from_grad = dot_nt(last_grad[...], end_first[...])
        yield
        far = rows // MINI < cols // MINI
        near = rows // MINI > cols // MINI
        cross = jnp.where(far, mix, 0.0) + jnp.where(near, mix_t, 0.0)
        from_pre = dot_nt(pre_grad, last_first[0])
        from_cross = dot_nn(cross, key)
        yield
        key_grad = end_rows[1] + error_grad - from_grad + from_pre - from_cross
        back_rate = rate_grad * float(HEAD_DIM) * rate * (1.0 - rate * (1.0 / rate_scale))
        lane = lax.broadcasted_iota(jnp.int32, (chunk, HEAD_DIM), 1)
        tail = jnp.where(lane == 0, back_rate, 0.0)
        packed = jnp.concatenate([end_rows[2], key_grad, -error_grad, tail], axis=1).astype(bf16)
        back_ref[place, :chunk] = packed
        yield
        count = 6
        size = grad_sum.shape[0] // count
        for index in range(count):
            at = slice(index * size, (index + 1) * size)
            grad_sum[at] = grad_sum[at] + dot_tn(rows_ref[0, 0, :, at], packed)
            yield

    def chain(following, previous):
        wide_ref[...] = to_wide[...]
        row_ref[...] = to_rows[...]
        spread_ref[...] = to_spread[...]
        low_ref[...] = to_low[...]
        mix_ref[...] = to_mix[...]
        state_ref[...] = to_state[...]
        sums_ref[...] = to_sums[...]
        first_next = first_w[...]
        first_next_low = first_next.astype(bf16)
        first_next_b = first_b[...]
        state = second_w[...]
        state_b = second_b[...]
        for step in reversed(range(steps)):
            at = slice(step * MINI, (step + 1) * MINI)
            grad = wide_ref[0, at, :] - dot_nn(low_ref[1, at, :], first_next_low) - first_next_b
            if step + 1 < steps:
                grad = grad - dot_nn(mix_ref[at, :], known_ref[...])
            state_low = state.astype(bf16)
            own_act = now_act[at, :]
            own_back = low_ref[0, at, :]
            back_base = row_ref[0, at, :] - dot_nt(own_act, state_low) - state_b
            act_base = wide_ref[1, at, :] - dot_nn(own_back, state_low)
            interleave(following, 1)
            own_low = now_second[0, step]
            slope = now_slope[at, :]
            back_act_grad = (grad * slope).astype(bf16)
            upon = dot_nt(back_act_grad, own_low)
            interleave(following, 1)
            upon = back_base + upon
            own_normal, own_gain, own_grad, own_beta, own_alpha = (
                row_ref[index, at, :] for index in range(1, 6)
            )
            cross, cross_beta, square_inverse = (spread_ref[index, at, :] for index in range(3))
            main = dot_nn(upon * own_grad, own_low)
            sides = dot_nn(jnp.concatenate([own_normal, own_gain, own_beta], axis=0), own_low)
            interleave(previous, 1)
            alpha = row_mean(upon)
            beta = row_mean(upon * own_normal)
            gamma = row_mean(upon * own_gain)
            kappa = row_mean(upon * own_beta)
            level = alpha * own_alpha + beta * cross[:, :HEAD_DIM] + gamma
            tilt = alpha * cross + beta * cross_beta + kappa
            key_res_grad = square_inverse[:, :HEAD_DIM] * (
                upon * own_grad
                - alpha * own_gain
                - beta * own_beta
                - level
                - own_normal * tilt[:, :HEAD_DIM]
            )
            key_res_low = key_res_grad.astype(bf16)
            from_res = (
                main
                - alpha * sides[MINI : 2 * MINI]
                - beta * sides[2 * MINI :]
                - jnp.concatenate([tilt, tilt], axis=1) * sides[:MINI]
            )
            factor = jnp.concatenate([square_inverse, square_inverse], axis=1)
            pre_grad = (act_base + factor * from_res) * slope + grad * now_curve[at, :]
            known_ref[at, :] = pre_grad.astype(bf16)
            state = state + dot_tn(
                jnp.concatenate([key_res_low, own_back], axis=0),
                jnp.concatenate([own_act, back_act_grad], axis=0),
            )
            state_b = state_b + jnp.sum(key_res_grad, axis=0, keepdims=True)
            row_ref[0, at, :] = upon
            interleave(following, 1)
            interleave(previous, 1)
        for generator in (following, previous):
            for _ in generator:
                pass
        pre_grad_all = known_ref[...]
        first_w[...] = first_next + dot_tn(low_ref[1], pre_grad_all) + state_ref[0]
        first_b[...] = (
            first_next_b
            + jnp.sum(pre_grad_all.astype(f32), axis=0, keepdims=True)
            + sums_ref[0:1]
        )
        second_w[...] = state + state_ref[1]
        second_b[...] = state_b + sums_ref[1:2, :HEAD_DIM]
        gain_sum[...] += sums_ref[2:3, :HEAD_DIM]
        bias_sum[...] += sums_ref[3:4, :HEAD_DIM]
        end_known[...] = pre_grad_all
        end_rows[0] = row_ref[0]
        end_rows[1] = row_ref[6]
        end_rows[2] = row_ref[7]
        end_first[...] = first_next_low

    @pl.when(turn == 0)
    def _():
        for _ in prepare():
            pass

    @pl.when((turn > 0) & (turn <= devices))
    def _():
        chain(prepare(), conclude())

    @pl.when(turn == devices + 1)
    def _():
        for _ in conclude():
            pass
        vector_ref[...] = jnp.zeros_like(vector_ref)
        for index in range(devices):
            first = slice(index * inner_part, (index + 1) * inner_part)
            small = slice(index * feature_part, (index + 1) * feature_part)
            vector_ref[index : index + 1, :inner_part] = first_b[:, first]
            for number, source in enumerate((second_b, gain_sum, bias_sum)):
                start = inner_part + number * feature_part
                vector_ref[index : index + 1, start : start + feature_part] = source[:, small]
        columns = jnp.transpose(vector_ref[...]).astype(bf16)
        lanes = slice(MATRIX_LANE, MATRIX_LANE + inner_part)
        for index in range(devices):
            first = slice(index * inner_part, (index + 1) * inner_part)
            back_ref[index, :HEAD_DIM, lanes] = first_w[:, first].astype(bf16)
            back_ref[index, HEAD_DIM : 2 * HEAD_DIM, lanes] = second_w[:, first].astype(bf16)
            back_ref[index, :chunk, VECTOR_LANE : VECTOR_LANE + 1] = columns[:, index : index + 1]
            back_ref[index, chunk:] = grad_sum[index * shard : (index + 1) * shard].astype(bf16)


def whole_block(shape):
    return pl.BlockSpec(shape, lambda index, *_: (0,) * len(shape))


STATE_SHAPES = ((HEAD_DIM, INNER), (1, INNER), (HEAD_DIM, INNER), (1, HEAD_DIM))


def chain_forward(packed, inner_part, feature_part):
    blocks, chunk, _ = packed.shape
    length = blocks * chunk
    steps = chunk // MINI
    row = (1, HEAD_DIM)

    def forth(shape):
        return pl.BlockSpec(
            shape, lambda turn: (jnp.minimum(turn, blocks - 1),) + (0,) * (len(shape) - 1)
        )

    def behind(shape):
        return pl.BlockSpec(
            shape, lambda turn: (jnp.maximum(turn - 1, 0),) + (0,) * (len(shape) - 1)
        )

    def of_length(width, dtype):
        return jax.ShapeDtypeStruct((length, width), dtype)

    wide = (chunk, INNER)
    return pl.pallas_call(
        functools.partial(forward_kernel, inner_part, feature_part),
        grid=(blocks + 1,),
        in_specs=[whole_block(packed.shape)],
        out_specs=[behind((1, HEAD_DIM, chunk))]
        + [forth(wide)] * 4
        + [
            forth((chunk, 2 * HEAD_DIM)),
            forth((1, HEAD_DIM, INNER)),
            forth((1, steps, HEAD_DIM, INNER)),
        ]
        + [behind(wide)] * 3
        + [whole_block(row)] * 2,
        out_shape=[jax.ShapeDtypeStruct((blocks, HEAD_DIM, chunk), bf16)]
        + [of_length(INNER, dtype) for dtype in (bf16, bf16, f32, f32)]
        + [
            of_length(2 * HEAD_DIM, f32),
            jax.ShapeDtypeStruct((blocks, HEAD_DIM, INNER), bf16),
            jax.ShapeDtypeStruct((blocks, steps, HEAD_DIM, INNER), bf16),
        ]
        + [of_length(INNER, dtype) for dtype in (bf16, f32, f32)]
        + [jax.ShapeDtypeStruct(row, f32)] * 2,
        scratch_shapes=[pltpu.VMEM(shape, f32) for shape in STATE_SHAPES]
        + [
            pltpu.VMEM(wide, bf16),
            pltpu.VMEM((chunk, HEAD_DIM), bf16),
            pltpu.VMEM(wide, f32),
        ]
        + [
            pltpu.VMEM((3, chunk, HEAD_DIM), f32),
            pltpu.VMEM((chunk, 2 * HEAD_DIM), f32),
            pltpu.VMEM((chunk, chunk), bf16),
        ]
        * 2
        + [
            pltpu.VMEM(wide, bf16),
            pltpu.VMEM(wide, bf16),
            pltpu.VMEM((chunk, HEAD_DIM), bf16),
            pltpu.VMEM((HEAD_DIM, INNER), bf16),
            pltpu.VMEM((HEAD_DIM, INNER), bf16),
            pltpu.VMEM((1, INNER), f32),
            pltpu.VMEM(row, f32),
        ],
        compiler_params=pltpu.CompilerParams(
            dimension_semantics=("arbitrary",), vmem_limit_bytes=VMEM_BYTES
        ),
        name="chain_forward",
    )(packed)


def chain_backward(packed, rows, sequence, head_grad, saved, inner_part, feature_part):
    act, grad_pre, slope, curve, norms, first_save, second_save = saved[:7]
    hidden, out_slope, out_norms, gain, bias = saved[7:]
    blocks, chunk, _ = packed.shape
    width = rows.shape[-1]
    shard = width // blocks
    steps = chunk // MINI
    row = (1, HEAD_DIM)
    wide = (chunk, INNER)
    narrow = (chunk, 2 * HEAD_DIM)

    def at(shape, delay):
        def index_map(turn, _):
            place = jnp.clip(blocks - 1 - turn + delay, 0, blocks - 1)
            return (place,) + (0,) * (len(shape) - 1)

        return pl.BlockSpec(shape, index_map)

    def rows_map(turn, chosen):
        return (chosen[0], jnp.clip(blocks + 1 - turn, 0, blocks - 1), 0, 0)

    state = (HEAD_DIM, INNER)
    carried = [
        pltpu.VMEM((2,) + wide, f32),
        pltpu.VMEM((8, chunk, HEAD_DIM), f32),
        pltpu.VMEM((3,) + narrow, f32),
        pltpu.VMEM((2, chunk, HEAD_DIM), bf16),
        pltpu.VMEM((chunk, chunk), bf16),
        pltpu.VMEM((2,) + state, f32),
        pltpu.VMEM((8, INNER), f32),
    ]
    return pl.pallas_call(
        functools.partial(backward_kernel, inner_part, feature_part),
        grid_spec=pltpu.PrefetchScalarGridSpec(
            num_scalar_prefetch=1,
            grid=(blocks + 2,),
            in_specs=[
                whole_block(packed.shape),
                pl.BlockSpec((1, 1, chunk, width), rows_map),
                at((1, HEAD_DIM, chunk), 0),
                at(wide, 0),
                at(wide, 0),
                at(wide, 0),
                at(wide, 0),
                at(narrow, 0),
                at(wide, 0),
                at((1,) + state, 0),
                at((1, 1) + state, 0),
                at(wide, 1),
                at(wide, 1),
                at(wide, 1),
                at((1, steps) + state, 1),
                at(wide, 2),
                at(narrow, 2),
                at((1,) + state, 2),
                whole_block(row),
                whole_block(row),
            ],
            out_specs=whole_block((blocks, chunk + shard, LANES)),
            scratch_shapes=[pltpu.VMEM(shape, f32) for shape in STATE_SHAPES + (row, row)]
            + [
                pltpu.VMEM(wide, bf16),
                pltpu.VMEM((chunk, 128), f32),
                pltpu.VMEM((width, LANES), f32),
            ]
            + carried
            + carried
            + [
                pltpu.VMEM(wide, bf16),
                pltpu.VMEM((3, chunk, HEAD_DIM), f32),
                pltpu.VMEM(state, bf16),
            ],
        ),
        out_shape=jax.ShapeDtypeStruct((blocks, chunk + shard, LANES), bf16),
        compiler_params=pltpu.CompilerParams(
            dimension_semantics=("arbitrary",), vmem_limit_bytes=VMEM_BYTES
        ),
        name="chain_backward",
    )(
        sequence,
        packed,
        rows,
        head_grad,
        act,
        grad_pre,
        hidden,
        out_slope,
        norms,
        out_norms,
        first_save,
        second_save,
        act,
        slope,
        curve,
        second_save,
        grad_pre,
        norms,
        first_save,
        gain,
        bias,
    )


def layer_norm_parts(values):
    centred = values - row_mean(values)
    inverse = lax.rsqrt(row_mean(centred * centred) + epsilon)
    return centred * inverse, inverse


def layer_norm_back(normal, inverse, scaling, grad):
    scaled = grad * scaling
    return inverse * (scaled - row_mean(scaled) - normal * row_mean(scaled * normal))


def start_kernel(
    head_count,
    rows_ref,
    weights_ref,
    gain_ref,
    inner_ref,
    packed_ref,
    normed_ref,
    matrix_ref,
):
    tensor_count = rows_ref.shape[0]
    seq_count, chunk, _ = normed_ref.shape
    rows = chunk // tensor_count
    matrix_ref[...] = jnp.zeros_like(matrix_ref)
    for head in range(head_count):
        first = head * 3 * HEAD_DIM
        rate = head_count * 3 * HEAD_DIM + head
        column = weights_ref[:, rate : rate + 1]
        matrix_ref[head, :, : 3 * HEAD_DIM] = weights_ref[:, first : first + 3 * HEAD_DIM]
        matrix_ref[head, :, RATE_LANE : RATE_LANE + 1] = column
        matrix_ref[head, :, RATE_LANE + 1 : RATE_LANE + 2] = column
    lane = lax.broadcasted_iota(jnp.int32, (chunk, LANES), 1)
    for sequence in range(seq_count):
        part = slice(sequence * rows, (sequence + 1) * rows)
        values = jnp.concatenate([rows_ref[index, part] for index in range(tensor_count)], axis=0)
        normal, _ = layer_norm_parts(values.astype(f32))
        normed = (normal * gain_ref[...]).astype(bf16)
        normed_ref[sequence] = normed
        for head in range(head_count):
            projected = dot_nn(normed, matrix_ref[head])
            rest = projected - projected.astype(bf16).astype(f32)
            projected = jnp.where(lane == RATE_LANE + 1, rest, projected).astype(bf16)
            packed_ref[head * seq_count + sequence] = jnp.where(
                lane >= VECTOR_LANE, inner_ref[head], projected
            )
    for index in range(head_count * seq_count, packed_ref.shape[0]):
        packed_ref[index] = jnp.zeros((chunk, LANES), bf16)


def feed_forward_kernel(
    heads_ref,
    rows_ref,
    weights_ref,
    out_ref,
    gain_ref,
    terms_ref,
    mixed_ref,
    normed_ref,
    back_ref,
    swiglu_ref,
    cot_ref,
):
    tensor_count, head_count, seq_count, _, chunk = heads_ref.shape
    ff_local = swiglu_ref.shape[1]
    rows = chunk // tensor_count
    total = seq_count * chunk
    for sequence in range(seq_count):
        part = slice(sequence * rows, (sequence + 1) * rows)
        other = slice((seq_count + sequence) * rows, (seq_count + sequence + 1) * rows)
        values = jnp.concatenate([rows_ref[index, part] for index in range(tensor_count)], axis=0)
        mixed = values.astype(f32)
        for index in range(tensor_count):
            heads = [heads_ref[index, head, sequence] for head in range(head_count)]
            heads = jnp.transpose(jnp.concatenate(heads, axis=0).astype(f32))
            mixed = mixed + dot_nt(heads, out_ref[index])
        for index in range(tensor_count):
            mixed_ref[index, sequence] = mixed[index * rows : (index + 1) * rows]
        normal, _ = layer_norm_parts(mixed)
        at = slice(sequence * chunk, (sequence + 1) * chunk)
        normed_ref[at] = (normal * gain_ref[...]).astype(bf16)
        for index in range(tensor_count):
            first = sequence * chunk + index * rows
            cot_ref[first : first + rows] = rows_ref[index, other]
    normed = normed_ref[...]
    cot = cot_ref[...]
    for first in range(0, ff_local, 256):
        at = slice(first, first + 256)
        beyond = slice(ff_local + first, ff_local + first + 256)
        gate = dot_nn(normed, weights_ref[:, at])
        up = dot_nn(normed, weights_ref[:, beyond])
        back = dot_nn(cot, weights_ref[:, 2 * ff_local + first : 2 * ff_local + first + 256])
        share = jax.nn.sigmoid(gate)
        silu = gate * share
        swiglu_ref[:, at] = (silu * up).astype(bf16)
        back_ref[:, at] = (back * up * (share * (1.0 + gate * (1.0 - share)))).astype(bf16)
        back_ref[:, beyond] = (back * silu).astype(bf16)
    ffn_term = dot_nt(back_ref[...], weights_ref[:, : 2 * ff_local]).astype(bf16)
    down_term = dot_nt(swiglu_ref[...], weights_ref[:, 2 * ff_local : 3 * ff_local]).astype(bf16)
    for sequence in range(seq_count):
        for index in range(tensor_count):
            first = sequence * chunk + index * rows
            terms_ref[index, sequence] = ffn_term[first : first + rows]
            terms_ref[index, seq_count + sequence] = down_term[first : first + rows]


def feed_forward_grad_kernel(normed_ref, back_ref, swiglu_ref, cot_ref, grads_ref):
    normed = jnp.transpose(normed_ref[...].astype(f32)).astype(bf16)
    cot = jnp.transpose(cot_ref[...].astype(f32)).astype(bf16)
    width = back_ref.shape[1]
    for first in range(0, width, 256):
        at = slice(first, first + 256)
        grads_ref[:, at] = dot_nn(normed, back_ref[:, at]).astype(bf16)
    for first in range(0, swiglu_ref.shape[1], 256):
        at = slice(width + first, width + first + 256)
        grads_ref[:, at] = dot_nn(cot, swiglu_ref[:, first : first + 256]).astype(bf16)


def head_back_kernel(grads_ref, out_ref, heads_ref, back_ref, out_grad_ref):
    head_count, seq_count, _, chunk = heads_ref.shape
    devices, shard, _ = out_grad_ref.shape
    total = None
    for sequence in range(seq_count):
        grads = grads_ref[sequence]
        back = jnp.transpose(dot_nn(grads, out_ref[...])).astype(bf16)
        for head in range(head_count):
            back_ref[head * seq_count + sequence] = back[head * HEAD_DIM : (head + 1) * HEAD_DIM]
        heads = [heads_ref[head, sequence] for head in range(head_count)]
        term = dot_nt(jnp.transpose(grads.astype(f32)), jnp.concatenate(heads, axis=0))
        total = term if total is None else total + term
    for index in range(head_count * seq_count, devices):
        back_ref[index] = jnp.zeros((HEAD_DIM, chunk), bf16)
    for index in range(devices):
        out_grad_ref[index] = total[index * shard : (index + 1) * shard].astype(bf16)


def matrix_output_kernel(sums_ref, out_ref, weights_ref, gate_up_ref, down_ref, out_grad_ref, gain_ref):
    ff_local = down_ref.shape[1]
    sums = sums_ref[...].astype(f32)
    for index in range(2):
        gate_up_ref[:, index, :] = sums[:, index * ff_local : (index + 1) * ff_local]
    down_ref[...] = sums[:, 2 * ff_local :]
    total = out_ref[0].astype(f32)
    for index in range(1, out_ref.shape[0]):
        total = total + out_ref[index].astype(f32)
    out_grad_ref[...] = jnp.transpose(total)
    products = sums[:, : 2 * ff_local] * weights_ref[:, : 2 * ff_local].astype(f32)
    gain = jnp.sum(products, axis=-1, keepdims=True)
    gain_ref[...] = jnp.broadcast_to(gain, gain_ref.shape)


def tail_kernel(
    received_ref,
    matrix_ref,
    own_ref,
    gain_two_ref,
    gains_ref,
    terms_ref,
    qkv_ref,
    small_ref,
    state_ref,
):
    head_count = matrix_ref.shape[0]
    shard = own_ref.shape[1]
    tensor_count, term_rows, width = terms_ref.shape
    chunk = received_ref.shape[1] - shard
    seq_count = (term_rows - 16) * tensor_count // chunk
    rows = chunk // tensor_count
    lane = lax.broadcasted_iota(jnp.int32, (chunk, LANES), 1)
    for sequence in range(seq_count):
        total = None
        for head in range(head_count):
            values = received_ref[head * seq_count + sequence, :chunk]
            values = jnp.where(lane <= RATE_LANE, values, jnp.zeros_like(values))
            term = dot_nt(values, matrix_ref[head])
            total = term if total is None else total + term
        for index in range(tensor_count):
            part = total[index * rows : (index + 1) * rows]
            terms_ref[index, sequence * rows : (sequence + 1) * rows] = part.astype(bf16)
    lane = lax.broadcasted_iota(jnp.int32, (shard, LANES), 1)
    column = lax.broadcasted_iota(jnp.int32, (shard, 128), 1)
    gain = None
    small = jnp.where(column == 1, gain_two_ref[...], 0.0)
    for head in range(head_count):
        grads = received_ref[head * seq_count, chunk:].astype(f32)
        state = received_ref[head * seq_count, :chunk, RATE_LANE:].astype(f32)
        for sequence in range(1, seq_count):
            grads = grads + received_ref[head * seq_count + sequence, chunk:].astype(f32)
            state = state + received_ref[
                head * seq_count + sequence, :chunk, RATE_LANE:
            ].astype(f32)
        state_ref[head] = state
        for index in range(3):
            at = slice(index * HEAD_DIM, (index + 1) * HEAD_DIM)
            qkv_ref[index, :, head * HEAD_DIM : (head + 1) * HEAD_DIM] = grads[:, at]
        products = jnp.where(lane <= RATE_LANE, grads * own_ref[head].astype(f32), 0.0)
        products = jnp.sum(products, axis=-1, keepdims=True)
        gain = products if gain is None else gain + products
        small = jnp.where(column == 2 + head, grads[:, RATE_LANE : RATE_LANE + 1], small)
    small = jnp.transpose(jnp.where(column == 0, gain, small))[: small_ref.shape[0]]
    small_ref[...] = small
    gain = small[:2] / gains_ref[...]
    high = gain.astype(bf16)
    low = (gain - high.astype(f32)).astype(bf16)
    block = jnp.concatenate([high.astype(f32), low.astype(f32), jnp.zeros((12, shard), f32)], axis=0)
    for index in range(tensor_count):
        first = seq_count * rows
        terms_ref[index, first:, :] = jnp.zeros((16, width), bf16)
        terms_ref[index, first:, :shard] = block.astype(bf16)


def whole_call(kernel, name, operands, results, vmem_bytes=GLUE_BYTES):
    def spec(shape):
        return pl.BlockSpec(shape, lambda: (0,) * len(shape))

    return pl.pallas_call(
        kernel,
        in_specs=[spec(operand.shape) for operand in operands],
        out_specs=[spec(result.shape) for result in results],
        out_shape=results,
        compiler_params=pltpu.CompilerParams(vmem_limit_bytes=vmem_bytes),
        name=name,
    )(*operands)


def dots(subscripts, left, right):
    return jnp.einsum(subscripts, left, right, preferred_element_type=f32)


def exchange(values, axis):
    return lax.all_to_all(values, axis, 0, 0, tiled=False)


def share_out(values, axis):
    count = lax.axis_size(axis)
    return exchange(jnp.broadcast_to(values[None], (count,) + values.shape), axis)


def ordered(first, then):
    return lax.optimization_barrier((first, then))


def inner_block(matrix_one, matrix_two, vectors, rows):
    width = matrix_one.shape[-1]
    matrices = jnp.concatenate([matrix_one, matrix_two], axis=-2)
    column = jnp.concatenate(vectors, axis=-1)[..., None]
    lead = [(0, 0)] * (column.ndim - 2)
    column = jnp.pad(
        column,
        lead + [(0, rows - column.shape[-2]), (VECTOR_LANE, LANES - VECTOR_LANE - 1)],
    )
    matrices = jnp.pad(
        matrices,
        lead + [(0, rows - matrices.shape[-2]), (MATRIX_LANE, LANES - MATRIX_LANE - width)],
    )
    return column + matrices


def local(
    tokens,
    gain_attn,
    gain_ffn,
    w_qkv,
    w_rate,
    w_out,
    w_gate_up,
    w_down,
    w_one,
    b_one,
    w_two,
    b_two,
    norm_gain_inner,
    norm_bias_inner,
    cotangent,
):
    device_count = lax.axis_size("dp")
    tensor_count = lax.axis_size("tensor")
    local_rows, seq_count, width = tokens.shape
    row_count = local_rows * seq_count
    chunk = local_rows * tensor_count
    head_count = w_rate.shape[1]
    local_width = head_count * HEAD_DIM
    shard = w_qkv.shape[0]
    part = gain_attn.shape[0]
    ff_local = w_down.shape[0]
    chain_count = seq_count * head_count
    inner_part = w_one.shape[2]
    feature_part = b_two.shape[1]
    assert chain_count <= device_count
    assert chunk == 2 * HEAD_DIM and inner_part <= 32 and part <= shard
    rank = lax.axis_index("tensor")
    place = lax.axis_index("dp")

    own_tokens = tokens.transpose(1, 0, 2).reshape(row_count, width)
    own_cot = cotangent.transpose(1, 0, 2).reshape(row_count, width)
    row_full = share_out(jnp.concatenate([own_tokens, own_cot], axis=0), "tensor")
    head_columns = w_qkv.reshape(shard, 3, head_count, HEAD_DIM).transpose(0, 2, 1, 3)
    gain_columns = jnp.pad(jnp.stack([gain_attn, gain_ffn], axis=1), ((0, shard - part), (0, 0)))
    qkv_pack = jnp.concatenate(
        [head_columns.reshape(shard, 3 * local_width), w_rate, gain_columns], axis=1
    )
    qkv_full = lax.all_gather(qkv_pack, "dp", axis=0, tiled=True)
    qkv_full, row_full = ordered(qkv_full, row_full)
    some_gains = qkv_full[:, 3 * local_width + head_count :]
    some_gains = some_gains.reshape(device_count, shard, 2)[:, :part].transpose(2, 0, 1)
    gains = lax.all_gather(some_gains.reshape(2, device_count * part), "tensor", axis=0)
    gains = gains.reshape(tensor_count, 2, device_count, part).transpose(1, 2, 0, 3)
    gains = gains.reshape(2, width).astype(f32)
    scale_attn, scale_ffn = gains[0:1], gains[1:2]

    ffn_pack = jnp.concatenate(
        [w_gate_up.reshape(shard, 2 * ff_local), w_down.T, w_out.T], axis=1
    )
    ffn_full = lax.all_gather(ffn_pack, "dp", axis=0, tiled=True)
    own_out = ffn_full[:, 3 * ff_local :]

    inner = inner_block(
        w_one,
        w_two.transpose(0, 2, 1),
        [b_one, b_two, norm_gain_inner, norm_bias_inner],
        chunk,
    )
    shape = jax.ShapeDtypeStruct
    packed, normed_attn, head_matrix = whole_call(
        functools.partial(start_kernel, head_count),
        "projections",
        (row_full, qkv_full, scale_attn, inner),
        (
            shape((device_count, chunk, LANES), bf16),
            shape((seq_count, chunk, width), bf16),
            shape((head_count, width, LANES), bf16),
        ),
    )
    chain_in = exchange(packed, "dp")
    chain_in, own_out = ordered(chain_in, own_out)
    out_full = lax.all_gather(own_out, "tensor", axis=0)

    normed_full = lax.all_gather(normed_attn, "dp", axis=1, tiled=False)

    forward_out = chain_forward(chain_in, inner_part, feature_part)
    saved = forward_out[1:]
    head_local = exchange(forward_out[0], "dp")[:chain_count]
    head_local = head_local.reshape(head_count, seq_count, HEAD_DIM, chunk)
    head_rows = lax.all_gather(head_local, "tensor", axis=0, tiled=False)

    group_rows = seq_count * chunk
    terms, mixed, normed_ffn, back_gate_up, swiglu, group_cot = whole_call(
        feed_forward_kernel,
        "feed_forward",
        (head_rows, row_full, ffn_full, out_full, scale_ffn),
        (
            shape((tensor_count, 2 * seq_count, local_rows, width), bf16),
            shape((tensor_count, seq_count, local_rows, width), f32),
            shape((group_rows, width), bf16),
            shape((group_rows, 2 * ff_local), bf16),
            shape((group_rows, ff_local), bf16),
            shape((group_rows, width), bf16),
        ),
        VMEM_BYTES,
    )
    ffn_sums = exchange(terms, "tensor")
    (ffn_grads,) = whole_call(
        feed_forward_grad_kernel,
        "feed_forward_grads",
        (normed_ffn, back_gate_up, swiglu, group_cot),
        (shape((width, 3 * ff_local), bf16),),
        VMEM_BYTES,
    )
    ffn_grad_sums = lax.psum_scatter(ffn_grads, "dp", scatter_dimension=0, tiled=True)
    ffn_sums, normed_full = ordered(ffn_sums, normed_full)
    ffn_sums = ffn_sums.astype(f32).sum(axis=0)
    own_mixed = lax.dynamic_index_in_dim(mixed, rank, 0, keepdims=False)
    own_normal, own_inverse = layer_norm_parts(own_mixed)
    back_mixed = own_cot.astype(f32).reshape(own_mixed.shape) + layer_norm_back(
        own_normal, own_inverse, scale_ffn, ffn_sums[:seq_count]
    )
    result = (own_mixed + ffn_sums[seq_count:]).astype(bf16)
    attn_grads = lax.all_gather(back_mixed.astype(bf16), "tensor", axis=1, tiled=True)
    back_head, out_terms = whole_call(
        head_back_kernel,
        "head_back",
        (attn_grads, own_out, head_local),
        (
            shape((device_count, HEAD_DIM, chunk), bf16),
            shape((device_count, shard, local_width), bf16),
        ),
    )
    head_grad = exchange(back_head, "dp")
    out_sums = exchange(out_terms, "dp")

    chosen = jnp.reshape(place % seq_count, (1,)).astype(jnp.int32)
    back_packed = chain_backward(
        chain_in, normed_full, chosen, head_grad, saved, inner_part, feature_part
    )
    received = exchange(back_packed, "dp")
    grad_gate_up, grad_down, grad_out, gain_two = whole_call(
        matrix_output_kernel,
        "matrix_outputs",
        (ffn_grad_sums, out_sums, ffn_pack),
        (
            shape((shard, 2, ff_local), f32),
            shape((shard, ff_local), f32),
            shape((local_width, shard), f32),
            shape((shard, 128), f32),
        ),
    )
    own_matrix = lax.dynamic_slice_in_dim(head_matrix, place * shard, shard, 1)
    own_gains = lax.dynamic_slice_in_dim(gains, place * shard, shard, 1)
    terms, grad_qkv, small, state_block = whole_call(
        tail_kernel,
        "tail",
        (received, head_matrix, own_matrix, gain_two, own_gains),
        (
            shape((tensor_count, row_count + 16, width), bf16),
            shape((3, shard, local_width), f32),
            shape((8, shard), f32),
            shape((head_count, chunk, LANES - RATE_LANE), f32),
        ),
    )
    tail = exchange(terms, "tensor").astype(f32).sum(axis=0)
    own_inputs = tokens.transpose(1, 0, 2).astype(f32)
    own_normal, own_inverse = layer_norm_parts(own_inputs)
    attn_sums = tail[:row_count].reshape(own_inputs.shape)
    input_grad = back_mixed + layer_norm_back(own_normal, own_inverse, scale_attn, attn_sums)
    gain_sums = tail[row_count : row_count + 2, :shard] + tail[row_count + 2 : row_count + 4, :shard]
    gain_sums = lax.dynamic_slice_in_dim(gain_sums, rank * part, part, 1)

    matrices = state_block[..., MATRIX_LANE - RATE_LANE :][..., :inner_part]
    grad_one = matrices[:, :HEAD_DIM]
    grad_two = matrices[:, HEAD_DIM : 2 * HEAD_DIM].transpose(0, 2, 1)
    columns = state_block[:, :, VECTOR_LANE - RATE_LANE]
    ends = [inner_part + index * feature_part for index in range(4)]
    grad_b_one = columns[:, : ends[0]]
    grad_b_two, grad_gain_inner, grad_bias_inner = (
        columns[:, ends[index] : ends[index + 1]] for index in range(3)
    )

    def by_token(values):
        return values.reshape(seq_count, local_rows, width).transpose(1, 0, 2)

    return (
        by_token(result),
        by_token(input_grad),
        gain_sums[0],
        gain_sums[1],
        grad_qkv.transpose(1, 0, 2),
        small[2 : 2 + head_count].T,
        grad_out,
        grad_gate_up,
        grad_down.T,
        grad_one,
        grad_b_one,
        grad_two,
        grad_b_two,
        grad_gain_inner,
        grad_bias_inner,
    )


def solution(mesh):
    rows = P(("dp", "tensor"), None, None)
    gains = P(("dp", "tensor"))
    placed = (
        rows,
        gains,
        gains,
        P("dp", None, "tensor"),
        P("dp", "tensor"),
        P("tensor", "dp"),
        P("dp", None, "tensor"),
        P("tensor", "dp"),
        P("tensor", None, "dp"),
        P("tensor", "dp"),
        P("tensor", "dp", None),
        P("tensor", "dp"),
        P("tensor", "dp"),
        P("tensor", "dp"),
    )
    return jax.shard_map(
        local,
        mesh=mesh,
        in_specs=placed + (rows,),
        out_specs=(rows,) + placed,
        check_vma=False,
    )
```

time: 336 us -> 297 us (0.88)
  Pallas kernels: 126 us -> 89 us
  waiting for transfers between devices: 58.6 us -> 70 us
  starting transfers between devices: 36.7 us -> 30.6 us
    pallas_call x1, Pallas kernels: 57.2 us -> 32.7 us  [chain_forward(): pl.pallas_call(functools.partial(forward_kernel, inner_part, feature_part...]
    all_gather x1, waiting for transfers between devices: 0.02 us -> 14.4 us  [local(): normed_full = lax.all_gather(normed_attn, 'dp', axis=1, tiled=False)]
    pallas_call x1, Pallas kernels: 53.6 us -> 39.8 us  [chain_backward(): pl.pallas_call(functools.partial(backward_kernel, inner_part, feature_par...]
    all_to_all x9 -> x7, waiting for transfers between devices: 45.3 us -> 34.4 us  [exchange(): return lax.all_to_all(values, axis, 0, 0, tiled=False)]
    reduce_scatter x1, waiting for transfers between devices: 0.02 us -> 7.27 us  [local(): lax.psum_scatter(ffn_grads, 'dp', scatter_dimension=0, tiled=True)]
    all_to_all x9 -> x7, starting transfers between devices: 36.5 us -> 30.5 us  [exchange(): return lax.all_to_all(values, axis, 0, 0, tiled=False)]
    pallas_call x5 -> x6, Pallas kernels: 15.4 us -> 16.6 us  [whole_call(): pl.pallas_call(kernel, in_specs=[spec(operand.shape) for operand in opera...]
  transfers between devices with their start and end apart: 13 -> 11, of which waited for: 8 -> 7; matrix products, arithmetic and copies ran while one was open for 7% -> 5% of each run, Pallas kernels for 38% -> 30%
where the time goes in v3:
time: 297 us; the launch traced here: 296 us
  Pallas kernels  89 us (30%)
  waiting for transfers between devices  70 us (24%)
  blocking collectives  67.7 us (23%)
  starting transfers between devices  30.6 us (10%)
  local copies, waits for them, and re-layouts  15.9 us (5%)
  between operations  14.2 us (5%)
  other arithmetic  8.27 us (3%)
    pallas_call x1, Pallas kernels, chain_backward(): pl.pallas_call(functools.partial(backward_kernel, inner_part, feature_par...  39.8 us
    all_gather x1, blocking collectives, local(): qkv_full = lax.all_gather(qkv_pack, 'dp', axis=0, tiled=True)  35.9 us
    all_to_all x7, waiting for transfers between devices, exchange(): return lax.all_to_all(values, axis, 0, 0, tiled=False)  34.4 us
    pallas_call x1, Pallas kernels, chain_forward(): pl.pallas_call(functools.partial(forward_kernel, inner_part, feature_part...  32.7 us
    all_to_all x7, starting transfers between devices, exchange(): return lax.all_to_all(values, axis, 0, 0, tiled=False)  30.5 us
    pallas_call x6, Pallas kernels, whole_call(): pl.pallas_call(kernel, in_specs=[spec(operand.shape) for operand in opera...  16.6 us
    all_gather x1, waiting for transfers between devices, local(): normed_full = lax.all_gather(normed_attn, 'dp', axis=1, tiled=False)  14.4 us
    all_to_all x1, blocking collectives, exchange(): return lax.all_to_all(values, axis, 0, 0, tiled=False)  13.3 us
  transfers between devices with their start and end apart: 11, of which 7 were waited for; matrix products, arithmetic and copies ran while one was open for 5% of the time, Pallas kernels for 30%

profile of v3, /device:TPU:0, one launch (start us, length us, event | category | flops | bytes accessed | tf_op | source)
XLA Modules:
  0.0 295.8 jit_solution(7548836181956750591)
XLA Ops:
  7.2 0.9 copy.96
  8.1 1.0 copy.106
  9.1 1.7 pad_maximum_fusion.weights_ref
  10.9 0.9 copy.91
  11.8 0.9 copy.90
  12.8 0.9 broadcast_in_dim.4
  13.7 4.2 %all-to-all-start = ((bf16[4,128,768]{2,1,0:T(8,128)(2,1)}), bf16[4,128,768]{2,1,0:T(8,128)(2,1)S(1)}, u32[]{:S(2)}, u32[]{:S(2)}) async-start(bf16[4,128,768]{2,1,0:T(8,128)(2,1)} %broadcast_in_dim.4), calls=%async_computation | async-start | bytes 1572864 | tf_op jit(solution)/shard_map/all_to_all | solution.py:1072
  19.2 35.9 %all_gather.27.weights_ref = bf16[768,581]{1,0:T(8,128)(2,1)S(1)} all-gather(bf16[96,581]{1,0:T(8,128)(2,1)S(1)} %fusion.14), channel_id=1, replica_groups=mesh['dp'=8,'tensor'=4] {'dp'}, dimensions={0}, use_global_device_ids=true | all-gather | bytes 1003968 | tf_op jit(solution)/shard_map/all_gather | solution.py:1143
  55.3 5.1 %all_gather.28 = bf16[4,2,192]{2,1,0:T(2,128)(2,1)S(1)} all-gather(bf16[1,2,192]{2,1,0:T(2,128)(2,1)S(1)} %copy.105), channel_id=1, replica_groups=mesh['dp'=8,'tensor'=4] {'tensor'}, dimensions={0}, use_global_device_ids=true | all-gather | bytes 3840 | tf_op jit(solution)/shard_map/all_gather | solution.py:1147
  60.6 2.2 projections.1
  62.8 0.8 copy-done.3
  63.6 5.7 %all-to-all-start.1 = ((bf16[8,128,256]{2,1,0:T(8,128)(2,1)}), bf16[8,128,256]{2,1,0:T(8,128)(2,1)S(1)}, u32[]{:S(2)}, u32[]{:S(2)}) async-start(bf16[8,128,256]{2,1,0:T(8,128)(2,1)} %copy-done.3), calls=%async_computation.1 | async-start | bytes 1048576 | tf_op jit(solution)/shard_map/all_to_all | solution.py:1072
  69.3 13.2 %all-gather.6.cloned.1.call-done.weights_ref = bf16[768,1728]{1,0:T(8,128)(2,1)} async-done(((bf16[96,1728]{1,0:T(8,128)(2,1)}), bf16[768,1728]{1,0:T(8,128)(2,1)}) %all-gather.6.cloned.1.call-update) | async-done | bytes 2654224 | tf_op jit(solution)/shard_map/all_gather | solution.py:1155
  82.5 1.8 slice.97.out_ref
  84.3 4.0 %all-to-all-done.1.packed_ref = bf16[8,128,256]{2,1,0:T(8,128)(2,1)S(1)} async-done(((bf16[8,128,256]{2,1,0:T(8,128)(2,1)}), bf16[8,128,256]{2,1,0:T(8,128)(2,1)S(1)}, u32[]{:S(2)}, u32[]{:S(2)}) %all-to-all-start.1) | async-done | bytes 524320 | tf_op jit(solution)/shard_map/all_to_all | solution.py:1072
  88.4 0.7 all-gather.10.cloned.1.call-update
  89.1 32.7 %chain_forward.1 = (bf16[8,64,128]{2,1,0:T(8,128)(2,1)}, bf16[1024,256]{1,0:T(8,128)(2,1)}, bf16[1024,256]{1,0:T(8,128)(2,1)}, f32[1024,256]{1,0:T(8,128)}, f32[...) custom-call(bf16[8,128,256]{2,1,0:T(8,128)(2,1)} %copy-done.5), custom_call_target="tpu_custom_call" | custom-call | tf_op jit(solution)/shard_map/chain_forward/pallas_call | solution.py:689
  121.7 3.7 %all-to-all-start.2 = ((bf16[8,64,128]{2,1,0:T(8,128)(2,1)}), bf16[8,64,128]{2,1,0:T(8,128)(2,1)S(1)}, u32[]{:S(2)}, u32[]{:S(2)}) async-start(bf16[8,64,128]{2,1,0:T(8,128)(2,1)} %get-tuple-element.57), calls=%async_computation.2 | async-start | bytes 262144 | tf_op jit(solution)/shard_map/all_to_all | solution.py:1072
  125.5 0.7 slice.79.gain_ref
  126.1 9.5 %all-to-all-done.2 = bf16[8,64,128]{2,1,0:T(8,128)(2,1)S(1)} async-done(((bf16[8,64,128]{2,1,0:T(8,128)(2,1)}), bf16[8,64,128]{2,1,0:T(8,128)(2,1)S(1)}, u32[]{:S(2)}, u32[]{:S(2)}) %all-to-all-start.2) | async-done | bytes 131104 | tf_op jit(solution)/shard_map/all_to_all | solution.py:1072
  135.7 7.0 %all_gather.30.heads_ref = bf16[4,3,2,64,128]{4,3,2,1,0:T(8,128)(2,1)} all-gather(bf16[1,3,2,64,128]{4,3,2,1,0:T(8,128)(2,1)S(1)} %bitcast.72), channel_id=1, replica_groups=mesh['dp'=8,'tensor'=4] {'tensor'}, dimensions={0}, use_global_device_ids=true | all-gather | bytes 491520 | tf_op jit(solution)/shard_map/all_gather | solution.py:1185
  142.7 6.8 %feed_forward.1 = (bf16[4,4,32,768]{3,2,1,0:T(8,128)(2,1)}, f32[4,2,32,768]{3,2,1,0:T(8,128)}, bf16[256,768]{1,0:T(8,128)(2,1)}, bf16[256,1024]{1,0:T(8,128)(2,1...) custom-call(bf16[4,3,2,64,128]{4,3,2,1,0:T(8,128)(2,1)} %all_gather.30.heads_ref, bf16[4,128,768]{2,1,0:T(8,128)(2,1)} %copy-done, ...), custom_call_target="tpu_custom_call" | custom-call | tf_op jit(solution)/shard_map/feed_forward/pallas_call | solution.py:1057
  149.5 3.6 %feed_forward_grads.1 = bf16[768,1536]{1,0:T(8,128)(2,1)} custom-call(bf16[256,768]{1,0:T(8,128)(2,1)} %get-tuple-element.78.normed_ref, bf16[256,1024]{1,0:T(8,128)(2,1)} %get-tuple-element.79.back_ref, bf16[256,512]{1,0:T(8,128)(2,1)} %get-tuple-element.80.swiglu_ref, bf16[256,768]{1,0:T(8,128)(2,1)} %get-tuple-element.81.cot_ref), custom_call_target="tpu_custom_call" | custom-call | tf_op jit(solution)/shard_map/feed_forward_grads/pallas_call | solution.py:1057
  153.1 3.6 %all-to-all-start.3 = ((bf16[4,4,32,768]{3,2,1,0:T(8,128)(2,1)}), bf16[4,4,32,768]{3,2,1,0:T(8,128)(2,1)S(1)}, u32[]{:S(2)}, u32[]{:S(2)}) async-start(bf16[4,4,32,768]{3,2,1,0:T(8,128)(2,1)} %get-tuple-element.60), calls=%async_computation.3 | async-start | bytes 1572864 | tf_op jit(solution)/shard_map/all_to_all | solution.py:1072
  156.9 1.0 dynamic-slice_reduce_fusion
  157.9 1.1 multiply_reduce_fusion.2
  159.0 14.4 %all-gather.10.cloned.1.call-done = bf16[2,1024,768]{2,1,0:T(8,128)(2,1)} async-done(((bf16[2,128,768]{2,1,0:T(8,128)(2,1)}), bf16[2,1024,768]{2,1,0:T(8,128)(2,1)}) %all-gather.10.cloned.1.call-update) | async-done | bytes 3145744 | tf_op jit(solution)/shard_map/all_gather | solution.py:1179
  173.6 1.1 fusion.13
  174.7 1.1 fusion.16
  175.8 6.5 %all_gather.35.grads_ref = bf16[2,128,768]{2,1,0:T(8,128)(2,1)S(1)} all-gather(bf16[2,32,768]{2,1,0:T(8,128)(2,1)S(1)} %fusion.16), channel_id=1, replica_groups=mesh['dp'=8,'tensor'=4] {'tensor'}, dimensions={1}, use_global_device_ids=true | all-gather | bytes 491520 | tf_op jit(solution)/shard_map/all_gather | solution.py:1219
  182.2 1.3 head_back.1
  183.5 13.3 %all_to_all.40.head_grad_ref = bf16[8,64,128]{2,1,0:T(8,128)(2,1)} all-to-all(bf16[8,64,128]{2,1,0:T(8,128)(2,1)S(1)} %get-tuple-element.64), channel_id=1, replica_groups=mesh['dp'=8,'tensor'=4] {'dp'}, dimensions={0} | all-to-all | bytes 262144 | tf_op jit(solution)/shard_map/all_to_all | solution.py:1072
  196.8 3.6 %all-to-all-start.6 = ((bf16[8,96,192]{2,1,0:T(8,128)(2,1)}), bf16[8,96,192]{2,1,0:T(8,128)(2,1)S(1)}, u32[]{:S(2)}, u32[]{:S(2)}) async-start(bf16[8,96,192]{2,1,0:T(8,128)(2,1)} %get-tuple-element.82), calls=%async_computation.7 | async-start | bytes 786432 | tf_op jit(solution)/shard_map/all_to_all | solution.py:1072
  200.5 39.8 %chain_backward.1 = bf16[8,224,256]{2,1,0:T(8,128)(2,1)} custom-call(s32[1]{0:T(128)} %bitcast.22.sequence_ref, bf16[8,128,256]{2,1,0:T(8,128)(2,1)} %copy-done.5, bf16[2,8,128,768]{3,2,1,0:T(8,128)(2,1)} %bitcast.74, bf16[8,64,128]{2,1,0:T(8,128)(2,1)} %all_to_all.40.head_grad_ref, bf16[1024,256]{1,0:T(8,128)(2,1)} %get-tuple-element.65.next_act.now_act, ...), custom_call_target="tpu_custom_call" | custom-call | tf_op jit(solution)/shard_map/chain_backward/pallas_call | solution.py:770
  240.3 6.1 %all-to-all-start.5 = ((bf16[8,224,256]{2,1,0:T(8,128)(2,1)}), bf16[8,224,256]{2,1,0:T(8,128)(2,1)S(1)}, u32[]{:S(2)}, u32[]{:S(2)}) async-start(bf16[8,224,256]{2,1,0:T(8,128)(2,1)} %chain_backward.1), calls=%async_computation.5 | async-start | bytes 1835008 | tf_op jit(solution)/shard_map/all_to_all | solution.py:1072
  247.0 7.3 %reduce-scatter.2.cloned.1.call-done.sums_ref = bf16[96,1536]{1,0:T(8,128)(2,1)} async-done(((bf16[768,1536]{1,0:T(8,128)(2,1)}), bf16[96,1536]{1,0:T(8,128)(2,1)}) %reduce-scatter.2.cloned.1.call-update) | async-done | bytes 294928 | tf_op jit(solution)/shard_map/reduce_scatter | solution.py:1210
  254.3 1.0 copy-done.4
  255.2 1.0 matrix_outputs.1
  256.2 15.5 %all-to-all-done.5.received_ref = bf16[8,224,256]{2,1,0:T(8,128)(2,1)S(1)} async-done(((bf16[8,224,256]{2,1,0:T(8,128)(2,1)}), bf16[8,224,256]{2,1,0:T(8,128)(2,1)S(1)}, u32[]{:S(2)}, u32[]{:S(2)}) %all-to-all-start.5) | async-done | bytes 917536 | tf_op jit(solution)/shard_map/all_to_all | solution.py:1072
  271.7 1.7 tail.1
  273.4 3.6 %all-to-all-start.7 = ((bf16[4,80,768]{2,1,0:T(8,128)(2,1)}), bf16[4,80,768]{2,1,0:T(8,128)(2,1)S(1)}, u32[]{:S(2)}, u32[]{:S(2)}) async-start(bf16[4,80,768]{2,1,0:T(8,128)(2,1)} %get-tuple-element.84), calls=%async_computation.8 | async-start | bytes 983040 | tf_op jit(solution)/shard_map/all_to_all | solution.py:1072
  277.7 0.7 copy.103
  278.4 0.7 copy.104
  279.4 0.7 fusion.18
  280.0 5.4 %all-to-all-done.7 = bf16[4,80,768]{2,1,0:T(8,128)(2,1)S(1)} async-done(((bf16[4,80,768]{2,1,0:T(8,128)(2,1)}), bf16[4,80,768]{2,1,0:T(8,128)(2,1)S(1)}, u32[]{:S(2)}, u32[]{:S(2)}) %all-to-all-start.7) | async-done | bytes 491552 | tf_op jit(solution)/shard_map/all_to_all | solution.py:1072
  286.0 1.1 fusion.9
  287.1 0.7 copy.101
  287.8 0.8 copy.102
  (101 shorter events, 4.8 us)
Async XLA Ops:
  7.2 75.3 %all-gather.6.cloned.1.call-start = ((), (), s32[]{:S(2)}) async-start(), calls=%async_computation.9 | async-start | bytes 3096576 | tf_op jit(solution)/shard_map/all_gather | solution.py:1155
  9.1 8.9 %copy-start.20 = (bf16[24]{0:T(256)(128)(2,1)S(1)}, bf16[24]{0:T(256)(128)(2,1)}, u32[]{:S(2)}) copy-start(bf16[24]{0:T(256)(128)(2,1)} %param.17) | copy-start | bytes 148
  9.1 8.9 %copy-start.21 = (bf16[24]{0:T(256)(128)(2,1)S(1)}, bf16[24]{0:T(256)(128)(2,1)}, u32[]{:S(2)}) copy-start(bf16[24]{0:T(256)(128)(2,1)} %param.16) | copy-start | bytes 148
  9.1 9.0 %copy-start.15 = (bf16[96,3]{0,1:T(4,128)(2,1)S(1)}, bf16[96,3]{0,1:T(4,128)(2,1)}, u32[]{:S(2)}) copy-start(bf16[96,3]{0,1:T(4,128)(2,1)} %param.19) | copy-start | bytes 1732
  9.1 9.1 %copy-start.9 = (bf16[96,3,192]{2,0,1:T(8,128)(2,1)S(1)}, bf16[96,3,192]{2,0,1:T(8,128)(2,1)}, u32[]{:S(2)}) copy-start(bf16[96,3,192]{2,0,1:T(8,128)(2,1)} %param.18) | copy-start | bytes 331780
  10.9 7.7 %copy-start.11 = (bf16[3,32,64]{2,1,0:T(8,128)(2,1)S(1)}, bf16[3,32,64]{2,1,0:T(8,128)(2,1)}, u32[]{:S(2)}) copy-start(bf16[3,32,64]{2,1,0:T(8,128)(2,1)} %param.25) | copy-start | bytes 36868
  10.9 7.7 %copy-start.12 = (bf16[3,64,32]{1,2,0:T(8,128)(2,1)S(1)}, bf16[3,64,32]{1,2,0:T(8,128)(2,1)}, u32[]{:S(2)}) copy-start(bf16[3,64,32]{1,2,0:T(8,128)(2,1)} %param.23) | copy-start | bytes 36868
  11.8 7.0 %copy-start.16 = (bf16[3,8]{1,0:T(4,128)(2,1)S(1)}, bf16[3,8]{1,0:T(4,128)(2,1)}, u32[]{:S(2)}) copy-start(bf16[3,8]{1,0:T(4,128)(2,1)} %param.28) | copy-start | bytes 148
  11.8 7.0 %copy-start.17 = (bf16[3,8]{1,0:T(4,128)(2,1)S(1)}, bf16[3,8]{1,0:T(4,128)(2,1)}, u32[]{:S(2)}) copy-start(bf16[3,8]{1,0:T(4,128)(2,1)} %param.27) | copy-start | bytes 148
  11.8 7.0 %copy-start.18 = (bf16[3,8]{1,0:T(4,128)(2,1)S(1)}, bf16[3,8]{1,0:T(4,128)(2,1)}, u32[]{:S(2)}) copy-start(bf16[3,8]{1,0:T(4,128)(2,1)} %param.26) | copy-start | bytes 148
  11.8 7.0 %copy-start.19 = (bf16[3,32]{1,0:T(4,128)(2,1)S(1)}, bf16[3,32]{1,0:T(4,128)(2,1)}, u32[]{:S(2)}) copy-start(bf16[3,32]{1,0:T(4,128)(2,1)} %param.24) | copy-start | bytes 580
  13.7 41.4 %all-to-all-start = ((bf16[4,128,768]{2,1,0:T(8,128)(2,1)}), bf16[4,128,768]{2,1,0:T(8,128)(2,1)S(1)}, u32[]{:S(2)}, u32[]{:S(2)}) async-start(bf16[4,128,768]{2,1,0:T(8,128)(2,1)} %broadcast_in_dim.4), calls=%async_computation | async-start | bytes 1572864 | tf_op jit(solution)/shard_map/all_to_all | solution.py:1072
  55.1 29.2 %copy-start = (bf16[4,128,768]{2,1,0:T(8,128)(2,1)}, bf16[4,128,768]{2,1,0:T(8,128)(2,1)S(1)}, u32[]{:S(2)}) copy-start(bf16[4,128,768]{2,1,0:T(8,128)(2,1)S(1)} %all-to-all-done.rows_ref) | copy-start | bytes 2359300
  62.8 0.8 copy-start.3
  63.6 24.7 %all-to-all-start.1 = ((bf16[8,128,256]{2,1,0:T(8,128)(2,1)}), bf16[8,128,256]{2,1,0:T(8,128)(2,1)S(1)}, u32[]{:S(2)}, u32[]{:S(2)}) async-start(bf16[8,128,256]{2,1,0:T(8,128)(2,1)} %copy-done.3), calls=%async_computation.1 | async-start | bytes 1048576 | tf_op jit(solution)/shard_map/all_to_all | solution.py:1072
  69.3 73.4 %all-gather.8.cloned.1.call-start = ((), (), s32[]{:S(2)}) async-start(), calls=%async_computation.11 | async-start | bytes 1966080 | tf_op jit(solution)/shard_map/all_gather | solution.py:1177
  88.3 0.8 copy-start.5
  88.3 85.2 %all-gather.10.cloned.1.call-start = ((), (), s32[]{:S(2)}) async-start(), calls=%async_computation.12 | async-start | bytes 3538944 | tf_op jit(solution)/shard_map/all_gather | solution.py:1179
  121.7 13.9 %all-to-all-start.2 = ((bf16[8,64,128]{2,1,0:T(8,128)(2,1)}), bf16[8,64,128]{2,1,0:T(8,128)(2,1)S(1)}, u32[]{:S(2)}, u32[]{:S(2)}) async-start(bf16[8,64,128]{2,1,0:T(8,128)(2,1)} %get-tuple-element.57), calls=%async_computation.2 | async-start | bytes 262144 | tf_op jit(solution)/shard_map/all_to_all | solution.py:1072
  125.4 128.9 %reduce-scatter.2.cloned.1.call-start = ((), (), s32[]{:S(2)}) async-start(), calls=%async_computation.10 | async-start | bytes 2654208 | tf_op jit(solution)/shard_map/reduce_scatter | solution.py:1210
  153.1 21.6 %copy-start.7 = (bf16[32,2,768]{2,1,0:T(2,128)(2,1)S(1)}, bf16[32,2,768]{2,1,0:T(2,128)(2,1)}, u32[]{:S(2)}) copy-start(bf16[32,2,768]{2,1,0:T(2,128)(2,1)} %param.29) | copy-start | bytes 294916
  153.1 29.1 %copy-start.1 = (bf16[768,192]{1,0:T(8,128)(2,1)S(1)}, bf16[768,192]{1,0:T(8,128)(2,1)}, u32[]{:S(2)}) copy-start(bf16[768,192]{1,0:T(8,128)(2,1)} %slice.97.out_ref) | copy-start | bytes 884740
  153.1 20.3 %all-to-all-start.3 = ((bf16[4,4,32,768]{3,2,1,0:T(8,128)(2,1)}), bf16[4,4,32,768]{3,2,1,0:T(8,128)(2,1)S(1)}, u32[]{:S(2)}, u32[]{:S(2)}) async-start(bf16[4,4,32,768]{3,2,1,0:T(8,128)(2,1)} %get-tuple-element.60), calls=%async_computation.3 | async-start | bytes 1572864 | tf_op jit(solution)/shard_map/all_to_all | solution.py:1072
  174.7 65.6 %copy-start.13 = (f32[2,32]{1,0:T(2,128)}, f32[2,32]{1,0:T(2,128)S(1)}, u32[]{:S(2)}) copy-start(f32[2,32]{1,0:T(2,128)S(1)} %get-tuple-element.167) | copy-start | bytes 772
  196.8 43.5 %all-to-all-start.6 = ((bf16[8,96,192]{2,1,0:T(8,128)(2,1)}), bf16[8,96,192]{2,1,0:T(8,128)(2,1)S(1)}, u32[]{:S(2)}, u32[]{:S(2)}) async-start(bf16[8,96,192]{2,1,0:T(8,128)(2,1)} %get-tuple-element.82), calls=%async_computation.7 | async-start | bytes 786432 | tf_op jit(solution)/shard_map/all_to_all | solution.py:1072
  200.5 45.9 %copy-start.6 = (bf16[32,2,768]{2,1,0:T(2,128)(2,1)S(1)}, bf16[32,2,768]{2,1,0:T(2,128)(2,1)}, u32[]{:S(2)}) copy-start(bf16[32,2,768]{2,1,0:T(2,128)(2,1)} %param.15) | copy-start | bytes 294916
  240.3 14.0 %copy-start.2 = (bf16[96,1728]{1,0:T(8,128)(2,1)S(1)}, bf16[96,1728]{1,0:T(8,128)(2,1)}, u32[]{:S(2)}) copy-start(bf16[96,1728]{1,0:T(8,128)(2,1)} %pad_maximum_fusion.weights_ref) | copy-start | bytes 995332
  240.3 31.4 %all-to-all-start.5 = ((bf16[8,224,256]{2,1,0:T(8,128)(2,1)}), bf16[8,224,256]{2,1,0:T(8,128)(2,1)S(1)}, u32[]{:S(2)}, u32[]{:S(2)}) async-start(bf16[8,224,256]{2,1,0:T(8,128)(2,1)} %chain_backward.1), calls=%async_computation.5 | async-start | bytes 1835008 | tf_op jit(solution)/shard_map/all_to_all | solution.py:1072
  254.3 1.0 copy-start.4
  273.4 12.6 %copy-start.8 = (bf16[32,2,768]{2,1,0:T(2,128)(2,1)S(1)}, bf16[32,2,768]{2,1,0:T(2,128)(2,1)}, u32[]{:S(2)}) copy-start(bf16[32,2,768]{2,1,0:T(2,128)(2,1)} %param.29) | copy-start | bytes 294916
  273.4 12.6 %copy-start.14 = (f32[2,32]{1,0:T(2,128)S(1)}, f32[2,32]{1,0:T(2,128)}, u32[]{:S(2)}) copy-start(f32[2,32]{1,0:T(2,128)} %copy-done.13) | copy-start | bytes 772
  273.4 12.1 %all-to-all-start.7 = ((bf16[4,80,768]{2,1,0:T(8,128)(2,1)}), bf16[4,80,768]{2,1,0:T(8,128)(2,1)S(1)}, u32[]{:S(2)}, u32[]{:S(2)}) async-start(bf16[4,80,768]{2,1,0:T(8,128)(2,1)} %get-tuple-element.84), calls=%async_computation.8 | async-start | bytes 983040 | tf_op jit(solution)/shard_map/all_to_all | solution.py:1072
  279.4 9.9 %copy-start.10 = (f32[3,128]{1,0:T(4,128)}, f32[3,128]{1,0:T(4,128)S(1)}, u32[]{:S(2)}) copy-start(f32[3,128]{1,0:T(4,128)S(1)} %slice_reduce_fusion) | copy-start | bytes 4612
Sparse Core Ops, SparseCore 0:
  11.0 71.5 all-gather.5
  88.4 19.1 all-gather.7
  110.4 62.9 all-gather.9
  176.8 77.4 reduce-scatter.1

commit v4 on v3

--- a/solution.py
+++ b/solution.py
@@ -11,11 +11,14 @@
 HEAD_DIM = 64
 INNER = 256
 MINI = 16
+SEQS = 2
 LANES = 256
 RATE_LANE = 3 * HEAD_DIM
 VECTOR_LANE = RATE_LANE + 2
 MATRIX_LANE = LANES - 32
 VMEM_BYTES = 56 * 1024 * 1024
+DP = ("outer", "inner")
+CHAIN_FLOPS = 20_000_000_000
 GLUE_BYTES = 32 * 1024 * 1024
 
 epsilon = 1e-05
@@ -276,14 +279,18 @@
                 own_base + own_gain * normal - scaled_mean - normal * along_half[:, :HEAD_DIM]
             )
             back_low = back_res.astype(bf16)
-            back_act = inverse * base_act + square_inverse * (
-                parts[MINI:] - along_wide * parts[:MINI]
-            )
-            grad = (back_act * slope).astype(bf16)
+            with_base = inverse * slope * base_act
+            with_part = square_inverse * slope
+            with_res = with_part * along_wide
+            grad_full = with_base + (with_part * parts[MINI:] - with_res * parts[:MINI])
+            grad = grad_full.astype(bf16)
             known_ref[at, :] = grad
             state = state - dot_tn(back_low, act)
             state_b = state_b - jnp.sum(back_res, axis=0, keepdims=True)
             slope_ref[at, :] = slope
+            back_act = inverse * base_act + square_inverse * (
+                parts[MINI:] - along_wide * parts[:MINI]
+            )
             curve_ref[at, :] = back_act * density * (2.0 - pre * pre)
             act_ref[at, :] = act
             grad_pre_ref[at, :] = grad
@@ -591,14 +598,14 @@
                 - own_normal * tilt[:, :HEAD_DIM]
             )
             key_res_low = key_res_grad.astype(bf16)
-            from_res = (
-                main
-                - alpha * sides[MINI : 2 * MINI]
-                - beta * sides[2 * MINI :]
-                - jnp.concatenate([tilt, tilt], axis=1) * sides[:MINI]
+            from_sides = (
+                alpha * sides[MINI : 2 * MINI]
+                + beta * sides[2 * MINI :]
+                + jnp.concatenate([tilt, tilt], axis=1) * sides[:MINI]
             )
-            factor = jnp.concatenate([square_inverse, square_inverse], axis=1)
-            pre_grad = (act_base + factor * from_res) * slope + grad * now_curve[at, :]
+            factor = jnp.concatenate([square_inverse, square_inverse], axis=1) * slope
+            known = act_base * slope + grad * now_curve[at, :] - factor * from_sides
+            pre_grad = known + factor * main
             known_ref[at, :] = pre_grad.astype(bf16)
             state = state + dot_tn(
                 jnp.concatenate([key_res_low, own_back], axis=0),
@@ -732,6 +739,9 @@
         compiler_params=pltpu.CompilerParams(
             dimension_semantics=("arbitrary",), vmem_limit_bytes=VMEM_BYTES
         ),
+        cost_estimate=pl.CostEstimate(
+            flops=CHAIN_FLOPS, transcendentals=0, bytes_accessed=16 * length * INNER
+        ),
         name="chain_forward",
     )(packed)
 
@@ -755,7 +765,8 @@
         return pl.BlockSpec(shape, index_map)
 
     def rows_map(turn, chosen):
-        return (chosen[0], jnp.clip(blocks + 1 - turn, 0, blocks - 1), 0, 0)
+        place = jnp.clip(blocks + 1 - turn, 0, blocks - 1)
+        return (place // SEQS, (place + chosen[0]) % SEQS, 0, 0)
 
     state = (HEAD_DIM, INNER)
     carried = [
@@ -812,6 +823,9 @@
         out_shape=jax.ShapeDtypeStruct((blocks, chunk + shard, LANES), bf16),
         compiler_params=pltpu.CompilerParams(
             dimension_semantics=("arbitrary",), vmem_limit_bytes=VMEM_BYTES
+        ),
+        cost_estimate=pl.CostEstimate(
+            flops=CHAIN_FLOPS, transcendentals=0, bytes_accessed=16 * blocks * chunk * INNER
         ),
         name="chain_backward",
     )(
@@ -1077,8 +1091,8 @@
     return exchange(jnp.broadcast_to(values[None], (count,) + values.shape), axis)
 
 
-def ordered(first, then):
-    return lax.optimization_barrier((first, then))
+def ordered(*values):
+    return lax.optimization_barrier(values)
 
 
 def inner_block(matrix_one, matrix_two, vectors, rows):
@@ -1114,7 +1128,7 @@
     norm_bias_inner,
     cotangent,
 ):
-    device_count = lax.axis_size("dp")
+    device_count = lax.axis_size(DP)
     tensor_count = lax.axis_size("tensor")
     local_rows, seq_count, width = tokens.shape
     row_count = local_rows * seq_count
@@ -1127,10 +1141,10 @@
     chain_count = seq_count * head_count
     inner_part = w_one.shape[2]
     feature_part = b_two.shape[1]
-    assert chain_count <= device_count
+    assert chain_count <= device_count and seq_count == SEQS
     assert chunk == 2 * HEAD_DIM and inner_part <= 32 and part <= shard
     rank = lax.axis_index("tensor")
-    place = lax.axis_index("dp")
+    place = lax.axis_index(DP)
 
     own_tokens = tokens.transpose(1, 0, 2).reshape(row_count, width)
     own_cot = cotangent.transpose(1, 0, 2).reshape(row_count, width)
@@ -1140,7 +1154,8 @@
     qkv_pack = jnp.concatenate(
         [head_columns.reshape(shard, 3 * local_width), w_rate, gain_columns], axis=1
     )
-    qkv_full = lax.all_gather(qkv_pack, "dp", axis=0, tiled=True)
+    qkv_half = lax.all_gather(qkv_pack, "inner", axis=0, tiled=True)
+    qkv_full = lax.all_gather(qkv_half, "outer", axis=0, tiled=True)
     qkv_full, row_full = ordered(qkv_full, row_full)
     some_gains = qkv_full[:, 3 * local_width + head_count :]
     some_gains = some_gains.reshape(device_count, shard, 2)[:, :part].transpose(2, 0, 1)
@@ -1152,7 +1167,7 @@
     ffn_pack = jnp.concatenate(
         [w_gate_up.reshape(shard, 2 * ff_local), w_down.T, w_out.T], axis=1
     )
-    ffn_full = lax.all_gather(ffn_pack, "dp", axis=0, tiled=True)
+    ffn_full = lax.all_gather(ffn_pack, DP, axis=0, tiled=True)
     own_out = ffn_full[:, 3 * ff_local :]
 
     inner = inner_block(
@@ -1172,15 +1187,20 @@
             shape((head_count, width, LANES), bf16),
         ),
     )
-    chain_in = exchange(packed, "dp")
-    chain_in, own_out = ordered(chain_in, own_out)
+    chain_in = exchange(packed, DP)
+
+    side = lax.axis_index("inner")
+    kept = lax.dynamic_index_in_dim(normed_attn, side, 0)
+    given = lax.dynamic_index_in_dim(normed_attn, 1 - side, 0)
+    taken = lax.ppermute(given, "inner", [(0, 1), (1, 0)])
+    pair = jnp.concatenate([kept, taken], axis=0)
+    chain_in, own_out, pair = ordered(chain_in, own_out, pair)
+    chain_rows = lax.all_gather(pair, "outer", axis=0)
     out_full = lax.all_gather(own_out, "tensor", axis=0)
-
-    normed_full = lax.all_gather(normed_attn, "dp", axis=1, tiled=False)
 
     forward_out = chain_forward(chain_in, inner_part, feature_part)
     saved = forward_out[1:]
-    head_local = exchange(forward_out[0], "dp")[:chain_count]
+    head_local = exchange(forward_out[0], DP)[:chain_count]
     head_local = head_local.reshape(head_count, seq_count, HEAD_DIM, chunk)
     head_rows = lax.all_gather(head_local, "tensor", axis=0, tiled=False)
 
@@ -1207,8 +1227,8 @@
         (shape((width, 3 * ff_local), bf16),),
         VMEM_BYTES,
     )
-    ffn_grad_sums = lax.psum_scatter(ffn_grads, "dp", scatter_dimension=0, tiled=True)
-    ffn_sums, normed_full = ordered(ffn_sums, normed_full)
+    ffn_grad_sums = lax.psum_scatter(ffn_grads, DP, scatter_dimension=0, tiled=True)
+    ffn_sums, chain_rows, _ = ordered(ffn_sums, chain_rows, ffn_grads)
     ffn_sums = ffn_sums.astype(f32).sum(axis=0)
     own_mixed = lax.dynamic_index_in_dim(mixed, rank, 0, keepdims=False)
     own_normal, own_inverse = layer_norm_parts(own_mixed)
@@ -1226,14 +1246,14 @@
             shape((device_count, shard, local_width), bf16),
         ),
     )
-    head_grad = exchange(back_head, "dp")
-    out_sums = exchange(out_terms, "dp")
-
-    chosen = jnp.reshape(place % seq_count, (1,)).astype(jnp.int32)
+    head_grad = exchange(back_head, DP)
+    out_sums = exchange(out_terms, DP)
+
+    chosen = jnp.reshape(side, (1,)).astype(jnp.int32)
     back_packed = chain_backward(
-        chain_in, normed_full, chosen, head_grad, saved, inner_part, feature_part
-    )
-    received = exchange(back_packed, "dp")
+        chain_in, chain_rows, chosen, head_grad, saved, inner_part, feature_part
+    )
+    received = exchange(back_packed, DP)
     grad_gate_up, grad_down, grad_out, gain_two = whole_call(
         matrix_output_kernel,
         "matrix_outputs",
@@ -1299,27 +1319,31 @@
 
 
 def solution(mesh):
-    rows = P(("dp", "tensor"), None, None)
-    gains = P(("dp", "tensor"))
+    devices = mesh.devices
+    dp_count, tensor_count = mesh.shape["dp"], mesh.shape["tensor"]
+    devices = devices.reshape(dp_count // SEQS, SEQS, tensor_count)
+    split = jax.sharding.Mesh(devices, DP + ("tensor",))
+    rows = P(DP + ("tensor",), None, None)
+    gains = P(DP + ("tensor",))
     placed = (
         rows,
         gains,
         gains,
-        P("dp", None, "tensor"),
-        P("dp", "tensor"),
-        P("tensor", "dp"),
-        P("dp", None, "tensor"),
-        P("tensor", "dp"),
-        P("tensor", None, "dp"),
-        P("tensor", "dp"),
-        P("tensor", "dp", None),
-        P("tensor", "dp"),
-        P("tensor", "dp"),
-        P("tensor", "dp"),
+        P(DP, None, "tensor"),
+        P(DP, "tensor"),
+        P("tensor", DP),
+        P(DP, None, "tensor"),
+        P("tensor", DP),
+        P("tensor", None, DP),
+        P("tensor", DP),
+        P("tensor", DP, None),
+        P("tensor", DP),
+        P("tensor", DP),
+        P("tensor", DP),
     )
     return jax.shard_map(
         local,
-        mesh=mesh,
+        mesh=split,
         in_specs=placed + (rows,),
         out_specs=(rows,) + placed,
         check_vma=False,

time: 297 us -> 284 us (0.956)
  waiting for transfers between devices: 70 us -> 55.7 us
    all_gather x2, waiting for transfers between devices: 27.6 us -> 0.01 us  [the longest x1 0.01 us: local(): ffn_full = lax.all_gather(ffn_pack, DP, axis=0, tiled=True)]
    all_to_all x7, waiting for transfers between devices: 34.4 us -> 45.9 us  [exchange(): return lax.all_to_all(values, axis, 0, 0, tiled=False)]
    ppermute x0 -> x1, waiting for transfers between devices: none -> 9.03 us  [local(): taken = lax.ppermute(given, 'inner', [(0, 1), (1, 0)])]
    reduce_scatter x1, waiting for transfers between devices: 7.27 us -> 0.02 us  [local(): lax.psum_scatter(ffn_grads, DP, scatter_dimension=0, tiled=True)]
    unnamed x54 -> x68, local copies, waits for them, and re-layouts: 8.87 us -> 7.71 us
    all_gather x1 -> x2, blocking collectives: 35.9 us -> 36.8 us  [the longest x1 28.7 us: local(): qkv_full = lax.all_gather(qkv_half, 'outer', axis=0, tiled=True)]
  transfers between devices with their start and end apart: 11 -> 12, of which waited for: 7 -> 6; matrix products, arithmetic and copies ran while one was open for 5% -> 5% of each run, Pallas kernels for 30% -> 31%
where the time goes in v4:
time: 284 us; the launch traced here: 283 us
  Pallas kernels  88.7 us (31%)
  blocking collectives  68.2 us (24%)
  waiting for transfers between devices  55.7 us (20%)
  starting transfers between devices  31.6 us (11%)
  local copies, waits for them, and re-layouts  15.3 us (5%)
  between operations  14.3 us (5%)
  other arithmetic  9.07 us (3%)
    all_to_all x7, waiting for transfers between devices, exchange(): return lax.all_to_all(values, axis, 0, 0, tiled=False)  45.9 us
    pallas_call x1, Pallas kernels, chain_backward(): pl.pallas_call(functools.partial(backward_kernel, inner_part, feature_par...  39.9 us
    pallas_call x1, Pallas kernels, chain_forward(): pl.pallas_call(functools.partial(forward_kernel, inner_part, feature_part...  32.6 us
    all_to_all x7, starting transfers between devices, exchange(): return lax.all_to_all(values, axis, 0, 0, tiled=False)  29.4 us
    all_gather x1, blocking collectives, local(): qkv_full = lax.all_gather(qkv_half, 'outer', axis=0, tiled=True)  28.7 us
    pallas_call x6, Pallas kernels, whole_call(): pl.pallas_call(kernel, in_specs=[spec(operand.shape) for operand in opera...  16.1 us
    all_to_all x1, blocking collectives, exchange(): return lax.all_to_all(values, axis, 0, 0, tiled=False)  13.3 us
    ppermute x1, waiting for transfers between devices, local(): taken = lax.ppermute(given, 'inner', [(0, 1), (1, 0)])  9.03 us
  transfers between devices with their start and end apart: 12, of which 6 were waited for; matrix products, arithmetic and copies ran while one was open for 5% of the time, Pallas kernels for 31%

profile of v4, /device:TPU:0, one launch (start us, length us, event | category | flops | bytes accessed | tf_op | source)
XLA Modules:
  0.0 282.9 jit_solution(5740274974552731974)
XLA Ops:
  7.2 0.9 copy.96
  8.2 1.0 copy.106
  9.1 1.7 pad_maximum_fusion.1.weights_ref
  11.0 0.9 broadcast_in_dim.4
  11.9 4.4 %all-to-all-start = ((bf16[4,128,768]{2,1,0:T(8,128)(2,1)}), bf16[4,128,768]{2,1,0:T(8,128)(2,1)S(1)}, u32[]{:S(2)}, u32[]{:S(2)}) async-start(bf16[4,128,768]{2,1,0:T(8,128)(2,1)} %broadcast_in_dim.4), calls=%async_computation | async-start | bytes 1572864 | tf_op jit(solution)/shard_map/all_to_all | solution.py:1086
  17.5 8.1 %all_gather.30 = bf16[192,581]{1,0:T(8,128)(2,1)S(1)} all-gather(bf16[96,581]{1,0:T(8,128)(2,1)S(1)} %fusion.14), channel_id=1, replica_groups=mesh['outer'=4,'inner'=2,'tensor'=4] {'inner'}, dimensions={0}, use_global_device_ids=true | all-gather | bytes 334656 | tf_op jit(solution)/shard_map/all_gather | solution.py:1157
  25.7 28.7 %all_gather.31.weights_ref = bf16[768,581]{1,0:T(8,128)(2,1)S(1)} all-gather(bf16[192,581]{1,0:T(8,128)(2,1)S(1)} %all_gather.30), channel_id=1, replica_groups=mesh['outer'=4,'inner'=2,'tensor'=4] {'outer'}, dimensions={0}, use_global_device_ids=true | all-gather | bytes 1115520 | tf_op jit(solution)/shard_map/all_gather | solution.py:1158
  54.6 5.1 %all_gather.32 = bf16[4,2,192]{2,1,0:T(2,128)(2,1)S(1)} all-gather(bf16[1,2,192]{2,1,0:T(2,128)(2,1)S(1)} %copy.105), channel_id=1, replica_groups=mesh['outer'=4,'inner'=2,'tensor'=4] {'tensor'}, dimensions={0}, use_global_device_ids=true | all-gather | bytes 3840 | tf_op jit(solution)/shard_map/all_gather | solution.py:1162
  61.1 1.8 projections.1
  62.9 0.8 copy-done.3
  63.7 4.7 %all-to-all-start.1 = ((bf16[8,128,256]{2,1,0:T(8,128)(2,1)}), bf16[8,128,256]{2,1,0:T(8,128)(2,1)S(1)}, u32[]{:S(2)}, u32[]{:S(2)}) async-start(bf16[8,128,256]{2,1,0:T(8,128)(2,1)} %copy-done.3), calls=%async_computation.1 | async-start | bytes 1048576 | tf_op jit(solution)/shard_map/all_to_all | solution.py:1086
  68.5 2.0 collective-permute-start
  70.5 9.0 %collective-permute-done = bf16[1,128,768]{2,1,0:T(8,128)(2,1)S(1)} collective-permute-done((bf16[1,128,768]{2,1,0:T(8,128)(2,1)S(1)}, bf16[1,128,768]{2,1,0:T(8,128)(2,1)S(1)}, u32[]{:S(2)}, u32[]{:S(2)}) %collective-permute-start) | collective-permute-done | bytes 196640 | tf_op jit(solution)/shard_map/ppermute | solution.py:1195
  79.6 0.8 pad_maximum_fusion
  80.3 1.8 slice.97.out_ref
  82.1 4.8 %all-to-all-done.1.packed_ref = bf16[8,128,256]{2,1,0:T(8,128)(2,1)S(1)} async-done(((bf16[8,128,256]{2,1,0:T(8,128)(2,1)}), bf16[8,128,256]{2,1,0:T(8,128)(2,1)S(1)}, u32[]{:S(2)}, u32[]{:S(2)}) %all-to-all-start.1) | async-done | bytes 524320 | tf_op jit(solution)/shard_map/all_to_all | solution.py:1086
  87.0 0.7 all-gather.10.cloned.1.call-update
  87.7 32.6 %chain_forward.1 = (bf16[8,64,128]{2,1,0:T(8,128)(2,1)}, bf16[1024,256]{1,0:T(8,128)(2,1)}, bf16[1024,256]{1,0:T(8,128)(2,1)}, f32[1024,256]{1,0:T(8,128)}, f32[...) custom-call(bf16[8,128,256]{2,1,0:T(8,128)(2,1)} %copy-done.10), custom_call_target="tpu_custom_call" | custom-call | flops 20000000000 | bytes 4194304 | tf_op jit(solution)/shard_map/chain_forward/pallas_call | solution.py:696
  120.3 3.4 %all-to-all-start.2 = ((bf16[8,64,128]{2,1,0:T(8,128)(2,1)}), bf16[8,64,128]{2,1,0:T(8,128)(2,1)S(1)}, u32[]{:S(2)}, u32[]{:S(2)}) async-start(bf16[8,64,128]{2,1,0:T(8,128)(2,1)} %get-tuple-element.59), calls=%async_computation.2 | async-start | bytes 262144 | tf_op jit(solution)/shard_map/all_to_all | solution.py:1086
  123.7 0.7 slice.79.gain_ref
  124.4 9.8 %all-to-all-done.2 = bf16[8,64,128]{2,1,0:T(8,128)(2,1)S(1)} async-done(((bf16[8,64,128]{2,1,0:T(8,128)(2,1)}), bf16[8,64,128]{2,1,0:T(8,128)(2,1)S(1)}, u32[]{:S(2)}, u32[]{:S(2)}) %all-to-all-start.2) | async-done | bytes 131104 | tf_op jit(solution)/shard_map/all_to_all | solution.py:1086
  134.2 6.9 %all_gather.34.heads_ref = bf16[4,3,2,64,128]{4,3,2,1,0:T(8,128)(2,1)} all-gather(bf16[1,3,2,64,128]{4,3,2,1,0:T(8,128)(2,1)S(1)} %bitcast.72), channel_id=1, replica_groups=mesh['outer'=4,'inner'=2,'tensor'=4] {'tensor'}, dimensions={0}, use_global_device_ids=true | all-gather | bytes 491520 | tf_op jit(solution)/shard_map/all_gather | solution.py:1205
  141.1 6.7 %feed_forward.1 = (bf16[4,4,32,768]{3,2,1,0:T(8,128)(2,1)}, f32[4,2,32,768]{3,2,1,0:T(8,128)}, bf16[256,768]{1,0:T(8,128)(2,1)}, bf16[256,1024]{1,0:T(8,128)(2,1...) custom-call(bf16[4,3,2,64,128]{4,3,2,1,0:T(8,128)(2,1)} %all_gather.34.heads_ref, bf16[4,128,768]{2,1,0:T(8,128)(2,1)} %copy-done, ...), custom_call_target="tpu_custom_call" | custom-call | tf_op jit(solution)/shard_map/feed_forward/pallas_call | solution.py:1071
  147.9 3.5 %all-to-all-start.3 = ((bf16[4,4,32,768]{3,2,1,0:T(8,128)(2,1)}), bf16[4,4,32,768]{3,2,1,0:T(8,128)(2,1)S(1)}, u32[]{:S(2)}, u32[]{:S(2)}) async-start(bf16[4,4,32,768]{3,2,1,0:T(8,128)(2,1)} %get-tuple-element.62), calls=%async_computation.3 | async-start | bytes 1572864 | tf_op jit(solution)/shard_map/all_to_all | solution.py:1086
  151.5 3.6 %feed_forward_grads.1 = bf16[768,1536]{1,0:T(8,128)(2,1)} custom-call(bf16[256,768]{1,0:T(8,128)(2,1)} %get-tuple-element.64.normed_ref, bf16[256,1024]{1,0:T(8,128)(2,1)} %get-tuple-element.65.back_ref, bf16[256,512]{1,0:T(8,128)(2,1)} %get-tuple-element.66.swiglu_ref, bf16[256,768]{1,0:T(8,128)(2,1)} %get-tuple-element.67.cot_ref), custom_call_target="tpu_custom_call" | custom-call | tf_op jit(solution)/shard_map/feed_forward_grads/pallas_call | solution.py:1071
  155.2 1.1 dynamic-slice_reduce_fusion
  156.3 1.1 multiply_reduce_fusion.2
  157.4 5.6 %all-to-all-done.3 = bf16[4,4,32,768]{3,2,1,0:T(8,128)(2,1)S(1)} async-done(((bf16[4,4,32,768]{3,2,1,0:T(8,128)(2,1)}), bf16[4,4,32,768]{3,2,1,0:T(8,128)(2,1)S(1)}, u32[]{:S(2)}, u32[]{:S(2)}) %all-to-all-start.3) | async-done | bytes 786464 | tf_op jit(solution)/shard_map/all_to_all | solution.py:1086
  163.1 1.1 fusion.13
  164.2 1.1 fusion.16
  165.3 6.1 %all_gather.39.grads_ref = bf16[2,128,768]{2,1,0:T(8,128)(2,1)S(1)} all-gather(bf16[2,32,768]{2,1,0:T(8,128)(2,1)S(1)} %fusion.16), channel_id=1, replica_groups=mesh['outer'=4,'inner'=2,'tensor'=4] {'tensor'}, dimensions={1}, use_global_device_ids=true | all-gather | bytes 491520 | tf_op jit(solution)/shard_map/all_gather | solution.py:1239
  171.4 1.3 head_back.1
  172.7 13.3 %all_to_all.40.head_grad_ref = bf16[8,64,128]{2,1,0:T(8,128)(2,1)} all-to-all(bf16[8,64,128]{2,1,0:T(8,128)(2,1)S(1)} %get-tuple-element.70), channel_id=1, replica_groups=mesh['outer'=4,'inner'=2,'tensor'=4] {'outer','inner'}, dimensions={0} | all-to-all | bytes 262144 | tf_op jit(solution)/shard_map/all_to_all | solution.py:1086
  186.1 3.7 %all-to-all-start.6 = ((bf16[8,96,192]{2,1,0:T(8,128)(2,1)}), bf16[8,96,192]{2,1,0:T(8,128)(2,1)S(1)}, u32[]{:S(2)}, u32[]{:S(2)}) async-start(bf16[8,96,192]{2,1,0:T(8,128)(2,1)} %get-tuple-element.84), calls=%async_computation.7 | async-start | bytes 786432 | tf_op jit(solution)/shard_map/all_to_all | solution.py:1086
  189.8 39.9 %chain_backward.1 = bf16[8,224,256]{2,1,0:T(8,128)(2,1)} custom-call(s32[1]{0:T(128)} %bitcast.22.sequence_ref, bf16[8,128,256]{2,1,0:T(8,128)(2,1)} %copy-done.10, bf16[4,2,128,768]{3,2,1,0:T(8,128)(2,1)} %bitcast.90, bf16[8,64,128]{2,1,0:T(8,128)(2,1)} %all_to_all.40.head_grad_ref, bf16[1024,256]{1,0:T(8,128)(2,1)} %get-tuple-element.71.next_act.now_act, ...), custom_call_target="tpu_custom_call" | custom-call | flops 20000000000 | bytes 4194304 | tf_op jit(solution)/shard_map/chain_backward/pallas_call | solution.py:781
  229.8 6.1 %all-to-all-start.5 = ((bf16[8,224,256]{2,1,0:T(8,128)(2,1)}), bf16[8,224,256]{2,1,0:T(8,128)(2,1)S(1)}, u32[]{:S(2)}, u32[]{:S(2)}) async-start(bf16[8,224,256]{2,1,0:T(8,128)(2,1)} %chain_backward.1), calls=%async_computation.5 | async-start | bytes 1835008 | tf_op jit(solution)/shard_map/all_to_all | solution.py:1086
  236.6 1.0 copy-done.4
  237.6 1.0 matrix_outputs.1
  238.6 20.3 %all-to-all-done.5.received_ref = bf16[8,224,256]{2,1,0:T(8,128)(2,1)S(1)} async-done(((bf16[8,224,256]{2,1,0:T(8,128)(2,1)}), bf16[8,224,256]{2,1,0:T(8,128)(2,1)S(1)}, u32[]{:S(2)}, u32[]{:S(2)}) %all-to-all-start.5) | async-done | bytes 917536 | tf_op jit(solution)/shard_map/all_to_all | solution.py:1086
  258.8 1.7 tail.1
  260.5 3.6 %all-to-all-start.7 = ((bf16[4,80,768]{2,1,0:T(8,128)(2,1)}), bf16[4,80,768]{2,1,0:T(8,128)(2,1)S(1)}, u32[]{:S(2)}, u32[]{:S(2)}) async-start(bf16[4,80,768]{2,1,0:T(8,128)(2,1)} %get-tuple-element.86), calls=%async_computation.8 | async-start | bytes 983040 | tf_op jit(solution)/shard_map/all_to_all | solution.py:1086
  264.8 0.7 copy.103
  265.5 0.7 copy.104
  266.5 0.7 fusion.18
  267.1 5.4 %all-to-all-done.7 = bf16[4,80,768]{2,1,0:T(8,128)(2,1)S(1)} async-done(((bf16[4,80,768]{2,1,0:T(8,128)(2,1)}), bf16[4,80,768]{2,1,0:T(8,128)(2,1)S(1)}, u32[]{:S(2)}, u32[]{:S(2)}) %all-to-all-start.7) | async-done | bytes 491552 | tf_op jit(solution)/shard_map/all_to_all | solution.py:1086
  273.1 1.1 fusion.9
  274.2 0.7 copy.101
  274.9 0.8 copy.102
  (120 shorter events, 6.0 us)
Async XLA Ops:
  7.2 3.7 %copy-start.7 = (bf16[32,2,768]{2,1,0:T(2,128)(2,1)S(1)}, bf16[32,2,768]{2,1,0:T(2,128)(2,1)}, u32[]{:S(2)}) copy-start(bf16[32,2,768]{2,1,0:T(2,128)(2,1)} %param.29) | copy-start | bytes 294916
  7.2 3.7 %copy-start.5 = (bf16[32,2,768]{2,1,0:T(2,128)(2,1)S(1)}, bf16[32,2,768]{2,1,0:T(2,128)(2,1)}, u32[]{:S(2)}) copy-start(bf16[32,2,768]{2,1,0:T(2,128)(2,1)} %param.15) | copy-start | bytes 294916
  7.2 73.1 %all-gather.6.cloned.1.call-start = ((), (), s32[]{:S(2)}) async-start(), calls=%async_computation.9 | async-start | bytes 3096576 | tf_op jit(solution)/shard_map/all_gather | solution.py:1170
  10.9 5.4 %copy-start.27 = (bf16[24]{0:T(256)(128)(2,1)S(1)}, bf16[24]{0:T(256)(128)(2,1)}, u32[]{:S(2)}) copy-start(bf16[24]{0:T(256)(128)(2,1)} %param.17) | copy-start | bytes 148
  10.9 5.4 %copy-start.28 = (bf16[24]{0:T(256)(128)(2,1)S(1)}, bf16[24]{0:T(256)(128)(2,1)}, u32[]{:S(2)}) copy-start(bf16[24]{0:T(256)(128)(2,1)} %param.16) | copy-start | bytes 148
  10.9 5.5 %copy-start.22 = (bf16[96,3]{0,1:T(4,128)(2,1)S(1)}, bf16[96,3]{0,1:T(4,128)(2,1)}, u32[]{:S(2)}) copy-start(bf16[96,3]{0,1:T(4,128)(2,1)} %param.19) | copy-start | bytes 1732
  10.9 5.6 %copy-start.15 = (bf16[96,3,192]{2,0,1:T(8,128)(2,1)S(1)}, bf16[96,3,192]{2,0,1:T(8,128)(2,1)}, u32[]{:S(2)}) copy-start(bf16[96,3,192]{2,0,1:T(8,128)(2,1)} %param.18) | copy-start | bytes 331780
  11.0 5.9 %copy-start.18 = (bf16[3,32,64]{2,1,0:T(8,128)(2,1)S(1)}, bf16[3,32,64]{2,1,0:T(8,128)(2,1)}, u32[]{:S(2)}) copy-start(bf16[3,32,64]{2,1,0:T(8,128)(2,1)} %param.25) | copy-start | bytes 36868
  11.0 5.9 %copy-start.19 = (bf16[3,64,32]{1,2,0:T(8,128)(2,1)S(1)}, bf16[3,64,32]{1,2,0:T(8,128)(2,1)}, u32[]{:S(2)}) copy-start(bf16[3,64,32]{1,2,0:T(8,128)(2,1)} %param.23) | copy-start | bytes 36868
  11.9 5.2 %copy-start.23 = (bf16[3,8]{1,0:T(4,128)(2,1)S(1)}, bf16[3,8]{1,0:T(4,128)(2,1)}, u32[]{:S(2)}) copy-start(bf16[3,8]{1,0:T(4,128)(2,1)} %param.28) | copy-start | bytes 148
  11.9 5.2 %copy-start.24 = (bf16[3,8]{1,0:T(4,128)(2,1)S(1)}, bf16[3,8]{1,0:T(4,128)(2,1)}, u32[]{:S(2)}) copy-start(bf16[3,8]{1,0:T(4,128)(2,1)} %param.27) | copy-start | bytes 148
  11.9 5.2 %copy-start.25 = (bf16[3,8]{1,0:T(4,128)(2,1)S(1)}, bf16[3,8]{1,0:T(4,128)(2,1)}, u32[]{:S(2)}) copy-start(bf16[3,8]{1,0:T(4,128)(2,1)} %param.26) | copy-start | bytes 148
  11.9 5.2 %copy-start.26 = (bf16[3,32]{1,0:T(4,128)(2,1)S(1)}, bf16[3,32]{1,0:T(4,128)(2,1)}, u32[]{:S(2)}) copy-start(bf16[3,32]{1,0:T(4,128)(2,1)} %param.24) | copy-start | bytes 580
  11.9 42.4 %all-to-all-start = ((bf16[4,128,768]{2,1,0:T(8,128)(2,1)}), bf16[4,128,768]{2,1,0:T(8,128)(2,1)S(1)}, u32[]{:S(2)}, u32[]{:S(2)}) async-start(bf16[4,128,768]{2,1,0:T(8,128)(2,1)} %broadcast_in_dim.4), calls=%async_computation | async-start | bytes 1572864 | tf_op jit(solution)/shard_map/all_to_all | solution.py:1086
  54.3 9.3 %copy-start = (bf16[4,128,768]{2,1,0:T(8,128)(2,1)}, bf16[4,128,768]{2,1,0:T(8,128)(2,1)S(1)}, u32[]{:S(2)}) copy-start(bf16[4,128,768]{2,1,0:T(8,128)(2,1)S(1)} %all-to-all-done.rows_ref) | copy-start | bytes 2359300
  59.7 0.6 copy-start.11
  60.4 0.6 copy-start.13
  62.9 0.8 copy-start.3
  63.7 23.2 %all-to-all-start.1 = ((bf16[8,128,256]{2,1,0:T(8,128)(2,1)}), bf16[8,128,256]{2,1,0:T(8,128)(2,1)S(1)}, u32[]{:S(2)}, u32[]{:S(2)}) async-start(bf16[8,128,256]{2,1,0:T(8,128)(2,1)} %copy-done.3), calls=%async_computation.1 | async-start | bytes 1048576 | tf_op jit(solution)/shard_map/all_to_all | solution.py:1086
  68.4 72.7 %all-gather.8.cloned.1.call-start = ((), (), s32[]{:S(2)}) async-start(), calls=%async_computation.11 | async-start | bytes 1966080 | tf_op jit(solution)/shard_map/all_gather | solution.py:1199
  68.5 11.1 %collective-permute-start = (bf16[1,128,768]{2,1,0:T(8,128)(2,1)S(1)}, bf16[1,128,768]{2,1,0:T(8,128)(2,1)S(1)}, u32[]{:S(2)}, u32[]{:S(2)}) collective-permute-start(bf16[1,128,768]{2,1,0:T(8,128)(2,1)S(1)} %get-tuple-element.158), channel_id=1, source_target_pairs={{0,4},{4,0},{1,5},{5,1},{2,6},{6,2},{3,7},{7,3},{8,12},{12,8},{9,1... | collective-permute-start | bytes 589832 | tf_op jit(solution)/shard_map/ppermute | solution.py:1195
  86.9 0.8 copy-start.10
  86.9 76.1 %all-gather.10.cloned.1.call-start = ((), (), s32[]{:S(2)}) async-start(), calls=%async_computation.12 | async-start | bytes 1966080 | tf_op jit(solution)/shard_map/all_gather | solution.py:1198
  87.7 36.0 %copy-start.16 = (f32[1,8,4,24]{3,1,0,2:T(8,128)S(1)}, f32[1,8,4,24]{3,1,0,2:T(8,128)}, u32[]{:S(2)}) copy-start(f32[1,8,4,24]{3,1,0,2:T(8,128)} %get-tuple-element.163) | copy-start | bytes 9220
  120.3 13.9 %all-to-all-start.2 = ((bf16[8,64,128]{2,1,0:T(8,128)(2,1)}), bf16[8,64,128]{2,1,0:T(8,128)(2,1)S(1)}, u32[]{:S(2)}, u32[]{:S(2)}) async-start(bf16[8,64,128]{2,1,0:T(8,128)(2,1)} %get-tuple-element.59), calls=%async_computation.2 | async-start | bytes 262144 | tf_op jit(solution)/shard_map/all_to_all | solution.py:1086
  147.9 15.1 %all-to-all-start.3 = ((bf16[4,4,32,768]{3,2,1,0:T(8,128)(2,1)}), bf16[4,4,32,768]{3,2,1,0:T(8,128)(2,1)S(1)}, u32[]{:S(2)}, u32[]{:S(2)}) async-start(bf16[4,4,32,768]{3,2,1,0:T(8,128)(2,1)} %get-tuple-element.62), calls=%async_computation.3 | async-start | bytes 1572864 | tf_op jit(solution)/shard_map/all_to_all | solution.py:1086
  151.4 85.2 %reduce-scatter.2.cloned.1.call-start = ((), (), s32[]{:S(2)}) async-start(), calls=%async_computation.10 | async-start | bytes 2654208 | tf_op jit(solution)/shard_map/reduce_scatter | solution.py:1230
  155.1 9.1 %copy-start.8 = (bf16[32,2,768]{2,1,0:T(2,128)(2,1)S(1)}, bf16[32,2,768]{2,1,0:T(2,128)(2,1)}, u32[]{:S(2)}) copy-start(bf16[32,2,768]{2,1,0:T(2,128)(2,1)} %param.29) | copy-start | bytes 294916
  155.2 16.3 %copy-start.1 = (bf16[768,192]{1,0:T(8,128)(2,1)S(1)}, bf16[768,192]{1,0:T(8,128)(2,1)}, u32[]{:S(2)}) copy-start(bf16[768,192]{1,0:T(8,128)(2,1)} %slice.97.out_ref) | copy-start | bytes 884740
  164.2 65.5 %copy-start.20 = (f32[2,32]{1,0:T(2,128)}, f32[2,32]{1,0:T(2,128)S(1)}, u32[]{:S(2)}) copy-start(f32[2,32]{1,0:T(2,128)S(1)} %get-tuple-element.171) | copy-start | bytes 772
  186.1 43.7 %all-to-all-start.6 = ((bf16[8,96,192]{2,1,0:T(8,128)(2,1)}), bf16[8,96,192]{2,1,0:T(8,128)(2,1)S(1)}, u32[]{:S(2)}, u32[]{:S(2)}) async-start(bf16[8,96,192]{2,1,0:T(8,128)(2,1)} %get-tuple-element.84), calls=%async_computation.7 | async-start | bytes 786432 | tf_op jit(solution)/shard_map/all_to_all | solution.py:1086
  229.7 6.2 %copy-start.6 = (bf16[32,2,768]{2,1,0:T(2,128)(2,1)S(1)}, bf16[32,2,768]{2,1,0:T(2,128)(2,1)}, u32[]{:S(2)}) copy-start(bf16[32,2,768]{2,1,0:T(2,128)(2,1)} %param.15) | copy-start | bytes 294916
  229.7 6.5 %copy-start.14 = (f32[1,8,4,24]{3,2,1,0:T(4,128)S(1)}, f32[1,8,4,24]{3,2,1,0:T(4,128)}, u32[]{:S(2)}) copy-start(f32[1,8,4,24]{3,2,1,0:T(4,128)} %copy-done.13) | copy-start | bytes 9220
  229.8 6.6 %copy-start.12 = (f32[4,2,8,24]{3,2,1,0:T(8,128)S(1)}, f32[4,2,8,24]{3,2,1,0:T(8,128)}, u32[]{:S(2)}) copy-start(f32[4,2,8,24]{3,2,1,0:T(8,128)} %copy-done.11) | copy-start | bytes 18436
  229.8 6.8 %copy-start.2 = (bf16[96,1728]{1,0:T(8,128)(2,1)S(1)}, bf16[96,1728]{1,0:T(8,128)(2,1)}, u32[]{:S(2)}) copy-start(bf16[96,1728]{1,0:T(8,128)(2,1)} %pad_maximum_fusion.1.weights_ref) | copy-start | bytes 995332
  229.8 29.0 %all-to-all-start.5 = ((bf16[8,224,256]{2,1,0:T(8,128)(2,1)}), bf16[8,224,256]{2,1,0:T(8,128)(2,1)S(1)}, u32[]{:S(2)}, u32[]{:S(2)}) async-start(bf16[8,224,256]{2,1,0:T(8,128)(2,1)} %chain_backward.1), calls=%async_computation.5 | async-start | bytes 1835008 | tf_op jit(solution)/shard_map/all_to_all | solution.py:1086
  236.6 1.0 copy-start.4
  260.5 12.6 %copy-start.9 = (bf16[32,2,768]{2,1,0:T(2,128)(2,1)S(1)}, bf16[32,2,768]{2,1,0:T(2,128)(2,1)}, u32[]{:S(2)}) copy-start(bf16[32,2,768]{2,1,0:T(2,128)(2,1)} %param.29) | copy-start | bytes 294916
  260.5 12.6 %copy-start.21 = (f32[2,32]{1,0:T(2,128)S(1)}, f32[2,32]{1,0:T(2,128)}, u32[]{:S(2)}) copy-start(f32[2,32]{1,0:T(2,128)} %copy-done.20) | copy-start | bytes 772
  260.5 12.1 %all-to-all-start.7 = ((bf16[4,80,768]{2,1,0:T(8,128)(2,1)}), bf16[4,80,768]{2,1,0:T(8,128)(2,1)S(1)}, u32[]{:S(2)}, u32[]{:S(2)}) async-start(bf16[4,80,768]{2,1,0:T(8,128)(2,1)} %get-tuple-element.86), calls=%async_computation.8 | async-start | bytes 983040 | tf_op jit(solution)/shard_map/all_to_all | solution.py:1086
  266.5 9.3 %copy-start.17 = (f32[3,128]{1,0:T(4,128)}, f32[3,128]{1,0:T(4,128)S(1)}, u32[]{:S(2)}) copy-start(f32[3,128]{1,0:T(4,128)S(1)} %slice_reduce_fusion) | copy-start | bytes 4612
Sparse Core Ops, SparseCore 0:
  11.0 68.3 all-gather.5
  87.0 18.2 all-gather.7
  107.4 40.0 all-gather.9
  155.4 73.1 reduce-scatter.1

commit v5 on v4

--- a/solution.py
+++ b/solution.py
@@ -18,7 +18,7 @@
 MATRIX_LANE = LANES - 32
 VMEM_BYTES = 56 * 1024 * 1024
 DP = ("outer", "inner")
-CHAIN_FLOPS = 20_000_000_000
+CHAIN_FLOPS = 27_000_000_000
 GLUE_BYTES = 32 * 1024 * 1024
 
 epsilon = 1e-05
@@ -250,7 +250,6 @@
             pre = pre_ref[at, :]
             if step >= 1:
                 taken = dot_nn(mix_ref[at, :], known_ref[...])
-                interleave(others, 1)
                 pre = pre - taken
             density, share = density_and_share(pre)
             act = (pre * share).astype(bf16)
@@ -560,29 +559,34 @@
         first_next_b = first_b[...]
         state = second_w[...]
         state_b = second_b[...]
+
+        def base_of(step):
+            at = slice(step * MINI, (step + 1) * MINI)
+            return wide_ref[0, at, :] - dot_nn(low_ref[1, at, :], first_next_low) - first_next_b
+
+        base = base_of(steps - 1)
         for step in reversed(range(steps)):
             at = slice(step * MINI, (step + 1) * MINI)
-            grad = wide_ref[0, at, :] - dot_nn(low_ref[1, at, :], first_next_low) - first_next_b
+            grad = base
             if step + 1 < steps:
-                grad = grad - dot_nn(mix_ref[at, :], known_ref[...])
+                grad = grad - taken
             state_low = state.astype(bf16)
             own_act = now_act[at, :]
             own_back = low_ref[0, at, :]
             back_base = row_ref[0, at, :] - dot_nt(own_act, state_low) - state_b
-            act_base = wide_ref[1, at, :] - dot_nn(own_back, state_low)
-            interleave(following, 1)
             own_low = now_second[0, step]
             slope = now_slope[at, :]
             back_act_grad = (grad * slope).astype(bf16)
             upon = dot_nt(back_act_grad, own_low)
-            interleave(following, 1)
             upon = back_base + upon
             own_normal, own_gain, own_grad, own_beta, own_alpha = (
                 row_ref[index, at, :] for index in range(1, 6)
             )
             cross, cross_beta, square_inverse = (spread_ref[index, at, :] for index in range(3))
             main = dot_nn(upon * own_grad, own_low)
+            act_base = wide_ref[1, at, :] - dot_nn(own_back, state_low)
             sides = dot_nn(jnp.concatenate([own_normal, own_gain, own_beta], axis=0), own_low)
+            interleave(following, 2)
             interleave(previous, 1)
             alpha = row_mean(upon)
             beta = row_mean(upon * own_normal)
@@ -607,14 +611,15 @@
             known = act_base * slope + grad * now_curve[at, :] - factor * from_sides
             pre_grad = known + factor * main
             known_ref[at, :] = pre_grad.astype(bf16)
+            if step > 0:
+                taken = dot_nn(mix_ref[(step - 1) * MINI : step * MINI, :], known_ref[...])
+                base = base_of(step - 1)
             state = state + dot_tn(
                 jnp.concatenate([key_res_low, own_back], axis=0),
                 jnp.concatenate([own_act, back_act_grad], axis=0),
             )
             state_b = state_b + jnp.sum(key_res_grad, axis=0, keepdims=True)
             row_ref[0, at, :] = upon
-            interleave(following, 1)
-            interleave(previous, 1)
         for generator in (following, previous):
             for _ in generator:
                 pass
@@ -1004,6 +1009,42 @@
     gain_ref[...] = jnp.broadcast_to(gain, gain_ref.shape)
 
 
+def feed_forward_back_kernel(
+    rank_ref, terms_ref, mixed_ref, cot_ref, gain_ref, back_ref, low_ref, result_ref
+):
+    seq_count = mixed_ref.shape[1]
+    for sequence in range(seq_count):
+        grad = terms_ref[0, sequence].astype(f32)
+        down = terms_ref[0, seq_count + sequence].astype(f32)
+        for index in range(1, terms_ref.shape[0]):
+            grad = grad + terms_ref[index, sequence].astype(f32)
+            down = down + terms_ref[index, seq_count + sequence].astype(f32)
+        mixed = mixed_ref[0, sequence]
+        normal, inverse = layer_norm_parts(mixed)
+        back = cot_ref[sequence].astype(f32)
+        back = back + layer_norm_back(normal, inverse, gain_ref[...], grad)
+        back_ref[sequence] = back
+        low_ref[sequence] = back.astype(bf16)
+        result_ref[sequence] = (mixed + down).astype(bf16)
+
+
+def input_grad_kernel(terms_ref, tokens_ref, back_ref, gain_ref, grad_ref, gains_ref):
+    seq_count, rows, _ = tokens_ref.shape
+    for sequence in range(seq_count):
+        at = slice(sequence * rows, (sequence + 1) * rows)
+        total = terms_ref[0, at].astype(f32)
+        for index in range(1, terms_ref.shape[0]):
+            total = total + terms_ref[index, at].astype(f32)
+        normal, inverse = layer_norm_parts(tokens_ref[sequence].astype(f32))
+        total = layer_norm_back(normal, inverse, gain_ref[...], total)
+        grad_ref[:, sequence, :] = back_ref[sequence] + total
+    total = terms_ref[0, seq_count * rows :].astype(f32)
+    for index in range(1, terms_ref.shape[0]):
+        total = total + terms_ref[index, seq_count * rows :].astype(f32)
+    width = gains_ref.shape[1]
+    gains_ref[...] = (total[:2] + total[2:4])[:, :width]
+
+
 def tail_kernel(
     received_ref,
     matrix_ref,
@@ -1229,14 +1270,28 @@
     )
     ffn_grad_sums = lax.psum_scatter(ffn_grads, DP, scatter_dimension=0, tiled=True)
     ffn_sums, chain_rows, _ = ordered(ffn_sums, chain_rows, ffn_grads)
-    ffn_sums = ffn_sums.astype(f32).sum(axis=0)
-    own_mixed = lax.dynamic_index_in_dim(mixed, rank, 0, keepdims=False)
-    own_normal, own_inverse = layer_norm_parts(own_mixed)
-    back_mixed = own_cot.astype(f32).reshape(own_mixed.shape) + layer_norm_back(
-        own_normal, own_inverse, scale_ffn, ffn_sums[:seq_count]
-    )
-    result = (own_mixed + ffn_sums[seq_count:]).astype(bf16)
-    attn_grads = lax.all_gather(back_mixed.astype(bf16), "tensor", axis=1, tiled=True)
+    own_shape = (seq_count, local_rows, width)
+    own_cot = own_cot.reshape(own_shape)
+
+    def fixed(operand):
+        return pl.BlockSpec(operand.shape, lambda turn, _: (0,) * operand.ndim)
+
+    chosen_mixed = pl.BlockSpec((1,) + own_shape, lambda turn, chosen: (chosen[0], 0, 0, 0))
+    own_block = pl.BlockSpec(own_shape, lambda turn, _: (0, 0, 0))
+    back_mixed, back_low, result = pl.pallas_call(
+        feed_forward_back_kernel,
+        grid_spec=pltpu.PrefetchScalarGridSpec(
+            num_scalar_prefetch=1,
+            grid=(1,),
+            in_specs=[fixed(ffn_sums), chosen_mixed, own_block, fixed(scale_ffn)],
+            out_specs=[own_block] * 3,
+        ),
+        out_shape=[shape(own_shape, dtype) for dtype in (f32, bf16, bf16)],
+        compiler_params=pltpu.CompilerParams(vmem_limit_bytes=GLUE_BYTES),
+        name="feed_forward_back",
+    )(jnp.reshape(rank, (1,)).astype(jnp.int32), ffn_sums, mixed, own_cot, scale_ffn)
+    result = result.transpose(1, 0, 2)
+    attn_grads = lax.all_gather(back_low, "tensor", axis=1, tiled=True)
     back_head, out_terms = whole_call(
         head_back_kernel,
         "head_back",
@@ -1278,12 +1333,12 @@
             shape((head_count, chunk, LANES - RATE_LANE), f32),
         ),
     )
-    tail = exchange(terms, "tensor").astype(f32).sum(axis=0)
-    own_inputs = tokens.transpose(1, 0, 2).astype(f32)
-    own_normal, own_inverse = layer_norm_parts(own_inputs)
-    attn_sums = tail[:row_count].reshape(own_inputs.shape)
-    input_grad = back_mixed + layer_norm_back(own_normal, own_inverse, scale_attn, attn_sums)
-    gain_sums = tail[row_count : row_count + 2, :shard] + tail[row_count + 2 : row_count + 4, :shard]
+    input_grad, gain_sums = whole_call(
+        input_grad_kernel,
+        "input_grad",
+        (exchange(terms, "tensor"), own_tokens.reshape(own_shape), back_mixed, scale_attn),
+        (shape(tokens.shape, f32), shape((2, shard), f32)),
+    )
     gain_sums = lax.dynamic_slice_in_dim(gain_sums, rank * part, part, 1)
 
     matrices = state_block[..., MATRIX_LANE - RATE_LANE :][..., :inner_part]
@@ -1296,12 +1351,9 @@
         columns[:, ends[index] : ends[index + 1]] for index in range(3)
     )
 
-    def by_token(values):
-        return values.reshape(seq_count, local_rows, width).transpose(1, 0, 2)
-
     return (
-        by_token(result),
-        by_token(input_grad),
+        result,
+        input_grad,
         gain_sums[0],
         gain_sums[1],
         grad_qkv.transpose(1, 0, 2),

time: 284 us -> 276 us (0.972)
  other arithmetic: 9.07 us -> 2.8 us
  Pallas kernels: 88.7 us -> 84.8 us
    pallas_call x1, Pallas kernels: 39.9 us -> 35.3 us  [chain_backward(): pl.pallas_call(functools.partial(backward_kernel, inner_part, feature_par...]
    reduce_sum x9 -> x0, other arithmetic: 4.02 us -> none  [the longest x7 3.86 us: row_mean(): return jnp.mean(values, axis=-1, keepdims=True)]
    unnamed x68 -> x55, local copies, waits for them, and re-layouts: 7.71 us -> 8.91 us
    pallas_call x6 -> x7, Pallas kernels: 16.1 us -> 17 us  [whole_call(): pl.pallas_call(kernel, in_specs=[spec(operand.shape) for operand in opera...]
  transfers between devices with their start and end apart: 12 -> 12, of which waited for: 6 -> 6; matrix products, arithmetic and copies ran while one was open for 5% -> 4% of each run, Pallas kernels for 31% -> 30%
where the time goes in v5:
time: 276 us; the launch traced here: 275 us
  Pallas kernels  84.8 us (31%)
  blocking collectives  68.4 us (25%)
  waiting for transfers between devices  56.7 us (21%)
  starting transfers between devices  31.2 us (11%)
  local copies, waits for them, and re-layouts  16.6 us (6%)
  between operations  14.2 us (5%)
  other arithmetic  2.8 us (1%)
    all_to_all x7, waiting for transfers between devices, exchange(): return lax.all_to_all(values, axis, 0, 0, tiled=False)  47.9 us
    pallas_call x1, Pallas kernels, chain_backward(): pl.pallas_call(functools.partial(backward_kernel, inner_part, feature_par...  35.3 us
    pallas_call x1, Pallas kernels, chain_forward(): pl.pallas_call(functools.partial(forward_kernel, inner_part, feature_part...  32.2 us
    all_to_all x7, starting transfers between devices, exchange(): return lax.all_to_all(values, axis, 0, 0, tiled=False)  29 us
    all_gather x1, blocking collectives, local(): qkv_full = lax.all_gather(qkv_half, 'outer', axis=0, tiled=True)  28.7 us
    pallas_call x7, Pallas kernels, whole_call(): pl.pallas_call(kernel, in_specs=[spec(operand.shape) for operand in opera...  17 us
    all_to_all x1, blocking collectives, exchange(): return lax.all_to_all(values, axis, 0, 0, tiled=False)  13.5 us
    unnamed x55, local copies, waits for them, and re-layouts  8.91 us
  transfers between devices with their start and end apart: 12, of which 6 were waited for; matrix products, arithmetic and copies ran while one was open for 4% of the time, Pallas kernels for 30%

profile of v5, /device:TPU:0, one launch (start us, length us, event | category | flops | bytes accessed | tf_op | source)
XLA Modules:
  0.0 274.7 jit_solution(14466567770307405427)
XLA Ops:
  7.2 1.0 copy.79
  8.2 0.9 copy.72
  9.1 1.6 pad_maximum_fusion.1.weights_ref
  11.0 0.9 broadcast_in_dim.4
  11.9 4.4 %all-to-all-start = ((bf16[4,128,768]{2,1,0:T(8,128)(2,1)}), bf16[4,128,768]{2,1,0:T(8,128)(2,1)S(1)}, u32[]{:S(2)}, u32[]{:S(2)}) async-start(bf16[4,128,768]{2,1,0:T(8,128)(2,1)} %broadcast_in_dim.4), calls=%async_computation | async-start | bytes 1572864 | tf_op jit(solution)/shard_map/all_to_all | solution.py:1127
  17.4 8.0 %all_gather.30 = bf16[192,581]{1,0:T(8,128)(2,1)S(1)} all-gather(bf16[96,581]{1,0:T(8,128)(2,1)S(1)} %fusion.1), channel_id=1, replica_groups=mesh['outer'=4,'inner'=2,'tensor'=4] {'inner'}, dimensions={0}, use_global_device_ids=true | all-gather | bytes 334656 | tf_op jit(solution)/shard_map/all_gather | solution.py:1198
  25.6 28.7 %all_gather.31.weights_ref = bf16[768,581]{1,0:T(8,128)(2,1)S(1)} all-gather(bf16[192,581]{1,0:T(8,128)(2,1)S(1)} %all_gather.30), channel_id=1, replica_groups=mesh['outer'=4,'inner'=2,'tensor'=4] {'outer'}, dimensions={0}, use_global_device_ids=true | all-gather | bytes 1115520 | tf_op jit(solution)/shard_map/all_gather | solution.py:1199
  54.5 5.1 %all_gather.32 = bf16[4,2,192]{2,1,0:T(2,128)(2,1)S(1)} all-gather(bf16[1,2,192]{2,1,0:T(2,128)(2,1)S(1)} %copy.78), channel_id=1, replica_groups=mesh['outer'=4,'inner'=2,'tensor'=4] {'tensor'}, dimensions={0}, use_global_device_ids=true | all-gather | bytes 3840 | tf_op jit(solution)/shard_map/all_gather | solution.py:1203
  59.8 1.8 projections.1
  61.6 0.8 copy-done.4
  62.4 0.7 copy-done.6
  63.2 4.7 %all-to-all-start.1 = ((bf16[8,128,256]{2,1,0:T(8,128)(2,1)}), bf16[8,128,256]{2,1,0:T(8,128)(2,1)S(1)}, u32[]{:S(2)}, u32[]{:S(2)}) async-start(bf16[8,128,256]{2,1,0:T(8,128)(2,1)} %copy-done.4), calls=%async_computation.1 | async-start | bytes 1048576 | tf_op jit(solution)/shard_map/all_to_all | solution.py:1127
  67.9 1.1 constant_dynamic-slice_fusion.4
  69.0 2.0 collective-permute-start
  71.0 8.0 %collective-permute-done = bf16[1,128,768]{2,1,0:T(8,128)(2,1)S(1)} collective-permute-done((bf16[1,128,768]{2,1,0:T(8,128)(2,1)S(1)}, bf16[1,128,768]{2,1,0:T(8,128)(2,1)S(1)}, u32[]{:S(2)}, u32[]{:S(2)}) %collective-permute-start) | collective-permute-done | bytes 196640 | tf_op jit(solution)/shard_map/ppermute | solution.py:1236
  79.0 0.8 pad_maximum_fusion
  79.8 1.8 slice.77.out_ref
  81.6 5.3 %all-to-all-done.1.packed_ref = bf16[8,128,256]{2,1,0:T(8,128)(2,1)S(1)} async-done(((bf16[8,128,256]{2,1,0:T(8,128)(2,1)}), bf16[8,128,256]{2,1,0:T(8,128)(2,1)S(1)}, u32[]{:S(2)}, u32[]{:S(2)}) %all-to-all-start.1) | async-done | bytes 524320 | tf_op jit(solution)/shard_map/all_to_all | solution.py:1127
  86.9 0.7 all-gather.10.cloned.1.call-update
  87.7 32.2 %chain_forward.1 = (bf16[8,64,128]{2,1,0:T(8,128)(2,1)}, bf16[1024,256]{1,0:T(8,128)(2,1)}, bf16[1024,256]{1,0:T(8,128)(2,1)}, f32[1024,256]{1,0:T(8,128)}, f32[...) custom-call(bf16[8,128,256]{2,1,0:T(8,128)(2,1)} %copy-done.9), custom_call_target="tpu_custom_call" | custom-call | flops 27000000512 | bytes 4194304 | tf_op jit(solution)/shard_map/chain_forward/pallas_call | solution.py:701
  119.9 3.4 %all-to-all-start.2 = ((bf16[8,64,128]{2,1,0:T(8,128)(2,1)}), bf16[8,64,128]{2,1,0:T(8,128)(2,1)S(1)}, u32[]{:S(2)}, u32[]{:S(2)}) async-start(bf16[8,64,128]{2,1,0:T(8,128)(2,1)} %get-tuple-element.64), calls=%async_computation.2 | async-start | bytes 262144 | tf_op jit(solution)/shard_map/all_to_all | solution.py:1127
  123.3 0.7 slice.64.gain_ref
  124.0 9.7 %all-to-all-done.2 = bf16[8,64,128]{2,1,0:T(8,128)(2,1)S(1)} async-done(((bf16[8,64,128]{2,1,0:T(8,128)(2,1)}), bf16[8,64,128]{2,1,0:T(8,128)(2,1)S(1)}, u32[]{:S(2)}, u32[]{:S(2)}) %all-to-all-start.2) | async-done | bytes 131104 | tf_op jit(solution)/shard_map/all_to_all | solution.py:1127
  133.7 6.9 %all_gather.34.heads_ref = bf16[4,3,2,64,128]{4,3,2,1,0:T(8,128)(2,1)} all-gather(bf16[1,3,2,64,128]{4,3,2,1,0:T(8,128)(2,1)S(1)} %bitcast.48), channel_id=1, replica_groups=mesh['outer'=4,'inner'=2,'tensor'=4] {'tensor'}, dimensions={0}, use_global_device_ids=true | all-gather | bytes 491520 | tf_op jit(solution)/shard_map/all_gather | solution.py:1246
  140.5 6.7 %feed_forward.1 = (bf16[4,4,32,768]{3,2,1,0:T(8,128)(2,1)}, f32[4,2,32,768]{3,2,1,0:T(8,128)}, bf16[256,768]{1,0:T(8,128)(2,1)}, bf16[256,1024]{1,0:T(8,128)(2,1...) custom-call(bf16[4,3,2,64,128]{4,3,2,1,0:T(8,128)(2,1)} %all_gather.34.heads_ref, bf16[4,128,768]{2,1,0:T(8,128)(2,1)} %copy-done, ...), custom_call_target="tpu_custom_call" | custom-call | tf_op jit(solution)/shard_map/feed_forward/pallas_call | solution.py:1112
  147.3 3.5 %all-to-all-start.3 = ((bf16[4,4,32,768]{3,2,1,0:T(8,128)(2,1)}), bf16[4,4,32,768]{3,2,1,0:T(8,128)(2,1)S(1)}, u32[]{:S(2)}, u32[]{:S(2)}) async-start(bf16[4,4,32,768]{3,2,1,0:T(8,128)(2,1)} %get-tuple-element.66), calls=%async_computation.3 | async-start | bytes 1572864 | tf_op jit(solution)/shard_map/all_to_all | solution.py:1127
  150.8 3.6 %feed_forward_grads.1 = bf16[768,1536]{1,0:T(8,128)(2,1)} custom-call(bf16[256,768]{1,0:T(8,128)(2,1)} %get-tuple-element.68.normed_ref, bf16[256,1024]{1,0:T(8,128)(2,1)} %get-tuple-element.69.back_ref, bf16[256,512]{1,0:T(8,128)(2,1)} %get-tuple-element.70.swiglu_ref, bf16[256,768]{1,0:T(8,128)(2,1)} %get-tuple-element.71.cot_ref), custom_call_target="tpu_custom_call" | custom-call | tf_op jit(solution)/shard_map/feed_forward_grads/pallas_call | solution.py:1112
  154.5 7.9 %all-to-all-done.3.terms_ref = bf16[4,4,32,768]{3,2,1,0:T(8,128)(2,1)S(1)} async-done(((bf16[4,4,32,768]{3,2,1,0:T(8,128)(2,1)}), bf16[4,4,32,768]{3,2,1,0:T(8,128)(2,1)S(1)}, u32[]{:S(2)}, u32[]{:S(2)}) %all-to-all-start.3) | async-done | bytes 786464 | tf_op jit(solution)/shard_map/all_to_all | solution.py:1127
  162.4 1.1 copy-done.3
  163.9 6.1 %all_gather.39.grads_ref = bf16[2,128,768]{2,1,0:T(8,128)(2,1)S(1)} all-gather(bf16[2,32,768]{2,1,0:T(8,128)(2,1)S(1)} %get-tuple-element.76), channel_id=1, replica_groups=mesh['outer'=4,'inner'=2,'tensor'=4] {'tensor'}, dimensions={1}, use_global_device_ids=true | all-gather | bytes 491520 | tf_op jit(solution)/shard_map/all_gather | solution.py:1294
  170.0 1.3 head_back.1
  171.3 13.5 %all_to_all.40.head_grad_ref = bf16[8,64,128]{2,1,0:T(8,128)(2,1)} all-to-all(bf16[8,64,128]{2,1,0:T(8,128)(2,1)S(1)} %get-tuple-element.77), channel_id=1, replica_groups=mesh['outer'=4,'inner'=2,'tensor'=4] {'outer','inner'}, dimensions={0} | all-to-all | bytes 262144 | tf_op jit(solution)/shard_map/all_to_all | solution.py:1127
  184.8 3.6 %all-to-all-start.6 = ((bf16[8,96,192]{2,1,0:T(8,128)(2,1)}), bf16[8,96,192]{2,1,0:T(8,128)(2,1)S(1)}, u32[]{:S(2)}, u32[]{:S(2)}) async-start(bf16[8,96,192]{2,1,0:T(8,128)(2,1)} %get-tuple-element.91), calls=%async_computation.7 | async-start | bytes 786432 | tf_op jit(solution)/shard_map/all_to_all | solution.py:1127
  188.5 35.3 %chain_backward.1 = bf16[8,224,256]{2,1,0:T(8,128)(2,1)} custom-call(s32[1]{0:T(128)} %bitcast.22.sequence_ref, bf16[8,128,256]{2,1,0:T(8,128)(2,1)} %copy-done.9, bf16[4,2,128,768]{3,2,1,0:T(8,128)(2,1)} %bitcast.66, bf16[8,64,128]{2,1,0:T(8,128)(2,1)} %all_to_all.40.head_grad_ref, bf16[1024,256]{1,0:T(8,128)(2,1)} %get-tuple-element.78.next_act.now_act, ...), custom_call_target="tpu_custom_call" | custom-call | flops 27000000512 | bytes 4194304 | tf_op jit(solution)/shard_map/chain_backward/pallas_call | solution.py:786
  223.8 5.9 %all-to-all-start.5 = ((bf16[8,224,256]{2,1,0:T(8,128)(2,1)}), bf16[8,224,256]{2,1,0:T(8,128)(2,1)S(1)}, u32[]{:S(2)}, u32[]{:S(2)}) async-start(bf16[8,224,256]{2,1,0:T(8,128)(2,1)} %chain_backward.1), calls=%async_computation.5 | async-start | bytes 1835008 | tf_op jit(solution)/shard_map/all_to_all | solution.py:1127
  230.0 0.7 copy.75
  230.7 1.0 copy-done.7
  231.7 1.0 matrix_outputs.1
  232.7 19.5 %all-to-all-done.5.received_ref = bf16[8,224,256]{2,1,0:T(8,128)(2,1)S(1)} async-done(((bf16[8,224,256]{2,1,0:T(8,128)(2,1)}), bf16[8,224,256]{2,1,0:T(8,128)(2,1)S(1)}, u32[]{:S(2)}, u32[]{:S(2)}) %all-to-all-start.5) | async-done | bytes 917536 | tf_op jit(solution)/shard_map/all_to_all | solution.py:1127
  252.1 1.6 tail.1
  253.7 0.8 copy-done.5
  254.6 3.5 %all-to-all-start.7 = ((bf16[4,80,768]{2,1,0:T(8,128)(2,1)}), bf16[4,80,768]{2,1,0:T(8,128)(2,1)S(1)}, u32[]{:S(2)}, u32[]{:S(2)}) async-start(bf16[4,80,768]{2,1,0:T(8,128)(2,1)} %copy-done.5), calls=%async_computation.8 | async-start | bytes 983040 | tf_op jit(solution)/shard_map/all_to_all | solution.py:1127
  258.1 0.6 slice_bitcast_fusion.1
  258.7 0.7 copy.76
  259.4 0.7 copy.77
  260.3 0.7 fusion.3
  261.0 5.6 %all-to-all-done.7.terms_ref = bf16[4,80,768]{2,1,0:T(8,128)(2,1)S(1)} async-done(((bf16[4,80,768]{2,1,0:T(8,128)(2,1)}), bf16[4,80,768]{2,1,0:T(8,128)(2,1)S(1)}, u32[]{:S(2)}, u32[]{:S(2)}) %all-to-all-start.7) | async-done | bytes 491552 | tf_op jit(solution)/shard_map/all_to_all | solution.py:1127
  266.5 1.0 input_grad.1
  (87 shorter events, 3.5 us)
Async XLA Ops:
  7.2 3.6 %copy-start.11 = (bf16[32,2,768]{2,1,0:T(2,128)(2,1)S(1)}, bf16[32,2,768]{2,1,0:T(2,128)(2,1)}, u32[]{:S(2)}) copy-start(bf16[32,2,768]{2,1,0:T(2,128)(2,1)} %param.15) | copy-start | bytes 294916
  7.2 3.6 %copy-start.12 = (bf16[32,2,768]{2,1,0:T(2,128)(2,1)S(1)}, bf16[32,2,768]{2,1,0:T(2,128)(2,1)}, u32[]{:S(2)}) copy-start(bf16[32,2,768]{2,1,0:T(2,128)(2,1)} %param.29) | copy-start | bytes 294916
  7.2 72.6 %all-gather.6.cloned.1.call-start = ((), (), s32[]{:S(2)}) async-start(), calls=%async_computation.9 | async-start | bytes 3096576 | tf_op jit(solution)/shard_map/all_gather | solution.py:1211
  10.8 5.4 %copy-start.10 = (bf16[96,3,192]{2,0,1:T(8,128)(2,1)S(1)}, bf16[96,3,192]{2,0,1:T(8,128)(2,1)}, u32[]{:S(2)}) copy-start(bf16[96,3,192]{2,0,1:T(8,128)(2,1)} %param.18) | copy-start | bytes 331780
  10.9 5.7 %copy-start.16 = (bf16[96,3]{0,1:T(4,128)(2,1)S(1)}, bf16[96,3]{0,1:T(4,128)(2,1)}, u32[]{:S(2)}) copy-start(bf16[96,3]{0,1:T(4,128)(2,1)} %param.19) | copy-start | bytes 1732
  10.9 5.8 %copy-start.21 = (bf16[24]{0:T(256)(128)(2,1)S(1)}, bf16[24]{0:T(256)(128)(2,1)}, u32[]{:S(2)}) copy-start(bf16[24]{0:T(256)(128)(2,1)} %param.17) | copy-start | bytes 148
  10.9 5.8 %copy-start.22 = (bf16[24]{0:T(256)(128)(2,1)S(1)}, bf16[24]{0:T(256)(128)(2,1)}, u32[]{:S(2)}) copy-start(bf16[24]{0:T(256)(128)(2,1)} %param.16) | copy-start | bytes 148
  10.9 5.9 %copy-start.14 = (bf16[3,32,64]{2,1,0:T(8,128)(2,1)S(1)}, bf16[3,32,64]{2,1,0:T(8,128)(2,1)}, u32[]{:S(2)}) copy-start(bf16[3,32,64]{2,1,0:T(8,128)(2,1)} %param.25) | copy-start | bytes 36868
  10.9 5.9 %copy-start.15 = (bf16[3,64,32]{1,2,0:T(8,128)(2,1)S(1)}, bf16[3,64,32]{1,2,0:T(8,128)(2,1)}, u32[]{:S(2)}) copy-start(bf16[3,64,32]{1,2,0:T(8,128)(2,1)} %param.23) | copy-start | bytes 36868
  11.9 5.2 %copy-start.17 = (bf16[3,8]{1,0:T(4,128)(2,1)S(1)}, bf16[3,8]{1,0:T(4,128)(2,1)}, u32[]{:S(2)}) copy-start(bf16[3,8]{1,0:T(4,128)(2,1)} %param.28) | copy-start | bytes 148
  11.9 5.2 %copy-start.18 = (bf16[3,8]{1,0:T(4,128)(2,1)S(1)}, bf16[3,8]{1,0:T(4,128)(2,1)}, u32[]{:S(2)}) copy-start(bf16[3,8]{1,0:T(4,128)(2,1)} %param.27) | copy-start | bytes 148
  11.9 5.2 %copy-start.19 = (bf16[3,8]{1,0:T(4,128)(2,1)S(1)}, bf16[3,8]{1,0:T(4,128)(2,1)}, u32[]{:S(2)}) copy-start(bf16[3,8]{1,0:T(4,128)(2,1)} %param.26) | copy-start | bytes 148
  11.9 5.2 %copy-start.20 = (bf16[3,32]{1,0:T(4,128)(2,1)S(1)}, bf16[3,32]{1,0:T(4,128)(2,1)}, u32[]{:S(2)}) copy-start(bf16[3,32]{1,0:T(4,128)(2,1)} %param.24) | copy-start | bytes 580
  11.9 42.4 %all-to-all-start = ((bf16[4,128,768]{2,1,0:T(8,128)(2,1)}), bf16[4,128,768]{2,1,0:T(8,128)(2,1)S(1)}, u32[]{:S(2)}, u32[]{:S(2)}) async-start(bf16[4,128,768]{2,1,0:T(8,128)(2,1)} %broadcast_in_dim.4), calls=%async_computation | async-start | bytes 1572864 | tf_op jit(solution)/shard_map/all_to_all | solution.py:1127
  54.3 8.9 %copy-start = (bf16[4,128,768]{2,1,0:T(8,128)(2,1)}, bf16[4,128,768]{2,1,0:T(8,128)(2,1)S(1)}, u32[]{:S(2)}) copy-start(bf16[4,128,768]{2,1,0:T(8,128)(2,1)S(1)} %all-to-all-done.rows_ref) | copy-start | bytes 2359300
  61.6 0.8 copy-start.4
  62.4 0.7 copy-start.6
  63.2 23.7 %all-to-all-start.1 = ((bf16[8,128,256]{2,1,0:T(8,128)(2,1)}), bf16[8,128,256]{2,1,0:T(8,128)(2,1)S(1)}, u32[]{:S(2)}, u32[]{:S(2)}) async-start(bf16[8,128,256]{2,1,0:T(8,128)(2,1)} %copy-done.4), calls=%async_computation.1 | async-start | bytes 1048576 | tf_op jit(solution)/shard_map/all_to_all | solution.py:1127
  67.9 72.7 %all-gather.8.cloned.1.call-start = ((), (), s32[]{:S(2)}) async-start(), calls=%async_computation.11 | async-start | bytes 1966080 | tf_op jit(solution)/shard_map/all_gather | solution.py:1240
  69.0 10.0 %collective-permute-start = (bf16[1,128,768]{2,1,0:T(8,128)(2,1)S(1)}, bf16[1,128,768]{2,1,0:T(8,128)(2,1)S(1)}, u32[]{:S(2)}, u32[]{:S(2)}) collective-permute-start(bf16[1,128,768]{2,1,0:T(8,128)(2,1)S(1)} %get-tuple-element.149), channel_id=1, source_target_pairs={{0,4},{4,0},{1,5},{5,1},{2,6},{6,2},{3,7},{7,3},{8,12},{12,8},{9,1... | collective-permute-start | bytes 589832 | tf_op jit(solution)/shard_map/ppermute | solution.py:1236
  86.8 0.8 copy-start.9
  86.9 75.5 %all-gather.10.cloned.1.call-start = ((), (), s32[]{:S(2)}) async-start(), calls=%async_computation.12 | async-start | bytes 1966080 | tf_op jit(solution)/shard_map/all_gather | solution.py:1239
  119.9 13.8 %all-to-all-start.2 = ((bf16[8,64,128]{2,1,0:T(8,128)(2,1)}), bf16[8,64,128]{2,1,0:T(8,128)(2,1)S(1)}, u32[]{:S(2)}, u32[]{:S(2)}) async-start(bf16[8,64,128]{2,1,0:T(8,128)(2,1)} %get-tuple-element.64), calls=%async_computation.2 | async-start | bytes 262144 | tf_op jit(solution)/shard_map/all_to_all | solution.py:1127
  147.3 15.1 %all-to-all-start.3 = ((bf16[4,4,32,768]{3,2,1,0:T(8,128)(2,1)}), bf16[4,4,32,768]{3,2,1,0:T(8,128)(2,1)S(1)}, u32[]{:S(2)}, u32[]{:S(2)}) async-start(bf16[4,4,32,768]{3,2,1,0:T(8,128)(2,1)} %get-tuple-element.66), calls=%async_computation.3 | async-start | bytes 1572864 | tf_op jit(solution)/shard_map/all_to_all | solution.py:1127
  150.8 79.9 %reduce-scatter.2.cloned.1.call-start = ((), (), s32[]{:S(2)}) async-start(), calls=%async_computation.10 | async-start | bytes 2654208 | tf_op jit(solution)/shard_map/reduce_scatter | solution.py:1271
  154.4 8.0 %copy-start.8 = (f32[1,768]{1,0:T(1,128)S(1)}, f32[1,768]{1,0:T(1,128)}, u32[]{:S(2)}) copy-start(f32[1,768]{1,0:T(1,128)} %slice.64.gain_ref) | copy-start | bytes 9220
  154.4 15.6 %copy-start.1 = (bf16[768,192]{1,0:T(8,128)(2,1)S(1)}, bf16[768,192]{1,0:T(8,128)(2,1)}, u32[]{:S(2)}) copy-start(bf16[768,192]{1,0:T(8,128)(2,1)} %slice.77.out_ref) | copy-start | bytes 884740
  162.4 1.1 copy-start.3
  184.8 39.0 %all-to-all-start.6 = ((bf16[8,96,192]{2,1,0:T(8,128)(2,1)}), bf16[8,96,192]{2,1,0:T(8,128)(2,1)S(1)}, u32[]{:S(2)}, u32[]{:S(2)}) async-start(bf16[8,96,192]{2,1,0:T(8,128)(2,1)} %get-tuple-element.91), calls=%async_computation.7 | async-start | bytes 786432 | tf_op jit(solution)/shard_map/all_to_all | solution.py:1127
  223.8 6.9 %copy-start.2 = (bf16[96,1728]{1,0:T(8,128)(2,1)S(1)}, bf16[96,1728]{1,0:T(8,128)(2,1)}, u32[]{:S(2)}) copy-start(bf16[96,1728]{1,0:T(8,128)(2,1)} %pad_maximum_fusion.1.weights_ref) | copy-start | bytes 995332
  223.8 28.3 %all-to-all-start.5 = ((bf16[8,224,256]{2,1,0:T(8,128)(2,1)}), bf16[8,224,256]{2,1,0:T(8,128)(2,1)S(1)}, u32[]{:S(2)}, u32[]{:S(2)}) async-start(bf16[8,224,256]{2,1,0:T(8,128)(2,1)} %chain_backward.1), calls=%async_computation.5 | async-start | bytes 1835008 | tf_op jit(solution)/shard_map/all_to_all | solution.py:1127
  230.7 1.0 copy-start.7
  253.7 0.8 copy-start.5
  254.6 11.9 %all-to-all-start.7 = ((bf16[4,80,768]{2,1,0:T(8,128)(2,1)}), bf16[4,80,768]{2,1,0:T(8,128)(2,1)S(1)}, u32[]{:S(2)}, u32[]{:S(2)}) async-start(bf16[4,80,768]{2,1,0:T(8,128)(2,1)} %copy-done.5), calls=%async_computation.8 | async-start | bytes 983040 | tf_op jit(solution)/shard_map/all_to_all | solution.py:1127
  260.3 7.8 %copy-start.13 = (f32[3,128]{1,0:T(4,128)}, f32[3,128]{1,0:T(4,128)S(1)}, u32[]{:S(2)}) copy-start(f32[3,128]{1,0:T(4,128)S(1)} %slice_reduce_fusion) | copy-start | bytes 4612
Sparse Core Ops, SparseCore 0:
  10.9 68.6 all-gather.5
  87.0 18.1 all-gather.7
  106.8 39.8 all-gather.9
  154.8 74.6 reduce-scatter.1

commit v6 on v5

--- a/solution.py
+++ b/solution.py
@@ -416,7 +416,11 @@
 
     def prepare():
         query, key, miss, logit = unpack(jnp.maximum(devices - 1 - turn, 0))
-        head_grad = jnp.transpose(head_grad_ref[0].astype(f32))
+        halves = []
+        for index in range(head_grad_ref.shape[1]):
+            values = head_grad_ref[0, index].astype(f32)
+            halves += [values[:, :HEAD_DIM], values[:, HEAD_DIM:]]
+        head_grad = jnp.concatenate(halves, axis=0)
         head_normal = next_out_norms[:, HEAD_DIM : 2 * HEAD_DIM]
         head_mean = mean_of(head_grad)
         head_tilt = mean_of(head_grad * head_normal)
@@ -791,7 +795,7 @@
             in_specs=[
                 whole_block(packed.shape),
                 pl.BlockSpec((1, 1, chunk, width), rows_map),
-                at((1, HEAD_DIM, chunk), 0),
+                at((1,) + head_grad.shape[1:], 0),
                 at(wide, 0),
                 at(wide, 0),
                 at(wide, 0),
@@ -976,20 +980,31 @@
         grads_ref[:, at] = dot_nn(cot, swiglu_ref[:, first : first + 256]).astype(bf16)
 
 
-def head_back_kernel(grads_ref, out_ref, heads_ref, back_ref, out_grad_ref):
-    head_count, seq_count, _, chunk = heads_ref.shape
+def head_back_kernel(grads_ref, out_ref, back_ref):
+    tensor_count = out_ref.shape[0]
+    seq_count, rows, _ = grads_ref.shape
+    head_count = out_ref.shape[2] // HEAD_DIM
+    for index in range(tensor_count):
+        for sequence in range(seq_count):
+            back = dot_nn(grads_ref[sequence], out_ref[index]).astype(bf16)
+            for head in range(head_count):
+                place = (head * seq_count + sequence) * tensor_count + index
+                values = back[:, head * HEAD_DIM : (head + 1) * HEAD_DIM]
+                back_ref[place, :, :HEAD_DIM] = values[: rows // 2]
+                back_ref[place, :, HEAD_DIM:] = values[rows // 2 :]
+    for place in range(head_count * seq_count * tensor_count, back_ref.shape[0]):
+        back_ref[place] = jnp.zeros((rows // 2, 2 * HEAD_DIM), bf16)
+
+
+def out_grad_kernel(grads_ref, heads_ref, out_grad_ref):
+    head_count, seq_count, _, _ = heads_ref.shape
     devices, shard, _ = out_grad_ref.shape
     total = None
     for sequence in range(seq_count):
-        grads = grads_ref[sequence]
-        back = jnp.transpose(dot_nn(grads, out_ref[...])).astype(bf16)
-        for head in range(head_count):
-            back_ref[head * seq_count + sequence] = back[head * HEAD_DIM : (head + 1) * HEAD_DIM]
         heads = [heads_ref[head, sequence] for head in range(head_count)]
-        term = dot_nt(jnp.transpose(grads.astype(f32)), jnp.concatenate(heads, axis=0))
+        grads = jnp.transpose(grads_ref[sequence].astype(f32))
+        term = dot_nt(grads, jnp.concatenate(heads, axis=0))
         total = term if total is None else total + term
-    for index in range(head_count * seq_count, devices):
-        back_ref[index] = jnp.zeros((HEAD_DIM, chunk), bf16)
     for index in range(devices):
         out_grad_ref[index] = total[index * shard : (index + 1) * shard].astype(bf16)
 
@@ -1287,21 +1302,28 @@
             out_specs=[own_block] * 3,
         ),
         out_shape=[shape(own_shape, dtype) for dtype in (f32, bf16, bf16)],
-        compiler_params=pltpu.CompilerParams(vmem_limit_bytes=GLUE_BYTES),
+        compiler_params=pltpu.CompilerParams(vmem_limit_bytes=VMEM_BYTES),
         name="feed_forward_back",
     )(jnp.reshape(rank, (1,)).astype(jnp.int32), ffn_sums, mixed, own_cot, scale_ffn)
     result = result.transpose(1, 0, 2)
-    attn_grads = lax.all_gather(back_low, "tensor", axis=1, tiled=True)
-    back_head, out_terms = whole_call(
+    (back_head,) = whole_call(
         head_back_kernel,
         "head_back",
-        (attn_grads, own_out, head_local),
-        (
-            shape((device_count, HEAD_DIM, chunk), bf16),
-            shape((device_count, shard, local_width), bf16),
-        ),
-    )
-    head_grad = exchange(back_head, DP)
+        (back_low, out_full),
+        (shape((device_count * tensor_count, local_rows // 2, 2 * HEAD_DIM), bf16),),
+        VMEM_BYTES,
+    )
+    back_head, back_low = ordered(back_head, back_low)
+    head_grad = exchange(back_head, DP + ("tensor",))
+    head_grad = head_grad.reshape(device_count, tensor_count, local_rows // 2, 2 * HEAD_DIM)
+    attn_grads = lax.all_gather(back_low, "tensor", axis=1, tiled=True)
+    (out_terms,) = whole_call(
+        out_grad_kernel,
+        "out_grads",
+        (attn_grads, head_local),
+        (shape((device_count, shard, local_width), bf16),),
+    )
+    head_grad, out_terms = ordered(head_grad, out_terms)
     out_sums = exchange(out_terms, DP)
 
     chosen = jnp.reshape(side, (1,)).astype(jnp.int32)

time: 276 us -> 273 us (0.989)
  blocking collectives: 68.4 us -> 56 us
  Pallas kernels: 84.8 us -> 89.6 us
  starting transfers between devices: 31.2 us -> 34.6 us
    all_to_all x1 -> x0, blocking collectives: 13.5 us -> none  [exchange(): return lax.all_to_all(values, axis, 0, 0, tiled=False)]
    all_to_all x7 -> x8, starting transfers between devices: 29 us -> 32.4 us  [exchange(): return lax.all_to_all(values, axis, 0, 0, tiled=False)]
    pallas_call x7 -> x8, Pallas kernels: 17 us -> 19.7 us  [whole_call(): pl.pallas_call(kernel, in_specs=[spec(operand.shape) for operand in opera...]
    all_to_all x7 -> x8, waiting for transfers between devices: 47.9 us -> 49.4 us  [exchange(): return lax.all_to_all(values, axis, 0, 0, tiled=False)]
    unnamed x55 -> x61, local copies, waits for them, and re-layouts: 8.91 us -> 8.69 us
  transfers between devices with their start and end apart: 12 -> 13, of which waited for: 6 -> 8; matrix products, arithmetic and copies ran while one was open for 4% -> 4% of each run, Pallas kernels for 30% -> 32%
where the time goes in v6:
time: 273 us; the launch traced here: 272 us
  Pallas kernels  89.6 us (33%)
  waiting for transfers between devices  58.6 us (21%)
  blocking collectives  56 us (21%)
  starting transfers between devices  34.6 us (13%)
  local copies, waits for them, and re-layouts  16.4 us (6%)
  between operations  14.2 us (5%)
  other arithmetic  2.83 us (1%)
    all_to_all x8, waiting for transfers between devices, exchange(): return lax.all_to_all(values, axis, 0, 0, tiled=False)  49.4 us
    pallas_call x1, Pallas kernels, chain_backward(): pl.pallas_call(functools.partial(backward_kernel, inner_part, feature_par...  35.4 us
    all_to_all x8, starting transfers between devices, exchange(): return lax.all_to_all(values, axis, 0, 0, tiled=False)  32.4 us
    pallas_call x1, Pallas kernels, chain_forward(): pl.pallas_call(functools.partial(forward_kernel, inner_part, feature_part...  32.2 us
    all_gather x1, blocking collectives, local(): qkv_full = lax.all_gather(qkv_half, 'outer', axis=0, tiled=True)  28.7 us
    pallas_call x8, Pallas kernels, whole_call(): pl.pallas_call(kernel, in_specs=[spec(operand.shape) for operand in opera...  19.7 us
    unnamed x61, local copies, waits for them, and re-layouts  8.69 us
    all_gather x1, blocking collectives, local(): qkv_half = lax.all_gather(qkv_pack, 'inner', axis=0, tiled=True)  8.06 us
  transfers between devices with their start and end apart: 13, of which 8 were waited for; matrix products, arithmetic and copies ran while one was open for 4% of the time, Pallas kernels for 32%

profile of v6, /device:TPU:0, one launch (start us, length us, event | category | flops | bytes accessed | tf_op | source)
XLA Modules:
  0.0 272.3 jit_solution(8335925299240712791)
XLA Ops:
  7.2 1.0 copy.79
  8.2 0.9 copy.72
  9.1 1.7 pad_maximum_fusion.1.weights_ref
  11.0 0.9 broadcast_in_dim.4
  11.9 4.4 %all-to-all-start = ((bf16[4,128,768]{2,1,0:T(8,128)(2,1)}), bf16[4,128,768]{2,1,0:T(8,128)(2,1)S(1)}, u32[]{:S(2)}, u32[]{:S(2)}) async-start(bf16[4,128,768]{2,1,0:T(8,128)(2,1)} %broadcast_in_dim.4), calls=%async_computation | async-start | bytes 1572864 | tf_op jit(solution)/shard_map/all_to_all | solution.py:1142
  17.4 8.1 %all_gather.30 = bf16[192,581]{1,0:T(8,128)(2,1)S(1)} all-gather(bf16[96,581]{1,0:T(8,128)(2,1)S(1)} %fusion.1), channel_id=1, replica_groups=mesh['outer'=4,'inner'=2,'tensor'=4] {'inner'}, dimensions={0}, use_global_device_ids=true | all-gather | bytes 334656 | tf_op jit(solution)/shard_map/all_gather | solution.py:1213
  25.6 28.7 %all_gather.31.weights_ref = bf16[768,581]{1,0:T(8,128)(2,1)S(1)} all-gather(bf16[192,581]{1,0:T(8,128)(2,1)S(1)} %all_gather.30), channel_id=1, replica_groups=mesh['outer'=4,'inner'=2,'tensor'=4] {'outer'}, dimensions={0}, use_global_device_ids=true | all-gather | bytes 1115520 | tf_op jit(solution)/shard_map/all_gather | solution.py:1214
  54.6 5.1 %all_gather.32 = bf16[4,2,192]{2,1,0:T(2,128)(2,1)S(1)} all-gather(bf16[1,2,192]{2,1,0:T(2,128)(2,1)S(1)} %copy.78), channel_id=1, replica_groups=mesh['outer'=4,'inner'=2,'tensor'=4] {'tensor'}, dimensions={0}, use_global_device_ids=true | all-gather | bytes 3840 | tf_op jit(solution)/shard_map/all_gather | solution.py:1218
  59.9 1.8 projections.1
  61.7 0.8 copy-done.2
  62.5 0.7 copy-done.4
  63.2 4.7 %all-to-all-start.1 = ((bf16[8,128,256]{2,1,0:T(8,128)(2,1)}), bf16[8,128,256]{2,1,0:T(8,128)(2,1)S(1)}, u32[]{:S(2)}, u32[]{:S(2)}) async-start(bf16[8,128,256]{2,1,0:T(8,128)(2,1)} %copy-done.2), calls=%async_computation.1 | async-start | bytes 1048576 | tf_op jit(solution)/shard_map/all_to_all | solution.py:1142
  68.0 1.1 constant_dynamic-slice_fusion.4
  69.1 2.0 collective-permute-start
  71.1 8.0 %collective-permute-done = bf16[1,128,768]{2,1,0:T(8,128)(2,1)S(1)} collective-permute-done((bf16[1,128,768]{2,1,0:T(8,128)(2,1)S(1)}, bf16[1,128,768]{2,1,0:T(8,128)(2,1)S(1)}, u32[]{:S(2)}, u32[]{:S(2)}) %collective-permute-start) | collective-permute-done | bytes 196640 | tf_op jit(solution)/shard_map/ppermute | solution.py:1251
  79.1 0.8 pad_maximum_fusion
  79.9 1.8 slice.77
  81.7 5.1 %all-to-all-done.1.packed_ref = bf16[8,128,256]{2,1,0:T(8,128)(2,1)S(1)} async-done(((bf16[8,128,256]{2,1,0:T(8,128)(2,1)}), bf16[8,128,256]{2,1,0:T(8,128)(2,1)S(1)}, u32[]{:S(2)}, u32[]{:S(2)}) %all-to-all-start.1) | async-done | bytes 524320 | tf_op jit(solution)/shard_map/all_to_all | solution.py:1142
  86.9 0.7 all-gather.10.cloned.1.call-update
  87.6 32.2 %chain_forward.1 = (bf16[8,64,128]{2,1,0:T(8,128)(2,1)}, bf16[1024,256]{1,0:T(8,128)(2,1)}, bf16[1024,256]{1,0:T(8,128)(2,1)}, f32[1024,256]{1,0:T(8,128)}, f32[...) custom-call(bf16[8,128,256]{2,1,0:T(8,128)(2,1)} %copy-done.9), custom_call_target="tpu_custom_call" | custom-call | flops 27000000512 | bytes 4194304 | tf_op jit(solution)/shard_map/chain_forward/pallas_call | solution.py:705
  119.8 3.4 %all-to-all-start.2 = ((bf16[8,64,128]{2,1,0:T(8,128)(2,1)}), bf16[8,64,128]{2,1,0:T(8,128)(2,1)S(1)}, u32[]{:S(2)}, u32[]{:S(2)}) async-start(bf16[8,64,128]{2,1,0:T(8,128)(2,1)} %get-tuple-element.66), calls=%async_computation.2 | async-start | bytes 262144 | tf_op jit(solution)/shard_map/all_to_all | solution.py:1142
  123.9 9.8 %all-to-all-done.2 = bf16[8,64,128]{2,1,0:T(8,128)(2,1)S(1)} async-done(((bf16[8,64,128]{2,1,0:T(8,128)(2,1)}), bf16[8,64,128]{2,1,0:T(8,128)(2,1)S(1)}, u32[]{:S(2)}, u32[]{:S(2)}) %all-to-all-start.2) | async-done | bytes 131104 | tf_op jit(solution)/shard_map/all_to_all | solution.py:1142
  133.7 6.9 %all_gather.34.heads_ref = bf16[4,3,2,64,128]{4,3,2,1,0:T(8,128)(2,1)} all-gather(bf16[1,3,2,64,128]{4,3,2,1,0:T(8,128)(2,1)S(1)} %bitcast.49), channel_id=1, replica_groups=mesh['outer'=4,'inner'=2,'tensor'=4] {'tensor'}, dimensions={0}, use_global_device_ids=true | all-gather | bytes 491520 | tf_op jit(solution)/shard_map/all_gather | solution.py:1261
  140.7 6.7 %feed_forward.1 = (bf16[4,4,32,768]{3,2,1,0:T(8,128)(2,1)}, f32[4,2,32,768]{3,2,1,0:T(8,128)}, bf16[256,768]{1,0:T(8,128)(2,1)}, bf16[256,1024]{1,0:T(8,128)(2,1...) custom-call(bf16[4,3,2,64,128]{4,3,2,1,0:T(8,128)(2,1)} %all_gather.34.heads_ref, bf16[4,128,768]{2,1,0:T(8,128)(2,1)} %copy-done, ...), custom_call_target="tpu_custom_call" | custom-call | tf_op jit(solution)/shard_map/feed_forward/pallas_call | solution.py:1127
  147.4 3.5 %all-to-all-start.3 = ((bf16[4,4,32,768]{3,2,1,0:T(8,128)(2,1)}), bf16[4,4,32,768]{3,2,1,0:T(8,128)(2,1)S(1)}, u32[]{:S(2)}, u32[]{:S(2)}) async-start(bf16[4,4,32,768]{3,2,1,0:T(8,128)(2,1)} %get-tuple-element.68), calls=%async_computation.3 | async-start | bytes 1572864 | tf_op jit(solution)/shard_map/all_to_all | solution.py:1142
  150.9 3.6 %feed_forward_grads.1 = bf16[768,1536]{1,0:T(8,128)(2,1)} custom-call(bf16[256,768]{1,0:T(8,128)(2,1)} %get-tuple-element.70.normed_ref, bf16[256,1024]{1,0:T(8,128)(2,1)} %get-tuple-element.71.back_ref, bf16[256,512]{1,0:T(8,128)(2,1)} %get-tuple-element.72.swiglu_ref, bf16[256,768]{1,0:T(8,128)(2,1)} %get-tuple-element.73.cot_ref), custom_call_target="tpu_custom_call" | custom-call | tf_op jit(solution)/shard_map/feed_forward_grads/pallas_call | solution.py:1127
  154.6 8.0 %all-to-all-done.3.terms_ref = bf16[4,4,32,768]{3,2,1,0:T(8,128)(2,1)S(1)} async-done(((bf16[4,4,32,768]{3,2,1,0:T(8,128)(2,1)}), bf16[4,4,32,768]{3,2,1,0:T(8,128)(2,1)S(1)}, u32[]{:S(2)}, u32[]{:S(2)}) %all-to-all-start.3) | async-done | bytes 786464 | tf_op jit(solution)/shard_map/all_to_all | solution.py:1142
  162.5 0.9 copy-done.7
  163.4 2.3 feed_forward_back.1
  165.7 2.9 %head_back.1 = bf16[32,16,128]{2,1,0:T(8,128)(2,1)} custom-call(bf16[2,32,768]{2,1,0:T(8,128)(2,1)} %get-tuple-element.80.grads_ref, bf16[4,768,192]{2,1,0:T(8,128)(2,1)} %bitcast.52), custom_call_target="tpu_custom_call" | custom-call | tf_op jit(solution)/shard_map/head_back/pallas_call | solution.py:1127
  168.6 2.6 all-to-all-start.4
  171.2 7.2 %all_gather.39.grads_ref = bf16[2,128,768]{2,1,0:T(8,128)(2,1)S(1)} all-gather(bf16[2,32,768]{2,1,0:T(8,128)(2,1)S(1)} %copy-done.10), channel_id=1, replica_groups=mesh['outer'=4,'inner'=2,'tensor'=4] {'tensor'}, dimensions={1}, use_global_device_ids=true | all-gather | bytes 491520 | tf_op jit(solution)/shard_map/all_gather | solution.py:1319
  178.4 1.2 out_grads.1
  179.6 1.3 all-to-all-done.4
  180.9 4.3 %all-to-all-start.6 = ((bf16[8,96,192]{2,1,0:T(8,128)(2,1)}), bf16[8,96,192]{2,1,0:T(8,128)(2,1)S(1)}, u32[]{:S(2)}, u32[]{:S(2)}) async-start(bf16[8,96,192]{2,1,0:T(8,128)(2,1)} %out_grads.1), calls=%async_computation.7 | async-start | bytes 786432 | tf_op jit(solution)/shard_map/all_to_all | solution.py:1142
  185.2 35.4 %chain_backward.1 = bf16[8,224,256]{2,1,0:T(8,128)(2,1)} custom-call(s32[1]{0:T(128)} %bitcast.22.sequence_ref, bf16[8,128,256]{2,1,0:T(8,128)(2,1)} %copy-done.9, bf16[4,2,128,768]{3,2,1,0:T(8,128)(2,1)} %bitcast.69, bf16[8,4,16,128]{3,2,1,0:T(8,128)(2,1)} %bitcast.64, bf16[1024,256]{1,0:T(8,128)(2,1)} %get-tuple-element.82.next_act.now_act, ...), custom_call_target="tpu_custom_call" | custom-call | flops 27000000512 | bytes 4194304 | tf_op jit(solution)/shard_map/chain_backward/pallas_call | solution.py:790
  220.6 6.1 %all-to-all-start.5 = ((bf16[8,224,256]{2,1,0:T(8,128)(2,1)}), bf16[8,224,256]{2,1,0:T(8,128)(2,1)S(1)}, u32[]{:S(2)}, u32[]{:S(2)}) async-start(bf16[8,224,256]{2,1,0:T(8,128)(2,1)} %chain_backward.1), calls=%async_computation.5 | async-start | bytes 1835008 | tf_op jit(solution)/shard_map/all_to_all | solution.py:1142
  226.9 0.7 copy.75
  228.1 1.0 copy-done.5
  229.1 1.0 matrix_outputs.1
  230.1 19.6 %all-to-all-done.5.received_ref = bf16[8,224,256]{2,1,0:T(8,128)(2,1)S(1)} async-done(((bf16[8,224,256]{2,1,0:T(8,128)(2,1)}), bf16[8,224,256]{2,1,0:T(8,128)(2,1)S(1)}, u32[]{:S(2)}, u32[]{:S(2)}) %all-to-all-start.5) | async-done | bytes 917536 | tf_op jit(solution)/shard_map/all_to_all | solution.py:1142
  249.7 1.6 tail.1
  251.3 0.8 copy-done.3
  252.2 3.5 %all-to-all-start.7 = ((bf16[4,80,768]{2,1,0:T(8,128)(2,1)}), bf16[4,80,768]{2,1,0:T(8,128)(2,1)S(1)}, u32[]{:S(2)}, u32[]{:S(2)}) async-start(bf16[4,80,768]{2,1,0:T(8,128)(2,1)} %copy-done.3), calls=%async_computation.8 | async-start | bytes 983040 | tf_op jit(solution)/shard_map/all_to_all | solution.py:1142
  256.3 0.7 copy.76
  257.0 0.7 copy.77
  258.6 5.6 %all-to-all-done.7.terms_ref = bf16[4,80,768]{2,1,0:T(8,128)(2,1)S(1)} async-done(((bf16[4,80,768]{2,1,0:T(8,128)(2,1)}), bf16[4,80,768]{2,1,0:T(8,128)(2,1)S(1)}, u32[]{:S(2)}, u32[]{:S(2)}) %all-to-all-start.7) | async-done | bytes 491552 | tf_op jit(solution)/shard_map/all_to_all | solution.py:1142
  264.1 1.0 input_grad.1
  (95 shorter events, 5.5 us)
Async XLA Ops:
  7.2 3.6 %copy-start.13 = (bf16[32,2,768]{2,1,0:T(2,128)(2,1)S(1)}, bf16[32,2,768]{2,1,0:T(2,128)(2,1)}, u32[]{:S(2)}) copy-start(bf16[32,2,768]{2,1,0:T(2,128)(2,1)} %param.15) | copy-start | bytes 294916
  7.2 3.7 %copy-start.14 = (bf16[32,2,768]{2,1,0:T(2,128)(2,1)S(1)}, bf16[32,2,768]{2,1,0:T(2,128)(2,1)}, u32[]{:S(2)}) copy-start(bf16[32,2,768]{2,1,0:T(2,128)(2,1)} %param.29) | copy-start | bytes 294916
  7.2 72.7 %all-gather.6.cloned.1.call-start = ((), (), s32[]{:S(2)}) async-start(), calls=%async_computation.9 | async-start | bytes 3096576 | tf_op jit(solution)/shard_map/all_gather | solution.py:1226
  10.9 5.4 %copy-start.11 = (bf16[96,3,192]{2,0,1:T(8,128)(2,1)S(1)}, bf16[96,3,192]{2,0,1:T(8,128)(2,1)}, u32[]{:S(2)}) copy-start(bf16[96,3,192]{2,0,1:T(8,128)(2,1)} %param.18) | copy-start | bytes 331780
  10.9 5.6 %copy-start.8 = (bf16[32,2,768]{2,0,1:T(8,128)(2,1)}, bf16[32,2,768]{2,0,1:T(8,128)(2,1)S(1)}, u32[]{:S(2)}) copy-start(bf16[32,2,768]{2,0,1:T(8,128)(2,1)S(1)} %copy.84) | copy-start | bytes 294916
  10.9 5.7 %copy-start.19 = (bf16[96,3]{0,1:T(4,128)(2,1)S(1)}, bf16[96,3]{0,1:T(4,128)(2,1)}, u32[]{:S(2)}) copy-start(bf16[96,3]{0,1:T(4,128)(2,1)} %param.19) | copy-start | bytes 1732
  10.9 5.8 %copy-start.24 = (bf16[24]{0:T(256)(128)(2,1)S(1)}, bf16[24]{0:T(256)(128)(2,1)}, u32[]{:S(2)}) copy-start(bf16[24]{0:T(256)(128)(2,1)} %param.17) | copy-start | bytes 148
  10.9 5.8 %copy-start.25 = (bf16[24]{0:T(256)(128)(2,1)S(1)}, bf16[24]{0:T(256)(128)(2,1)}, u32[]{:S(2)}) copy-start(bf16[24]{0:T(256)(128)(2,1)} %param.16) | copy-start | bytes 148
  11.0 5.9 %copy-start.17 = (bf16[3,32,64]{2,1,0:T(8,128)(2,1)S(1)}, bf16[3,32,64]{2,1,0:T(8,128)(2,1)}, u32[]{:S(2)}) copy-start(bf16[3,32,64]{2,1,0:T(8,128)(2,1)} %param.25) | copy-start | bytes 36868
  11.0 5.9 %copy-start.18 = (bf16[3,64,32]{1,2,0:T(8,128)(2,1)S(1)}, bf16[3,64,32]{1,2,0:T(8,128)(2,1)}, u32[]{:S(2)}) copy-start(bf16[3,64,32]{1,2,0:T(8,128)(2,1)} %param.23) | copy-start | bytes 36868
  11.9 5.2 %copy-start.20 = (bf16[3,8]{1,0:T(4,128)(2,1)S(1)}, bf16[3,8]{1,0:T(4,128)(2,1)}, u32[]{:S(2)}) copy-start(bf16[3,8]{1,0:T(4,128)(2,1)} %param.28) | copy-start | bytes 148
  11.9 5.2 %copy-start.21 = (bf16[3,8]{1,0:T(4,128)(2,1)S(1)}, bf16[3,8]{1,0:T(4,128)(2,1)}, u32[]{:S(2)}) copy-start(bf16[3,8]{1,0:T(4,128)(2,1)} %param.27) | copy-start | bytes 148
  11.9 5.2 %copy-start.22 = (bf16[3,8]{1,0:T(4,128)(2,1)S(1)}, bf16[3,8]{1,0:T(4,128)(2,1)}, u32[]{:S(2)}) copy-start(bf16[3,8]{1,0:T(4,128)(2,1)} %param.26) | copy-start | bytes 148
  11.9 5.2 %copy-start.23 = (bf16[3,32]{1,0:T(4,128)(2,1)S(1)}, bf16[3,32]{1,0:T(4,128)(2,1)}, u32[]{:S(2)}) copy-start(bf16[3,32]{1,0:T(4,128)(2,1)} %param.24) | copy-start | bytes 580
  11.9 42.4 %all-to-all-start = ((bf16[4,128,768]{2,1,0:T(8,128)(2,1)}), bf16[4,128,768]{2,1,0:T(8,128)(2,1)S(1)}, u32[]{:S(2)}, u32[]{:S(2)}) async-start(bf16[4,128,768]{2,1,0:T(8,128)(2,1)} %broadcast_in_dim.4), calls=%async_computation | async-start | bytes 1572864 | tf_op jit(solution)/shard_map/all_to_all | solution.py:1142
  54.4 8.9 %copy-start = (bf16[4,128,768]{2,1,0:T(8,128)(2,1)}, bf16[4,128,768]{2,1,0:T(8,128)(2,1)S(1)}, u32[]{:S(2)}) copy-start(bf16[4,128,768]{2,1,0:T(8,128)(2,1)S(1)} %all-to-all-done.rows_ref) | copy-start | bytes 2359300
  61.7 0.8 copy-start.2
  62.5 0.7 copy-start.4
  63.2 23.6 %all-to-all-start.1 = ((bf16[8,128,256]{2,1,0:T(8,128)(2,1)}), bf16[8,128,256]{2,1,0:T(8,128)(2,1)S(1)}, u32[]{:S(2)}, u32[]{:S(2)}) async-start(bf16[8,128,256]{2,1,0:T(8,128)(2,1)} %copy-done.2), calls=%async_computation.1 | async-start | bytes 1048576 | tf_op jit(solution)/shard_map/all_to_all | solution.py:1142
  68.0 72.7 %all-gather.8.cloned.1.call-start = ((), (), s32[]{:S(2)}) async-start(), calls=%async_computation.11 | async-start | bytes 1966080 | tf_op jit(solution)/shard_map/all_gather | solution.py:1255
  69.1 10.0 %collective-permute-start = (bf16[1,128,768]{2,1,0:T(8,128)(2,1)S(1)}, bf16[1,128,768]{2,1,0:T(8,128)(2,1)S(1)}, u32[]{:S(2)}, u32[]{:S(2)}) collective-permute-start(bf16[1,128,768]{2,1,0:T(8,128)(2,1)S(1)} %get-tuple-element.153), channel_id=1, source_target_pairs={{0,4},{4,0},{1,5},{5,1},{2,6},{6,2},{3,7},{7,3},{8,12},{12,8},{9,1... | collective-permute-start | bytes 589832 | tf_op jit(solution)/shard_map/ppermute | solution.py:1251
  86.8 0.8 copy-start.9
  86.8 75.7 %all-gather.10.cloned.1.call-start = ((), (), s32[]{:S(2)}) async-start(), calls=%async_computation.12 | async-start | bytes 1966080 | tf_op jit(solution)/shard_map/all_gather | solution.py:1254
  119.8 13.9 %all-to-all-start.2 = ((bf16[8,64,128]{2,1,0:T(8,128)(2,1)}), bf16[8,64,128]{2,1,0:T(8,128)(2,1)S(1)}, u32[]{:S(2)}, u32[]{:S(2)}) async-start(bf16[8,64,128]{2,1,0:T(8,128)(2,1)} %get-tuple-element.66), calls=%async_computation.2 | async-start | bytes 262144 | tf_op jit(solution)/shard_map/all_to_all | solution.py:1142
  147.4 15.1 %all-to-all-start.3 = ((bf16[4,4,32,768]{3,2,1,0:T(8,128)(2,1)}), bf16[4,4,32,768]{3,2,1,0:T(8,128)(2,1)S(1)}, u32[]{:S(2)}, u32[]{:S(2)}) async-start(bf16[4,4,32,768]{3,2,1,0:T(8,128)(2,1)} %get-tuple-element.68), calls=%async_computation.3 | async-start | bytes 1572864 | tf_op jit(solution)/shard_map/all_to_all | solution.py:1142
  150.9 77.2 %reduce-scatter.2.cloned.1.call-start = ((), (), s32[]{:S(2)}) async-start(), calls=%async_computation.10 | async-start | bytes 2654208 | tf_op jit(solution)/shard_map/reduce_scatter | solution.py:1286
  162.5 0.9 copy-start.7
  165.7 5.5 %copy-start.10 = (bf16[2,32,768]{2,1,0:T(8,128)(2,1)S(1)}, bf16[2,32,768]{2,1,0:T(8,128)(2,1)}, u32[]{:S(2)}) copy-start(bf16[2,32,768]{2,1,0:T(8,128)(2,1)} %get-tuple-element.80.grads_ref) | copy-start | bytes 294916
  168.6 12.3 %all-to-all-start.4 = ((bf16[32,16,128]{2,1,0:T(8,128)(2,1)}), bf16[32,16,128]{2,1,0:T(8,128)(2,1)S(1)}, u32[]{:S(2)}, u32[]{:S(2)}) async-start(bf16[32,16,128]{2,1,0:T(8,128)(2,1)} %head_back.1), calls=%async_computation.4 | async-start | bytes 262144 | tf_op jit(solution)/shard_map/all_to_all | solution.py:1142
  180.9 4.3 %copy-start.12 = (bf16[32,16,128]{2,1,0:T(8,128)(2,1)}, bf16[32,16,128]{2,1,0:T(8,128)(2,1)S(1)}, u32[]{:S(2)}) copy-start(bf16[32,16,128]{2,1,0:T(8,128)(2,1)S(1)} %all-to-all-done.4) | copy-start | bytes 393220
  180.9 39.7 %all-to-all-start.6 = ((bf16[8,96,192]{2,1,0:T(8,128)(2,1)}), bf16[8,96,192]{2,1,0:T(8,128)(2,1)S(1)}, u32[]{:S(2)}, u32[]{:S(2)}) async-start(bf16[8,96,192]{2,1,0:T(8,128)(2,1)} %out_grads.1), calls=%async_computation.7 | async-start | bytes 786432 | tf_op jit(solution)/shard_map/all_to_all | solution.py:1142
  220.6 6.4 %copy-start.15 = (bf16[2,32,768]{2,1,0:T(8,128)(2,1)S(1)}, bf16[2,32,768]{2,1,0:T(8,128)(2,1)}, u32[]{:S(2)}) copy-start(bf16[2,32,768]{2,1,0:T(8,128)(2,1)} %get-tuple-element.76) | copy-start | bytes 294916
  220.6 7.5 %copy-start.1 = (bf16[96,1728]{1,0:T(8,128)(2,1)S(1)}, bf16[96,1728]{1,0:T(8,128)(2,1)}, u32[]{:S(2)}) copy-start(bf16[96,1728]{1,0:T(8,128)(2,1)} %pad_maximum_fusion.1.weights_ref) | copy-start | bytes 995332
  220.6 29.1 %all-to-all-start.5 = ((bf16[8,224,256]{2,1,0:T(8,128)(2,1)}), bf16[8,224,256]{2,1,0:T(8,128)(2,1)S(1)}, u32[]{:S(2)}, u32[]{:S(2)}) async-start(bf16[8,224,256]{2,1,0:T(8,128)(2,1)} %chain_backward.1), calls=%async_computation.5 | async-start | bytes 1835008 | tf_op jit(solution)/shard_map/all_to_all | solution.py:1142
  228.1 1.0 copy-start.5
  249.7 14.4 %copy-start.6 = (f32[2,32,768]{2,1,0:T(8,128)S(1)}, f32[2,32,768]{2,1,0:T(8,128)}, u32[]{:S(2)}) copy-start(f32[2,32,768]{2,1,0:T(8,128)} %get-tuple-element.98.back_ref) | copy-start | bytes 589828
  251.3 0.8 copy-start.3
  252.2 11.9 %all-to-all-start.7 = ((bf16[4,80,768]{2,1,0:T(8,128)(2,1)}), bf16[4,80,768]{2,1,0:T(8,128)(2,1)S(1)}, u32[]{:S(2)}, u32[]{:S(2)}) async-start(bf16[4,80,768]{2,1,0:T(8,128)(2,1)} %copy-done.3), calls=%async_computation.8 | async-start | bytes 983040 | tf_op jit(solution)/shard_map/all_to_all | solution.py:1142
  257.9 7.8 %copy-start.16 = (f32[3,128]{1,0:T(4,128)}, f32[3,128]{1,0:T(4,128)S(1)}, u32[]{:S(2)}) copy-start(f32[3,128]{1,0:T(4,128)S(1)} %slice_reduce_fusion) | copy-start | bytes 4612
Sparse Core Ops, SparseCore 0:
  10.9 68.6 all-gather.5
  87.0 18.1 all-gather.7
  106.8 39.9 all-gather.9
  154.9 73.1 reduce-scatter.1

commit v7 on v6

--- a/solution.py
+++ b/solution.py
@@ -980,7 +980,7 @@
         grads_ref[:, at] = dot_nn(cot, swiglu_ref[:, first : first + 256]).astype(bf16)
 
 
-def head_back_kernel(grads_ref, out_ref, back_ref):
+def head_back(grads_ref, out_ref, back_ref):
     tensor_count = out_ref.shape[0]
     seq_count, rows, _ = grads_ref.shape
     head_count = out_ref.shape[2] // HEAD_DIM
@@ -1025,7 +1025,16 @@
 
 
 def feed_forward_back_kernel(
-    rank_ref, terms_ref, mixed_ref, cot_ref, gain_ref, back_ref, low_ref, result_ref
+    rank_ref,
+    terms_ref,
+    mixed_ref,
+    cot_ref,
+    gain_ref,
+    out_ref,
+    back_ref,
+    low_ref,
+    result_ref,
+    heads_ref,
 ):
     seq_count = mixed_ref.shape[1]
     for sequence in range(seq_count):
@@ -1041,6 +1050,7 @@
         back_ref[sequence] = back
         low_ref[sequence] = back.astype(bf16)
         result_ref[sequence] = (mixed + down).astype(bf16)
+    head_back(low_ref, out_ref, heads_ref)
 
 
 def input_grad_kernel(terms_ref, tokens_ref, back_ref, gain_ref, grad_ref, gains_ref):
@@ -1289,30 +1299,32 @@
     own_cot = own_cot.reshape(own_shape)
 
     def fixed(operand):
-        return pl.BlockSpec(operand.shape, lambda turn, _: (0,) * operand.ndim)
+        return pl.BlockSpec(operand.shape, lambda turn, _: (0,) * len(operand.shape))
 
     chosen_mixed = pl.BlockSpec((1,) + own_shape, lambda turn, chosen: (chosen[0], 0, 0, 0))
     own_block = pl.BlockSpec(own_shape, lambda turn, _: (0, 0, 0))
-    back_mixed, back_low, result = pl.pallas_call(
+    head_shape = shape(
+        (device_count * tensor_count, local_rows // 2, 2 * HEAD_DIM), bf16
+    )
+    back_mixed, back_low, result, back_head = pl.pallas_call(
         feed_forward_back_kernel,
         grid_spec=pltpu.PrefetchScalarGridSpec(
             num_scalar_prefetch=1,
             grid=(1,),
-            in_specs=[fixed(ffn_sums), chosen_mixed, own_block, fixed(scale_ffn)],
-            out_specs=[own_block] * 3,
+            in_specs=[
+                fixed(ffn_sums),
+                chosen_mixed,
+                own_block,
+                fixed(scale_ffn),
+                fixed(out_full),
+            ],
+            out_specs=[own_block] * 3 + [fixed(head_shape)],
         ),
-        out_shape=[shape(own_shape, dtype) for dtype in (f32, bf16, bf16)],
+        out_shape=[shape(own_shape, dtype) for dtype in (f32, bf16, bf16)] + [head_shape],
         compiler_params=pltpu.CompilerParams(vmem_limit_bytes=VMEM_BYTES),
         name="feed_forward_back",
-    )(jnp.reshape(rank, (1,)).astype(jnp.int32), ffn_sums, mixed, own_cot, scale_ffn)
+    )(jnp.reshape(rank, (1,)).astype(jnp.int32), ffn_sums, mixed, own_cot, scale_ffn, out_full)
     result = result.transpose(1, 0, 2)
-    (back_head,) = whole_call(
-        head_back_kernel,
-        "head_back",
-        (back_low, out_full),
-        (shape((device_count * tensor_count, local_rows // 2, 2 * HEAD_DIM), bf16),),
-        VMEM_BYTES,
-    )
     back_head, back_low = ordered(back_head, back_low)
     head_grad = exchange(back_head, DP + ("tensor",))
     head_grad = head_grad.reshape(device_count, tensor_count, local_rows // 2, 2 * HEAD_DIM)

time: 273 us -> 272 us (level)
    pallas_call x8 -> x7, Pallas kernels: 19.7 us -> 16.9 us  [whole_call(): pl.pallas_call(kernel, in_specs=[spec(operand.shape) for operand in opera...]
    unnamed x61 -> x59, local copies, waits for them, and re-layouts: 8.69 us -> 8.67 us
where the time goes in v7:
time: 272 us; the launch traced here: 271 us
  Pallas kernels  87.9 us (32%)
  waiting for transfers between devices  58.5 us (22%)
  blocking collectives  56.5 us (21%)
  starting transfers between devices  34.5 us (13%)
  local copies, waits for them, and re-layouts  16.4 us (6%)
  between operations  14.2 us (5%)
  other arithmetic  2.85 us (1%)
    all_to_all x8, waiting for transfers between devices, exchange(): return lax.all_to_all(values, axis, 0, 0, tiled=False)  47.4 us
    pallas_call x1, Pallas kernels, chain_backward(): pl.pallas_call(functools.partial(backward_kernel, inner_part, feature_par...  35.4 us
    all_to_all x8, starting transfers between devices, exchange(): return lax.all_to_all(values, axis, 0, 0, tiled=False)  32.3 us
    pallas_call x1, Pallas kernels, chain_forward(): pl.pallas_call(functools.partial(forward_kernel, inner_part, feature_part...  32.2 us
    all_gather x1, blocking collectives, local(): qkv_full = lax.all_gather(qkv_half, 'outer', axis=0, tiled=True)  28.7 us
    pallas_call x7, Pallas kernels, whole_call(): pl.pallas_call(kernel, in_specs=[spec(operand.shape) for operand in opera...  16.9 us
    unnamed x59, local copies, waits for them, and re-layouts  8.67 us
    all_gather x1, blocking collectives, local(): qkv_half = lax.all_gather(qkv_pack, 'inner', axis=0, tiled=True)  8.07 us
  transfers between devices with their start and end apart: 13, of which 8 were waited for; matrix products, arithmetic and copies ran while one was open for 4% of the time, Pallas kernels for 32%

profile of v7, /device:TPU:0, one launch (start us, length us, event | category | flops | bytes accessed | tf_op | source)
XLA Modules:
  0.0 270.8 jit_solution(1097371530899230020)
XLA Ops:
  7.2 1.0 copy.79
  8.2 0.9 copy.72
  9.1 1.7 pad_maximum_fusion.1.weights_ref
  11.0 0.9 broadcast_in_dim.4
  11.9 4.4 %all-to-all-start = ((bf16[4,128,768]{2,1,0:T(8,128)(2,1)}), bf16[4,128,768]{2,1,0:T(8,128)(2,1)S(1)}, u32[]{:S(2)}, u32[]{:S(2)}) async-start(bf16[4,128,768]{2,1,0:T(8,128)(2,1)} %broadcast_in_dim.4), calls=%async_computation | async-start | bytes 1572864 | tf_op jit(solution)/shard_map/all_to_all | solution.py:1152
  17.5 8.1 %all_gather.30 = bf16[192,581]{1,0:T(8,128)(2,1)S(1)} all-gather(bf16[96,581]{1,0:T(8,128)(2,1)S(1)} %fusion.1), channel_id=1, replica_groups=mesh['outer'=4,'inner'=2,'tensor'=4] {'inner'}, dimensions={0}, use_global_device_ids=true | all-gather | bytes 334656 | tf_op jit(solution)/shard_map/all_gather | solution.py:1223
  25.7 28.7 %all_gather.31.weights_ref = bf16[768,581]{1,0:T(8,128)(2,1)S(1)} all-gather(bf16[192,581]{1,0:T(8,128)(2,1)S(1)} %all_gather.30), channel_id=1, replica_groups=mesh['outer'=4,'inner'=2,'tensor'=4] {'outer'}, dimensions={0}, use_global_device_ids=true | all-gather | bytes 1115520 | tf_op jit(solution)/shard_map/all_gather | solution.py:1224
  54.6 5.1 %all_gather.32 = bf16[4,2,192]{2,1,0:T(2,128)(2,1)S(1)} all-gather(bf16[1,2,192]{2,1,0:T(2,128)(2,1)S(1)} %copy.78), channel_id=1, replica_groups=mesh['outer'=4,'inner'=2,'tensor'=4] {'tensor'}, dimensions={0}, use_global_device_ids=true | all-gather | bytes 3840 | tf_op jit(solution)/shard_map/all_gather | solution.py:1228
  59.9 1.8 projections.1
  61.7 0.8 copy-done.2
  62.5 0.7 copy-done.4
  63.2 4.7 %all-to-all-start.1 = ((bf16[8,128,256]{2,1,0:T(8,128)(2,1)}), bf16[8,128,256]{2,1,0:T(8,128)(2,1)S(1)}, u32[]{:S(2)}, u32[]{:S(2)}) async-start(bf16[8,128,256]{2,1,0:T(8,128)(2,1)} %copy-done.2), calls=%async_computation.1 | async-start | bytes 1048576 | tf_op jit(solution)/shard_map/all_to_all | solution.py:1152
  68.0 1.1 constant_dynamic-slice_fusion.4
  69.1 2.0 collective-permute-start
  71.1 8.0 %collective-permute-done = bf16[1,128,768]{2,1,0:T(8,128)(2,1)S(1)} collective-permute-done((bf16[1,128,768]{2,1,0:T(8,128)(2,1)S(1)}, bf16[1,128,768]{2,1,0:T(8,128)(2,1)S(1)}, u32[]{:S(2)}, u32[]{:S(2)}) %collective-permute-start) | collective-permute-done | bytes 196640 | tf_op jit(solution)/shard_map/ppermute | solution.py:1261
  79.1 0.8 pad_maximum_fusion
  79.9 1.8 slice.77
  81.7 5.2 %all-to-all-done.1.packed_ref = bf16[8,128,256]{2,1,0:T(8,128)(2,1)S(1)} async-done(((bf16[8,128,256]{2,1,0:T(8,128)(2,1)}), bf16[8,128,256]{2,1,0:T(8,128)(2,1)S(1)}, u32[]{:S(2)}, u32[]{:S(2)}) %all-to-all-start.1) | async-done | bytes 524320 | tf_op jit(solution)/shard_map/all_to_all | solution.py:1152
  86.9 0.7 all-gather.10.cloned.1.call-update
  87.6 32.2 %chain_forward.1 = (bf16[8,64,128]{2,1,0:T(8,128)(2,1)}, bf16[1024,256]{1,0:T(8,128)(2,1)}, bf16[1024,256]{1,0:T(8,128)(2,1)}, f32[1024,256]{1,0:T(8,128)}, f32[...) custom-call(bf16[8,128,256]{2,1,0:T(8,128)(2,1)} %copy-done.9), custom_call_target="tpu_custom_call" | custom-call | flops 27000000512 | bytes 4194304 | tf_op jit(solution)/shard_map/chain_forward/pallas_call | solution.py:705
  119.9 3.4 %all-to-all-start.2 = ((bf16[8,64,128]{2,1,0:T(8,128)(2,1)}), bf16[8,64,128]{2,1,0:T(8,128)(2,1)S(1)}, u32[]{:S(2)}, u32[]{:S(2)}) async-start(bf16[8,64,128]{2,1,0:T(8,128)(2,1)} %get-tuple-element.67), calls=%async_computation.2 | async-start | bytes 262144 | tf_op jit(solution)/shard_map/all_to_all | solution.py:1152
  123.9 9.8 %all-to-all-done.2 = bf16[8,64,128]{2,1,0:T(8,128)(2,1)S(1)} async-done(((bf16[8,64,128]{2,1,0:T(8,128)(2,1)}), bf16[8,64,128]{2,1,0:T(8,128)(2,1)S(1)}, u32[]{:S(2)}, u32[]{:S(2)}) %all-to-all-start.2) | async-done | bytes 131104 | tf_op jit(solution)/shard_map/all_to_all | solution.py:1152
  133.8 6.9 %all_gather.34.heads_ref = bf16[4,3,2,64,128]{4,3,2,1,0:T(8,128)(2,1)} all-gather(bf16[1,3,2,64,128]{4,3,2,1,0:T(8,128)(2,1)S(1)} %bitcast.49), channel_id=1, replica_groups=mesh['outer'=4,'inner'=2,'tensor'=4] {'tensor'}, dimensions={0}, use_global_device_ids=true | all-gather | bytes 491520 | tf_op jit(solution)/shard_map/all_gather | solution.py:1271
  140.7 6.7 %feed_forward.1 = (bf16[4,4,32,768]{3,2,1,0:T(8,128)(2,1)}, f32[4,2,32,768]{3,2,1,0:T(8,128)}, bf16[256,768]{1,0:T(8,128)(2,1)}, bf16[256,1024]{1,0:T(8,128)(2,1...) custom-call(bf16[4,3,2,64,128]{4,3,2,1,0:T(8,128)(2,1)} %all_gather.34.heads_ref, bf16[4,128,768]{2,1,0:T(8,128)(2,1)} %copy-done, ...), custom_call_target="tpu_custom_call" | custom-call | tf_op jit(solution)/shard_map/feed_forward/pallas_call | solution.py:1137
  147.4 3.5 %all-to-all-start.3 = ((bf16[4,4,32,768]{3,2,1,0:T(8,128)(2,1)}), bf16[4,4,32,768]{3,2,1,0:T(8,128)(2,1)S(1)}, u32[]{:S(2)}, u32[]{:S(2)}) async-start(bf16[4,4,32,768]{3,2,1,0:T(8,128)(2,1)} %get-tuple-element.69), calls=%async_computation.3 | async-start | bytes 1572864 | tf_op jit(solution)/shard_map/all_to_all | solution.py:1152
  151.0 3.6 %feed_forward_grads.1 = bf16[768,1536]{1,0:T(8,128)(2,1)} custom-call(bf16[256,768]{1,0:T(8,128)(2,1)} %get-tuple-element.71.normed_ref, bf16[256,1024]{1,0:T(8,128)(2,1)} %get-tuple-element.72.back_ref, bf16[256,512]{1,0:T(8,128)(2,1)} %get-tuple-element.73.swiglu_ref, bf16[256,768]{1,0:T(8,128)(2,1)} %get-tuple-element.74.cot_ref), custom_call_target="tpu_custom_call" | custom-call | tf_op jit(solution)/shard_map/feed_forward_grads/pallas_call | solution.py:1137
  154.6 8.0 %all-to-all-done.3.terms_ref = bf16[4,4,32,768]{3,2,1,0:T(8,128)(2,1)S(1)} async-done(((bf16[4,4,32,768]{3,2,1,0:T(8,128)(2,1)}), bf16[4,4,32,768]{3,2,1,0:T(8,128)(2,1)S(1)}, u32[]{:S(2)}, u32[]{:S(2)}) %all-to-all-start.3) | async-done | bytes 786464 | tf_op jit(solution)/shard_map/all_to_all | solution.py:1152
  162.6 0.9 copy-done.7
  163.5 3.4 %feed_forward_back.1 = (f32[2,32,768]{2,1,0:T(8,128)}, bf16[2,32,768]{2,1,0:T(8,128)(2,1)}, bf16[2,32,768]{2,1,0:T(8,128)(2,1)}, bf16[32,16,128]{2,1,0:T(8,128)(2,1)}) custom-call(s32[1]{0:T(128)} %bitcast.rank_ref, bf16[4,4,32,768]{3,2,1,0:T(8,128)(2,1)} %copy-done.7, f32[4,2,32,768]{3,2,1,0:T(8,128)} %get-tuple-element.76.mixed_ref, ...), custom_call_target="tpu_custom_call" | custom-call | tf_op jit(solution)/shard_map/feed_forward_back/pallas_call | solution.py:1309
  166.9 2.6 all-to-all-start.4
  169.5 7.7 %all_gather.39.grads_ref = bf16[2,128,768]{2,1,0:T(8,128)(2,1)S(1)} all-gather(bf16[2,32,768]{2,1,0:T(8,128)(2,1)} %get-tuple-element.82), channel_id=1, replica_groups=mesh['outer'=4,'inner'=2,'tensor'=4] {'tensor'}, dimensions={1}, use_global_device_ids=true | all-gather | bytes 491520 | tf_op jit(solution)/shard_map/all_gather | solution.py:1331
  177.2 1.2 out_grads.1
  178.3 1.2 all-to-all-done.4
  179.6 4.2 %all-to-all-start.6 = ((bf16[8,96,192]{2,1,0:T(8,128)(2,1)}), bf16[8,96,192]{2,1,0:T(8,128)(2,1)S(1)}, u32[]{:S(2)}, u32[]{:S(2)}) async-start(bf16[8,96,192]{2,1,0:T(8,128)(2,1)} %out_grads.1), calls=%async_computation.7 | async-start | bytes 786432 | tf_op jit(solution)/shard_map/all_to_all | solution.py:1152
  183.8 35.4 %chain_backward.1 = bf16[8,224,256]{2,1,0:T(8,128)(2,1)} custom-call(s32[1]{0:T(128)} %bitcast.22.sequence_ref, bf16[8,128,256]{2,1,0:T(8,128)(2,1)} %copy-done.9, bf16[4,2,128,768]{3,2,1,0:T(8,128)(2,1)} %bitcast.69, bf16[8,4,16,128]{3,2,1,0:T(8,128)(2,1)} %bitcast.64, bf16[1024,256]{1,0:T(8,128)(2,1)} %get-tuple-element.84.next_act.now_act, ...), custom_call_target="tpu_custom_call" | custom-call | flops 27000000512 | bytes 4194304 | tf_op jit(solution)/shard_map/chain_backward/pallas_call | solution.py:790
  219.2 6.1 %all-to-all-start.5 = ((bf16[8,224,256]{2,1,0:T(8,128)(2,1)}), bf16[8,224,256]{2,1,0:T(8,128)(2,1)S(1)}, u32[]{:S(2)}, u32[]{:S(2)}) async-start(bf16[8,224,256]{2,1,0:T(8,128)(2,1)} %chain_backward.1), calls=%async_computation.5 | async-start | bytes 1835008 | tf_op jit(solution)/shard_map/all_to_all | solution.py:1152
  225.5 0.7 copy.75
  226.3 2.3 reduce-scatter.2.cloned.1.call-done.sums_ref
  228.6 1.0 copy-done.5
  229.5 1.0 matrix_outputs.1
  230.5 17.7 %all-to-all-done.5.received_ref = bf16[8,224,256]{2,1,0:T(8,128)(2,1)S(1)} async-done(((bf16[8,224,256]{2,1,0:T(8,128)(2,1)}), bf16[8,224,256]{2,1,0:T(8,128)(2,1)S(1)}, u32[]{:S(2)}, u32[]{:S(2)}) %all-to-all-start.5) | async-done | bytes 917536 | tf_op jit(solution)/shard_map/all_to_all | solution.py:1152
  248.2 1.6 tail.1
  249.8 0.8 copy-done.3
  250.7 3.5 %all-to-all-start.7 = ((bf16[4,80,768]{2,1,0:T(8,128)(2,1)}), bf16[4,80,768]{2,1,0:T(8,128)(2,1)S(1)}, u32[]{:S(2)}, u32[]{:S(2)}) async-start(bf16[4,80,768]{2,1,0:T(8,128)(2,1)} %copy-done.3), calls=%async_computation.8 | async-start | bytes 983040 | tf_op jit(solution)/shard_map/all_to_all | solution.py:1152
  254.8 0.7 copy.76
  255.5 0.7 copy.77
  257.1 5.6 %all-to-all-done.7.terms_ref = bf16[4,80,768]{2,1,0:T(8,128)(2,1)S(1)} async-done(((bf16[4,80,768]{2,1,0:T(8,128)(2,1)}), bf16[4,80,768]{2,1,0:T(8,128)(2,1)S(1)}, u32[]{:S(2)}, u32[]{:S(2)}) %all-to-all-start.7) | async-done | bytes 491552 | tf_op jit(solution)/shard_map/all_to_all | solution.py:1152
  262.6 1.0 input_grad.1
  (92 shorter events, 5.0 us)
Async XLA Ops:
  7.2 3.6 %copy-start.12 = (bf16[32,2,768]{2,1,0:T(2,128)(2,1)S(1)}, bf16[32,2,768]{2,1,0:T(2,128)(2,1)}, u32[]{:S(2)}) copy-start(bf16[32,2,768]{2,1,0:T(2,128)(2,1)} %param.15) | copy-start | bytes 294916
  7.2 3.7 %copy-start.13 = (bf16[32,2,768]{2,1,0:T(2,128)(2,1)S(1)}, bf16[32,2,768]{2,1,0:T(2,128)(2,1)}, u32[]{:S(2)}) copy-start(bf16[32,2,768]{2,1,0:T(2,128)(2,1)} %param.29) | copy-start | bytes 294916
  7.2 72.7 %all-gather.6.cloned.1.call-start = ((), (), s32[]{:S(2)}) async-start(), calls=%async_computation.9 | async-start | bytes 3096576 | tf_op jit(solution)/shard_map/all_gather | solution.py:1236
  10.9 5.4 %copy-start.10 = (bf16[96,3,192]{2,0,1:T(8,128)(2,1)S(1)}, bf16[96,3,192]{2,0,1:T(8,128)(2,1)}, u32[]{:S(2)}) copy-start(bf16[96,3,192]{2,0,1:T(8,128)(2,1)} %param.18) | copy-start | bytes 331780
  10.9 5.6 %copy-start.8 = (bf16[32,2,768]{2,0,1:T(8,128)(2,1)}, bf16[32,2,768]{2,0,1:T(8,128)(2,1)S(1)}, u32[]{:S(2)}) copy-start(bf16[32,2,768]{2,0,1:T(8,128)(2,1)S(1)} %copy.84) | copy-start | bytes 294916
  10.9 5.7 %copy-start.18 = (bf16[96,3]{0,1:T(4,128)(2,1)S(1)}, bf16[96,3]{0,1:T(4,128)(2,1)}, u32[]{:S(2)}) copy-start(bf16[96,3]{0,1:T(4,128)(2,1)} %param.19) | copy-start | bytes 1732
  10.9 5.8 %copy-start.23 = (bf16[24]{0:T(256)(128)(2,1)S(1)}, bf16[24]{0:T(256)(128)(2,1)}, u32[]{:S(2)}) copy-start(bf16[24]{0:T(256)(128)(2,1)} %param.17) | copy-start | bytes 148
  11.0 5.8 %copy-start.24 = (bf16[24]{0:T(256)(128)(2,1)S(1)}, bf16[24]{0:T(256)(128)(2,1)}, u32[]{:S(2)}) copy-start(bf16[24]{0:T(256)(128)(2,1)} %param.16) | copy-start | bytes 148
  11.0 5.9 %copy-start.16 = (bf16[3,32,64]{2,1,0:T(8,128)(2,1)S(1)}, bf16[3,32,64]{2,1,0:T(8,128)(2,1)}, u32[]{:S(2)}) copy-start(bf16[3,32,64]{2,1,0:T(8,128)(2,1)} %param.25) | copy-start | bytes 36868
  11.0 5.9 %copy-start.17 = (bf16[3,64,32]{1,2,0:T(8,128)(2,1)S(1)}, bf16[3,64,32]{1,2,0:T(8,128)(2,1)}, u32[]{:S(2)}) copy-start(bf16[3,64,32]{1,2,0:T(8,128)(2,1)} %param.23) | copy-start | bytes 36868
  11.9 5.2 %copy-start.19 = (bf16[3,8]{1,0:T(4,128)(2,1)S(1)}, bf16[3,8]{1,0:T(4,128)(2,1)}, u32[]{:S(2)}) copy-start(bf16[3,8]{1,0:T(4,128)(2,1)} %param.28) | copy-start | bytes 148
  11.9 5.2 %copy-start.20 = (bf16[3,8]{1,0:T(4,128)(2,1)S(1)}, bf16[3,8]{1,0:T(4,128)(2,1)}, u32[]{:S(2)}) copy-start(bf16[3,8]{1,0:T(4,128)(2,1)} %param.27) | copy-start | bytes 148
  11.9 5.2 %copy-start.21 = (bf16[3,8]{1,0:T(4,128)(2,1)S(1)}, bf16[3,8]{1,0:T(4,128)(2,1)}, u32[]{:S(2)}) copy-start(bf16[3,8]{1,0:T(4,128)(2,1)} %param.26) | copy-start | bytes 148
  11.9 5.2 %copy-start.22 = (bf16[3,32]{1,0:T(4,128)(2,1)S(1)}, bf16[3,32]{1,0:T(4,128)(2,1)}, u32[]{:S(2)}) copy-start(bf16[3,32]{1,0:T(4,128)(2,1)} %param.24) | copy-start | bytes 580
  11.9 42.4 %all-to-all-start = ((bf16[4,128,768]{2,1,0:T(8,128)(2,1)}), bf16[4,128,768]{2,1,0:T(8,128)(2,1)S(1)}, u32[]{:S(2)}, u32[]{:S(2)}) async-start(bf16[4,128,768]{2,1,0:T(8,128)(2,1)} %broadcast_in_dim.4), calls=%async_computation | async-start | bytes 1572864 | tf_op jit(solution)/shard_map/all_to_all | solution.py:1152
  54.4 8.9 %copy-start = (bf16[4,128,768]{2,1,0:T(8,128)(2,1)}, bf16[4,128,768]{2,1,0:T(8,128)(2,1)S(1)}, u32[]{:S(2)}) copy-start(bf16[4,128,768]{2,1,0:T(8,128)(2,1)S(1)} %all-to-all-done.rows_ref) | copy-start | bytes 2359300
  61.7 0.8 copy-start.2
  62.5 0.7 copy-start.4
  63.2 23.6 %all-to-all-start.1 = ((bf16[8,128,256]{2,1,0:T(8,128)(2,1)}), bf16[8,128,256]{2,1,0:T(8,128)(2,1)S(1)}, u32[]{:S(2)}, u32[]{:S(2)}) async-start(bf16[8,128,256]{2,1,0:T(8,128)(2,1)} %copy-done.2), calls=%async_computation.1 | async-start | bytes 1048576 | tf_op jit(solution)/shard_map/all_to_all | solution.py:1152
  68.0 72.7 %all-gather.8.cloned.1.call-start = ((), (), s32[]{:S(2)}) async-start(), calls=%async_computation.11 | async-start | bytes 1966080 | tf_op jit(solution)/shard_map/all_gather | solution.py:1265
  69.1 10.0 %collective-permute-start = (bf16[1,128,768]{2,1,0:T(8,128)(2,1)S(1)}, bf16[1,128,768]{2,1,0:T(8,128)(2,1)S(1)}, u32[]{:S(2)}, u32[]{:S(2)}) collective-permute-start(bf16[1,128,768]{2,1,0:T(8,128)(2,1)S(1)} %get-tuple-element.155), channel_id=1, source_target_pairs={{0,4},{4,0},{1,5},{5,1},{2,6},{6,2},{3,7},{7,3},{8,12},{12,8},{9,1... | collective-permute-start | bytes 589832 | tf_op jit(solution)/shard_map/ppermute | solution.py:1261
  86.8 0.8 copy-start.9
  86.8 75.7 %all-gather.10.cloned.1.call-start = ((), (), s32[]{:S(2)}) async-start(), calls=%async_computation.12 | async-start | bytes 1966080 | tf_op jit(solution)/shard_map/all_gather | solution.py:1264
  119.9 13.9 %all-to-all-start.2 = ((bf16[8,64,128]{2,1,0:T(8,128)(2,1)}), bf16[8,64,128]{2,1,0:T(8,128)(2,1)S(1)}, u32[]{:S(2)}, u32[]{:S(2)}) async-start(bf16[8,64,128]{2,1,0:T(8,128)(2,1)} %get-tuple-element.67), calls=%async_computation.2 | async-start | bytes 262144 | tf_op jit(solution)/shard_map/all_to_all | solution.py:1152
  147.4 15.1 %all-to-all-start.3 = ((bf16[4,4,32,768]{3,2,1,0:T(8,128)(2,1)}), bf16[4,4,32,768]{3,2,1,0:T(8,128)(2,1)S(1)}, u32[]{:S(2)}, u32[]{:S(2)}) async-start(bf16[4,4,32,768]{3,2,1,0:T(8,128)(2,1)} %get-tuple-element.69), calls=%async_computation.3 | async-start | bytes 1572864 | tf_op jit(solution)/shard_map/all_to_all | solution.py:1152
  150.9 77.6 %reduce-scatter.2.cloned.1.call-start = ((), (), s32[]{:S(2)}) async-start(), calls=%async_computation.10 | async-start | bytes 2654208 | tf_op jit(solution)/shard_map/reduce_scatter | solution.py:1296
  162.6 0.9 copy-start.7
  166.9 12.7 %all-to-all-start.4 = ((bf16[32,16,128]{2,1,0:T(8,128)(2,1)}), bf16[32,16,128]{2,1,0:T(8,128)(2,1)S(1)}, u32[]{:S(2)}, u32[]{:S(2)}) async-start(bf16[32,16,128]{2,1,0:T(8,128)(2,1)} %get-tuple-element.81), calls=%async_computation.4 | async-start | bytes 262144 | tf_op jit(solution)/shard_map/all_to_all | solution.py:1152
  179.6 4.2 %copy-start.11 = (bf16[32,16,128]{2,1,0:T(8,128)(2,1)}, bf16[32,16,128]{2,1,0:T(8,128)(2,1)S(1)}, u32[]{:S(2)}) copy-start(bf16[32,16,128]{2,1,0:T(8,128)(2,1)S(1)} %all-to-all-done.4) | copy-start | bytes 393220
  179.6 39.6 %all-to-all-start.6 = ((bf16[8,96,192]{2,1,0:T(8,128)(2,1)}), bf16[8,96,192]{2,1,0:T(8,128)(2,1)S(1)}, u32[]{:S(2)}, u32[]{:S(2)}) async-start(bf16[8,96,192]{2,1,0:T(8,128)(2,1)} %out_grads.1), calls=%async_computation.7 | async-start | bytes 786432 | tf_op jit(solution)/shard_map/all_to_all | solution.py:1152
  219.2 6.3 %copy-start.14 = (bf16[2,32,768]{2,1,0:T(8,128)(2,1)S(1)}, bf16[2,32,768]{2,1,0:T(8,128)(2,1)}, u32[]{:S(2)}) copy-start(bf16[2,32,768]{2,1,0:T(8,128)(2,1)} %get-tuple-element.77) | copy-start | bytes 294916
  219.2 9.4 %copy-start.1 = (bf16[96,1728]{1,0:T(8,128)(2,1)S(1)}, bf16[96,1728]{1,0:T(8,128)(2,1)}, u32[]{:S(2)}) copy-start(bf16[96,1728]{1,0:T(8,128)(2,1)} %pad_maximum_fusion.1.weights_ref) | copy-start | bytes 995332
  219.2 29.0 %all-to-all-start.5 = ((bf16[8,224,256]{2,1,0:T(8,128)(2,1)}), bf16[8,224,256]{2,1,0:T(8,128)(2,1)S(1)}, u32[]{:S(2)}, u32[]{:S(2)}) async-start(bf16[8,224,256]{2,1,0:T(8,128)(2,1)} %chain_backward.1), calls=%async_computation.5 | async-start | bytes 1835008 | tf_op jit(solution)/shard_map/all_to_all | solution.py:1152
  228.6 1.0 copy-start.5
  248.2 14.4 %copy-start.6 = (f32[2,32,768]{2,1,0:T(8,128)S(1)}, f32[2,32,768]{2,1,0:T(8,128)}, u32[]{:S(2)}) copy-start(f32[2,32,768]{2,1,0:T(8,128)} %get-tuple-element.100.back_ref) | copy-start | bytes 589828
  249.8 0.8 copy-start.3
  250.7 11.9 %all-to-all-start.7 = ((bf16[4,80,768]{2,1,0:T(8,128)(2,1)}), bf16[4,80,768]{2,1,0:T(8,128)(2,1)S(1)}, u32[]{:S(2)}, u32[]{:S(2)}) async-start(bf16[4,80,768]{2,1,0:T(8,128)(2,1)} %copy-done.3), calls=%async_computation.8 | async-start | bytes 983040 | tf_op jit(solution)/shard_map/all_to_all | solution.py:1152
  256.4 7.8 %copy-start.15 = (f32[3,128]{1,0:T(4,128)}, f32[3,128]{1,0:T(4,128)S(1)}, u32[]{:S(2)}) copy-start(f32[3,128]{1,0:T(4,128)S(1)} %slice_reduce_fusion) | copy-start | bytes 4612
Sparse Core Ops, SparseCore 0:
  10.9 68.6 all-gather.5
  87.0 18.1 all-gather.7
  106.8 39.9 all-gather.9
  155.0 73.5 reduce-scatter.1

commit v8 on v7

--- a/solution.py
+++ b/solution.py
@@ -923,7 +923,6 @@
     normed_ref,
     back_ref,
     swiglu_ref,
-    cot_ref,
 ):
     tensor_count, head_count, seq_count, _, chunk = heads_ref.shape
     ff_local = swiglu_ref.shape[1]
@@ -931,7 +930,6 @@
     total = seq_count * chunk
     for sequence in range(seq_count):
         part = slice(sequence * rows, (sequence + 1) * rows)
-        other = slice((seq_count + sequence) * rows, (seq_count + sequence + 1) * rows)
         values = jnp.concatenate([rows_ref[index, part] for index in range(tensor_count)], axis=0)
         mixed = values.astype(f32)
         for index in range(tensor_count):
@@ -943,11 +941,8 @@
         normal, _ = layer_norm_parts(mixed)
         at = slice(sequence * chunk, (sequence + 1) * chunk)
         normed_ref[at] = (normal * gain_ref[...]).astype(bf16)
-        for index in range(tensor_count):
-            first = sequence * chunk + index * rows
-            cot_ref[first : first + rows] = rows_ref[index, other]
     normed = normed_ref[...]
-    cot = cot_ref[...]
+    cot = cotangent_rows(rows_ref, seq_count, rows)
     for first in range(0, ff_local, 256):
         at = slice(first, first + 256)
         beyond = slice(ff_local + first, ff_local + first + 256)
@@ -968,9 +963,21 @@
             terms_ref[index, seq_count + sequence] = down_term[first : first + rows]
 
 
-def feed_forward_grad_kernel(normed_ref, back_ref, swiglu_ref, cot_ref, grads_ref):
+def cotangent_rows(rows_ref, seq_count, rows):
+    count = rows_ref.shape[0]
+    parts = [
+        rows_ref[index, (seq_count + sequence) * rows : (seq_count + sequence + 1) * rows]
+        for sequence in range(seq_count)
+        for index in range(count)
+    ]
+    return jnp.concatenate(parts, axis=0)
+
+
+def feed_forward_grad_kernel(normed_ref, back_ref, swiglu_ref, rows_ref, grads_ref):
+    rows = normed_ref.shape[0] // (SEQS * rows_ref.shape[0])
     normed = jnp.transpose(normed_ref[...].astype(f32)).astype(bf16)
-    cot = jnp.transpose(cot_ref[...].astype(f32)).astype(bf16)
+    cot = cotangent_rows(rows_ref, SEQS, rows)
+    cot = jnp.transpose(cot.astype(f32)).astype(bf16)
     width = back_ref.shape[1]
     for first in range(0, width, 256):
         at = slice(first, first + 256)
@@ -1271,7 +1278,7 @@
     head_rows = lax.all_gather(head_local, "tensor", axis=0, tiled=False)
 
     group_rows = seq_count * chunk
-    terms, mixed, normed_ffn, back_gate_up, swiglu, group_cot = whole_call(
+    terms, mixed, normed_ffn, back_gate_up, swiglu = whole_call(
         feed_forward_kernel,
         "feed_forward",
         (head_rows, row_full, ffn_full, out_full, scale_ffn),
@@ -1281,7 +1288,6 @@
             shape((group_rows, width), bf16),
             shape((group_rows, 2 * ff_local), bf16),
             shape((group_rows, ff_local), bf16),
-            shape((group_rows, width), bf16),
         ),
         VMEM_BYTES,
     )
@@ -1289,7 +1295,7 @@
     (ffn_grads,) = whole_call(
         feed_forward_grad_kernel,
         "feed_forward_grads",
-        (normed_ffn, back_gate_up, swiglu, group_cot),
+        (normed_ffn, back_gate_up, swiglu, row_full),
         (shape((width, 3 * ff_local), bf16),),
         VMEM_BYTES,
     )

time: 272 us -> 272 us (level)
  no operation moved by 1% of the time
where the time goes in v8:
time: 272 us; the launch traced here: 271 us
  Pallas kernels  88 us (32%)
  waiting for transfers between devices  58.6 us (22%)
  blocking collectives  56.3 us (21%)
  starting transfers between devices  34.5 us (13%)
  local copies, waits for them, and re-layouts  16.4 us (6%)
  between operations  14.2 us (5%)
  other arithmetic  2.85 us (1%)
    all_to_all x8, waiting for transfers between devices, exchange(): return lax.all_to_all(values, axis, 0, 0, tiled=False)  47.7 us
    pallas_call x1, Pallas kernels, chain_backward(): pl.pallas_call(functools.partial(backward_kernel, inner_part, feature_par...  35.4 us
    all_to_all x8, starting transfers between devices, exchange(): return lax.all_to_all(values, axis, 0, 0, tiled=False)  32.3 us
    pallas_call x1, Pallas kernels, chain_forward(): pl.pallas_call(functools.partial(forward_kernel, inner_part, feature_part...  32.2 us
    all_gather x1, blocking collectives, local(): qkv_full = lax.all_gather(qkv_half, 'outer', axis=0, tiled=True)  28.7 us
    pallas_call x7, Pallas kernels, whole_call(): pl.pallas_call(kernel, in_specs=[spec(operand.shape) for operand in opera...  17 us
    unnamed x59, local copies, waits for them, and re-layouts  8.67 us
    all_gather x1, blocking collectives, local(): qkv_half = lax.all_gather(qkv_pack, 'inner', axis=0, tiled=True)  8.07 us
  transfers between devices with their start and end apart: 13, of which 8 were waited for; matrix products, arithmetic and copies ran while one was open for 4% of the time, Pallas kernels for 32%

profile of v8, /device:TPU:0, one launch (start us, length us, event | category | flops | bytes accessed | tf_op | source)
XLA Modules:
  0.0 270.8 jit_solution(15804039038907897091)
XLA Ops:
  7.2 1.0 copy.79
  8.2 0.9 copy.72
  9.1 1.7 pad_maximum_fusion.1.weights_ref
  11.0 0.9 broadcast_in_dim.4
  11.9 4.4 %all-to-all-start = ((bf16[4,128,768]{2,1,0:T(8,128)(2,1)}), bf16[4,128,768]{2,1,0:T(8,128)(2,1)S(1)}, u32[]{:S(2)}, u32[]{:S(2)}) async-start(bf16[4,128,768]{2,1,0:T(8,128)(2,1)} %broadcast_in_dim.4), calls=%async_computation | async-start | bytes 1572864 | tf_op jit(solution)/shard_map/all_to_all | solution.py:1159
  17.5 8.1 %all_gather.30 = bf16[192,581]{1,0:T(8,128)(2,1)S(1)} all-gather(bf16[96,581]{1,0:T(8,128)(2,1)S(1)} %fusion.1), channel_id=1, replica_groups=mesh['outer'=4,'inner'=2,'tensor'=4] {'inner'}, dimensions={0}, use_global_device_ids=true | all-gather | bytes 334656 | tf_op jit(solution)/shard_map/all_gather | solution.py:1230
  25.6 28.7 %all_gather.31.weights_ref = bf16[768,581]{1,0:T(8,128)(2,1)S(1)} all-gather(bf16[192,581]{1,0:T(8,128)(2,1)S(1)} %all_gather.30), channel_id=1, replica_groups=mesh['outer'=4,'inner'=2,'tensor'=4] {'outer'}, dimensions={0}, use_global_device_ids=true | all-gather | bytes 1115520 | tf_op jit(solution)/shard_map/all_gather | solution.py:1231
  54.6 5.1 %all_gather.32 = bf16[4,2,192]{2,1,0:T(2,128)(2,1)S(1)} all-gather(bf16[1,2,192]{2,1,0:T(2,128)(2,1)S(1)} %copy.78), channel_id=1, replica_groups=mesh['outer'=4,'inner'=2,'tensor'=4] {'tensor'}, dimensions={0}, use_global_device_ids=true | all-gather | bytes 3840 | tf_op jit(solution)/shard_map/all_gather | solution.py:1235
  59.9 1.8 projections.1
  61.7 0.8 copy-done.2
  62.5 0.7 copy-done.4
  63.2 4.7 %all-to-all-start.1 = ((bf16[8,128,256]{2,1,0:T(8,128)(2,1)}), bf16[8,128,256]{2,1,0:T(8,128)(2,1)S(1)}, u32[]{:S(2)}, u32[]{:S(2)}) async-start(bf16[8,128,256]{2,1,0:T(8,128)(2,1)} %copy-done.2), calls=%async_computation.1 | async-start | bytes 1048576 | tf_op jit(solution)/shard_map/all_to_all | solution.py:1159
  68.0 1.1 constant_dynamic-slice_fusion.4
  69.1 2.0 collective-permute-start
  71.1 8.0 %collective-permute-done = bf16[1,128,768]{2,1,0:T(8,128)(2,1)S(1)} collective-permute-done((bf16[1,128,768]{2,1,0:T(8,128)(2,1)S(1)}, bf16[1,128,768]{2,1,0:T(8,128)(2,1)S(1)}, u32[]{:S(2)}, u32[]{:S(2)}) %collective-permute-start) | collective-permute-done | bytes 196640 | tf_op jit(solution)/shard_map/ppermute | solution.py:1268
  79.1 0.8 pad_maximum_fusion
  79.9 1.8 slice.77
  81.7 5.2 %all-to-all-done.1.packed_ref = bf16[8,128,256]{2,1,0:T(8,128)(2,1)S(1)} async-done(((bf16[8,128,256]{2,1,0:T(8,128)(2,1)}), bf16[8,128,256]{2,1,0:T(8,128)(2,1)S(1)}, u32[]{:S(2)}, u32[]{:S(2)}) %all-to-all-start.1) | async-done | bytes 524320 | tf_op jit(solution)/shard_map/all_to_all | solution.py:1159
  86.9 0.7 all-gather.10.cloned.1.call-update
  87.6 32.2 %chain_forward.1 = (bf16[8,64,128]{2,1,0:T(8,128)(2,1)}, bf16[1024,256]{1,0:T(8,128)(2,1)}, bf16[1024,256]{1,0:T(8,128)(2,1)}, f32[1024,256]{1,0:T(8,128)}, f32[...) custom-call(bf16[8,128,256]{2,1,0:T(8,128)(2,1)} %copy-done.9), custom_call_target="tpu_custom_call" | custom-call | flops 27000000512 | bytes 4194304 | tf_op jit(solution)/shard_map/chain_forward/pallas_call | solution.py:705
  119.9 3.4 %all-to-all-start.2 = ((bf16[8,64,128]{2,1,0:T(8,128)(2,1)}), bf16[8,64,128]{2,1,0:T(8,128)(2,1)S(1)}, u32[]{:S(2)}, u32[]{:S(2)}) async-start(bf16[8,64,128]{2,1,0:T(8,128)(2,1)} %get-tuple-element.66), calls=%async_computation.2 | async-start | bytes 262144 | tf_op jit(solution)/shard_map/all_to_all | solution.py:1159
  123.9 9.8 %all-to-all-done.2 = bf16[8,64,128]{2,1,0:T(8,128)(2,1)S(1)} async-done(((bf16[8,64,128]{2,1,0:T(8,128)(2,1)}), bf16[8,64,128]{2,1,0:T(8,128)(2,1)S(1)}, u32[]{:S(2)}, u32[]{:S(2)}) %all-to-all-start.2) | async-done | bytes 131104 | tf_op jit(solution)/shard_map/all_to_all | solution.py:1159
  133.8 6.9 %all_gather.34.heads_ref = bf16[4,3,2,64,128]{4,3,2,1,0:T(8,128)(2,1)} all-gather(bf16[1,3,2,64,128]{4,3,2,1,0:T(8,128)(2,1)S(1)} %bitcast.49), channel_id=1, replica_groups=mesh['outer'=4,'inner'=2,'tensor'=4] {'tensor'}, dimensions={0}, use_global_device_ids=true | all-gather | bytes 491520 | tf_op jit(solution)/shard_map/all_gather | solution.py:1278
  140.7 6.7 %feed_forward.1 = (bf16[4,4,32,768]{3,2,1,0:T(8,128)(2,1)}, f32[4,2,32,768]{3,2,1,0:T(8,128)}, bf16[256,768]{1,0:T(8,128)(2,1)}, bf16[256,1024]{1,0:T(8,128)(2,1)}, bf16[256,512]{1,0:T(8,128)(2,1)}) custom-call(bf16[4,3,2,64,128]{4,3,2,1,0:T(8,128)(2,1)} %all_gather.34.heads_ref, bf16[4,128,768]{2,1,0:T(8,128)(2,1)} %copy-done, ...), custom_call_target="tpu_custom_call" | custom-call | tf_op jit(solution)/shard_map/feed_forward/pallas_call | solution.py:1144
  147.4 3.5 %all-to-all-start.3 = ((bf16[4,4,32,768]{3,2,1,0:T(8,128)(2,1)}), bf16[4,4,32,768]{3,2,1,0:T(8,128)(2,1)S(1)}, u32[]{:S(2)}, u32[]{:S(2)}) async-start(bf16[4,4,32,768]{3,2,1,0:T(8,128)(2,1)} %get-tuple-element.68), calls=%async_computation.3 | async-start | bytes 1572864 | tf_op jit(solution)/shard_map/all_to_all | solution.py:1159
  151.0 3.7 %feed_forward_grads.1 = bf16[768,1536]{1,0:T(8,128)(2,1)} custom-call(bf16[256,768]{1,0:T(8,128)(2,1)} %get-tuple-element.70.normed_ref, bf16[256,1024]{1,0:T(8,128)(2,1)} %get-tuple-element.71.back_ref, bf16[256,512]{1,0:T(8,128)(2,1)} %get-tuple-element.72.swiglu_ref, bf16[4,128,768]{2,1,0:T(8,128)(2,1)} %copy-done), custom_call_target="tpu_custom_call" | custom-call | tf_op jit(solution)/shard_map/feed_forward_grads/pallas_call | solution.py:1144
  154.7 7.8 %all-to-all-done.3.terms_ref = bf16[4,4,32,768]{3,2,1,0:T(8,128)(2,1)S(1)} async-done(((bf16[4,4,32,768]{3,2,1,0:T(8,128)(2,1)}), bf16[4,4,32,768]{3,2,1,0:T(8,128)(2,1)S(1)}, u32[]{:S(2)}, u32[]{:S(2)}) %all-to-all-start.3) | async-done | bytes 786464 | tf_op jit(solution)/shard_map/all_to_all | solution.py:1159
  162.5 0.9 copy-done.7
  163.4 3.4 %feed_forward_back.1 = (f32[2,32,768]{2,1,0:T(8,128)}, bf16[2,32,768]{2,1,0:T(8,128)(2,1)}, bf16[2,32,768]{2,1,0:T(8,128)(2,1)}, bf16[32,16,128]{2,1,0:T(8,128)(2,1)}) custom-call(s32[1]{0:T(128)} %bitcast.rank_ref, bf16[4,4,32,768]{3,2,1,0:T(8,128)(2,1)} %copy-done.7, f32[4,2,32,768]{3,2,1,0:T(8,128)} %get-tuple-element.74.mixed_ref, ...), custom_call_target="tpu_custom_call" | custom-call | tf_op jit(solution)/shard_map/feed_forward_back/pallas_call | solution.py:1315
  166.9 2.6 all-to-all-start.4
  169.4 7.5 %all_gather.39.grads_ref = bf16[2,128,768]{2,1,0:T(8,128)(2,1)S(1)} all-gather(bf16[2,32,768]{2,1,0:T(8,128)(2,1)} %get-tuple-element.80), channel_id=1, replica_groups=mesh['outer'=4,'inner'=2,'tensor'=4] {'tensor'}, dimensions={1}, use_global_device_ids=true | all-gather | bytes 491520 | tf_op jit(solution)/shard_map/all_gather | solution.py:1337
  176.9 1.2 out_grads.1
  178.1 1.5 all-to-all-done.4
  179.5 4.2 %all-to-all-start.6 = ((bf16[8,96,192]{2,1,0:T(8,128)(2,1)}), bf16[8,96,192]{2,1,0:T(8,128)(2,1)S(1)}, u32[]{:S(2)}, u32[]{:S(2)}) async-start(bf16[8,96,192]{2,1,0:T(8,128)(2,1)} %out_grads.1), calls=%async_computation.7 | async-start | bytes 786432 | tf_op jit(solution)/shard_map/all_to_all | solution.py:1159
  183.8 35.4 %chain_backward.1 = bf16[8,224,256]{2,1,0:T(8,128)(2,1)} custom-call(s32[1]{0:T(128)} %bitcast.22.sequence_ref, bf16[8,128,256]{2,1,0:T(8,128)(2,1)} %copy-done.9, bf16[4,2,128,768]{3,2,1,0:T(8,128)(2,1)} %bitcast.69, bf16[8,4,16,128]{3,2,1,0:T(8,128)(2,1)} %bitcast.64, bf16[1024,256]{1,0:T(8,128)(2,1)} %get-tuple-element.82.next_act.now_act, ...), custom_call_target="tpu_custom_call" | custom-call | flops 27000000512 | bytes 4194304 | tf_op jit(solution)/shard_map/chain_backward/pallas_call | solution.py:790
  219.2 6.1 %all-to-all-start.5 = ((bf16[8,224,256]{2,1,0:T(8,128)(2,1)}), bf16[8,224,256]{2,1,0:T(8,128)(2,1)S(1)}, u32[]{:S(2)}, u32[]{:S(2)}) async-start(bf16[8,224,256]{2,1,0:T(8,128)(2,1)} %chain_backward.1), calls=%async_computation.5 | async-start | bytes 1835008 | tf_op jit(solution)/shard_map/all_to_all | solution.py:1159
  225.5 0.7 copy.75
  226.3 2.1 reduce-scatter.2.cloned.1.call-done.sums_ref
  228.4 1.0 copy-done.5
  229.4 1.0 matrix_outputs.1
  230.4 17.9 %all-to-all-done.5.received_ref = bf16[8,224,256]{2,1,0:T(8,128)(2,1)S(1)} async-done(((bf16[8,224,256]{2,1,0:T(8,128)(2,1)}), bf16[8,224,256]{2,1,0:T(8,128)(2,1)S(1)}, u32[]{:S(2)}, u32[]{:S(2)}) %all-to-all-start.5) | async-done | bytes 917536 | tf_op jit(solution)/shard_map/all_to_all | solution.py:1159
  248.3 1.6 tail.1
  249.8 0.8 copy-done.3
  250.7 3.5 %all-to-all-start.7 = ((bf16[4,80,768]{2,1,0:T(8,128)(2,1)}), bf16[4,80,768]{2,1,0:T(8,128)(2,1)S(1)}, u32[]{:S(2)}, u32[]{:S(2)}) async-start(bf16[4,80,768]{2,1,0:T(8,128)(2,1)} %copy-done.3), calls=%async_computation.8 | async-start | bytes 983040 | tf_op jit(solution)/shard_map/all_to_all | solution.py:1159
  254.8 0.7 copy.76
  255.5 0.7 copy.77
  257.1 5.6 %all-to-all-done.7.terms_ref = bf16[4,80,768]{2,1,0:T(8,128)(2,1)S(1)} async-done(((bf16[4,80,768]{2,1,0:T(8,128)(2,1)}), bf16[4,80,768]{2,1,0:T(8,128)(2,1)S(1)}, u32[]{:S(2)}, u32[]{:S(2)}) %all-to-all-start.7) | async-done | bytes 491552 | tf_op jit(solution)/shard_map/all_to_all | solution.py:1159
  262.7 1.0 input_grad.1
  (92 shorter events, 5.0 us)
Async XLA Ops:
  7.2 3.6 %copy-start.12 = (bf16[32,2,768]{2,1,0:T(2,128)(2,1)S(1)}, bf16[32,2,768]{2,1,0:T(2,128)(2,1)}, u32[]{:S(2)}) copy-start(bf16[32,2,768]{2,1,0:T(2,128)(2,1)} %param.15) | copy-start | bytes 294916
  7.2 3.7 %copy-start.13 = (bf16[32,2,768]{2,1,0:T(2,128)(2,1)S(1)}, bf16[32,2,768]{2,1,0:T(2,128)(2,1)}, u32[]{:S(2)}) copy-start(bf16[32,2,768]{2,1,0:T(2,128)(2,1)} %param.29) | copy-start | bytes 294916
  7.2 72.7 %all-gather.6.cloned.1.call-start = ((), (), s32[]{:S(2)}) async-start(), calls=%async_computation.9 | async-start | bytes 3096576 | tf_op jit(solution)/shard_map/all_gather | solution.py:1243
  10.9 5.4 %copy-start.10 = (bf16[96,3,192]{2,0,1:T(8,128)(2,1)S(1)}, bf16[96,3,192]{2,0,1:T(8,128)(2,1)}, u32[]{:S(2)}) copy-start(bf16[96,3,192]{2,0,1:T(8,128)(2,1)} %param.18) | copy-start | bytes 331780
  10.9 5.6 %copy-start.8 = (bf16[32,2,768]{2,0,1:T(8,128)(2,1)}, bf16[32,2,768]{2,0,1:T(8,128)(2,1)S(1)}, u32[]{:S(2)}) copy-start(bf16[32,2,768]{2,0,1:T(8,128)(2,1)S(1)} %copy.84) | copy-start | bytes 294916
  10.9 5.7 %copy-start.18 = (bf16[96,3]{0,1:T(4,128)(2,1)S(1)}, bf16[96,3]{0,1:T(4,128)(2,1)}, u32[]{:S(2)}) copy-start(bf16[96,3]{0,1:T(4,128)(2,1)} %param.19) | copy-start | bytes 1732
  10.9 5.8 %copy-start.23 = (bf16[24]{0:T(256)(128)(2,1)S(1)}, bf16[24]{0:T(256)(128)(2,1)}, u32[]{:S(2)}) copy-start(bf16[24]{0:T(256)(128)(2,1)} %param.17) | copy-start | bytes 148
  11.0 5.8 %copy-start.24 = (bf16[24]{0:T(256)(128)(2,1)S(1)}, bf16[24]{0:T(256)(128)(2,1)}, u32[]{:S(2)}) copy-start(bf16[24]{0:T(256)(128)(2,1)} %param.16) | copy-start | bytes 148
  11.0 5.9 %copy-start.16 = (bf16[3,32,64]{2,1,0:T(8,128)(2,1)S(1)}, bf16[3,32,64]{2,1,0:T(8,128)(2,1)}, u32[]{:S(2)}) copy-start(bf16[3,32,64]{2,1,0:T(8,128)(2,1)} %param.25) | copy-start | bytes 36868
  11.0 5.9 %copy-start.17 = (bf16[3,64,32]{1,2,0:T(8,128)(2,1)S(1)}, bf16[3,64,32]{1,2,0:T(8,128)(2,1)}, u32[]{:S(2)}) copy-start(bf16[3,64,32]{1,2,0:T(8,128)(2,1)} %param.23) | copy-start | bytes 36868
  11.9 5.2 %copy-start.19 = (bf16[3,8]{1,0:T(4,128)(2,1)S(1)}, bf16[3,8]{1,0:T(4,128)(2,1)}, u32[]{:S(2)}) copy-start(bf16[3,8]{1,0:T(4,128)(2,1)} %param.28) | copy-start | bytes 148
  11.9 5.2 %copy-start.20 = (bf16[3,8]{1,0:T(4,128)(2,1)S(1)}, bf16[3,8]{1,0:T(4,128)(2,1)}, u32[]{:S(2)}) copy-start(bf16[3,8]{1,0:T(4,128)(2,1)} %param.27) | copy-start | bytes 148
  11.9 5.2 %copy-start.21 = (bf16[3,8]{1,0:T(4,128)(2,1)S(1)}, bf16[3,8]{1,0:T(4,128)(2,1)}, u32[]{:S(2)}) copy-start(bf16[3,8]{1,0:T(4,128)(2,1)} %param.26) | copy-start | bytes 148
  11.9 5.2 %copy-start.22 = (bf16[3,32]{1,0:T(4,128)(2,1)S(1)}, bf16[3,32]{1,0:T(4,128)(2,1)}, u32[]{:S(2)}) copy-start(bf16[3,32]{1,0:T(4,128)(2,1)} %param.24) | copy-start | bytes 580
  11.9 42.4 %all-to-all-start = ((bf16[4,128,768]{2,1,0:T(8,128)(2,1)}), bf16[4,128,768]{2,1,0:T(8,128)(2,1)S(1)}, u32[]{:S(2)}, u32[]{:S(2)}) async-start(bf16[4,128,768]{2,1,0:T(8,128)(2,1)} %broadcast_in_dim.4), calls=%async_computation | async-start | bytes 1572864 | tf_op jit(solution)/shard_map/all_to_all | solution.py:1159
  54.4 8.9 %copy-start = (bf16[4,128,768]{2,1,0:T(8,128)(2,1)}, bf16[4,128,768]{2,1,0:T(8,128)(2,1)S(1)}, u32[]{:S(2)}) copy-start(bf16[4,128,768]{2,1,0:T(8,128)(2,1)S(1)} %all-to-all-done.rows_ref) | copy-start | bytes 2359300
  61.7 0.8 copy-start.2
  62.5 0.7 copy-start.4
  63.2 23.6 %all-to-all-start.1 = ((bf16[8,128,256]{2,1,0:T(8,128)(2,1)}), bf16[8,128,256]{2,1,0:T(8,128)(2,1)S(1)}, u32[]{:S(2)}, u32[]{:S(2)}) async-start(bf16[8,128,256]{2,1,0:T(8,128)(2,1)} %copy-done.2), calls=%async_computation.1 | async-start | bytes 1048576 | tf_op jit(solution)/shard_map/all_to_all | solution.py:1159
  68.0 72.7 %all-gather.8.cloned.1.call-start = ((), (), s32[]{:S(2)}) async-start(), calls=%async_computation.11 | async-start | bytes 1966080 | tf_op jit(solution)/shard_map/all_gather | solution.py:1272
  69.1 10.0 %collective-permute-start = (bf16[1,128,768]{2,1,0:T(8,128)(2,1)S(1)}, bf16[1,128,768]{2,1,0:T(8,128)(2,1)S(1)}, u32[]{:S(2)}, u32[]{:S(2)}) collective-permute-start(bf16[1,128,768]{2,1,0:T(8,128)(2,1)S(1)} %get-tuple-element.153), channel_id=1, source_target_pairs={{0,4},{4,0},{1,5},{5,1},{2,6},{6,2},{3,7},{7,3},{8,12},{12,8},{9,1... | collective-permute-start | bytes 589832 | tf_op jit(solution)/shard_map/ppermute | solution.py:1268
  86.8 0.8 copy-start.9
  86.8 75.7 %all-gather.10.cloned.1.call-start = ((), (), s32[]{:S(2)}) async-start(), calls=%async_computation.12 | async-start | bytes 1966080 | tf_op jit(solution)/shard_map/all_gather | solution.py:1271
  119.9 13.9 %all-to-all-start.2 = ((bf16[8,64,128]{2,1,0:T(8,128)(2,1)}), bf16[8,64,128]{2,1,0:T(8,128)(2,1)S(1)}, u32[]{:S(2)}, u32[]{:S(2)}) async-start(bf16[8,64,128]{2,1,0:T(8,128)(2,1)} %get-tuple-element.66), calls=%async_computation.2 | async-start | bytes 262144 | tf_op jit(solution)/shard_map/all_to_all | solution.py:1159
  147.4 15.1 %all-to-all-start.3 = ((bf16[4,4,32,768]{3,2,1,0:T(8,128)(2,1)}), bf16[4,4,32,768]{3,2,1,0:T(8,128)(2,1)S(1)}, u32[]{:S(2)}, u32[]{:S(2)}) async-start(bf16[4,4,32,768]{3,2,1,0:T(8,128)(2,1)} %get-tuple-element.68), calls=%async_computation.3 | async-start | bytes 1572864 | tf_op jit(solution)/shard_map/all_to_all | solution.py:1159
  150.9 77.5 %reduce-scatter.2.cloned.1.call-start = ((), (), s32[]{:S(2)}) async-start(), calls=%async_computation.10 | async-start | bytes 2654208 | tf_op jit(solution)/shard_map/reduce_scatter | solution.py:1302
  162.5 0.9 copy-start.7
  166.9 12.7 %all-to-all-start.4 = ((bf16[32,16,128]{2,1,0:T(8,128)(2,1)}), bf16[32,16,128]{2,1,0:T(8,128)(2,1)S(1)}, u32[]{:S(2)}, u32[]{:S(2)}) async-start(bf16[32,16,128]{2,1,0:T(8,128)(2,1)} %get-tuple-element.79), calls=%async_computation.4 | async-start | bytes 262144 | tf_op jit(solution)/shard_map/all_to_all | solution.py:1159
  179.5 4.2 %copy-start.11 = (bf16[32,16,128]{2,1,0:T(8,128)(2,1)}, bf16[32,16,128]{2,1,0:T(8,128)(2,1)S(1)}, u32[]{:S(2)}) copy-start(bf16[32,16,128]{2,1,0:T(8,128)(2,1)S(1)} %all-to-all-done.4) | copy-start | bytes 393220
  179.5 39.7 %all-to-all-start.6 = ((bf16[8,96,192]{2,1,0:T(8,128)(2,1)}), bf16[8,96,192]{2,1,0:T(8,128)(2,1)S(1)}, u32[]{:S(2)}, u32[]{:S(2)}) async-start(bf16[8,96,192]{2,1,0:T(8,128)(2,1)} %out_grads.1), calls=%async_computation.7 | async-start | bytes 786432 | tf_op jit(solution)/shard_map/all_to_all | solution.py:1159
  219.2 6.3 %copy-start.14 = (bf16[2,32,768]{2,1,0:T(8,128)(2,1)S(1)}, bf16[2,32,768]{2,1,0:T(8,128)(2,1)}, u32[]{:S(2)}) copy-start(bf16[2,32,768]{2,1,0:T(8,128)(2,1)} %get-tuple-element.75) | copy-start | bytes 294916
  219.2 9.2 %copy-start.1 = (bf16[96,1728]{1,0:T(8,128)(2,1)S(1)}, bf16[96,1728]{1,0:T(8,128)(2,1)}, u32[]{:S(2)}) copy-start(bf16[96,1728]{1,0:T(8,128)(2,1)} %pad_maximum_fusion.1.weights_ref) | copy-start | bytes 995332
  219.2 29.1 %all-to-all-start.5 = ((bf16[8,224,256]{2,1,0:T(8,128)(2,1)}), bf16[8,224,256]{2,1,0:T(8,128)(2,1)S(1)}, u32[]{:S(2)}, u32[]{:S(2)}) async-start(bf16[8,224,256]{2,1,0:T(8,128)(2,1)} %chain_backward.1), calls=%async_computation.5 | async-start | bytes 1835008 | tf_op jit(solution)/shard_map/all_to_all | solution.py:1159
  228.4 1.0 copy-start.5
  248.3 14.4 %copy-start.6 = (f32[2,32,768]{2,1,0:T(8,128)S(1)}, f32[2,32,768]{2,1,0:T(8,128)}, u32[]{:S(2)}) copy-start(f32[2,32,768]{2,1,0:T(8,128)} %get-tuple-element.98.back_ref) | copy-start | bytes 589828
  249.8 0.8 copy-start.3
  250.7 11.9 %all-to-all-start.7 = ((bf16[4,80,768]{2,1,0:T(8,128)(2,1)}), bf16[4,80,768]{2,1,0:T(8,128)(2,1)S(1)}, u32[]{:S(2)}, u32[]{:S(2)}) async-start(bf16[4,80,768]{2,1,0:T(8,128)(2,1)} %copy-done.3), calls=%async_computation.8 | async-start | bytes 983040 | tf_op jit(solution)/shard_map/all_to_all | solution.py:1159
  256.4 7.8 %copy-start.15 = (f32[3,128]{1,0:T(4,128)}, f32[3,128]{1,0:T(4,128)S(1)}, u32[]{:S(2)}) copy-start(f32[3,128]{1,0:T(4,128)S(1)} %slice_reduce_fusion) | copy-start | bytes 4612
Sparse Core Ops, SparseCore 0:
  10.9 68.6 all-gather.5
  87.0 18.1 all-gather.7
  106.8 39.9 all-gather.9
  154.9 73.4 reduce-scatter.1
